TPU v7x, 512 devices: a whole 4x8x8 slice. The times are simulated.
512 devices in a mesh: phase: 8 (over x, core), expert: 64 (over y, z).
Axes of the slice: x: 4, y: 8, z: 8, core: 2. Of those that a mesh axis runs over, the one named last changes fastest.
Arguments:
- fwd_acts: bfloat16 [8, 8192, 2048], P('phase', 'expert'), may hold values from -6 to 6
- fwd_routes: int32 [8, 8192, 1], P('phase', 'expert'), may hold values from 0 to 7; in each aligned block of 128 rows (0 to 127, 128 to 255, ..., all dimensions but the last counted through in order) at most 18 rows name the same one
- fwd_weights: float32 [8, 8192, 1], P('phase', 'expert'), may hold values from 0.1 to 1
- fwd_lengths: int32 [8, 16], P('phase'), may hold values from 1 to 2048, 8192 in all within a row
- fwd_tenants: int32 [8, 16], P('phase'), may hold values from 0 to 1
- bwd_acts: bfloat16 [8, 8192, 2048], P('phase', 'expert'), may hold values from -6 to 6
- bwd_routes: int32 [8, 8192, 1], P('phase', 'expert'), may hold values from 0 to 7; in each aligned block of 128 rows (0 to 127, 128 to 255, ..., all dimensions but the last counted through in order) at most 18 rows name the same one
- bwd_weights: float32 [8, 8192, 1], P('phase', 'expert'), may hold values from 0.1 to 1
- bwd_lengths: int32 [8, 16], P('phase'), may hold values from 1 to 2048, 8192 in all within a row
- bwd_tenants: int32 [8, 16], P('phase'), may hold values from 0 to 1
- bwd_cotangent: bfloat16 [8, 8192, 2048], P('phase', 'expert'), may hold values from -6 to 6
- prompts: bfloat16 [8, 2, 10, 2048], P('phase'), may hold values from -6 to 6
- norm_gain: float32 [8, 2048], P('phase'), may hold values from 0.1 to 1.9
- w_gate: bfloat16 [8, 64, 2048, 128], P('phase', 'expert'), may hold values from -0.125 to 0.125
- w_up: bfloat16 [8, 64, 2048, 128], P('phase', 'expert'), may hold values from -0.125 to 0.125
- w_down: bfloat16 [8, 64, 128, 2048], P('phase', 'expert'), may hold values from -0.1875 to 0.1875
Outputs:
- next_acts: bfloat16 [8, 8192, 2048], P('phase', 'expert')
- prev_grads: bfloat16 [8, 8192, 2048], P('phase', 'expert')
- prompt_grads: bfloat16 [8, 2, 10, 2048], P('phase')
Inputs may be any that keep to these rules, and one draw needn't show every extreme that they name: `fwd_routes`: each row names 1 different experts; among the 128 tokens of one device no expert is named by more than 18 rows, a bound that some block reaches. `bwd_routes`: each row names 1 different experts; among the 128 tokens of one device no expert is named by more than 18 rows, a bound that some block reaches.
All inputs are finite; a program needn't handle non-finite values.
Results may differ from a plain program's by a relative error of at most 0.008.
Values may be sent and summed in bfloat16 or wider, within the bound.
No kernel may reach another device: no remote copies, remote signals or barrier semaphores. Data moves between devices by JAX's collectives and lax.ppermute only.
A program may use at most 128 MiB of HBM per device.

v0:
```python
import jax
import jax.numpy as jnp
from jax import lax
from jax.sharding import PartitionSpec as P

EXPERTS = 8
TENANTS = 2
PLEN = 10
CAP = 18


EPS = 1e-06


def shifted(block, axis, distance):
    devices = range(lax.axis_size(axis))
    route = [(i - distance, i) for i in devices if i - distance in devices]
    return lax.ppermute(block, axis, route)


def token_layout(lengths, tenants, tok_count):
    first_row = lax.axis_index("expert") * tok_count
    token_index = first_row + jnp.arange(tok_count, dtype=jnp.int32)
    seg_ends = jnp.cumsum(lengths)
    seg_starts = seg_ends - lengths
    member = (seg_starts[None, :] <= token_index[:, None]).astype(jnp.int32)
    segment = jnp.sum(member, axis=1) - 1
    chosen = (jnp.arange(lengths.shape[0], dtype=jnp.int32)[None, :] == segment[:, None]).astype(
        jnp.int32
    )
    position = token_index - jnp.sum(chosen * seg_starts[None, :], axis=1)
    tenant = jnp.sum(chosen * tenants[None, :], axis=1)
    return (position, tenant)


def prepare(acts, lengths, tenants, prompt_table, gain_row):
    tok_count = acts.shape[0]
    position, tenant = token_layout(lengths, tenants, tok_count)
    prompt_slot = position < PLEN
    flat_index = tenant * PLEN + jnp.minimum(position, PLEN - 1)
    selector = (
        flat_index[:, None] == jnp.arange(TENANTS * PLEN, dtype=jnp.int32)[None, :]
    ) & prompt_slot[:, None]
    flat_table = prompt_table.reshape(TENANTS * PLEN, prompt_table.shape[-1])
    prompt_rows = jnp.dot(
        selector.astype(jnp.bfloat16), flat_table, preferred_element_type=jnp.float32
    ).astype(jnp.bfloat16)
    inputs = jnp.where(prompt_slot[:, None], prompt_rows, acts)
    widened = inputs.astype(jnp.float32)
    inv_scale = lax.rsqrt(jnp.mean(widened * widened, axis=1, keepdims=True) + EPS)
    normed = (widened * inv_scale * gain_row[None, :]).astype(jnp.bfloat16)
    return (selector, widened, inv_scale, normed, prompt_slot)


def routing(routes, weights):
    tok_count, top_count = routes.shape
    flattened = routes.reshape(tok_count * top_count)
    onehot = (flattened[:, None] == jnp.arange(EXPERTS, dtype=jnp.int32)[None, :]).astype(jnp.int32)
    ranking = jnp.sum((jnp.cumsum(onehot, axis=0) - 1) * onehot, axis=1)
    target = (flattened * CAP + ranking).reshape(tok_count, top_count)
    matches = target[:, :, None] == jnp.arange(EXPERTS * CAP, dtype=jnp.int32)[None, None, :]
    picker = jnp.transpose(jnp.any(matches, axis=1).astype(jnp.bfloat16))
    mixing = jnp.sum(jnp.where(matches, weights[:, :, None], 0.0), axis=1)
    return (picker, mixing)


def dispatch(picker, sources):
    shards = lax.axis_size("expert") // EXPERTS
    stacked, tok_count, model_width = sources.shape
    packed = jnp.einsum("qn,mnd->mqd", picker, sources, preferred_element_type=jnp.float32).astype(
        jnp.bfloat16
    )
    packed = jnp.broadcast_to(
        packed.reshape(stacked, 1, EXPERTS * CAP, model_width),
        (stacked, shards, EXPERTS * CAP, model_width),
    )
    packed = packed.reshape(stacked, shards * EXPERTS, CAP, model_width)
    received = lax.all_to_all(packed, "expert", split_axis=1, concat_axis=1, tiled=True)
    return received


def give_back(partial_value):
    shards = lax.axis_size("expert") // EXPERTS
    returned = lax.all_to_all(partial_value, "expert", split_axis=0, concat_axis=0, tiled=True)
    return jnp.sum(
        returned.reshape(shards, EXPERTS * CAP, partial_value.shape[-1]).astype(jnp.float32), axis=0
    )


def expert_forward(slot_rows, gate_weight, up_weight, down_weight):
    gate_pre = jnp.dot(slot_rows, gate_weight, preferred_element_type=jnp.float32)
    upper = jnp.dot(slot_rows, up_weight, preferred_element_type=jnp.float32)
    hidden = (jax.nn.silu(gate_pre) * upper).astype(jnp.bfloat16)
    return jnp.dot(hidden, down_weight, preferred_element_type=jnp.float32).astype(jnp.bfloat16)


def expert_backward(slot_rows, slot_grads, gate_weight, up_weight, down_weight):
    gate_pre = jnp.dot(slot_rows, gate_weight, preferred_element_type=jnp.float32)
    upper = jnp.dot(slot_rows, up_weight, preferred_element_type=jnp.float32)
    contract = (((1,), (1,)), ((), ()))
    hidden_grad = lax.dot_general(
        slot_grads, down_weight, contract, preferred_element_type=jnp.float32
    )
    sigmoid_gate = jax.nn.sigmoid(gate_pre)
    gate_grad = (
        hidden_grad * upper * sigmoid_gate * (1.0 + gate_pre * (1.0 - sigmoid_gate))
    ).astype(jnp.bfloat16)
    up_grad = (hidden_grad * (gate_pre * sigmoid_gate)).astype(jnp.bfloat16)
    back_rows = lax.dot_general(
        gate_grad, gate_weight, contract, preferred_element_type=jnp.float32
    )
    back_rows = back_rows + lax.dot_general(
        up_grad, up_weight, contract, preferred_element_type=jnp.float32
    )
    return back_rows.astype(jnp.bfloat16)


def on_device(
    fwd_acts,
    fwd_routes,
    fwd_weights,
    fwd_lengths,
    fwd_tenants,
    bwd_acts,
    bwd_routes,
    bwd_weights,
    bwd_lengths,
    bwd_tenants,
    bwd_cotangent,
    prompts,
    norm_gain,
    w_gate,
    w_up,
    w_down,
):
    gate_weight = w_gate[0, 0]
    up_weight = w_up[0, 0]
    down_weight = w_down[0, 0]
    gain_row = norm_gain[0]
    prompt_table = prompts[0]
    model_width = fwd_acts.shape[-1]
    fwd_select, fwd_wide, fwd_scale, fwd_normed, fwd_slot = prepare(
        fwd_acts[0], fwd_lengths[0], fwd_tenants[0], prompt_table, gain_row
    )
    fwd_picker, fwd_mixing = routing(fwd_routes[0], fwd_weights[0])
    arrived = dispatch(fwd_picker, fwd_normed[None])
    senders = arrived.shape[1]
    partial_value = expert_forward(
        arrived[0].reshape(senders * CAP, model_width), gate_weight, up_weight, down_weight
    )
    summed = give_back(partial_value.reshape(senders, CAP, model_width))
    mixed_out = fwd_wide + jnp.dot(fwd_mixing, summed, precision=lax.Precision.HIGHEST)
    leaving = mixed_out.astype(jnp.bfloat16)
    next_acts = shifted(leaving, "phase", 1)
    bwd_select, bwd_wide, bwd_scale, bwd_normed, bwd_slot = prepare(
        bwd_acts[0], bwd_lengths[0], bwd_tenants[0], prompt_table, gain_row
    )
    bwd_picker, bwd_mixing = routing(bwd_routes[0], bwd_weights[0])
    cotangent = bwd_cotangent[0]
    arrived_back = dispatch(bwd_picker, jnp.stack([bwd_normed, cotangent]))
    partial_back = expert_backward(
        arrived_back[0].reshape(senders * CAP, model_width),
        arrived_back[1].reshape(senders * CAP, model_width),
        gate_weight,
        up_weight,
        down_weight,
    )
    summed_back = give_back(partial_back.reshape(senders, CAP, model_width))
    normed_grad = jnp.dot(bwd_mixing, summed_back, precision=lax.Precision.HIGHEST)
    scaled = normed_grad * gain_row[None, :]
    inner = jnp.mean(bwd_wide * scaled, axis=1, keepdims=True)
    input_grad = (
        cotangent.astype(jnp.float32) + bwd_scale * scaled - bwd_wide * bwd_scale**3 * inner
    )
    to_prev = jnp.where(bwd_slot[:, None], 0.0, input_grad).astype(jnp.bfloat16)
    prev_grads = shifted(to_prev, "phase", -1)
    local_sums = jnp.dot(
        jnp.transpose(bwd_select.astype(jnp.float32)), input_grad, precision=lax.Precision.HIGHEST
    )
    totals = lax.psum(local_sums, "expert")
    prompt_grads = totals.reshape(1, TENANTS, PLEN, model_width).astype(jnp.bfloat16)
    return (next_acts[None], prev_grads[None], prompt_grads)


def solution(mesh):
    placed = (
        P("phase", "expert", None),
        P("phase", "expert", None),
        P("phase", "expert", None),
        P("phase", None),
        P("phase", None),
        P("phase", "expert", None),
        P("phase", "expert", None),
        P("phase", "expert", None),
        P("phase", None),
        P("phase", None),
        P("phase", "expert", None),
        P("phase", None, None, None),
        P("phase", None),
        P("phase", "expert", None, None),
        P("phase", "expert", None, None),
        P("phase", "expert", None, None),
    )
    return jax.shard_map(
        on_device,
        mesh=mesh,
        in_specs=placed,
        out_specs=(
            P("phase", "expert", None),
            P("phase", "expert", None),
            P("phase", None, None, None),
        ),
        check_vma=False,
    )
```

profile of v0, /device:TPU:36, one launch (start us, length us, event | category | flops | bytes accessed | tf_op | source)
XLA Modules:
  0.0 1311.5 jit_solution(975837895841320012)
XLA Ops:
  10.5 2.7 broadcast_in_dim.97
  13.3 7.6 broadcast_in_dim.98
  20.8 16.6 %all-to-all-start = ((bf16[1,64,18,2048]{3,2,0,1:T(8,128)(2,1)}), bf16[1,64,18,2048]{3,2,0,1:T(8,128)(2,1)}, u32[]{:S(2)}, u32[]{:S(2)}) async-start(bf16[1,64,18,2048]{3,2,0,1:T(8,128)(2,1)} %bitcast.72), calls=%async_computation | async-start | bytes 12582912 | tf_op jit(solution)/shard_map/all_to_all | solution.py:78
  40.2 2.3 copy.29
  42.5 214.9 %all-to-all-done = bf16[1,64,18,2048]{3,2,0,1:T(8,128)(2,1)} async-done(((bf16[1,64,18,2048]{3,2,0,1:T(8,128)(2,1)}), bf16[1,64,18,2048]{3,2,0,1:T(8,128)(2,1)}, u32[]{:S(2)}, u32[]{:S(2)}) %all-to-all-start) | async-done | bytes 4718624 | tf_op jit(solution)/shard_map/all_to_all | solution.py:78
  257.4 8.3 broadcast_in_dim.104
  265.7 20.2 %all-to-all-start.2 = ((bf16[2,64,18,2048]{3,0,2,1:T(2,128)(2,1)}), bf16[2,64,18,2048]{3,0,2,1:T(2,128)(2,1)}, u32[]{:S(2)}, u32[]{:S(2)}) async-start(bf16[2,64,18,2048]{3,0,2,1:T(2,128)(2,1)} %bitcast.71), calls=%async_computation.2 | async-start | bytes 18874368 | tf_op jit(solution)/shard_map/all_to_all | solution.py:78
  285.9 7.8 reshape_squeeze.21
  293.8 4.6 fusion.37
  298.3 9.6 convolution_convert_fusion
  307.9 7.6 reshape.228
  315.5 246.5 %all-to-all-done.2 = bf16[2,64,18,2048]{3,0,2,1:T(2,128)(2,1)} async-done(((bf16[2,64,18,2048]{3,0,2,1:T(2,128)(2,1)}), bf16[2,64,18,2048]{3,0,2,1:T(2,128)(2,1)}, u32[]{:S(2)}, u32[]{:S(2)}) %all-to-all-start.2) | async-done | bytes 9437216 | tf_op jit(solution)/shard_map/all_to_all | solution.py:78
  562.0 44.8 %all-to-all-start.1 = ((bf16[64,18,2048]{2,1,0:T(8,128)(2,1)}), bf16[64,18,2048]{2,1,0:T(8,128)(2,1)}, u32[]{:S(2)}, u32[]{:S(2)}) async-start(bf16[64,18,2048]{2,1,0:T(8,128)(2,1)} %reshape.228), calls=%async_computation.1 | async-start | bytes 12582912 | tf_op jit(solution)/shard_map/all_to_all | solution.py:84
  606.8 48.0 %slice_reduce_fusion = (bf16[64,18,2048]{2,1,0:T(8,128)(2,1)}, bf16[64,18,2048]{2,1,0:T(8,128)(2,1)}) fusion(bf16[2,64,18,2048]{3,0,2,1:T(2,128)(2,1)} %all-to-all-done.2), kind=kLoop, calls=%fused_computation.1 | loop fusion | bytes 18874368 | tf_op jit(solution)/shard_map/slice | solution.py:162
  654.8 7.7 reshape_squeeze.23
  662.6 7.7 reshape_squeeze.24
  670.3 4.0 fusion.26
  674.3 2.2 fusion.35
  676.5 11.1 fusion.12
  687.6 7.5 fusion
  695.2 7.6 reshape.230
  702.8 99.0 %all-to-all-done.1 = bf16[64,18,2048]{2,1,0:T(8,128)(2,1)} async-done(((bf16[64,18,2048]{2,1,0:T(8,128)(2,1)}), bf16[64,18,2048]{2,1,0:T(8,128)(2,1)}, u32[]{:S(2)}, u32[]{:S(2)}) %all-to-all-start.1) | async-done | bytes 4718624 | tf_op jit(solution)/shard_map/all_to_all | solution.py:84
  801.8 16.9 %all-to-all-start.3 = ((bf16[64,18,2048]{2,1,0:T(8,128)(2,1)}), bf16[64,18,2048]{2,1,0:T(8,128)(2,1)}, u32[]{:S(2)}, u32[]{:S(2)}) async-start(bf16[64,18,2048]{2,1,0:T(8,128)(2,1)} %reshape.230), calls=%async_computation.3 | async-start | bytes 12582912 | tf_op jit(solution)/shard_map/all_to_all | solution.py:84
  818.7 8.5 reshape.231
  827.3 5.8 reduce_sum.130
  833.0 3.1 fusion.4
  836.2 1.9 collective-permute-start
  838.1 175.9 %all-to-all-done.3 = bf16[64,18,2048]{2,1,0:T(8,128)(2,1)} async-done(((bf16[64,18,2048]{2,1,0:T(8,128)(2,1)}), bf16[64,18,2048]{2,1,0:T(8,128)(2,1)}, u32[]{:S(2)}, u32[]{:S(2)}) %all-to-all-start.3) | async-done | bytes 4718624 | tf_op jit(solution)/shard_map/all_to_all | solution.py:84
  1014.0 8.6 reshape.233
  1022.5 4.7 reduce_sum.136
  1028.9 1.9 collective-permute-start.1
  1031.3 276.7 %all-reduce.1 = bf16[20,2048]{1,0:T(8,128)(2,1)S(1)} all-reduce(f32[20,2048]{1,0:T(8,128)S(1)} %fusion.53), channel_id=1, replica_groups=mesh['phase'=8,'expert'=64] {'expert'}, use_global_device_ids=true, to_apply=%region_17.18 | all-reduce | flops 40960 | bytes 245760 | tf_op jit(solution)/shard_map/psum | solution.py:180
  (62 shorter events, 18.0 us)
Async XLA Ops:
  0.6 297.7 %copy-start = (bf16[1,1,2048,128]{3,2,1,0:T(8,128)(2,1)S(1)}, bf16[1,1,2048,128]{3,2,1,0:T(8,128)(2,1)}, u32[]{:S(2)}) copy-start(bf16[1,1,2048,128]{3,2,1,0:T(8,128)(2,1)} %param.30) | copy-start | bytes 1572868
  20.8 16.7 %copy-start.7 = (s32[1,128,1]{1,2,0:T(1,128)S(1)}, s32[1,128,1]{1,2,0:T(1,128)}, u32[]{:S(2)}) copy-start(s32[1,128,1]{1,2,0:T(1,128)} %param.22) | copy-start | bytes 1540
  20.8 16.9 %copy-start.10 = (s32[1,16]{1,0:T(1,128)S(1)}, s32[1,16]{1,0:T(1,128)}, u32[]{:S(2)}) copy-start(s32[1,16]{1,0:T(1,128)} %param.25) | copy-start | bytes 196
  20.8 18.7 %copy-start.6 = (f32[1,2048]{1,0:T(1,128)S(1)}, f32[1,2048]{1,0:T(1,128)}, u32[]{:S(2)}) copy-start(f32[1,2048]{1,0:T(1,128)} %param.28) | copy-start | bytes 24580
  20.8 18.9 %copy-start.4 = (bf16[1,128,2048]{2,1,0:T(8,128)(2,1)S(1)}, bf16[1,128,2048]{2,1,0:T(8,128)(2,1)}, u32[]{:S(2)}) copy-start(bf16[1,128,2048]{2,1,0:T(8,128)(2,1)} %param.26) | copy-start | bytes 1572868
  20.8 236.6 %all-to-all-start = ((bf16[1,64,18,2048]{3,2,0,1:T(8,128)(2,1)}), bf16[1,64,18,2048]{3,2,0,1:T(8,128)(2,1)}, u32[]{:S(2)}, u32[]{:S(2)}) async-start(bf16[1,64,18,2048]{3,2,0,1:T(8,128)(2,1)} %bitcast.72), calls=%async_computation | async-start | bytes 12582912 | tf_op jit(solution)/shard_map/all_to_all | solution.py:78
  265.7 296.3 %all-to-all-start.2 = ((bf16[2,64,18,2048]{3,0,2,1:T(2,128)(2,1)}), bf16[2,64,18,2048]{3,0,2,1:T(2,128)(2,1)}, u32[]{:S(2)}, u32[]{:S(2)}) async-start(bf16[2,64,18,2048]{3,0,2,1:T(2,128)(2,1)} %bitcast.71), calls=%async_computation.2 | async-start | bytes 18874368 | tf_op jit(solution)/shard_map/all_to_all | solution.py:78
  285.9 7.8 copy-start.2
  562.0 239.8 %all-to-all-start.1 = ((bf16[64,18,2048]{2,1,0:T(8,128)(2,1)}), bf16[64,18,2048]{2,1,0:T(8,128)(2,1)}, u32[]{:S(2)}, u32[]{:S(2)}) async-start(bf16[64,18,2048]{2,1,0:T(8,128)(2,1)} %reshape.228), calls=%async_computation.1 | async-start | bytes 12582912 | tf_op jit(solution)/shard_map/all_to_all | solution.py:84
  670.2 4.0 copy-start.1
  670.3 4.0 copy-start.3
  801.8 212.2 %all-to-all-start.3 = ((bf16[64,18,2048]{2,1,0:T(8,128)(2,1)}), bf16[64,18,2048]{2,1,0:T(8,128)(2,1)}, u32[]{:S(2)}, u32[]{:S(2)}) async-start(bf16[64,18,2048]{2,1,0:T(8,128)(2,1)} %reshape.230), calls=%async_computation.3 | async-start | bytes 12582912 | tf_op jit(solution)/shard_map/all_to_all | solution.py:84
  827.3 5.8 copy-start.8
  836.2 194.6 %collective-permute-start = (bf16[128,2048]{1,0:T(8,128)(2,1)}, bf16[128,2048]{1,0:T(8,128)(2,1)}, u32[]{:S(2)}, u32[]{:S(2)}) collective-permute-start(bf16[128,2048]{1,0:T(8,128)(2,1)} %fusion.4), channel_id=1, source_target_pairs={{0,64},{64,128},{128,192},{192,256},{256,320},{320,384},{384,448},... | collective-permute-start | bytes 1572872 | tf_op jit(solution)/shard_map/ppermute | solution.py:18
  1022.5 4.7 copy-start.9
  1022.5 6.0 copy-start.5
  1028.9 279.9 %collective-permute-start.1 = (bf16[128,2048]{1,0:T(8,128)(2,1)S(1)}, bf16[128,2048]{1,0:T(8,128)(2,1)S(1)}, u32[]{:S(2)}, u32[]{:S(2)}) collective-permute-start(bf16[128,2048]{1,0:T(8,128)(2,1)S(1)} %get-tuple-element.23), channel_id=1, source_target_pairs={{64,0},{128,64},{192,128},{256,192},{320,256},{384,320},{448,384},... | collective-permute-start | bytes 1572872 | tf_op jit(solution)/shard_map/ppermute | solution.py:18
where the time goes:
time: 1310 us
  waiting for transfers between devices  736 us (56%)
  blocking collectives  277 us (21%)
  local copies, waits for them, and re-layouts  129 us (10%)
  starting transfers between devices  102 us (8%)
  matrix products  48.4 us (4%)
  other arithmetic  17.9 us (1%)
    all_to_all x2, waiting for transfers between devices, dispatch(): lax.all_to_all(packed, 'expert', split_axis=1, concat_axis=1, tiled=True)  461 us
    psum x1, blocking collectives, on_device(): totals = lax.psum(local_sums, 'expert')  277 us
    all_to_all x2, waiting for transfers between devices, give_back(): lax.all_to_all(partial_value, 'expert', split_axis=0, concat_axis=0, tile...  275 us
    all_to_all x2, starting transfers between devices, give_back(): lax.all_to_all(partial_value, 'expert', split_axis=0, concat_axis=0, tile...  61.7 us
    slice x1, local copies, waits for them, and re-layouts, on_device(): arrived_back[0].reshape(senders * CAP, model_width)  48 us
    all_to_all x2, starting transfers between devices, dispatch(): lax.all_to_all(packed, 'expert', split_axis=1, concat_axis=1, tiled=True)  36.9 us
  transfers between devices with their start and end apart: 6, of which 4 were waited for; matrix products, arithmetic and copies ran while one was open for 13% of the time, Pallas kernels for 0%

commit v1 on v0

v1 whole, which is shorter than its diff:
```python
import functools

import jax
import jax.numpy as jnp
from jax import lax
from jax.experimental import pallas as pl
from jax.experimental.pallas import tpu as pltpu
from jax.sharding import Mesh, PartitionSpec as P

EXPERTS = 8
TENANTS = 2
PLEN = 10
SLOTS = TENANTS * PLEN
CAP = 18
ROWS = 40
COT_ROWS = 24
BLOCK = ROWS + COT_ROWS
FWD_AT = 16
EXTRA = 128
NO_SLOT = 31

EPS = 1e-06
BF16 = jnp.bfloat16
F32 = jnp.float32


def token_layout(lengths, tenants, first_row, tok_count):
    count = lengths.shape[0]
    token_index = first_row + jnp.arange(tok_count, dtype=jnp.int32)
    order = jnp.arange(count, dtype=jnp.int32)
    earlier = order[:, None] < order[None, :]
    seg_starts = jnp.sum(jnp.where(earlier, lengths[:, None], 0), axis=0)
    seg_ends = seg_starts + lengths
    chosen = (seg_starts[None, :] <= token_index[:, None]) & (token_index[:, None] < seg_ends[None, :])
    position = token_index - jnp.sum(jnp.where(chosen, seg_starts[None, :], 0), axis=1)
    tenant = jnp.sum(jnp.where(chosen, tenants[None, :], 0), axis=1)
    return position, tenant


def prepare(acts, lengths, tenants, flat_table, gain_row, first_row):
    tok_count = acts.shape[0]
    position, tenant = token_layout(lengths, tenants, first_row, tok_count)
    prompt_slot = position < PLEN
    slot = jnp.where(prompt_slot, tenant * PLEN + position, NO_SLOT)
    selector = slot[:, None] == jnp.arange(SLOTS, dtype=jnp.int32)[None, :]
    prompt_rows = jnp.dot(selector.astype(BF16), flat_table, preferred_element_type=F32).astype(BF16)
    inputs = jnp.where(prompt_slot[:, None], prompt_rows, acts)
    widened = inputs.astype(F32)
    inv_scale = lax.rsqrt(jnp.mean(widened * widened, axis=1, keepdims=True) + EPS)
    normed = (widened * inv_scale * gain_row[None, :]).astype(BF16)
    return inputs, inv_scale, normed, prompt_slot, slot, selector


def ranks(routes):
    tok_count = routes.shape[0]
    at = jnp.arange(tok_count, dtype=jnp.int32)
    same = (routes[None, :] == routes[:, None]) & (at[None, :] < at[:, None])
    return jnp.sum(same.astype(jnp.int32), axis=1)


def expert_kernel(parts, has_acc, final, *refs):
    x_ref, c_ref = refs[:2]
    at = 2
    shards = []
    for count in parts:
        shards.append((refs[at : at + count], refs[at + count : at + 2 * count]))
        at += 2 * count
    acc_ref = None
    if has_acc:
        acc_ref = refs[at]
        at += 1
    out_ref = refs[at]
    total = refs[at + 1] if final else out_ref
    blocks = x_ref.shape[0] // ROWS
    width = x_ref.shape[1]
    step = 512
    contract = (((1,), (1,)), ((), ()))
    row = lax.broadcasted_iota(jnp.int32, (blocks, ROWS - FWD_AT, 1), 1) + FWD_AT
    is_fwd = (row >= CAP) & (row < 2 * CAP)

    for number, (gu_refs, d_refs) in enumerate(shards):
        depth = width // len(gu_refs)
        gu_out = None
        for k, ref in enumerate(gu_refs):
            piece = jnp.dot(
                x_ref[:, k * depth : (k + 1) * depth], ref[...], preferred_element_type=F32
            )
            gu_out = piece if gu_out is None else gu_out + piece
        if len(d_refs) == 1:
            down = d_refs[0][...]
        else:
            down = jnp.concatenate([ref[...] for ref in d_refs], axis=0)
        half = gu_out.shape[1] // 2
        hidden_grad = lax.dot_general(c_ref[...], down, contract, preferred_element_type=F32)
        gate = gu_out[:, :half].reshape(blocks, ROWS, half)
        upper = gu_out[:, half:].reshape(blocks, ROWS, half)
        gate_f, up_f = gate[:, FWD_AT:], upper[:, FWD_AT:]
        hidden = gate_f / (1.0 + jnp.exp(-gate_f)) * up_f
        hidden = jnp.where(is_fwd, hidden, 0.0)
        hidden = hidden.reshape(blocks * (ROWS - FWD_AT), half).astype(BF16)
        gate_b = gate[:, :COT_ROWS].reshape(blocks * COT_ROWS, half)
        up_b = upper[:, :COT_ROWS].reshape(blocks * COT_ROWS, half)
        sig = 1.0 / (1.0 + jnp.exp(-gate_b))
        gate_grad = hidden_grad * up_b * sig * (1.0 + gate_b * (1.0 - sig))
        up_grad = hidden_grad * (gate_b * sig)
        grads = jnp.concatenate([gate_grad.astype(BF16), up_grad.astype(BF16)], axis=1)
        first = number == 0 and not has_acc
        last = final and number == len(shards) - 1
        for n in range(width // step):
            cols = slice(n * step, (n + 1) * step)
            part, inner = divmod(n * step, depth)
            gu_rows = gu_refs[part][inner : inner + step, :]
            back = lax.dot_general(grads, gu_rows, contract, preferred_element_type=F32)
            fwd = jnp.dot(hidden, down[:, cols], preferred_element_type=F32)
            back = back.reshape(blocks, COT_ROWS, step)
            fwd = fwd.reshape(blocks, ROWS - FWD_AT, step)
            pieces = [
                back[:, :FWD_AT],
                back[:, FWD_AT:] + fwd[:, : COT_ROWS - FWD_AT],
                fwd[:, COT_ROWS - FWD_AT :],
            ]
            value = jnp.concatenate(pieces, axis=1).reshape(blocks * ROWS, step)
            if not first:
                source = acc_ref if number == 0 else total
                value = value + source[:, cols]
            if last:
                out_ref[:, cols] = value.astype(out_ref.dtype)
            else:
                total[:, cols] = value


def expert_step(rows, cots, shards, acc, final):
    parts = tuple(len(gu) for gu, _ in shards)
    operands = [rows, cots]
    for gu, d in shards:
        operands += list(gu) + list(d)
    if acc is not None:
        operands.append(acc)
    shape = rows.shape
    whole = pl.BlockSpec(memory_space=pltpu.VMEM)
    scratch = [pltpu.VMEM(shape, F32)] if final else []
    return pl.pallas_call(
        functools.partial(expert_kernel, parts, acc is not None, final),
        out_shape=jax.ShapeDtypeStruct(shape, BF16 if final else F32),
        in_specs=[whole] * len(operands),
        out_specs=whole,
        scratch_shapes=scratch,
        compiler_params=pltpu.CompilerParams(vmem_limit_bytes=40 * 1024 * 1024),
    )(*operands)


def rotated(value, axis, distance):
    size = lax.axis_size(axis)
    return lax.ppermute(value, axis, [(i, (i + distance) % size) for i in range(size)])


def shifted(block, axis, distance):
    size = lax.axis_size(axis)
    route = [(i, i + distance) for i in range(size) if 0 <= i + distance < size]
    return lax.ppermute(block, axis, route)


def summed(value, axis):
    size = lax.axis_size(axis)
    distance = 1
    while distance < size:
        other = lax.ppermute(value.astype(BF16), axis, [(i, i ^ distance) for i in range(size)])
        value = value.astype(BF16).astype(F32) + other.astype(F32)
        distance *= 2
    return value


def on_device(
    fwd_acts,
    fwd_routes,
    fwd_weights,
    fwd_lengths,
    fwd_tenants,
    bwd_acts,
    bwd_routes,
    bwd_weights,
    bwd_lengths,
    bwd_tenants,
    bwd_cotangent,
    prompts,
    norm_gain,
    w_gate,
    w_up,
    w_down,
):
    tok_count, width = fwd_acts.shape[1:]
    gain_row = norm_gain[0]
    flat_table = prompts[0].reshape(SLOTS, width)
    splits = lax.axis_size("split")

    own_gu = jnp.concatenate([w_gate[0, 0], w_up[0, 0]], axis=1)
    own_d = w_down[0, 0]
    rounds = []
    gu_a = gu_b = own_gu
    d_a = d_b = own_d
    for _ in range(splits // 2 - 1):
        gu_a, gu_b = rotated(gu_a, "split", 1), rotated(gu_b, "split", -1)
        d_a, d_b = rotated(d_a, "split", 1), rotated(d_b, "split", -1)
        rounds.append([((gu_a,), (d_a,)), ((gu_b,), (d_b,))])
    half_k, half_h = width // 2, own_d.shape[0] // 2
    last = (
        (rotated(gu_a[:half_k], "split", 1), rotated(gu_b[half_k:], "split", -1)),
        (rotated(d_a[:half_h], "split", 1), rotated(d_b[half_h:], "split", -1)),
    )

    first_row = (lax.axis_index("split") * lax.axis_size("column") + lax.axis_index("column")) * tok_count
    fwd_in, _, fwd_normed, _, _, _ = prepare(
        fwd_acts[0], fwd_lengths[0], fwd_tenants[0], flat_table, gain_row, first_row
    )
    bwd_in, bwd_scale, bwd_normed, bwd_slot, slot, selector = prepare(
        bwd_acts[0], bwd_lengths[0], bwd_tenants[0], flat_table, gain_row, first_row
    )
    cotangent = bwd_cotangent[0]
    f_route, b_route = fwd_routes[0, :, 0], bwd_routes[0, :, 0]
    f_rank, b_rank = ranks(f_route), ranks(b_route)
    weight_b = bwd_weights[0, :, 0]
    high = lax.reduce_precision(weight_b, 8, 7)
    low = weight_b - high
    lane = jnp.arange(EXTRA, dtype=jnp.int32)[None, :]
    extra = jnp.where(lane == 0, high[:, None], 0.0)
    extra = jnp.where(lane == 1, low[:, None], extra)
    extra = jnp.where(lane == 2, slot.astype(F32)[:, None], extra).astype(BF16)
    blank = jnp.zeros((tok_count, EXTRA), BF16)
    sources = jnp.concatenate(
        [
            jnp.concatenate([bwd_normed, extra], axis=1),
            jnp.concatenate([fwd_normed, blank], axis=1),
            jnp.concatenate([cotangent, blank], axis=1),
        ],
        axis=0,
    )
    target = jnp.concatenate(
        [
            b_route * BLOCK + b_rank,
            f_route * BLOCK + CAP + f_rank,
            b_route * BLOCK + ROWS + b_rank,
        ]
    )
    picker = target[None, :] == jnp.arange(EXPERTS * BLOCK, dtype=jnp.int32)[:, None]
    packed = jnp.dot(picker.astype(BF16), sources, preferred_element_type=F32).astype(BF16)
    packed = packed.reshape(EXPERTS, BLOCK, width + EXTRA)
    arrived = lax.all_to_all(packed, "column", split_axis=0, concat_axis=0, tiled=True)
    rows = arrived[:, :ROWS, :width].reshape(EXPERTS * ROWS, width)
    cots = arrived[:, ROWS:, :width].reshape(EXPERTS * COT_ROWS, width)
    notes = arrived[:, :ROWS, width : width + 3].astype(F32).reshape(EXPERTS * ROWS, 3)

    acc = expert_step(rows, cots, [((own_gu,), (own_d,))] + rounds[0] + rounds[1], None, False)
    for pair in rounds[2:]:
        acc = expert_step(rows, cots, pair, acc, False)
    partial = expert_step(rows, cots, [last], acc, True)

    returned = lax.all_to_all(
        partial.reshape(EXPERTS, ROWS, width), "column", split_axis=0, concat_axis=0, tiled=True
    ).reshape(EXPERTS * ROWS, width)

    slot_iota = jnp.arange(SLOTS, dtype=F32)[:, None]
    at_slot = notes[:, 2][None, :] == slot_iota
    weighing = jnp.concatenate(
        [jnp.where(at_slot, notes[:, 0][None, :], 0.0), jnp.where(at_slot, notes[:, 1][None, :], 0.0)], axis=0
    ).astype(BF16)
    both = jnp.dot(weighing, partial, preferred_element_type=F32)
    slot_q = (both[:SLOTS] + both[SLOTS:]) * gain_row[None, :]
    slot_in = flat_table.astype(F32)
    slot_scale = lax.rsqrt(jnp.mean(slot_in * slot_in, axis=1, keepdims=True) + EPS)
    slot_inner = jnp.mean(slot_in * slot_q, axis=1, keepdims=True)
    slot_cot = jnp.dot(jnp.transpose(selector.astype(BF16)), cotangent, preferred_element_type=F32)
    local_sums = slot_cot + slot_scale * slot_q - slot_in * slot_scale**3 * slot_inner
    totals = summed(summed(local_sums, "column"), "split")
    prompt_grads = totals.astype(BF16).reshape(1, TENANTS, PLEN, width)

    home = jnp.arange(EXPERTS * ROWS, dtype=jnp.int32)[None, :]
    f_take = ((f_route * ROWS + CAP + f_rank)[:, None] == home).astype(BF16)
    b_take = ((b_route * ROWS + b_rank)[:, None] == home).astype(BF16)
    f_out = jnp.dot(f_take, returned, preferred_element_type=F32)
    leaving = (fwd_in.astype(F32) + fwd_weights[0] * f_out).astype(BF16)
    next_acts = shifted(leaving, "phase", 1)
    back_out = jnp.dot(b_take, returned, preferred_element_type=F32)
    scaled = bwd_weights[0] * back_out * gain_row[None, :]
    wide = bwd_in.astype(F32)
    inner = jnp.mean(wide * scaled, axis=1, keepdims=True)
    input_grad = cotangent.astype(F32) + bwd_scale * scaled - wide * bwd_scale**3 * inner
    to_prev = jnp.where(bwd_slot[:, None], 0.0, input_grad).astype(BF16)
    prev_grads = shifted(to_prev, "phase", -1)
    return next_acts[None], prev_grads[None], prompt_grads


def solution(mesh):
    names = mesh.axis_names
    phases, experts = mesh.shape[names[0]], mesh.shape[names[1]]
    grid = mesh.devices.reshape(phases, experts // EXPERTS, EXPERTS)
    inner = Mesh(grid, ("phase", "split", "column"))
    both = ("split", "column")
    tokens = P("phase", both, None)
    per_phase = P("phase", None)
    weights = P("phase", both, None, None)
    table = P("phase", None, None, None)
    placed = (
        tokens,
        tokens,
        tokens,
        per_phase,
        per_phase,
        tokens,
        tokens,
        tokens,
        per_phase,
        per_phase,
        tokens,
        table,
        per_phase,
        weights,
        weights,
        weights,
    )
    return jax.shard_map(
        on_device,
        mesh=inner,
        in_specs=placed,
        out_specs=(tokens, tokens, table),
        check_vma=False,
    )
```

time: 1310 us -> 265 us (0.20)
  the two profiles are of different devices: /device:TPU:36 before, /device:TPU:1 now
where the time goes in v1:
time: 265 us; the launch traced here: 264 us
  starting transfers between devices  115 us (43%)
  waiting for transfers between devices  98.6 us (37%)
  local copies, waits for them, and re-layouts  17.9 us (7%)
  Pallas kernels  15.7 us (6%)
  matrix products  7.72 us (3%)
  other arithmetic  7.39 us (3%)
    ppermute x16, waiting for transfers between devices, rotated(): lax.ppermute(value, axis, [(i, (i + distance) % size) for i in range(size)])  61.8 us
    ppermute x16, starting transfers between devices, rotated(): lax.ppermute(value, axis, [(i, (i + distance) % size) for i in range(size)])  54.1 us
    ppermute x6, waiting for transfers between devices, summed(): lax.ppermute(value.astype(BF16), axis, [(i, i ^ distance) for i in range(...  32.4 us
    ppermute x6, starting transfers between devices, summed(): lax.ppermute(value.astype(BF16), axis, [(i, i ^ distance) for i in range(...  27.4 us
    ppermute x2, starting transfers between devices, shifted(): return lax.ppermute(block, axis, route)  17 us
    pallas_call x3, Pallas kernels, expert_step(): pl.pallas_call(functools.partial(expert_kernel, parts, acc is not None, f...  15.7 us
    all_to_all x1, starting transfers between devices, on_device(): lax.all_to_all(packed, 'column', split_axis=0, concat_axis=0, tiled=True)  11 us
    unnamed x64, local copies, waits for them, and re-layouts  8.31 us
  transfers between devices with their start and end apart: 26, of which 10 were waited for; matrix products, arithmetic and copies ran while one was open for 6% of the time, Pallas kernels for 4%

profile of v1, /device:TPU:1, one launch (start us, length us, event | category | flops | bytes accessed | tf_op | source)
XLA Modules:
  0.0 263.8 jit_solution(15264661924234469580)
XLA Ops:
  9.0 2.7 %convolution_convert_fusion = bf16[512,2176]{1,0:T(8,128)(2,1)} fusion(bf16[128,2048]{1,0:T(8,128)(2,1)S(1)} %bitcast.68, bf16[128,2048]{1,0:T(8,128)(2,1)S(1)} %get-tuple-element.36, bf16[128,128]{1,0:T(8,128)(2,1)S(1)} %select_convert_fusion.1, bf16[128,2048]{1,0:T(8,128)(2,1)S(1)} %get-tuple-element.35, s32[384]{0:T(512)S(1)} %pad_add_fusion), kind=kOutput, calls=%fused_computation.2 | convolution fusion | flops 868646912 | bytes 3835392 | tf_op jit(solution)/shard_map/dot_general | solution.py:245
  11.7 11.0 %all-to-all-start = ((bf16[8,64,2176]{2,1,0:T(8,128)(2,1)}), bf16[8,64,2176]{2,1,0:T(8,128)(2,1)}, u32[]{:S(2)}, u32[]{:S(2)}) async-start(bf16[8,64,2176]{2,1,0:T(8,128)(2,1)} %bitcast.16), calls=%async_computation | async-start | bytes 4456448 | tf_op jit(solution)/shard_map/all_to_all | solution.py:247
  22.9 3.3 %collective-permute-start = (bf16[2048,256]{1,0:T(8,128)(2,1)S(1)}, bf16[2048,256]{1,0:T(8,128)(2,1)S(1)}, u32[]{:S(2)}, u32[]{:S(2)}) collective-permute-start(bf16[2048,256]{1,0:T(8,128)(2,1)S(1)} %pad_maximum_fusion.refs_2_), channel_id=1, source_target_pairs={{0,8},{8,16},{16,24},{24,32},{32,40},{40,48},{48,56},{56,0},{1,9},... | collective-permute-start | bytes 3145736 | tf_op jit(solution)/shard_map/ppermute | solution.py:154
  26.2 3.8 %collective-permute-start.4 = (bf16[2048,256]{1,0:T(8,128)(2,1)S(1)}, bf16[2048,256]{1,0:T(8,128)(2,1)S(1)}, u32[]{:S(2)}, u32[]{:S(2)}) collective-permute-start(bf16[2048,256]{1,0:T(8,128)(2,1)S(1)} %pad_maximum_fusion.refs_2_), channel_id=1, source_target_pairs={{0,56},{8,0},{16,8},{24,16},{32,24},{40,32},{48,40},{56,48},{1,57}... | collective-permute-start | bytes 3145736 | tf_op jit(solution)/shard_map/ppermute | solution.py:154
  30.1 20.7 %collective-permute-done.refs_4_ = bf16[2048,256]{1,0:T(8,128)(2,1)S(1)} collective-permute-done((bf16[2048,256]{1,0:T(8,128)(2,1)S(1)}, bf16[2048,256]{1,0:T(8,128)(2,1)S(1)}, u32[]{:S(2)}, u32[]{:S(2)}) %collective-permute-start) | collective-permute-done | bytes 1048608 | tf_op jit(solution)/shard_map/ppermute | solution.py:154
  53.7 4.6 %collective-permute-start.5 = (bf16[2048,256]{1,0:T(8,128)(2,1)S(1)}, bf16[2048,256]{1,0:T(8,128)(2,1)}, u32[]{:S(2)}, u32[]{:S(2)}) collective-permute-start(bf16[2048,256]{1,0:T(8,128)(2,1)S(1)} %collective-permute-done.4.refs_6_), channel_id=1, source_target_pairs={{0,56},{8,0},{16,8},{24,16},{32,24},{40,32},{48,40},{56,48},{1,57}... | collective-permute-start | bytes 3145736 | tf_op jit(solution)/shard_map/ppermute | solution.py:154
  61.2 4.6 %collective-permute-start.12 = (bf16[128,2048]{1,0:T(8,128)(2,1)S(1)}, bf16[128,2048]{1,0:T(8,128)(2,1)S(1)}, u32[]{:S(2)}, u32[]{:S(2)}) collective-permute-start(bf16[128,2048]{1,0:T(8,128)(2,1)S(1)} %bitcast.60), channel_id=1, source_target_pairs={{0,56},{8,0},{16,8},{24,16},{32,24},{40,32},{48,40},{56,48},{1,57}... | collective-permute-start | bytes 1572872 | tf_op jit(solution)/shard_map/ppermute | solution.py:154
  65.8 11.4 %collective-permute-done.1.refs_8_ = bf16[2048,256]{1,0:T(8,128)(2,1)} collective-permute-done((bf16[2048,256]{1,0:T(8,128)(2,1)S(1)}, bf16[2048,256]{1,0:T(8,128)(2,1)}, u32[]{:S(2)}, u32[]{:S(2)}) %collective-permute-start.1) | collective-permute-done | bytes 1048608 | tf_op jit(solution)/shard_map/ppermute | solution.py:154
  79.1 5.3 %collective-permute-start.6 = (bf16[2048,256]{1,0:T(8,128)(2,1)}, bf16[2048,256]{1,0:T(8,128)(2,1)S(1)}, u32[]{:S(2)}, u32[]{:S(2)}) collective-permute-start(bf16[2048,256]{1,0:T(8,128)(2,1)} %collective-permute-done.5.refs_10_), channel_id=1, source_target_pairs={{0,56},{8,0},{16,8},{24,16},{32,24},{40,32},{48,40},{56,48},{1,57}... | collective-permute-start | bytes 3145736 | tf_op jit(solution)/shard_map/ppermute | solution.py:154
  84.4 3.9 %collective-permute-done.8.refs_5_ = bf16[128,2048]{1,0:T(8,128)(2,1)S(1)} collective-permute-done((bf16[128,2048]{1,0:T(8,128)(2,1)S(1)}, bf16[128,2048]{1,0:T(8,128)(2,1)S(1)}, u32[]{:S(2)}, u32[]{:S(2)}) %collective-permute-start.8) | collective-permute-done | bytes 524320 | tf_op jit(solution)/shard_map/ppermute | solution.py:154
  91.0 4.6 %collective-permute-start.13 = (bf16[128,2048]{1,0:T(8,128)(2,1)S(1)}, bf16[128,2048]{1,0:T(8,128)(2,1)}, u32[]{:S(2)}, u32[]{:S(2)}) collective-permute-start(bf16[128,2048]{1,0:T(8,128)(2,1)S(1)} %collective-permute-done.12.refs_7_), channel_id=1, source_target_pairs={{0,56},{8,0},{16,8},{24,16},{32,24},{40,32},{48,40},{56,48},{1,57}... | collective-permute-start | bytes 1572872 | tf_op jit(solution)/shard_map/ppermute | solution.py:154
  96.4 25.7 %collective-permute-done.9.refs_9_ = bf16[128,2048]{1,0:T(8,128)(2,1)} collective-permute-done((bf16[128,2048]{1,0:T(8,128)(2,1)S(1)}, bf16[128,2048]{1,0:T(8,128)(2,1)}, u32[]{:S(2)}, u32[]{:S(2)}) %collective-permute-start.9) | collective-permute-done | bytes 524320 | tf_op jit(solution)/shard_map/ppermute | solution.py:154
  124.1 5.3 %collective-permute-start.14 = (bf16[128,2048]{1,0:T(8,128)(2,1)}, bf16[128,2048]{1,0:T(8,128)(2,1)}, u32[]{:S(2)}, u32[]{:S(2)}) collective-permute-start(bf16[128,2048]{1,0:T(8,128)(2,1)} %collective-permute-done.13.refs_11_), channel_id=1, source_target_pairs={{0,56},{8,0},{16,8},{24,16},{32,24},{40,32},{48,40},{56,48},{1,57}... | collective-permute-start | bytes 1572872 | tf_op jit(solution)/shard_map/ppermute | solution.py:154
  133.3 4.6 %collective-permute-start.7 = (bf16[1024,256]{1,0:T(8,128)(2,1)}, bf16[1024,256]{1,0:T(8,128)(2,1)}, u32[]{:S(2)}, u32[]{:S(2)}) collective-permute-start(bf16[1024,256]{1,0:T(8,128)(2,1)} %slice.51), channel_id=1, source_target_pairs={{0,56},{8,0},{16,8},{24,16},{32,24},{40,32},{48,40},{56,48},{1,57}... | collective-permute-start | bytes 1572872 | tf_op jit(solution)/shard_map/ppermute | solution.py:154
  143.7 4.7 %collective-permute-start.15 = (bf16[64,2048]{1,0:T(8,128)(2,1)}, bf16[64,2048]{1,0:T(8,128)(2,1)}, u32[]{:S(2)}, u32[]{:S(2)}) collective-permute-start(bf16[64,2048]{1,0:T(8,128)(2,1)} %slice.53), channel_id=1, source_target_pairs={{0,56},{8,0},{16,8},{24,16},{32,24},{40,32},{48,40},{56,48},{1,57}... | collective-permute-start | bytes 786440 | tf_op jit(solution)/shard_map/ppermute | solution.py:154
  154.1 7.9 %shard_map.175.refs_6_ = f32[320,2048]{1,0:T(8,128)S(1)} custom-call(bf16[320,2048]{1,0:T(8,128)(2,1)S(1)} %bitcast.53, bf16[192,2048]{1,0:T(8,128)(2,1)S(1)} %bitcast.56, bf16[2048,256]{1,0:T(8,128)(2,1)S(1)} %pad_maximum_fusion.refs_2_, bf16[128,2048]{1,0:T(8,128)(2,1)S(1)} %bitcast.61, bf16[2048,256]{1,0:T(8,128)(2,1)S(1)} %copy-done.1, ...), custom_call_target="tpu_custom_call" | custom-call | tf_op jit(solution)/shard_map/pallas_call | solution.py:142
  162.0 3.9 %shard_map.176.refs_6_ = f32[320,2048]{1,0:T(8,128)S(1)} custom-call(bf16[320,2048]{1,0:T(8,128)(2,1)S(1)} %bitcast.54, bf16[192,2048]{1,0:T(8,128)(2,1)S(1)} %bitcast.57, bf16[2048,256]{1,0:T(8,128)(2,1)S(1)} %collective-permute-done.2.refs_2_, bf16[128,2048]{1,0:T(8,128)(2,1)} %collective-permute-done.10.refs_3_, ...), custom_call_target="tpu_custom_call" | custom-call | tf_op jit(solution)/shard_map/pallas_call | solution.py:142
  166.0 3.9 %shard_map.177 = bf16[320,2048]{1,0:T(8,128)(2,1)} custom-call(bf16[320,2048]{1,0:T(8,128)(2,1)S(1)} %bitcast.55, bf16[192,2048]{1,0:T(8,128)(2,1)S(1)} %bitcast.58, bf16[1024,256]{1,0:T(8,128)(2,1)} %collective-permute-done.3.refs_2_, bf16[1024,256]{1,0:T(8,128)(2,1)} %collective-permute-done.7.refs_3_, ...), custom_call_target="tpu_custom_call" | custom-call | tf_op jit(solution)/shard_map/pallas_call | solution.py:142
  172.1 2.8 %collective-permute-start.18 = (bf16[20,2048]{1,0:T(8,128)(2,1)S(1)}, bf16[20,2048]{1,0:T(8,128)(2,1)S(1)}, u32[]{:S(2)}, u32[]{:S(2)}) collective-permute-start(bf16[20,2048]{1,0:T(8,128)(2,1)S(1)} %fusion.11), channel_id=1, source_target_pairs={{0,1},{1,0},{2,3},{3,2},{4,5},{5,4},{6,7},{7,6},{8,9},{9,8},{10,11... | collective-permute-start | bytes 245768 | tf_op jit(solution)/shard_map/ppermute | solution.py:167
  175.0 5.5 %all-to-all-start.1 = ((bf16[8,40,2048]{2,1,0:T(8,128)(2,1)}), bf16[8,40,2048]{2,1,0:T(8,128)(2,1)S(1)}, u32[]{:S(2)}, u32[]{:S(2)}) async-start(bf16[8,40,2048]{2,1,0:T(8,128)(2,1)} %bitcast.22), calls=%async_computation.1 | async-start | bytes 2621440 | tf_op jit(solution)/shard_map/all_to_all | solution.py:257
  180.5 4.3 %collective-permute-start.19 = (bf16[20,2048]{1,0:T(8,128)(2,1)S(1)}, bf16[20,2048]{1,0:T(8,128)(2,1)S(1)}, u32[]{:S(2)}, u32[]{:S(2)}) collective-permute-start(bf16[20,2048]{1,0:T(8,128)(2,1)S(1)} %add_convert_fusion.5), channel_id=1, source_target_pairs={{0,2},{1,3},{2,0},{3,1},{4,6},{5,7},{6,4},{7,5},{8,10},{9,11},{10,... | collective-permute-start | bytes 245768 | tf_op jit(solution)/shard_map/ppermute | solution.py:167
  184.8 20.8 %collective-permute-done.19 = bf16[20,2048]{1,0:T(8,128)(2,1)S(1)} collective-permute-done((bf16[20,2048]{1,0:T(8,128)(2,1)S(1)}, bf16[20,2048]{1,0:T(8,128)(2,1)S(1)}, u32[]{:S(2)}, u32[]{:S(2)}) %collective-permute-start.19) | collective-permute-done | bytes 81952 | tf_op jit(solution)/shard_map/ppermute | solution.py:167
  205.6 9.2 %collective-permute-start.20 = (bf16[20,2048]{1,0:T(8,128)(2,1)S(1)}, bf16[20,2048]{1,0:T(8,128)(2,1)S(1)}, u32[]{:S(2)}, u32[]{:S(2)}) collective-permute-start(bf16[20,2048]{1,0:T(8,128)(2,1)S(1)} %add_convert_fusion.4), channel_id=1, source_target_pairs={{0,4},{1,5},{2,6},{3,7},{4,0},{5,1},{6,2},{7,3},{8,12},{9,13},{10,... | collective-permute-start | bytes 245768 | tf_op jit(solution)/shard_map/ppermute | solution.py:167
  214.7 3.7 %collective-permute-done.20 = bf16[20,2048]{1,0:T(8,128)(2,1)S(1)} collective-permute-done((bf16[20,2048]{1,0:T(8,128)(2,1)S(1)}, bf16[20,2048]{1,0:T(8,128)(2,1)S(1)}, u32[]{:S(2)}, u32[]{:S(2)}) %collective-permute-start.20) | collective-permute-done | bytes 81952 | tf_op jit(solution)/shard_map/ppermute | solution.py:167
  218.5 1.9 collective-permute-start.21
  220.4 3.4 %collective-permute-done.21 = bf16[20,2048]{1,0:T(8,128)(2,1)S(1)} collective-permute-done((bf16[20,2048]{1,0:T(8,128)(2,1)S(1)}, bf16[20,2048]{1,0:T(8,128)(2,1)S(1)}, u32[]{:S(2)}, u32[]{:S(2)}) %collective-permute-start.21) | collective-permute-done | bytes 81952 | tf_op jit(solution)/shard_map/ppermute | solution.py:167
  223.9 2.8 %collective-permute-start.22 = (bf16[20,2048]{1,0:T(8,128)(2,1)S(1)}, bf16[20,2048]{1,0:T(8,128)(2,1)S(1)}, u32[]{:S(2)}, u32[]{:S(2)}) collective-permute-start(bf16[20,2048]{1,0:T(8,128)(2,1)S(1)} %add_convert_fusion.2), channel_id=1, source_target_pairs={{0,16},{8,24},{16,0},{24,8},{32,48},{40,56},{48,32},{56,40},{1,17}... | collective-permute-start | bytes 245768 | tf_op jit(solution)/shard_map/ppermute | solution.py:167
  226.7 4.5 %collective-permute-done.22 = bf16[20,2048]{1,0:T(8,128)(2,1)S(1)} collective-permute-done((bf16[20,2048]{1,0:T(8,128)(2,1)S(1)}, bf16[20,2048]{1,0:T(8,128)(2,1)S(1)}, u32[]{:S(2)}, u32[]{:S(2)}) %collective-permute-start.22) | collective-permute-done | bytes 81952 | tf_op jit(solution)/shard_map/ppermute | solution.py:167
  231.2 6.4 %collective-permute-start.23 = (bf16[20,2048]{1,0:T(8,128)(2,1)S(1)}, bf16[20,2048]{1,0:T(8,128)(2,1)}, u32[]{:S(2)}, u32[]{:S(2)}) collective-permute-start(bf16[20,2048]{1,0:T(8,128)(2,1)S(1)} %add_convert_fusion.1), channel_id=1, source_target_pairs={{0,32},{8,40},{16,48},{24,56},{32,0},{40,8},{48,16},{56,24},{1,33}... | collective-permute-start | bytes 245768 | tf_op jit(solution)/shard_map/ppermute | solution.py:167
  238.6 14.0 %collective-permute-start.17 = (bf16[128,2048]{1,0:T(8,128)(2,1)S(1)}, bf16[128,2048]{1,0:T(8,128)(2,1)S(1)}, u32[]{:S(2)}, u32[]{:S(2)}) collective-permute-start(bf16[128,2048]{1,0:T(8,128)(2,1)S(1)} %select_convert_fusion), channel_id=1, source_target_pairs={{64,0},{128,64},{192,128},{256,192},{320,256},{384,320},{448,384},... | collective-permute-start | bytes 1572872 | tf_op jit(solution)/shard_map/ppermute | solution.py:160
  253.1 3.0 %collective-permute-start.16 = (bf16[128,2048]{1,0:T(8,128)(2,1)S(1)}, bf16[128,2048]{1,0:T(8,128)(2,1)S(1)}, u32[]{:S(2)}, u32[]{:S(2)}) collective-permute-start(bf16[128,2048]{1,0:T(8,128)(2,1)S(1)} %fusion.5), channel_id=1, source_target_pairs={{0,64},{64,128},{128,192},{192,256},{256,320},{320,384},{384,448},... | collective-permute-start | bytes 1572872 | tf_op jit(solution)/shard_map/ppermute | solution.py:160
  257.8 2.7 %collective-permute-done.17 = bf16[128,2048]{1,0:T(8,128)(2,1)S(1)} collective-permute-done((bf16[128,2048]{1,0:T(8,128)(2,1)S(1)}, bf16[128,2048]{1,0:T(8,128)(2,1)S(1)}, u32[]{:S(2)}, u32[]{:S(2)}) %collective-permute-start.17) | collective-permute-done | bytes 524320 | tf_op jit(solution)/shard_map/ppermute | solution.py:160
  (141 shorter events, 45.4 us)
Async XLA Ops:
  11.7 136.7 %all-to-all-start = ((bf16[8,64,2176]{2,1,0:T(8,128)(2,1)}), bf16[8,64,2176]{2,1,0:T(8,128)(2,1)}, u32[]{:S(2)}, u32[]{:S(2)}) async-start(bf16[8,64,2176]{2,1,0:T(8,128)(2,1)} %bitcast.16), calls=%async_computation | async-start | bytes 4456448 | tf_op jit(solution)/shard_map/all_to_all | solution.py:247
  22.7 36.5 %copy-start.4 = (bf16[1,1,128,2048]{3,2,1,0:T(8,128)(2,1)S(1)}, bf16[1,1,128,2048]{3,2,1,0:T(8,128)(2,1)}, u32[]{:S(2)}) copy-start(bf16[1,1,128,2048]{3,2,1,0:T(8,128)(2,1)} %param.31) | copy-start | bytes 1572868
  22.7 106.6 %copy-start.19 = (bf16[1,2,10,2048]{3,1,2,0:T(2,128)(2,1)S(1)}, bf16[1,2,10,2048]{3,1,2,0:T(2,128)(2,1)}, u32[]{:S(2)}) copy-start(bf16[1,2,10,2048]{3,1,2,0:T(2,128)(2,1)} %param.27) | copy-start | bytes 245764
  22.9 27.9 %collective-permute-start = (bf16[2048,256]{1,0:T(8,128)(2,1)S(1)}, bf16[2048,256]{1,0:T(8,128)(2,1)S(1)}, u32[]{:S(2)}, u32[]{:S(2)}) collective-permute-start(bf16[2048,256]{1,0:T(8,128)(2,1)S(1)} %pad_maximum_fusion.refs_2_), channel_id=1, source_target_pairs={{0,8},{8,16},{16,24},{24,32},{32,40},{40,48},{48,56},{56,0},{1,9},... | collective-permute-start | bytes 3145736 | tf_op jit(solution)/shard_map/ppermute | solution.py:154
  26.2 27.5 %collective-permute-start.4 = (bf16[2048,256]{1,0:T(8,128)(2,1)S(1)}, bf16[2048,256]{1,0:T(8,128)(2,1)S(1)}, u32[]{:S(2)}, u32[]{:S(2)}) collective-permute-start(bf16[2048,256]{1,0:T(8,128)(2,1)S(1)} %pad_maximum_fusion.refs_2_), channel_id=1, source_target_pairs={{0,56},{8,0},{16,8},{24,16},{32,24},{40,32},{48,40},{56,48},{1,57}... | collective-permute-start | bytes 3145736 | tf_op jit(solution)/shard_map/ppermute | solution.py:154
  50.8 26.4 %collective-permute-start.1 = (bf16[2048,256]{1,0:T(8,128)(2,1)S(1)}, bf16[2048,256]{1,0:T(8,128)(2,1)}, u32[]{:S(2)}, u32[]{:S(2)}) collective-permute-start(bf16[2048,256]{1,0:T(8,128)(2,1)S(1)} %collective-permute-done.refs_4_), channel_id=1, source_target_pairs={{0,8},{8,16},{16,24},{24,32},{32,40},{40,48},{48,56},{56,0},{1,9},... | collective-permute-start | bytes 3145736 | tf_op jit(solution)/shard_map/ppermute | solution.py:154
  53.7 25.4 %collective-permute-start.5 = (bf16[2048,256]{1,0:T(8,128)(2,1)S(1)}, bf16[2048,256]{1,0:T(8,128)(2,1)}, u32[]{:S(2)}, u32[]{:S(2)}) collective-permute-start(bf16[2048,256]{1,0:T(8,128)(2,1)S(1)} %collective-permute-done.4.refs_6_), channel_id=1, source_target_pairs={{0,56},{8,0},{16,8},{24,16},{32,24},{40,32},{48,40},{56,48},{1,57}... | collective-permute-start | bytes 3145736 | tf_op jit(solution)/shard_map/ppermute | solution.py:154
  59.3 29.0 %collective-permute-start.8 = (bf16[128,2048]{1,0:T(8,128)(2,1)S(1)}, bf16[128,2048]{1,0:T(8,128)(2,1)S(1)}, u32[]{:S(2)}, u32[]{:S(2)}) collective-permute-start(bf16[128,2048]{1,0:T(8,128)(2,1)S(1)} %bitcast.59), channel_id=1, source_target_pairs={{0,8},{8,16},{16,24},{24,32},{32,40},{40,48},{48,56},{56,0},{1,9},... | collective-permute-start | bytes 1572872 | tf_op jit(solution)/shard_map/ppermute | solution.py:154
  61.2 29.8 %collective-permute-start.12 = (bf16[128,2048]{1,0:T(8,128)(2,1)S(1)}, bf16[128,2048]{1,0:T(8,128)(2,1)S(1)}, u32[]{:S(2)}, u32[]{:S(2)}) collective-permute-start(bf16[128,2048]{1,0:T(8,128)(2,1)S(1)} %bitcast.60), channel_id=1, source_target_pairs={{0,56},{8,0},{16,8},{24,16},{32,24},{40,32},{48,40},{56,48},{1,57}... | collective-permute-start | bytes 1572872 | tf_op jit(solution)/shard_map/ppermute | solution.py:154
  77.2 52.5 %collective-permute-start.2 = (bf16[2048,256]{1,0:T(8,128)(2,1)}, bf16[2048,256]{1,0:T(8,128)(2,1)S(1)}, u32[]{:S(2)}, u32[]{:S(2)}) collective-permute-start(bf16[2048,256]{1,0:T(8,128)(2,1)} %collective-permute-done.1.refs_8_), channel_id=1, source_target_pairs={{0,8},{8,16},{16,24},{24,32},{32,40},{40,48},{48,56},{56,0},{1,9},... | collective-permute-start | bytes 3145736 | tf_op jit(solution)/shard_map/ppermute | solution.py:154
  79.1 53.4 %collective-permute-start.6 = (bf16[2048,256]{1,0:T(8,128)(2,1)}, bf16[2048,256]{1,0:T(8,128)(2,1)S(1)}, u32[]{:S(2)}, u32[]{:S(2)}) collective-permute-start(bf16[2048,256]{1,0:T(8,128)(2,1)} %collective-permute-done.5.refs_10_), channel_id=1, source_target_pairs={{0,56},{8,0},{16,8},{24,16},{32,24},{40,32},{48,40},{56,48},{1,57}... | collective-permute-start | bytes 3145736 | tf_op jit(solution)/shard_map/ppermute | solution.py:154
  88.3 33.8 %collective-permute-start.9 = (bf16[128,2048]{1,0:T(8,128)(2,1)S(1)}, bf16[128,2048]{1,0:T(8,128)(2,1)}, u32[]{:S(2)}, u32[]{:S(2)}) collective-permute-start(bf16[128,2048]{1,0:T(8,128)(2,1)S(1)} %collective-permute-done.8.refs_5_), channel_id=1, source_target_pairs={{0,8},{8,16},{16,24},{24,32},{32,40},{40,48},{48,56},{56,0},{1,9},... | collective-permute-start | bytes 1572872 | tf_op jit(solution)/shard_map/ppermute | solution.py:154
  91.0 33.0 %collective-permute-start.13 = (bf16[128,2048]{1,0:T(8,128)(2,1)S(1)}, bf16[128,2048]{1,0:T(8,128)(2,1)}, u32[]{:S(2)}, u32[]{:S(2)}) collective-permute-start(bf16[128,2048]{1,0:T(8,128)(2,1)S(1)} %collective-permute-done.12.refs_7_), channel_id=1, source_target_pairs={{0,56},{8,0},{16,8},{24,16},{32,24},{40,32},{48,40},{56,48},{1,57}... | collective-permute-start | bytes 1572872 | tf_op jit(solution)/shard_map/ppermute | solution.py:154
  122.1 16.3 %collective-permute-start.10 = (bf16[128,2048]{1,0:T(8,128)(2,1)}, bf16[128,2048]{1,0:T(8,128)(2,1)}, u32[]{:S(2)}, u32[]{:S(2)}) collective-permute-start(bf16[128,2048]{1,0:T(8,128)(2,1)} %collective-permute-done.9.refs_9_), channel_id=1, source_target_pairs={{0,8},{8,16},{16,24},{24,32},{32,40},{40,48},{48,56},{56,0},{1,9},... | collective-permute-start | bytes 1572872 | tf_op jit(solution)/shard_map/ppermute | solution.py:154
  124.1 17.9 %collective-permute-start.14 = (bf16[128,2048]{1,0:T(8,128)(2,1)}, bf16[128,2048]{1,0:T(8,128)(2,1)}, u32[]{:S(2)}, u32[]{:S(2)}) collective-permute-start(bf16[128,2048]{1,0:T(8,128)(2,1)} %collective-permute-done.13.refs_11_), channel_id=1, source_target_pairs={{0,56},{8,0},{16,8},{24,16},{32,24},{40,32},{48,40},{56,48},{1,57}... | collective-permute-start | bytes 1572872 | tf_op jit(solution)/shard_map/ppermute | solution.py:154
  129.7 18.7 %copy-start.26 = (f32[20]{0:T(128)}, f32[20]{0:T(128)S(1)}, u32[]{:S(2)}) copy-start(f32[20]{0:T(128)S(1)} %rsqrt.36) | copy-start | bytes 244
  130.6 35.4 %collective-permute-start.3 = (bf16[1024,256]{1,0:T(8,128)(2,1)}, bf16[1024,256]{1,0:T(8,128)(2,1)}, u32[]{:S(2)}, u32[]{:S(2)}) collective-permute-start(bf16[1024,256]{1,0:T(8,128)(2,1)} %slice.50), channel_id=1, source_target_pairs={{0,8},{8,16},{16,24},{24,32},{32,40},{40,48},{48,56},{56,0},{1,9},... | collective-permute-start | bytes 1572872 | tf_op jit(solution)/shard_map/ppermute | solution.py:154
  133.3 32.7 %collective-permute-start.7 = (bf16[1024,256]{1,0:T(8,128)(2,1)}, bf16[1024,256]{1,0:T(8,128)(2,1)}, u32[]{:S(2)}, u32[]{:S(2)}) collective-permute-start(bf16[1024,256]{1,0:T(8,128)(2,1)} %slice.51), channel_id=1, source_target_pairs={{0,56},{8,0},{16,8},{24,16},{32,24},{40,32},{48,40},{56,48},{1,57}... | collective-permute-start | bytes 1572872 | tf_op jit(solution)/shard_map/ppermute | solution.py:154
  140.1 25.9 %collective-permute-start.11 = (bf16[64,2048]{1,0:T(8,128)(2,1)}, bf16[64,2048]{1,0:T(8,128)(2,1)S(1)}, u32[]{:S(2)}, u32[]{:S(2)}) collective-permute-start(bf16[64,2048]{1,0:T(8,128)(2,1)} %slice.52), channel_id=1, source_target_pairs={{0,8},{8,16},{16,24},{24,32},{32,40},{40,48},{48,56},{56,0},{1,9},... | collective-permute-start | bytes 786440 | tf_op jit(solution)/shard_map/ppermute | solution.py:154
  143.7 22.3 %collective-permute-start.15 = (bf16[64,2048]{1,0:T(8,128)(2,1)}, bf16[64,2048]{1,0:T(8,128)(2,1)}, u32[]{:S(2)}, u32[]{:S(2)}) collective-permute-start(bf16[64,2048]{1,0:T(8,128)(2,1)} %slice.53), channel_id=1, source_target_pairs={{0,56},{8,0},{16,8},{24,16},{32,24},{40,32},{48,40},{56,48},{1,57}... | collective-permute-start | bytes 786440 | tf_op jit(solution)/shard_map/ppermute | solution.py:154
  172.1 65.5 %copy-start.11 = (f32[128,2048]{1,0:T(8,128)S(1)}, f32[128,2048]{1,0:T(8,128)}, u32[]{:S(2)}) copy-start(f32[128,2048]{1,0:T(8,128)} %copy-done.10) | copy-start | bytes 3145732
  172.1 8.3 %collective-permute-start.18 = (bf16[20,2048]{1,0:T(8,128)(2,1)S(1)}, bf16[20,2048]{1,0:T(8,128)(2,1)S(1)}, u32[]{:S(2)}, u32[]{:S(2)}) collective-permute-start(bf16[20,2048]{1,0:T(8,128)(2,1)S(1)} %fusion.11), channel_id=1, source_target_pairs={{0,1},{1,0},{2,3},{3,2},{4,5},{5,4},{6,7},{7,6},{8,9},{9,8},{10,11... | collective-permute-start | bytes 245768 | tf_op jit(solution)/shard_map/ppermute | solution.py:167
  175.0 62.6 %all-to-all-start.1 = ((bf16[8,40,2048]{2,1,0:T(8,128)(2,1)}), bf16[8,40,2048]{2,1,0:T(8,128)(2,1)S(1)}, u32[]{:S(2)}, u32[]{:S(2)}) async-start(bf16[8,40,2048]{2,1,0:T(8,128)(2,1)} %bitcast.22), calls=%async_computation.1 | async-start | bytes 2621440 | tf_op jit(solution)/shard_map/all_to_all | solution.py:257
  180.5 25.0 %collective-permute-start.19 = (bf16[20,2048]{1,0:T(8,128)(2,1)S(1)}, bf16[20,2048]{1,0:T(8,128)(2,1)S(1)}, u32[]{:S(2)}, u32[]{:S(2)}) collective-permute-start(bf16[20,2048]{1,0:T(8,128)(2,1)S(1)} %add_convert_fusion.5), channel_id=1, source_target_pairs={{0,2},{1,3},{2,0},{3,1},{4,6},{5,7},{6,4},{7,5},{8,10},{9,11},{10,... | collective-permute-start | bytes 245768 | tf_op jit(solution)/shard_map/ppermute | solution.py:167
  205.6 32.7 %copy-start.25 = (f32[128]{0:T(128)S(1)}, f32[128]{0:T(128)}, u32[]{:S(2)}) copy-start(f32[128]{0:T(128)} %get-tuple-element.44) | copy-start | bytes 1540
  205.6 12.9 %collective-permute-start.20 = (bf16[20,2048]{1,0:T(8,128)(2,1)S(1)}, bf16[20,2048]{1,0:T(8,128)(2,1)S(1)}, u32[]{:S(2)}, u32[]{:S(2)}) collective-permute-start(bf16[20,2048]{1,0:T(8,128)(2,1)S(1)} %add_convert_fusion.4), channel_id=1, source_target_pairs={{0,4},{1,5},{2,6},{3,7},{4,0},{5,1},{6,2},{7,3},{8,12},{9,13},{10,... | collective-permute-start | bytes 245768 | tf_op jit(solution)/shard_map/ppermute | solution.py:167
  218.5 5.4 %collective-permute-start.21 = (bf16[20,2048]{1,0:T(8,128)(2,1)S(1)}, bf16[20,2048]{1,0:T(8,128)(2,1)S(1)}, u32[]{:S(2)}, u32[]{:S(2)}) collective-permute-start(bf16[20,2048]{1,0:T(8,128)(2,1)S(1)} %add_convert_fusion.3), channel_id=1, source_target_pairs={{0,8},{8,0},{16,24},{24,16},{32,40},{40,32},{48,56},{56,48},{1,9},... | collective-permute-start | bytes 245768 | tf_op jit(solution)/shard_map/ppermute | solution.py:167
  223.9 7.3 %collective-permute-start.22 = (bf16[20,2048]{1,0:T(8,128)(2,1)S(1)}, bf16[20,2048]{1,0:T(8,128)(2,1)S(1)}, u32[]{:S(2)}, u32[]{:S(2)}) collective-permute-start(bf16[20,2048]{1,0:T(8,128)(2,1)S(1)} %add_convert_fusion.2), channel_id=1, source_target_pairs={{0,16},{8,24},{16,0},{24,8},{32,48},{40,56},{48,32},{56,40},{1,17}... | collective-permute-start | bytes 245768 | tf_op jit(solution)/shard_map/ppermute | solution.py:167
  231.2 24.9 %collective-permute-start.23 = (bf16[20,2048]{1,0:T(8,128)(2,1)S(1)}, bf16[20,2048]{1,0:T(8,128)(2,1)}, u32[]{:S(2)}, u32[]{:S(2)}) collective-permute-start(bf16[20,2048]{1,0:T(8,128)(2,1)S(1)} %add_convert_fusion.1), channel_id=1, source_target_pairs={{0,32},{8,40},{16,48},{24,56},{32,0},{40,8},{48,16},{56,24},{1,33}... | collective-permute-start | bytes 245768 | tf_op jit(solution)/shard_map/ppermute | solution.py:167
  238.2 14.4 %copy-start.24 = (f32[1,128,1]{1,2,0:T(1,128)S(1)}, f32[1,128,1]{1,2,0:T(1,128)}, u32[]{:S(2)}) copy-start(f32[1,128,1]{1,2,0:T(1,128)} %param.18) | copy-start | bytes 1540
  238.6 21.9 %collective-permute-start.17 = (bf16[128,2048]{1,0:T(8,128)(2,1)S(1)}, bf16[128,2048]{1,0:T(8,128)(2,1)S(1)}, u32[]{:S(2)}, u32[]{:S(2)}) collective-permute-start(bf16[128,2048]{1,0:T(8,128)(2,1)S(1)} %select_convert_fusion), channel_id=1, source_target_pairs={{64,0},{128,64},{192,128},{256,192},{320,256},{384,320},{448,384},... | collective-permute-start | bytes 1572872 | tf_op jit(solution)/shard_map/ppermute | solution.py:160
  253.1 9.1 %collective-permute-start.16 = (bf16[128,2048]{1,0:T(8,128)(2,1)S(1)}, bf16[128,2048]{1,0:T(8,128)(2,1)S(1)}, u32[]{:S(2)}, u32[]{:S(2)}) collective-permute-start(bf16[128,2048]{1,0:T(8,128)(2,1)S(1)} %fusion.5), channel_id=1, source_target_pairs={{0,64},{64,128},{128,192},{192,256},{256,320},{320,384},{384,448},... | collective-permute-start | bytes 1572872 | tf_op jit(solution)/shard_map/ppermute | solution.py:160
  (23 other events, 100.9 us)

commit v2 on v1

--- a/solution.py
+++ b/solution.py
@@ -129,6 +129,10 @@
                 total[:, cols] = value
 
 
+def w_hidden(shards):
+    return sum(d.shape[0] for _, ds in shards for d in ds)
+
+
 def expert_step(rows, cots, shards, acc, final):
     parts = tuple(len(gu) for gu, _ in shards)
     operands = [rows, cots]
@@ -139,6 +143,12 @@
     shape = rows.shape
     whole = pl.BlockSpec(memory_space=pltpu.VMEM)
     scratch = [pltpu.VMEM(shape, F32)] if final else []
+    hidden = w_hidden(shards)
+    cost = pl.CostEstimate(
+        flops=2 * hidden * shape[1] * (2 * shape[0] + 4 * cots.shape[0]),
+        transcendentals=hidden * 2 * cots.shape[0],
+        bytes_accessed=sum(o.size * o.dtype.itemsize for o in operands) + 4 * rows.size,
+    )
     return pl.pallas_call(
         functools.partial(expert_kernel, parts, acc is not None, final),
         out_shape=jax.ShapeDtypeStruct(shape, BF16 if final else F32),
@@ -146,6 +156,7 @@
         out_specs=whole,
         scratch_shapes=scratch,
         compiler_params=pltpu.CompilerParams(vmem_limit_bytes=40 * 1024 * 1024),
+        cost_estimate=cost,
     )(*operands)
 
 
@@ -199,14 +210,9 @@
     gu_a = gu_b = own_gu
     d_a = d_b = own_d
     for _ in range(splits // 2 - 1):
+        d_a, d_b = rotated(d_a, "split", 1), rotated(d_b, "split", -1)
         gu_a, gu_b = rotated(gu_a, "split", 1), rotated(gu_b, "split", -1)
-        d_a, d_b = rotated(d_a, "split", 1), rotated(d_b, "split", -1)
         rounds.append([((gu_a,), (d_a,)), ((gu_b,), (d_b,))])
-    half_k, half_h = width // 2, own_d.shape[0] // 2
-    last = (
-        (rotated(gu_a[:half_k], "split", 1), rotated(gu_b[half_k:], "split", -1)),
-        (rotated(d_a[:half_h], "split", 1), rotated(d_b[half_h:], "split", -1)),
-    )
 
     first_row = (lax.axis_index("split") * lax.axis_size("column") + lax.axis_index("column")) * tok_count
     fwd_in, _, fwd_normed, _, _, _ = prepare(
@@ -244,12 +250,19 @@
     picker = target[None, :] == jnp.arange(EXPERTS * BLOCK, dtype=jnp.int32)[:, None]
     packed = jnp.dot(picker.astype(BF16), sources, preferred_element_type=F32).astype(BF16)
     packed = packed.reshape(EXPERTS, BLOCK, width + EXTRA)
+    packed, _ = lax.optimization_barrier((packed, rounds[0][0][1][0]))
     arrived = lax.all_to_all(packed, "column", split_axis=0, concat_axis=0, tiled=True)
     rows = arrived[:, :ROWS, :width].reshape(EXPERTS * ROWS, width)
     cots = arrived[:, ROWS:, :width].reshape(EXPERTS * COT_ROWS, width)
     notes = arrived[:, :ROWS, width : width + 3].astype(F32).reshape(EXPERTS * ROWS, 3)
 
     acc = expert_step(rows, cots, [((own_gu,), (own_d,))] + rounds[0] + rounds[1], None, False)
+    half_k, half_h = width // 2, own_d.shape[0] // 2
+    halves = (gu_a[:half_k], gu_b[half_k:], d_a[:half_h], d_b[half_h:])
+    last = (
+        (rotated(halves[0], "split", 1), rotated(halves[1], "split", -1)),
+        (rotated(halves[2], "split", 1), rotated(halves[3], "split", -1)),
+    )
     for pair in rounds[2:]:
         acc = expert_step(rows, cots, pair, acc, False)
     partial = expert_step(rows, cots, [last], acc, True)
@@ -270,7 +283,7 @@
     slot_inner = jnp.mean(slot_in * slot_q, axis=1, keepdims=True)
     slot_cot = jnp.dot(jnp.transpose(selector.astype(BF16)), cotangent, preferred_element_type=F32)
     local_sums = slot_cot + slot_scale * slot_q - slot_in * slot_scale**3 * slot_inner
-    totals = summed(summed(local_sums, "column"), "split")
+    totals = summed(summed(local_sums, "split"), "column")
     prompt_grads = totals.astype(BF16).reshape(1, TENANTS, PLEN, width)
 
     home = jnp.arange(EXPERTS * ROWS, dtype=jnp.int32)[None, :]

time: 265 us -> 258 us (0.974)
  waiting for transfers between devices: 98.6 us -> 87.2 us
  local copies, waits for them, and re-layouts: 17.9 us -> 23.8 us
    ppermute x6, waiting for transfers between devices: 32.4 us -> 14.6 us  [summed(): lax.ppermute(value.astype(BF16), axis, [(i, i ^ distance) for i in range(...]
    unnamed x64 -> x84, local copies, waits for them, and re-layouts: 8.31 us -> 16 us
    ppermute x16, waiting for transfers between devices: 61.8 us -> 68.1 us  [rotated(): lax.ppermute(value, axis, [(i, (i + distance) % size) for i in range(size)])]
    ppermute x2, starting transfers between devices: 17 us -> 11.5 us  [shifted(): return lax.ppermute(block, axis, route)]
  transfers between devices with their start and end apart: 26 -> 26, of which waited for: 10 -> 10; matrix products, arithmetic and copies ran while one was open for 6% -> 9% of each run, Pallas kernels for 4% -> 4%
where the time goes in v2:
time: 258 us; the launch traced here: 255 us
  starting transfers between devices  113 us (44%)
  waiting for transfers between devices  87.2 us (34%)
  local copies, waits for them, and re-layouts  23.8 us (9%)
  Pallas kernels  14.5 us (6%)
  matrix products  7.69 us (3%)
  other arithmetic  7.35 us (3%)
    ppermute x16, waiting for transfers between devices, rotated(): lax.ppermute(value, axis, [(i, (i + distance) % size) for i in range(size)])  68.1 us
    ppermute x16, starting transfers between devices, rotated(): lax.ppermute(value, axis, [(i, (i + distance) % size) for i in range(size)])  54.6 us
    ppermute x6, starting transfers between devices, summed(): lax.ppermute(value.astype(BF16), axis, [(i, i ^ distance) for i in range(...  28.1 us
    unnamed x84, local copies, waits for them, and re-layouts  16 us
    ppermute x6, waiting for transfers between devices, summed(): lax.ppermute(value.astype(BF16), axis, [(i, i ^ distance) for i in range(...  14.6 us
    pallas_call x3, Pallas kernels, expert_step(): pl.pallas_call(functools.partial(expert_kernel, parts, acc is not None, f...  14.5 us
    all_to_all x1, starting transfers between devices, on_device(): lax.all_to_all(packed, 'column', split_axis=0, concat_axis=0, tiled=True)  12.9 us
    ppermute x2, starting transfers between devices, shifted(): return lax.ppermute(block, axis, route)  11.5 us
  transfers between devices with their start and end apart: 26, of which 10 were waited for; matrix products, arithmetic and copies ran while one was open for 9% of the time, Pallas kernels for 4%

profile of v2, /device:TPU:1, one launch (start us, length us, event | category | flops | bytes accessed | tf_op | source)
XLA Modules:
  0.0 255.3 jit_solution(6340321879618160990)
XLA Ops:
  0.7 4.2 %collective-permute-start = (bf16[128,2048]{1,0:T(8,128)(2,1)}, bf16[128,2048]{1,0:T(8,128)(2,1)S(1)}, u32[]{:S(2)}, u32[]{:S(2)}) collective-permute-start(bf16[128,2048]{1,0:T(8,128)(2,1)} %bitcast.59), channel_id=1, source_target_pairs={{0,8},{8,16},{16,24},{24,32},{32,40},{40,48},{48,56},{56,0},{1,9},... | collective-permute-start | bytes 1572872 | tf_op jit(solution)/shard_map/ppermute | solution.py:165
  13.1 2.7 %convolution_convert_fusion = bf16[512,2176]{1,0:T(8,128)(2,1)} fusion(bf16[128,2048]{1,0:T(8,128)(2,1)S(1)} %bitcast.69, bf16[128,2048]{1,0:T(8,128)(2,1)S(1)} %get-tuple-element.38, bf16[128,128]{1,0:T(8,128)(2,1)S(1)} %select_convert_fusion.1, bf16[128,2048]{1,0:T(8,128)(2,1)S(1)} %get-tuple-element.37, s32[384]{0:T(512)S(1)} %pad_add_fusion), kind=kOutput, calls=%fused_computation.2 | convolution fusion | flops 868646912 | bytes 3835392 | tf_op jit(solution)/shard_map/dot_general | solution.py:251
  15.8 12.9 %all-to-all-start = ((bf16[8,64,2176]{2,1,0:T(8,128)(2,1)}), bf16[8,64,2176]{2,1,0:T(8,128)(2,1)}, u32[]{:S(2)}, u32[]{:S(2)}) async-start(bf16[8,64,2176]{2,1,0:T(8,128)(2,1)} %bitcast.64), calls=%async_computation | async-start | bytes 4456448 | tf_op jit(solution)/shard_map/all_to_all | solution.py:254
  28.9 2.1 collective-permute-start.1
  31.0 4.6 %collective-permute-start.5 = (bf16[2048,256]{1,0:T(8,128)(2,1)S(1)}, bf16[2048,256]{1,0:T(8,128)(2,1)S(1)}, u32[]{:S(2)}, u32[]{:S(2)}) collective-permute-start(bf16[2048,256]{1,0:T(8,128)(2,1)S(1)} %pad_maximum_fusion.refs_2_), channel_id=1, source_target_pairs={{0,56},{8,0},{16,8},{24,16},{32,24},{40,32},{48,40},{56,48},{1,57}... | collective-permute-start | bytes 3145736 | tf_op jit(solution)/shard_map/ppermute | solution.py:165
  36.5 18.9 %collective-permute-done.1.refs_4_ = bf16[2048,256]{1,0:T(8,128)(2,1)S(1)} collective-permute-done((bf16[2048,256]{1,0:T(8,128)(2,1)S(1)}, bf16[2048,256]{1,0:T(8,128)(2,1)S(1)}, u32[]{:S(2)}, u32[]{:S(2)}) %collective-permute-start.1) | collective-permute-done | bytes 1048608 | tf_op jit(solution)/shard_map/ppermute | solution.py:165
  58.3 4.6 %collective-permute-start.6 = (bf16[2048,256]{1,0:T(8,128)(2,1)S(1)}, bf16[2048,256]{1,0:T(8,128)(2,1)}, u32[]{:S(2)}, u32[]{:S(2)}) collective-permute-start(bf16[2048,256]{1,0:T(8,128)(2,1)S(1)} %collective-permute-done.5.refs_6_), channel_id=1, source_target_pairs={{0,56},{8,0},{16,8},{24,16},{32,24},{40,32},{48,40},{56,48},{1,57}... | collective-permute-start | bytes 3145736 | tf_op jit(solution)/shard_map/ppermute | solution.py:165
  65.8 3.4 %collective-permute-start.9 = (bf16[128,2048]{1,0:T(8,128)(2,1)S(1)}, bf16[128,2048]{1,0:T(8,128)(2,1)}, u32[]{:S(2)}, u32[]{:S(2)}) collective-permute-start(bf16[128,2048]{1,0:T(8,128)(2,1)S(1)} %collective-permute-done.refs_5_), channel_id=1, source_target_pairs={{0,8},{8,16},{16,24},{24,32},{32,40},{40,48},{48,56},{56,0},{1,9},... | collective-permute-start | bytes 1572872 | tf_op jit(solution)/shard_map/ppermute | solution.py:165
  69.2 24.8 %collective-permute-done.12.refs_7_ = bf16[128,2048]{1,0:T(8,128)(2,1)S(1)} collective-permute-done((bf16[128,2048]{1,0:T(8,128)(2,1)S(1)}, bf16[128,2048]{1,0:T(8,128)(2,1)S(1)}, u32[]{:S(2)}, u32[]{:S(2)}) %collective-permute-start.12) | collective-permute-done | bytes 524320 | tf_op jit(solution)/shard_map/ppermute | solution.py:165
  94.0 5.3 %collective-permute-start.13 = (bf16[128,2048]{1,0:T(8,128)(2,1)S(1)}, bf16[128,2048]{1,0:T(8,128)(2,1)}, u32[]{:S(2)}, u32[]{:S(2)}) collective-permute-start(bf16[128,2048]{1,0:T(8,128)(2,1)S(1)} %collective-permute-done.12.refs_7_), channel_id=1, source_target_pairs={{0,56},{8,0},{16,8},{24,16},{32,24},{40,32},{48,40},{56,48},{1,57}... | collective-permute-start | bytes 1572872 | tf_op jit(solution)/shard_map/ppermute | solution.py:165
  102.0 4.6 %collective-permute-start.7 = (bf16[2048,256]{1,0:T(8,128)(2,1)}, bf16[2048,256]{1,0:T(8,128)(2,1)S(1)}, u32[]{:S(2)}, u32[]{:S(2)}) collective-permute-start(bf16[2048,256]{1,0:T(8,128)(2,1)} %collective-permute-done.6.refs_10_), channel_id=1, source_target_pairs={{0,56},{8,0},{16,8},{24,16},{32,24},{40,32},{48,40},{56,48},{1,57}... | collective-permute-start | bytes 3145736 | tf_op jit(solution)/shard_map/ppermute | solution.py:165
  108.5 4.6 %collective-permute-start.14 = (bf16[128,2048]{1,0:T(8,128)(2,1)}, bf16[128,2048]{1,0:T(8,128)(2,1)S(1)}, u32[]{:S(2)}, u32[]{:S(2)}) collective-permute-start(bf16[128,2048]{1,0:T(8,128)(2,1)} %collective-permute-done.13.refs_11_), channel_id=1, source_target_pairs={{0,56},{8,0},{16,8},{24,16},{32,24},{40,32},{48,40},{56,48},{1,57}... | collective-permute-start | bytes 1572872 | tf_op jit(solution)/shard_map/ppermute | solution.py:165
  114.0 21.5 %collective-permute-done.10.refs_3_ = bf16[128,2048]{1,0:T(8,128)(2,1)S(1)} collective-permute-done((bf16[128,2048]{1,0:T(8,128)(2,1)}, bf16[128,2048]{1,0:T(8,128)(2,1)S(1)}, u32[]{:S(2)}, u32[]{:S(2)}) %collective-permute-start.10) | collective-permute-done | bytes 524320 | tf_op jit(solution)/shard_map/ppermute | solution.py:165
  138.1 3.0 %collective-permute-done.14.refs_5_ = bf16[128,2048]{1,0:T(8,128)(2,1)S(1)} collective-permute-done((bf16[128,2048]{1,0:T(8,128)(2,1)}, bf16[128,2048]{1,0:T(8,128)(2,1)S(1)}, u32[]{:S(2)}, u32[]{:S(2)}) %collective-permute-start.14) | collective-permute-done | bytes 524320 | tf_op jit(solution)/shard_map/ppermute | solution.py:165
  141.9 5.2 %collective-permute-start.15 = (bf16[64,2048]{1,0:T(8,128)(2,1)}, bf16[64,2048]{1,0:T(8,128)(2,1)}, u32[]{:S(2)}, u32[]{:S(2)}) collective-permute-start(bf16[64,2048]{1,0:T(8,128)(2,1)} %slice.53), channel_id=1, source_target_pairs={{0,56},{8,0},{16,8},{24,16},{32,24},{40,32},{48,40},{56,48},{1,57}... | collective-permute-start | bytes 786440 | tf_op jit(solution)/shard_map/ppermute | solution.py:165
  150.8 4.7 %collective-permute-start.8 = (bf16[1024,256]{1,0:T(8,128)(2,1)}, bf16[1024,256]{1,0:T(8,128)(2,1)}, u32[]{:S(2)}, u32[]{:S(2)}) collective-permute-start(bf16[1024,256]{1,0:T(8,128)(2,1)} %slice.51), channel_id=1, source_target_pairs={{0,56},{8,0},{16,8},{24,16},{32,24},{40,32},{48,40},{56,48},{1,57}... | collective-permute-start | bytes 1572872 | tf_op jit(solution)/shard_map/ppermute | solution.py:165
  159.5 7.9 %shard_map.175.refs_6_ = f32[320,2048]{1,0:T(8,128)S(1)} custom-call(bf16[320,2048]{1,0:T(8,128)(2,1)S(1)} %bitcast.53, bf16[192,2048]{1,0:T(8,128)(2,1)S(1)} %bitcast.56, bf16[2048,256]{1,0:T(8,128)(2,1)S(1)} %copy-done.9, bf16[128,2048]{1,0:T(8,128)(2,1)S(1)} %bitcast.61, bf16[2048,256]{1,0:T(8,128)(2,1)S(1)} %copy-done.11, ...), custom_call_target="tpu_custom_call" | custom-call | flops 3690987520 | bytes 12582912 | tf_op jit(solution)/shard_map/pallas_call | solution.py:152
  176.6 2.7 %shard_map.176.refs_6_ = f32[320,2048]{1,0:T(8,128)S(1)} custom-call(bf16[320,2048]{1,0:T(8,128)(2,1)S(1)} %bitcast.54, bf16[192,2048]{1,0:T(8,128)(2,1)S(1)} %bitcast.57, bf16[2048,256]{1,0:T(8,128)(2,1)S(1)} %collective-permute-done.3.refs_2_, bf16[128,2048]{1,0:T(8,128)(2,1)S(1)} %copy-done.5, bf16[2048,256]{1,0:T(8,128)(2,1)S(1)} %copy-done.3, ...), custom_call_target="tpu_custom_call" | custom-call | flops 1476395008 | bytes 10485760 | tf_op jit(solution)/shard_map/pallas_call | solution.py:152
  179.4 3.9 %shard_map.177 = bf16[320,2048]{1,0:T(8,128)(2,1)} custom-call(bf16[320,2048]{1,0:T(8,128)(2,1)S(1)} %bitcast.55, bf16[192,2048]{1,0:T(8,128)(2,1)S(1)} %bitcast.58, bf16[1024,256]{1,0:T(8,128)(2,1)} %collective-permute-done.4.refs_2_, bf16[1024,256]{1,0:T(8,128)(2,1)} %collective-permute-done.8.refs_3_, ...), custom_call_target="tpu_custom_call" | custom-call | flops 738197504 | bytes 8912896 | tf_op jit(solution)/shard_map/pallas_call | solution.py:152
  187.6 6.1 %all-to-all-start.1 = ((bf16[8,40,2048]{2,1,0:T(8,128)(2,1)}), bf16[8,40,2048]{2,1,0:T(8,128)(2,1)S(1)}, u32[]{:S(2)}, u32[]{:S(2)}) async-start(bf16[8,40,2048]{2,1,0:T(8,128)(2,1)} %bitcast.22), calls=%async_computation.1 | async-start | bytes 2621440 | tf_op jit(solution)/shard_map/all_to_all | solution.py:270
  193.7 3.9 %collective-permute-start.19 = (bf16[20,2048]{1,0:T(8,128)(2,1)S(1)}, bf16[20,2048]{1,0:T(8,128)(2,1)S(1)}, u32[]{:S(2)}, u32[]{:S(2)}) collective-permute-start(bf16[20,2048]{1,0:T(8,128)(2,1)S(1)} %add_convert_fusion.5), channel_id=1, source_target_pairs={{0,16},{8,24},{16,0},{24,8},{32,48},{40,56},{48,32},{56,40},{1,17}... | collective-permute-start | bytes 245768 | tf_op jit(solution)/shard_map/ppermute | solution.py:178
  197.6 2.4 collective-permute-done.19
  200.0 6.0 %collective-permute-start.20 = (bf16[20,2048]{1,0:T(8,128)(2,1)S(1)}, bf16[20,2048]{1,0:T(8,128)(2,1)S(1)}, u32[]{:S(2)}, u32[]{:S(2)}) collective-permute-start(bf16[20,2048]{1,0:T(8,128)(2,1)S(1)} %add_convert_fusion.4), channel_id=1, source_target_pairs={{0,32},{8,40},{16,48},{24,56},{32,0},{40,8},{48,16},{56,24},{1,33}... | collective-permute-start | bytes 245768 | tf_op jit(solution)/shard_map/ppermute | solution.py:178
  206.0 3.4 %collective-permute-done.20 = bf16[20,2048]{1,0:T(8,128)(2,1)S(1)} collective-permute-done((bf16[20,2048]{1,0:T(8,128)(2,1)S(1)}, bf16[20,2048]{1,0:T(8,128)(2,1)S(1)}, u32[]{:S(2)}, u32[]{:S(2)}) %collective-permute-start.20) | collective-permute-done | bytes 81952 | tf_op jit(solution)/shard_map/ppermute | solution.py:178
  209.4 3.5 %collective-permute-start.21 = (bf16[20,2048]{1,0:T(8,128)(2,1)S(1)}, bf16[20,2048]{1,0:T(8,128)(2,1)S(1)}, u32[]{:S(2)}, u32[]{:S(2)}) collective-permute-start(bf16[20,2048]{1,0:T(8,128)(2,1)S(1)} %add_convert_fusion.3), channel_id=1, source_target_pairs={{0,1},{1,0},{2,3},{3,2},{4,5},{5,4},{6,7},{7,6},{8,9},{9,8},{10,11... | collective-permute-start | bytes 245768 | tf_op jit(solution)/shard_map/ppermute | solution.py:178
  212.9 6.1 %collective-permute-done.21 = bf16[20,2048]{1,0:T(8,128)(2,1)S(1)} collective-permute-done((bf16[20,2048]{1,0:T(8,128)(2,1)S(1)}, bf16[20,2048]{1,0:T(8,128)(2,1)S(1)}, u32[]{:S(2)}, u32[]{:S(2)}) %collective-permute-start.21) | collective-permute-done | bytes 81952 | tf_op jit(solution)/shard_map/ppermute | solution.py:178
  219.0 5.0 %collective-permute-start.22 = (bf16[20,2048]{1,0:T(8,128)(2,1)S(1)}, bf16[20,2048]{1,0:T(8,128)(2,1)S(1)}, u32[]{:S(2)}, u32[]{:S(2)}) collective-permute-start(bf16[20,2048]{1,0:T(8,128)(2,1)S(1)} %add_convert_fusion.2), channel_id=1, source_target_pairs={{0,2},{1,3},{2,0},{3,1},{4,6},{5,7},{6,4},{7,5},{8,10},{9,11},{10,... | collective-permute-start | bytes 245768 | tf_op jit(solution)/shard_map/ppermute | solution.py:178
  224.0 2.8 %collective-permute-done.22 = bf16[20,2048]{1,0:T(8,128)(2,1)S(1)} collective-permute-done((bf16[20,2048]{1,0:T(8,128)(2,1)S(1)}, bf16[20,2048]{1,0:T(8,128)(2,1)S(1)}, u32[]{:S(2)}, u32[]{:S(2)}) %collective-permute-start.22) | collective-permute-done | bytes 81952 | tf_op jit(solution)/shard_map/ppermute | solution.py:178
  226.8 7.6 %collective-permute-start.23 = (bf16[20,2048]{1,0:T(8,128)(2,1)S(1)}, bf16[20,2048]{1,0:T(8,128)(2,1)}, u32[]{:S(2)}, u32[]{:S(2)}) collective-permute-start(bf16[20,2048]{1,0:T(8,128)(2,1)S(1)} %add_convert_fusion.1), channel_id=1, source_target_pairs={{0,4},{1,5},{2,6},{3,7},{4,0},{5,1},{6,2},{7,3},{8,12},{9,13},{10,... | collective-permute-start | bytes 245768 | tf_op jit(solution)/shard_map/ppermute | solution.py:178
  235.5 8.5 %collective-permute-start.17 = (bf16[128,2048]{1,0:T(8,128)(2,1)S(1)}, bf16[128,2048]{1,0:T(8,128)(2,1)S(1)}, u32[]{:S(2)}, u32[]{:S(2)}) collective-permute-start(bf16[128,2048]{1,0:T(8,128)(2,1)S(1)} %select_convert_fusion), channel_id=1, source_target_pairs={{64,0},{128,64},{192,128},{256,192},{320,256},{384,320},{448,384},... | collective-permute-start | bytes 1572872 | tf_op jit(solution)/shard_map/ppermute | solution.py:171
  244.6 3.0 %collective-permute-start.16 = (bf16[128,2048]{1,0:T(8,128)(2,1)S(1)}, bf16[128,2048]{1,0:T(8,128)(2,1)S(1)}, u32[]{:S(2)}, u32[]{:S(2)}) collective-permute-start(bf16[128,2048]{1,0:T(8,128)(2,1)S(1)} %fusion.5), channel_id=1, source_target_pairs={{0,64},{64,128},{128,192},{192,256},{256,320},{320,384},{384,448},... | collective-permute-start | bytes 1572872 | tf_op jit(solution)/shard_map/ppermute | solution.py:171
  249.3 2.7 %collective-permute-done.17 = bf16[128,2048]{1,0:T(8,128)(2,1)S(1)} collective-permute-done((bf16[128,2048]{1,0:T(8,128)(2,1)S(1)}, bf16[128,2048]{1,0:T(8,128)(2,1)S(1)}, u32[]{:S(2)}, u32[]{:S(2)}) %collective-permute-start.17) | collective-permute-done | bytes 524320 | tf_op jit(solution)/shard_map/ppermute | solution.py:171
  (161 shorter events, 51.4 us)
Async XLA Ops:
  0.7 15.1 %collective-permute-start = (bf16[128,2048]{1,0:T(8,128)(2,1)}, bf16[128,2048]{1,0:T(8,128)(2,1)S(1)}, u32[]{:S(2)}, u32[]{:S(2)}) collective-permute-start(bf16[128,2048]{1,0:T(8,128)(2,1)} %bitcast.59), channel_id=1, source_target_pairs={{0,8},{8,16},{16,24},{24,32},{32,40},{40,48},{48,56},{56,0},{1,9},... | collective-permute-start | bytes 1572872 | tf_op jit(solution)/shard_map/ppermute | solution.py:165
  15.8 50.0 %copy-start.16 = (bf16[128,2048]{1,0:T(8,128)(2,1)}, bf16[128,2048]{1,0:T(8,128)(2,1)S(1)}, u32[]{:S(2)}) copy-start(bf16[128,2048]{1,0:T(8,128)(2,1)S(1)} %collective-permute-done.refs_5_) | copy-start | bytes 1572868
  15.8 139.7 %all-to-all-start = ((bf16[8,64,2176]{2,1,0:T(8,128)(2,1)}), bf16[8,64,2176]{2,1,0:T(8,128)(2,1)}, u32[]{:S(2)}, u32[]{:S(2)}) async-start(bf16[8,64,2176]{2,1,0:T(8,128)(2,1)} %bitcast.64), calls=%async_computation | async-start | bytes 4456448 | tf_op jit(solution)/shard_map/all_to_all | solution.py:254
  28.8 35.1 %copy-start.14 = (bf16[1,1,128,2048]{3,2,1,0:T(8,128)(2,1)S(1)}, bf16[1,1,128,2048]{3,2,1,0:T(8,128)(2,1)}, u32[]{:S(2)}) copy-start(bf16[1,1,128,2048]{3,2,1,0:T(8,128)(2,1)} %param.31) | copy-start | bytes 1572868
  28.8 84.3 %copy-start.29 = (bf16[1,2,10,2048]{3,1,2,0:T(2,128)(2,1)S(1)}, bf16[1,2,10,2048]{3,1,2,0:T(2,128)(2,1)}, u32[]{:S(2)}) copy-start(bf16[1,2,10,2048]{3,1,2,0:T(2,128)(2,1)} %param.27) | copy-start | bytes 245764
  28.9 26.5 %collective-permute-start.1 = (bf16[2048,256]{1,0:T(8,128)(2,1)S(1)}, bf16[2048,256]{1,0:T(8,128)(2,1)S(1)}, u32[]{:S(2)}, u32[]{:S(2)}) collective-permute-start(bf16[2048,256]{1,0:T(8,128)(2,1)S(1)} %pad_maximum_fusion.refs_2_), channel_id=1, source_target_pairs={{0,8},{8,16},{16,24},{24,32},{32,40},{40,48},{48,56},{56,0},{1,9},... | collective-permute-start | bytes 3145736 | tf_op jit(solution)/shard_map/ppermute | solution.py:165
  31.0 27.3 %collective-permute-start.5 = (bf16[2048,256]{1,0:T(8,128)(2,1)S(1)}, bf16[2048,256]{1,0:T(8,128)(2,1)S(1)}, u32[]{:S(2)}, u32[]{:S(2)}) collective-permute-start(bf16[2048,256]{1,0:T(8,128)(2,1)S(1)} %pad_maximum_fusion.refs_2_), channel_id=1, source_target_pairs={{0,56},{8,0},{16,8},{24,16},{32,24},{40,32},{48,40},{56,48},{1,57}... | collective-permute-start | bytes 3145736 | tf_op jit(solution)/shard_map/ppermute | solution.py:165
  55.4 44.7 %collective-permute-start.2 = (bf16[2048,256]{1,0:T(8,128)(2,1)S(1)}, bf16[2048,256]{1,0:T(8,128)(2,1)}, u32[]{:S(2)}, u32[]{:S(2)}) collective-permute-start(bf16[2048,256]{1,0:T(8,128)(2,1)S(1)} %collective-permute-done.1.refs_4_), channel_id=1, source_target_pairs={{0,8},{8,16},{16,24},{24,32},{32,40},{40,48},{48,56},{56,0},{1,9},... | collective-permute-start | bytes 3145736 | tf_op jit(solution)/shard_map/ppermute | solution.py:165
  58.3 43.7 %collective-permute-start.6 = (bf16[2048,256]{1,0:T(8,128)(2,1)S(1)}, bf16[2048,256]{1,0:T(8,128)(2,1)}, u32[]{:S(2)}, u32[]{:S(2)}) collective-permute-start(bf16[2048,256]{1,0:T(8,128)(2,1)S(1)} %collective-permute-done.5.refs_6_), channel_id=1, source_target_pairs={{0,56},{8,0},{16,8},{24,16},{32,24},{40,32},{48,40},{56,48},{1,57}... | collective-permute-start | bytes 3145736 | tf_op jit(solution)/shard_map/ppermute | solution.py:165
  63.9 30.1 %collective-permute-start.12 = (bf16[128,2048]{1,0:T(8,128)(2,1)S(1)}, bf16[128,2048]{1,0:T(8,128)(2,1)S(1)}, u32[]{:S(2)}, u32[]{:S(2)}) collective-permute-start(bf16[128,2048]{1,0:T(8,128)(2,1)S(1)} %bitcast.60), channel_id=1, source_target_pairs={{0,56},{8,0},{16,8},{24,16},{32,24},{40,32},{48,40},{56,48},{1,57}... | collective-permute-start | bytes 1572872 | tf_op jit(solution)/shard_map/ppermute | solution.py:165
  65.8 40.8 %collective-permute-start.9 = (bf16[128,2048]{1,0:T(8,128)(2,1)S(1)}, bf16[128,2048]{1,0:T(8,128)(2,1)}, u32[]{:S(2)}, u32[]{:S(2)}) collective-permute-start(bf16[128,2048]{1,0:T(8,128)(2,1)S(1)} %collective-permute-done.refs_5_), channel_id=1, source_target_pairs={{0,8},{8,16},{16,24},{24,32},{32,40},{40,48},{48,56},{56,0},{1,9},... | collective-permute-start | bytes 1572872 | tf_op jit(solution)/shard_map/ppermute | solution.py:165
  94.0 14.6 %collective-permute-start.13 = (bf16[128,2048]{1,0:T(8,128)(2,1)S(1)}, bf16[128,2048]{1,0:T(8,128)(2,1)}, u32[]{:S(2)}, u32[]{:S(2)}) collective-permute-start(bf16[128,2048]{1,0:T(8,128)(2,1)S(1)} %collective-permute-done.12.refs_7_), channel_id=1, source_target_pairs={{0,56},{8,0},{16,8},{24,16},{32,24},{40,32},{48,40},{56,48},{1,57}... | collective-permute-start | bytes 1572872 | tf_op jit(solution)/shard_map/ppermute | solution.py:165
  100.1 47.0 %collective-permute-start.3 = (bf16[2048,256]{1,0:T(8,128)(2,1)}, bf16[2048,256]{1,0:T(8,128)(2,1)S(1)}, u32[]{:S(2)}, u32[]{:S(2)}) collective-permute-start(bf16[2048,256]{1,0:T(8,128)(2,1)} %collective-permute-done.2.refs_8_), channel_id=1, source_target_pairs={{0,8},{8,16},{16,24},{24,32},{32,40},{40,48},{48,56},{56,0},{1,9},... | collective-permute-start | bytes 3145736 | tf_op jit(solution)/shard_map/ppermute | solution.py:165
  102.0 47.9 %collective-permute-start.7 = (bf16[2048,256]{1,0:T(8,128)(2,1)}, bf16[2048,256]{1,0:T(8,128)(2,1)S(1)}, u32[]{:S(2)}, u32[]{:S(2)}) collective-permute-start(bf16[2048,256]{1,0:T(8,128)(2,1)} %collective-permute-done.6.refs_10_), channel_id=1, source_target_pairs={{0,56},{8,0},{16,8},{24,16},{32,24},{40,32},{48,40},{56,48},{1,57}... | collective-permute-start | bytes 3145736 | tf_op jit(solution)/shard_map/ppermute | solution.py:165
  106.6 28.9 %collective-permute-start.10 = (bf16[128,2048]{1,0:T(8,128)(2,1)}, bf16[128,2048]{1,0:T(8,128)(2,1)S(1)}, u32[]{:S(2)}, u32[]{:S(2)}) collective-permute-start(bf16[128,2048]{1,0:T(8,128)(2,1)} %collective-permute-done.9.refs_9_), channel_id=1, source_target_pairs={{0,8},{8,16},{16,24},{24,32},{32,40},{40,48},{48,56},{56,0},{1,9},... | collective-permute-start | bytes 1572872 | tf_op jit(solution)/shard_map/ppermute | solution.py:165
  108.5 32.6 %collective-permute-start.14 = (bf16[128,2048]{1,0:T(8,128)(2,1)}, bf16[128,2048]{1,0:T(8,128)(2,1)S(1)}, u32[]{:S(2)}, u32[]{:S(2)}) collective-permute-start(bf16[128,2048]{1,0:T(8,128)(2,1)} %collective-permute-done.13.refs_11_), channel_id=1, source_target_pairs={{0,56},{8,0},{16,8},{24,16},{32,24},{40,32},{48,40},{56,48},{1,57}... | collective-permute-start | bytes 1572872 | tf_op jit(solution)/shard_map/ppermute | solution.py:165
  113.5 43.7 %copy-start.36 = (f32[20]{0:T(128)}, f32[20]{0:T(128)S(1)}, u32[]{:S(2)}) copy-start(f32[20]{0:T(128)S(1)} %rsqrt.36) | copy-start | bytes 244
  136.2 43.1 %collective-permute-start.11 = (bf16[64,2048]{1,0:T(8,128)(2,1)}, bf16[64,2048]{1,0:T(8,128)(2,1)S(1)}, u32[]{:S(2)}, u32[]{:S(2)}) collective-permute-start(bf16[64,2048]{1,0:T(8,128)(2,1)} %slice.52), channel_id=1, source_target_pairs={{0,8},{8,16},{16,24},{24,32},{32,40},{40,48},{48,56},{56,0},{1,9},... | collective-permute-start | bytes 786440 | tf_op jit(solution)/shard_map/ppermute | solution.py:165
  141.9 37.5 %collective-permute-start.15 = (bf16[64,2048]{1,0:T(8,128)(2,1)}, bf16[64,2048]{1,0:T(8,128)(2,1)}, u32[]{:S(2)}, u32[]{:S(2)}) collective-permute-start(bf16[64,2048]{1,0:T(8,128)(2,1)} %slice.53), channel_id=1, source_target_pairs={{0,56},{8,0},{16,8},{24,16},{32,24},{40,32},{48,40},{56,48},{1,57}... | collective-permute-start | bytes 786440 | tf_op jit(solution)/shard_map/ppermute | solution.py:165
  148.0 31.4 %collective-permute-start.4 = (bf16[1024,256]{1,0:T(8,128)(2,1)}, bf16[1024,256]{1,0:T(8,128)(2,1)}, u32[]{:S(2)}, u32[]{:S(2)}) collective-permute-start(bf16[1024,256]{1,0:T(8,128)(2,1)} %slice.50), channel_id=1, source_target_pairs={{0,8},{8,16},{16,24},{24,32},{32,40},{40,48},{48,56},{56,0},{1,9},... | collective-permute-start | bytes 1572872 | tf_op jit(solution)/shard_map/ppermute | solution.py:165
  150.8 28.6 %collective-permute-start.8 = (bf16[1024,256]{1,0:T(8,128)(2,1)}, bf16[1024,256]{1,0:T(8,128)(2,1)}, u32[]{:S(2)}, u32[]{:S(2)}) collective-permute-start(bf16[1024,256]{1,0:T(8,128)(2,1)} %slice.51), channel_id=1, source_target_pairs={{0,56},{8,0},{16,8},{24,16},{32,24},{40,32},{48,40},{56,48},{1,57}... | collective-permute-start | bytes 1572872 | tf_op jit(solution)/shard_map/ppermute | solution.py:165
  185.5 49.0 %copy-start.21 = (f32[128,2048]{1,0:T(8,128)S(1)}, f32[128,2048]{1,0:T(8,128)}, u32[]{:S(2)}) copy-start(f32[128,2048]{1,0:T(8,128)} %copy-done.20) | copy-start | bytes 3145732
  185.5 8.1 %collective-permute-start.18 = (bf16[20,2048]{1,0:T(8,128)(2,1)S(1)}, bf16[20,2048]{1,0:T(8,128)(2,1)S(1)}, u32[]{:S(2)}, u32[]{:S(2)}) collective-permute-start(bf16[20,2048]{1,0:T(8,128)(2,1)S(1)} %fusion.11), channel_id=1, source_target_pairs={{0,8},{8,0},{16,24},{24,16},{32,40},{40,32},{48,56},{56,48},{1,9},... | collective-permute-start | bytes 245768 | tf_op jit(solution)/shard_map/ppermute | solution.py:178
  187.6 46.9 %all-to-all-start.1 = ((bf16[8,40,2048]{2,1,0:T(8,128)(2,1)}), bf16[8,40,2048]{2,1,0:T(8,128)(2,1)S(1)}, u32[]{:S(2)}, u32[]{:S(2)}) async-start(bf16[8,40,2048]{2,1,0:T(8,128)(2,1)} %bitcast.22), calls=%async_computation.1 | async-start | bytes 2621440 | tf_op jit(solution)/shard_map/all_to_all | solution.py:270
  193.7 6.3 %collective-permute-start.19 = (bf16[20,2048]{1,0:T(8,128)(2,1)S(1)}, bf16[20,2048]{1,0:T(8,128)(2,1)S(1)}, u32[]{:S(2)}, u32[]{:S(2)}) collective-permute-start(bf16[20,2048]{1,0:T(8,128)(2,1)S(1)} %add_convert_fusion.5), channel_id=1, source_target_pairs={{0,16},{8,24},{16,0},{24,8},{32,48},{40,56},{48,32},{56,40},{1,17}... | collective-permute-start | bytes 245768 | tf_op jit(solution)/shard_map/ppermute | solution.py:178
  200.0 35.1 %copy-start.35 = (f32[128]{0:T(128)S(1)}, f32[128]{0:T(128)}, u32[]{:S(2)}) copy-start(f32[128]{0:T(128)} %get-tuple-element.46) | copy-start | bytes 1540
  200.0 9.4 %collective-permute-start.20 = (bf16[20,2048]{1,0:T(8,128)(2,1)S(1)}, bf16[20,2048]{1,0:T(8,128)(2,1)S(1)}, u32[]{:S(2)}, u32[]{:S(2)}) collective-permute-start(bf16[20,2048]{1,0:T(8,128)(2,1)S(1)} %add_convert_fusion.4), channel_id=1, source_target_pairs={{0,32},{8,40},{16,48},{24,56},{32,0},{40,8},{48,16},{56,24},{1,33}... | collective-permute-start | bytes 245768 | tf_op jit(solution)/shard_map/ppermute | solution.py:178
  209.4 9.6 %collective-permute-start.21 = (bf16[20,2048]{1,0:T(8,128)(2,1)S(1)}, bf16[20,2048]{1,0:T(8,128)(2,1)S(1)}, u32[]{:S(2)}, u32[]{:S(2)}) collective-permute-start(bf16[20,2048]{1,0:T(8,128)(2,1)S(1)} %add_convert_fusion.3), channel_id=1, source_target_pairs={{0,1},{1,0},{2,3},{3,2},{4,5},{5,4},{6,7},{7,6},{8,9},{9,8},{10,11... | collective-permute-start | bytes 245768 | tf_op jit(solution)/shard_map/ppermute | solution.py:178
  219.0 7.8 %collective-permute-start.22 = (bf16[20,2048]{1,0:T(8,128)(2,1)S(1)}, bf16[20,2048]{1,0:T(8,128)(2,1)S(1)}, u32[]{:S(2)}, u32[]{:S(2)}) collective-permute-start(bf16[20,2048]{1,0:T(8,128)(2,1)S(1)} %add_convert_fusion.2), channel_id=1, source_target_pairs={{0,2},{1,3},{2,0},{3,1},{4,6},{5,7},{6,4},{7,5},{8,10},{9,11},{10,... | collective-permute-start | bytes 245768 | tf_op jit(solution)/shard_map/ppermute | solution.py:178
  226.8 20.7 %collective-permute-start.23 = (bf16[20,2048]{1,0:T(8,128)(2,1)S(1)}, bf16[20,2048]{1,0:T(8,128)(2,1)}, u32[]{:S(2)}, u32[]{:S(2)}) collective-permute-start(bf16[20,2048]{1,0:T(8,128)(2,1)S(1)} %add_convert_fusion.1), channel_id=1, source_target_pairs={{0,4},{1,5},{2,6},{3,7},{4,0},{5,1},{6,2},{7,3},{8,12},{9,13},{10,... | collective-permute-start | bytes 245768 | tf_op jit(solution)/shard_map/ppermute | solution.py:178
  235.5 16.5 %collective-permute-start.17 = (bf16[128,2048]{1,0:T(8,128)(2,1)S(1)}, bf16[128,2048]{1,0:T(8,128)(2,1)S(1)}, u32[]{:S(2)}, u32[]{:S(2)}) collective-permute-start(bf16[128,2048]{1,0:T(8,128)(2,1)S(1)} %select_convert_fusion), channel_id=1, source_target_pairs={{64,0},{128,64},{192,128},{256,192},{320,256},{384,320},{448,384},... | collective-permute-start | bytes 1572872 | tf_op jit(solution)/shard_map/ppermute | solution.py:171
  244.6 9.1 %collective-permute-start.16 = (bf16[128,2048]{1,0:T(8,128)(2,1)S(1)}, bf16[128,2048]{1,0:T(8,128)(2,1)S(1)}, u32[]{:S(2)}, u32[]{:S(2)}) collective-permute-start(bf16[128,2048]{1,0:T(8,128)(2,1)S(1)} %fusion.5), channel_id=1, source_target_pairs={{0,64},{64,128},{128,192},{192,256},{256,320},{320,384},{384,448},... | collective-permute-start | bytes 1572872 | tf_op jit(solution)/shard_map/ppermute | solution.py:171
  (33 other events, 176.5 us)

commit v3 on v2

--- a/solution.py
+++ b/solution.py
@@ -59,18 +59,19 @@
 
 
 def expert_kernel(parts, has_acc, final, *refs):
-    x_ref, c_ref = refs[:2]
-    at = 2
-    shards = []
+    refs = list(refs)
+    x_ref, c_ref = refs.pop(0), refs.pop(0)
+    sources = []
     for count in parts:
-        shards.append((refs[at : at + count], refs[at + count : at + 2 * count]))
-        at += 2 * count
+        sources.append((refs[:count], refs[count : 2 * count]))
+        refs = refs[2 * count :]
     acc_ref = None
     if has_acc:
-        acc_ref = refs[at]
-        at += 1
-    out_ref = refs[at]
-    total = refs[at + 1] if final else out_ref
+        acc_ref, _ = refs.pop(0), refs.pop(0)
+    slot_refs = [refs.pop(0) for _ in range(5)] if final else None
+    out_ref, note_ref = refs.pop(0), refs.pop(0)
+    gu_ref, down_ref, sems = refs.pop(0), refs.pop(0), refs.pop(0)
+
     blocks = x_ref.shape[0] // ROWS
     width = x_ref.shape[1]
     step = 512
@@ -78,18 +79,22 @@
     row = lax.broadcasted_iota(jnp.int32, (blocks, ROWS - FWD_AT, 1), 1) + FWD_AT
     is_fwd = (row >= CAP) & (row < 2 * CAP)
 
-    for number, (gu_refs, d_refs) in enumerate(shards):
-        depth = width // len(gu_refs)
-        gu_out = None
-        for k, ref in enumerate(gu_refs):
-            piece = jnp.dot(
-                x_ref[:, k * depth : (k + 1) * depth], ref[...], preferred_element_type=F32
-            )
-            gu_out = piece if gu_out is None else gu_out + piece
-        if len(d_refs) == 1:
-            down = d_refs[0][...]
-        else:
-            down = jnp.concatenate([ref[...] for ref in d_refs], axis=0)
+    fetches = []
+    for number, pair in enumerate(sources):
+        group = []
+        for side, (pieces, held) in enumerate(zip(pair, (gu_ref, down_ref))):
+            for k, ref in enumerate(pieces):
+                into = held.at[number, pl.ds(k * ref.shape[0], ref.shape[0]), :]
+                group.append(pltpu.make_async_copy(ref, into, sems.at[number, side, k]))
+        fetches.append(group)
+        for copy in group:
+            copy.start()
+
+    for number, group in enumerate(fetches):
+        for copy in group:
+            copy.wait()
+        down = down_ref[number]
+        gu_out = jnp.dot(x_ref[...], gu_ref[number], preferred_element_type=F32)
         half = gu_out.shape[1] // 2
         hidden_grad = lax.dot_general(c_ref[...], down, contract, preferred_element_type=F32)
         gate = gu_out[:, :half].reshape(blocks, ROWS, half)
@@ -105,13 +110,10 @@
         up_grad = hidden_grad * (gate_b * sig)
         grads = jnp.concatenate([gate_grad.astype(BF16), up_grad.astype(BF16)], axis=1)
         first = number == 0 and not has_acc
-        last = final and number == len(shards) - 1
         for n in range(width // step):
             cols = slice(n * step, (n + 1) * step)
-            part, inner = divmod(n * step, depth)
-            gu_rows = gu_refs[part][inner : inner + step, :]
-            back = lax.dot_general(grads, gu_rows, contract, preferred_element_type=F32)
-            fwd = jnp.dot(hidden, down[:, cols], preferred_element_type=F32)
+            back = lax.dot_general(grads, gu_ref[number, cols, :], contract, preferred_element_type=F32)
+            fwd = jnp.dot(hidden, down_ref[number, :, cols], preferred_element_type=F32)
             back = back.reshape(blocks, COT_ROWS, step)
             fwd = fwd.reshape(blocks, ROWS - FWD_AT, step)
             pieces = [
@@ -121,41 +123,58 @@
             ]
             value = jnp.concatenate(pieces, axis=1).reshape(blocks * ROWS, step)
             if not first:
-                source = acc_ref if number == 0 else total
+                source = acc_ref if number == 0 else out_ref
                 value = value + source[:, cols]
-            if last:
-                out_ref[:, cols] = value.astype(out_ref.dtype)
-            else:
-                total[:, cols] = value
-
-
-def w_hidden(shards):
-    return sum(d.shape[0] for _, ds in shards for d in ds)
-
-
-def expert_step(rows, cots, shards, acc, final):
+            out_ref[:, cols] = value.astype(out_ref.dtype)
+
+    if final:
+        weighing_ref, gain_ref, slot_in_ref, scale_ref, cot_ref = slot_refs
+        both = jnp.dot(weighing_ref[...], out_ref[...], preferred_element_type=F32)
+        count = weighing_ref.shape[0] // 2
+        slot_q = (both[:count] + both[count:]) * gain_ref[...]
+        slot_in = slot_in_ref[...]
+        scale = scale_ref[...]
+        inner = jnp.mean(slot_in * slot_q, axis=1, keepdims=True)
+        note_ref[...] = cot_ref[...] + scale * slot_q - slot_in * (scale * scale * scale * inner)
+    else:
+        note_ref[...] = jnp.zeros_like(note_ref)
+
+
+def expert_step(rows, cots, shards, before=None, slot_data=None):
+    final = slot_data is not None
     parts = tuple(len(gu) for gu, _ in shards)
     operands = [rows, cots]
     for gu, d in shards:
         operands += list(gu) + list(d)
-    if acc is not None:
-        operands.append(acc)
+    near = pl.BlockSpec(memory_space=pltpu.VMEM)
+    specs = [near, near] + [pl.BlockSpec(memory_space=pl.ANY)] * (len(operands) - 2)
+    if before is not None:
+        operands += list(before)
+        specs += [near, near]
+    if final:
+        operands += list(slot_data)
+        specs += [near] * len(slot_data)
     shape = rows.shape
-    whole = pl.BlockSpec(memory_space=pltpu.VMEM)
-    scratch = [pltpu.VMEM(shape, F32)] if final else []
-    hidden = w_hidden(shards)
+    gu_shape = (sum(g.shape[0] for g in shards[0][0]), shards[0][0][0].shape[1])
+    d_shape = (sum(d.shape[0] for d in shards[0][1]), shape[1])
+    hidden = len(shards) * d_shape[0]
     cost = pl.CostEstimate(
         flops=2 * hidden * shape[1] * (2 * shape[0] + 4 * cots.shape[0]),
         transcendentals=hidden * 2 * cots.shape[0],
         bytes_accessed=sum(o.size * o.dtype.itemsize for o in operands) + 4 * rows.size,
     )
+    note = (SLOTS if final else 8, shape[1] if final else 128)
     return pl.pallas_call(
-        functools.partial(expert_kernel, parts, acc is not None, final),
-        out_shape=jax.ShapeDtypeStruct(shape, BF16 if final else F32),
-        in_specs=[whole] * len(operands),
-        out_specs=whole,
-        scratch_shapes=scratch,
-        compiler_params=pltpu.CompilerParams(vmem_limit_bytes=40 * 1024 * 1024),
+        functools.partial(expert_kernel, parts, before is not None, final),
+        out_shape=(jax.ShapeDtypeStruct(shape, BF16 if final else F32), jax.ShapeDtypeStruct(note, F32)),
+        in_specs=specs,
+        out_specs=(near, near),
+        scratch_shapes=[
+            pltpu.VMEM((len(shards), *gu_shape), BF16),
+            pltpu.VMEM((len(shards), *d_shape), BF16),
+            pltpu.SemaphoreType.DMA((len(shards), 2, max(parts))),
+        ],
+        compiler_params=pltpu.CompilerParams(vmem_limit_bytes=32 * 1024 * 1024),
         cost_estimate=cost,
     )(*operands)
 
@@ -202,17 +221,27 @@
     tok_count, width = fwd_acts.shape[1:]
     gain_row = norm_gain[0]
     flat_table = prompts[0].reshape(SLOTS, width)
-    splits = lax.axis_size("split")
 
     own_gu = jnp.concatenate([w_gate[0, 0], w_up[0, 0]], axis=1)
     own_d = w_down[0, 0]
-    rounds = []
-    gu_a = gu_b = own_gu
-    d_a = d_b = own_d
-    for _ in range(splits // 2 - 1):
-        d_a, d_b = rotated(d_a, "split", 1), rotated(d_b, "split", -1)
-        gu_a, gu_b = rotated(gu_a, "split", 1), rotated(gu_b, "split", -1)
-        rounds.append([((gu_a,), (d_a,)), ((gu_b,), (d_b,))])
+    gu_ring, d_ring = [(own_gu, own_gu)], [(own_d, own_d)]
+
+    def onward(ring):
+        up, down = ring[-1]
+        ring.append((rotated(up, "split", 1), rotated(down, "split", -1)))
+
+    def held_back(ring, note):
+        up, down, note = lax.optimization_barrier((*ring[-1], note))
+        ring[-1] = (up, down)
+        return note
+
+    def shards(step):
+        return [((gu_ring[step][k],), (d_ring[step][k],)) for k in range(2)]
+
+    for _ in range(2):
+        onward(gu_ring)
+        onward(d_ring)
+    onward(gu_ring)
 
     first_row = (lax.axis_index("split") * lax.axis_size("column") + lax.axis_index("column")) * tok_count
     fwd_in, _, fwd_normed, _, _, _ = prepare(
@@ -250,39 +279,39 @@
     picker = target[None, :] == jnp.arange(EXPERTS * BLOCK, dtype=jnp.int32)[:, None]
     packed = jnp.dot(picker.astype(BF16), sources, preferred_element_type=F32).astype(BF16)
     packed = packed.reshape(EXPERTS, BLOCK, width + EXTRA)
-    packed, _ = lax.optimization_barrier((packed, rounds[0][0][1][0]))
+    packed, _ = lax.optimization_barrier((packed, gu_ring[1]))
     arrived = lax.all_to_all(packed, "column", split_axis=0, concat_axis=0, tiled=True)
     rows = arrived[:, :ROWS, :width].reshape(EXPERTS * ROWS, width)
     cots = arrived[:, ROWS:, :width].reshape(EXPERTS * COT_ROWS, width)
     notes = arrived[:, :ROWS, width : width + 3].astype(F32).reshape(EXPERTS * ROWS, 3)
 
-    acc = expert_step(rows, cots, [((own_gu,), (own_d,))] + rounds[0] + rounds[1], None, False)
+    at_slot = notes[:, 2][None, :] == jnp.arange(SLOTS, dtype=F32)[:, None]
+    weighing = jnp.concatenate(
+        [jnp.where(at_slot, notes[:, 0][None, :], 0.0), jnp.where(at_slot, notes[:, 1][None, :], 0.0)], axis=0
+    ).astype(BF16)
+    slot_in = flat_table.astype(F32)
+    slot_scale = lax.rsqrt(jnp.mean(slot_in * slot_in, axis=1, keepdims=True) + EPS)
+    slot_cot = jnp.dot(jnp.transpose(selector.astype(BF16)), cotangent, preferred_element_type=F32)
+    slot_data = (weighing, norm_gain, slot_in, slot_scale, slot_cot)
+
+    acc, note = expert_step(rows, cots, [((own_gu,), (own_d,))] + shards(1))
+    note = held_back(d_ring, note)
+    onward(d_ring)
+    acc, note = expert_step(rows, cots, shards(2), (acc, note))
+    note = held_back(d_ring, note)
+    gu_up, gu_down = gu_ring[-1]
+    d_up, d_down = d_ring[-1]
     half_k, half_h = width // 2, own_d.shape[0] // 2
-    halves = (gu_a[:half_k], gu_b[half_k:], d_a[:half_h], d_b[half_h:])
     last = (
-        (rotated(halves[0], "split", 1), rotated(halves[1], "split", -1)),
-        (rotated(halves[2], "split", 1), rotated(halves[3], "split", -1)),
-    )
-    for pair in rounds[2:]:
-        acc = expert_step(rows, cots, pair, acc, False)
-    partial = expert_step(rows, cots, [last], acc, True)
+        (rotated(gu_up[:half_k], "split", 1), rotated(gu_down[half_k:], "split", -1)),
+        (rotated(d_up[:half_h], "split", 1), rotated(d_down[half_h:], "split", -1)),
+    )
+    before = expert_step(rows, cots, shards(3), (acc, note))
+    partial, local_sums = expert_step(rows, cots, [last], before, slot_data)
 
     returned = lax.all_to_all(
         partial.reshape(EXPERTS, ROWS, width), "column", split_axis=0, concat_axis=0, tiled=True
     ).reshape(EXPERTS * ROWS, width)
-
-    slot_iota = jnp.arange(SLOTS, dtype=F32)[:, None]
-    at_slot = notes[:, 2][None, :] == slot_iota
-    weighing = jnp.concatenate(
-        [jnp.where(at_slot, notes[:, 0][None, :], 0.0), jnp.where(at_slot, notes[:, 1][None, :], 0.0)], axis=0
-    ).astype(BF16)
-    both = jnp.dot(weighing, partial, preferred_element_type=F32)
-    slot_q = (both[:SLOTS] + both[SLOTS:]) * gain_row[None, :]
-    slot_in = flat_table.astype(F32)
-    slot_scale = lax.rsqrt(jnp.mean(slot_in * slot_in, axis=1, keepdims=True) + EPS)
-    slot_inner = jnp.mean(slot_in * slot_q, axis=1, keepdims=True)
-    slot_cot = jnp.dot(jnp.transpose(selector.astype(BF16)), cotangent, preferred_element_type=F32)
-    local_sums = slot_cot + slot_scale * slot_q - slot_in * slot_scale**3 * slot_inner
     totals = summed(summed(local_sums, "split"), "column")
     prompt_grads = totals.astype(BF16).reshape(1, TENANTS, PLEN, width)
 

time: 258 us -> 239 us (0.926)
  waiting for transfers between devices: 87.2 us -> 75.4 us
  local copies, waits for them, and re-layouts: 23.8 us -> 18.6 us
  Pallas kernels: 14.5 us -> 17.5 us
    ppermute x16, waiting for transfers between devices: 68.1 us -> 42.4 us  [rotated(): lax.ppermute(value, axis, [(i, (i + distance) % size) for i in range(size)])]
    unnamed x84 -> x74, local copies, waits for them, and re-layouts: 16 us -> 7.52 us
    all_to_all x1, waiting for transfers between devices: 0.01 us -> 7.71 us  [on_device(): lax.all_to_all(packed, 'column', split_axis=0, concat_axis=0, tiled=True)]
    ppermute x6, waiting for transfers between devices: 14.6 us -> 20 us  [summed(): lax.ppermute(value.astype(BF16), axis, [(i, i ^ distance) for i in range(...]
    ppermute x6, starting transfers between devices: 28.1 us -> 24.9 us  [summed(): lax.ppermute(value.astype(BF16), axis, [(i, i ^ distance) for i in range(...]
    pallas_call x3 -> x4, Pallas kernels: 14.5 us -> 17.5 us  [expert_step(): pl.pallas_call(functools.partial(expert_kernel, parts, before is not None...]
  transfers between devices with their start and end apart: 26 -> 26, of which waited for: 10 -> 13; matrix products, arithmetic and copies ran while one was open for 9% -> 11% of each run, Pallas kernels for 4% -> 6%
where the time goes in v3:
time: 239 us; the launch traced here: 238 us
  starting transfers between devices  111 us (46%)
  waiting for transfers between devices  75.4 us (32%)
  local copies, waits for them, and re-layouts  18.6 us (8%)
  Pallas kernels  17.5 us (7%)
  matrix products  8.16 us (3%)
  other arithmetic  5.14 us (2%)
    ppermute x16, starting transfers between devices, rotated(): lax.ppermute(value, axis, [(i, (i + distance) % size) for i in range(size)])  52.2 us
    ppermute x16, waiting for transfers between devices, rotated(): lax.ppermute(value, axis, [(i, (i + distance) % size) for i in range(size)])  42.4 us
    ppermute x6, starting transfers between devices, summed(): lax.ppermute(value.astype(BF16), axis, [(i, i ^ distance) for i in range(...  24.9 us
    ppermute x6, waiting for transfers between devices, summed(): lax.ppermute(value.astype(BF16), axis, [(i, i ^ distance) for i in range(...  20 us
    pallas_call x4, Pallas kernels, expert_step(): pl.pallas_call(functools.partial(expert_kernel, parts, before is not None...  17.5 us
    all_to_all x1, starting transfers between devices, on_device(): lax.all_to_all(packed, 'column', split_axis=0, concat_axis=0, tiled=True)  14 us
    ppermute x2, starting transfers between devices, shifted(): return lax.ppermute(block, axis, route)  13.9 us
    all_to_all x1, waiting for transfers between devices, on_device(): lax.all_to_all(packed, 'column', split_axis=0, concat_axis=0, tiled=True)  7.71 us
  transfers between devices with their start and end apart: 26, of which 13 were waited for; matrix products, arithmetic and copies ran while one was open for 11% of the time, Pallas kernels for 6%

profile of v3, /device:TPU:1, one launch (start us, length us, event | category | flops | bytes accessed | tf_op | source)
XLA Modules:
  0.0 237.9 jit_solution(16430815988981872898)
XLA Ops:
  2.1 4.2 %collective-permute-start = (bf16[2048,256]{1,0:T(8,128)(2,1)S(1)}, bf16[2048,256]{1,0:T(8,128)(2,1)S(1)}, u32[]{:S(2)}, u32[]{:S(2)}) collective-permute-start(bf16[2048,256]{1,0:T(8,128)(2,1)S(1)} %pad_maximum_fusion.refs_2_), channel_id=1, source_target_pairs={{0,8},{8,16},{16,24},{24,32},{32,40},{40,48},{48,56},{56,0},{1,9},... | collective-permute-start | bytes 3145736 | tf_op jit(solution)/shard_map/ppermute | solution.py:184
  6.3 3.8 %collective-permute-start.1 = (bf16[2048,256]{1,0:T(8,128)(2,1)S(1)}, bf16[2048,256]{1,0:T(8,128)(2,1)}, u32[]{:S(2)}, u32[]{:S(2)}) collective-permute-start(bf16[2048,256]{1,0:T(8,128)(2,1)S(1)} %pad_maximum_fusion.refs_2_), channel_id=1, source_target_pairs={{0,56},{8,0},{16,8},{24,16},{32,24},{40,32},{48,40},{56,48},{1,57}... | collective-permute-start | bytes 3145736 | tf_op jit(solution)/shard_map/ppermute | solution.py:184
  18.4 7.4 %collective-permute-done.refs_4_ = bf16[2048,256]{1,0:T(8,128)(2,1)S(1)} collective-permute-done((bf16[2048,256]{1,0:T(8,128)(2,1)S(1)}, bf16[2048,256]{1,0:T(8,128)(2,1)S(1)}, u32[]{:S(2)}, u32[]{:S(2)}) %collective-permute-start) | collective-permute-done | bytes 1048608 | tf_op jit(solution)/shard_map/ppermute | solution.py:184
  28.2 14.0 %all-to-all-start = ((bf16[8,64,2176]{2,1,0:T(8,128)(2,1)}), bf16[8,64,2176]{2,1,0:T(8,128)(2,1)}, u32[]{:S(2)}, u32[]{:S(2)}) async-start(bf16[8,64,2176]{2,1,0:T(8,128)(2,1)} %bitcast.67), calls=%async_computation | async-start | bytes 4456448 | tf_op jit(solution)/shard_map/all_to_all | solution.py:283
  42.2 3.2 %collective-permute-start.2 = (bf16[2048,256]{1,0:T(8,128)(2,1)S(1)}, bf16[2048,256]{1,0:T(8,128)(2,1)}, u32[]{:S(2)}, u32[]{:S(2)}) collective-permute-start(bf16[2048,256]{1,0:T(8,128)(2,1)S(1)} %collective-permute-done.refs_4_), channel_id=1, source_target_pairs={{0,8},{8,16},{16,24},{24,32},{32,40},{40,48},{48,56},{56,0},{1,9},... | collective-permute-start | bytes 3145736 | tf_op jit(solution)/shard_map/ppermute | solution.py:184
  45.4 4.1 %collective-permute-start.5 = (bf16[2048,256]{1,0:T(8,128)(2,1)}, bf16[2048,256]{1,0:T(8,128)(2,1)}, u32[]{:S(2)}, u32[]{:S(2)}) collective-permute-start(bf16[2048,256]{1,0:T(8,128)(2,1)} %collective-permute-done.1.refs_6_), channel_id=1, source_target_pairs={{0,56},{8,0},{16,8},{24,16},{32,24},{40,32},{48,40},{56,48},{1,57}... | collective-permute-start | bytes 3145736 | tf_op jit(solution)/shard_map/ppermute | solution.py:184
  49.5 3.4 %collective-permute-start.10 = (bf16[128,2048]{1,0:T(8,128)(2,1)S(1)}, bf16[128,2048]{1,0:T(8,128)(2,1)}, u32[]{:S(2)}, u32[]{:S(2)}) collective-permute-start(bf16[128,2048]{1,0:T(8,128)(2,1)S(1)} %bitcast.62), channel_id=1, source_target_pairs={{0,56},{8,0},{16,8},{24,16},{32,24},{40,32},{48,40},{56,48},{1,57}... | collective-permute-start | bytes 1572872 | tf_op jit(solution)/shard_map/ppermute | solution.py:184
  54.8 14.5 %collective-permute-done.2.refs_2_ = bf16[2048,256]{1,0:T(8,128)(2,1)} collective-permute-done((bf16[2048,256]{1,0:T(8,128)(2,1)S(1)}, bf16[2048,256]{1,0:T(8,128)(2,1)}, u32[]{:S(2)}, u32[]{:S(2)}) %collective-permute-start.2) | collective-permute-done | bytes 1048608 | tf_op jit(solution)/shard_map/ppermute | solution.py:184
  71.6 4.1 %collective-permute-start.6 = (bf16[2048,256]{1,0:T(8,128)(2,1)}, bf16[2048,256]{1,0:T(8,128)(2,1)}, u32[]{:S(2)}, u32[]{:S(2)}) collective-permute-start(bf16[2048,256]{1,0:T(8,128)(2,1)} %collective-permute-done.5.refs_4_), channel_id=1, source_target_pairs={{0,56},{8,0},{16,8},{24,16},{32,24},{40,32},{48,40},{56,48},{1,57}... | collective-permute-start | bytes 3145736 | tf_op jit(solution)/shard_map/ppermute | solution.py:184
  75.8 7.1 %collective-permute-done.10.refs_7_ = bf16[128,2048]{1,0:T(8,128)(2,1)} collective-permute-done((bf16[128,2048]{1,0:T(8,128)(2,1)S(1)}, bf16[128,2048]{1,0:T(8,128)(2,1)}, u32[]{:S(2)}, u32[]{:S(2)}) %collective-permute-start.10) | collective-permute-done | bytes 524320 | tf_op jit(solution)/shard_map/ppermute | solution.py:184
  82.9 4.0 %collective-permute-start.11 = (bf16[128,2048]{1,0:T(8,128)(2,1)}, bf16[128,2048]{1,0:T(8,128)(2,1)}, u32[]{:S(2)}, u32[]{:S(2)}) collective-permute-start(bf16[128,2048]{1,0:T(8,128)(2,1)} %collective-permute-done.10.refs_7_), channel_id=1, source_target_pairs={{0,56},{8,0},{16,8},{24,16},{32,24},{40,32},{48,40},{56,48},{1,57}... | collective-permute-start | bytes 1572872 | tf_op jit(solution)/shard_map/ppermute | solution.py:184
  89.0 7.7 %all-to-all-done = bf16[8,64,2176]{2,1,0:T(8,128)(2,1)} async-done(((bf16[8,64,2176]{2,1,0:T(8,128)(2,1)}), bf16[8,64,2176]{2,1,0:T(8,128)(2,1)}, u32[]{:S(2)}, u32[]{:S(2)}) %all-to-all-start) | async-done | bytes 2228256 | tf_op jit(solution)/shard_map/all_to_all | solution.py:283
  99.5 4.8 %shard_map.175 = (f32[320,2048]{1,0:T(8,128)S(1)}, f32[8,128]{1,0:T(8,128)S(1)}) custom-call(bf16[320,2048]{1,0:T(8,128)(2,1)S(1)} %bitcast.52, bf16[192,2048]{1,0:T(8,128)(2,1)S(1)} %bitcast.56, bf16[2048,256]{1,0:T(8,128)(2,1)S(1)} %copy-done.3, bf16[128,2048]{1,0:T(8,128)(2,1)S(1)} %bitcast.64, bf16[2048,256]{1,0:T(8,128)(2,1)S(1)} %copy-done.7, ...), custom_call_target="tpu_custom_call" | custom-call | flops 2214592512 | bytes 9437184 | tf_op jit(solution)/shard_map/pallas_call | solution.py:167
  106.0 10.6 %collective-permute-done.11.refs_5_ = bf16[128,2048]{1,0:T(8,128)(2,1)} collective-permute-done((bf16[128,2048]{1,0:T(8,128)(2,1)}, bf16[128,2048]{1,0:T(8,128)(2,1)}, u32[]{:S(2)}, u32[]{:S(2)}) %collective-permute-start.11) | collective-permute-done | bytes 524320 | tf_op jit(solution)/shard_map/ppermute | solution.py:184
  116.6 3.9 %collective-permute-start.12 = (bf16[128,2048]{1,0:T(8,128)(2,1)}, bf16[128,2048]{1,0:T(8,128)(2,1)}, u32[]{:S(2)}, u32[]{:S(2)}) collective-permute-start(bf16[128,2048]{1,0:T(8,128)(2,1)} %collective-permute-done.9.refs_3_), channel_id=1, source_target_pairs={{0,8},{8,16},{16,24},{24,32},{32,40},{40,48},{48,56},{56,0},{1,9},... | collective-permute-start | bytes 1572872 | tf_op jit(solution)/shard_map/ppermute | solution.py:184
  130.7 3.8 %collective-permute-start.7 = (bf16[1024,256]{1,0:T(8,128)(2,1)}, bf16[1024,256]{1,0:T(8,128)(2,1)}, u32[]{:S(2)}, u32[]{:S(2)}) collective-permute-start(bf16[1024,256]{1,0:T(8,128)(2,1)} %slice.43), channel_id=1, source_target_pairs={{0,56},{8,0},{16,8},{24,16},{32,24},{40,32},{48,40},{56,48},{1,57}... | collective-permute-start | bytes 1572872 | tf_op jit(solution)/shard_map/ppermute | solution.py:184
  140.7 4.5 %shard_map.176 = (f32[320,2048]{1,0:T(8,128)S(1)}, f32[8,128]{1,0:T(8,128)S(1)}) custom-call(bf16[320,2048]{1,0:T(8,128)(2,1)S(1)} %bitcast.53, bf16[192,2048]{1,0:T(8,128)(2,1)S(1)} %bitcast.57, bf16[2048,256]{1,0:T(8,128)(2,1)} %collective-permute-done.2.refs_2_, bf16[128,2048]{1,0:T(8,128)(2,1)} %collective-permute-done.9.refs_3_, ...), custom_call_target="tpu_custom_call" | custom-call | flops 1476395008 | bytes 10489856 | tf_op jit(solution)/shard_map/pallas_call | solution.py:167
  149.1 4.8 %collective-permute-start.15 = (bf16[64,2048]{1,0:T(8,128)(2,1)S(1)}, bf16[64,2048]{1,0:T(8,128)(2,1)S(1)}, u32[]{:S(2)}, u32[]{:S(2)}) collective-permute-start(bf16[64,2048]{1,0:T(8,128)(2,1)S(1)} %slice.35), channel_id=1, source_target_pairs={{0,56},{8,0},{16,8},{24,16},{32,24},{40,32},{48,40},{56,48},{1,57}... | collective-permute-start | bytes 786440 | tf_op jit(solution)/shard_map/ppermute | solution.py:184
  153.9 4.2 %shard_map.177 = (f32[320,2048]{1,0:T(8,128)S(1)}, f32[8,128]{1,0:T(8,128)S(1)}) custom-call(bf16[320,2048]{1,0:T(8,128)(2,1)S(1)} %bitcast.54, bf16[192,2048]{1,0:T(8,128)(2,1)S(1)} %bitcast.58, bf16[2048,256]{1,0:T(8,128)(2,1)S(1)} %collective-permute-done.3.refs_2_, bf16[128,2048]{1,0:T(8,128)(2,1)} %collective-permute-done.12.refs_3_, ...), custom_call_target="tpu_custom_call" | custom-call | flops 1476395008 | bytes 10489856 | tf_op jit(solution)/shard_map/pallas_call | solution.py:167
  158.2 4.0 %shard_map.178 = (bf16[320,2048]{1,0:T(8,128)(2,1)}, f32[20,2048]{1,0:T(8,128)S(1)}) custom-call(bf16[320,2048]{1,0:T(8,128)(2,1)S(1)} %bitcast.55, bf16[192,2048]{1,0:T(8,128)(2,1)S(1)} %bitcast.59, bf16[1024,256]{1,0:T(8,128)(2,1)} %collective-permute-done.4.refs_2_, bf16[1024,256]{1,0:T(8,128)(2,1)} %collective-permute-done.7.refs_3_, ...), custom_call_target="tpu_custom_call" | custom-call | flops 738197504 | bytes 9278544 | tf_op jit(solution)/shard_map/pallas_call | solution.py:167
  164.2 6.5 %all-to-all-start.1 = ((bf16[8,40,2048]{2,1,0:T(8,128)(2,1)}), bf16[8,40,2048]{2,1,0:T(8,128)(2,1)S(1)}, u32[]{:S(2)}, u32[]{:S(2)}) async-start(bf16[8,40,2048]{2,1,0:T(8,128)(2,1)} %bitcast.22), calls=%async_computation.1 | async-start | bytes 2621440 | tf_op jit(solution)/shard_map/all_to_all | solution.py:312
  170.7 5.6 %collective-permute-start.19 = (bf16[20,2048]{1,0:T(8,128)(2,1)S(1)}, bf16[20,2048]{1,0:T(8,128)(2,1)S(1)}, u32[]{:S(2)}, u32[]{:S(2)}) collective-permute-start(bf16[20,2048]{1,0:T(8,128)(2,1)S(1)} %add_convert_fusion.5), channel_id=1, source_target_pairs={{0,16},{8,24},{16,0},{24,8},{32,48},{40,56},{48,32},{56,40},{1,17}... | collective-permute-start | bytes 245768 | tf_op jit(solution)/shard_map/ppermute | solution.py:197
  176.3 2.9 %collective-permute-done.19 = bf16[20,2048]{1,0:T(8,128)(2,1)S(1)} collective-permute-done((bf16[20,2048]{1,0:T(8,128)(2,1)S(1)}, bf16[20,2048]{1,0:T(8,128)(2,1)S(1)}, u32[]{:S(2)}, u32[]{:S(2)}) %collective-permute-start.19) | collective-permute-done | bytes 81952 | tf_op jit(solution)/shard_map/ppermute | solution.py:197
  179.3 3.7 %collective-permute-start.20 = (bf16[20,2048]{1,0:T(8,128)(2,1)S(1)}, bf16[20,2048]{1,0:T(8,128)(2,1)S(1)}, u32[]{:S(2)}, u32[]{:S(2)}) collective-permute-start(bf16[20,2048]{1,0:T(8,128)(2,1)S(1)} %add_convert_fusion.4), channel_id=1, source_target_pairs={{0,32},{8,40},{16,48},{24,56},{32,0},{40,8},{48,16},{56,24},{1,33}... | collective-permute-start | bytes 245768 | tf_op jit(solution)/shard_map/ppermute | solution.py:197
  183.0 6.3 %collective-permute-done.20 = bf16[20,2048]{1,0:T(8,128)(2,1)S(1)} collective-permute-done((bf16[20,2048]{1,0:T(8,128)(2,1)S(1)}, bf16[20,2048]{1,0:T(8,128)(2,1)S(1)}, u32[]{:S(2)}, u32[]{:S(2)}) %collective-permute-start.20) | collective-permute-done | bytes 81952 | tf_op jit(solution)/shard_map/ppermute | solution.py:197
  192.2 6.3 %collective-permute-done.21 = bf16[20,2048]{1,0:T(8,128)(2,1)S(1)} collective-permute-done((bf16[20,2048]{1,0:T(8,128)(2,1)S(1)}, bf16[20,2048]{1,0:T(8,128)(2,1)S(1)}, u32[]{:S(2)}, u32[]{:S(2)}) %collective-permute-start.21) | collective-permute-done | bytes 81952 | tf_op jit(solution)/shard_map/ppermute | solution.py:197
  198.5 4.3 %collective-permute-start.22 = (bf16[20,2048]{1,0:T(8,128)(2,1)S(1)}, bf16[20,2048]{1,0:T(8,128)(2,1)S(1)}, u32[]{:S(2)}, u32[]{:S(2)}) collective-permute-start(bf16[20,2048]{1,0:T(8,128)(2,1)S(1)} %add_convert_fusion.2), channel_id=1, source_target_pairs={{0,2},{1,3},{2,0},{3,1},{4,6},{5,7},{6,4},{7,5},{8,10},{9,11},{10,... | collective-permute-start | bytes 245768 | tf_op jit(solution)/shard_map/ppermute | solution.py:197
  202.9 4.5 %collective-permute-done.22 = bf16[20,2048]{1,0:T(8,128)(2,1)S(1)} collective-permute-done((bf16[20,2048]{1,0:T(8,128)(2,1)S(1)}, bf16[20,2048]{1,0:T(8,128)(2,1)S(1)}, u32[]{:S(2)}, u32[]{:S(2)}) %collective-permute-start.22) | collective-permute-done | bytes 81952 | tf_op jit(solution)/shard_map/ppermute | solution.py:197
  207.3 6.5 %collective-permute-start.23 = (bf16[20,2048]{1,0:T(8,128)(2,1)S(1)}, bf16[20,2048]{1,0:T(8,128)(2,1)S(1)}, u32[]{:S(2)}, u32[]{:S(2)}) collective-permute-start(bf16[20,2048]{1,0:T(8,128)(2,1)S(1)} %add_convert_fusion.1), channel_id=1, source_target_pairs={{0,4},{1,5},{2,6},{3,7},{4,0},{5,1},{6,2},{7,3},{8,12},{9,13},{10,... | collective-permute-start | bytes 245768 | tf_op jit(solution)/shard_map/ppermute | solution.py:197
  215.7 10.9 %collective-permute-start.17 = (bf16[128,2048]{1,0:T(8,128)(2,1)}, bf16[128,2048]{1,0:T(8,128)(2,1)S(1)}, u32[]{:S(2)}, u32[]{:S(2)}) collective-permute-start(bf16[128,2048]{1,0:T(8,128)(2,1)} %select_convert_fusion), channel_id=1, source_target_pairs={{64,0},{128,64},{192,128},{256,192},{320,256},{384,320},{448,384},... | collective-permute-start | bytes 1572872 | tf_op jit(solution)/shard_map/ppermute | solution.py:190
  227.1 3.0 %collective-permute-start.16 = (bf16[128,2048]{1,0:T(8,128)(2,1)S(1)}, bf16[128,2048]{1,0:T(8,128)(2,1)S(1)}, u32[]{:S(2)}, u32[]{:S(2)}) collective-permute-start(bf16[128,2048]{1,0:T(8,128)(2,1)S(1)} %fusion.5), channel_id=1, source_target_pairs={{0,64},{64,128},{128,192},{192,256},{256,320},{320,384},{384,448},... | collective-permute-start | bytes 1572872 | tf_op jit(solution)/shard_map/ppermute | solution.py:190
  231.0 3.8 %collective-permute-done.17 = bf16[128,2048]{1,0:T(8,128)(2,1)S(1)} collective-permute-done((bf16[128,2048]{1,0:T(8,128)(2,1)}, bf16[128,2048]{1,0:T(8,128)(2,1)S(1)}, u32[]{:S(2)}, u32[]{:S(2)}) %collective-permute-start.17) | collective-permute-done | bytes 524320 | tf_op jit(solution)/shard_map/ppermute | solution.py:190
  (150 shorter events, 53.9 us)
Async XLA Ops:
  2.1 23.7 %collective-permute-start = (bf16[2048,256]{1,0:T(8,128)(2,1)S(1)}, bf16[2048,256]{1,0:T(8,128)(2,1)S(1)}, u32[]{:S(2)}, u32[]{:S(2)}) collective-permute-start(bf16[2048,256]{1,0:T(8,128)(2,1)S(1)} %pad_maximum_fusion.refs_2_), channel_id=1, source_target_pairs={{0,8},{8,16},{16,24},{24,32},{32,40},{40,48},{48,56},{56,0},{1,9},... | collective-permute-start | bytes 3145736 | tf_op jit(solution)/shard_map/ppermute | solution.py:184
  6.3 21.9 %collective-permute-start.1 = (bf16[2048,256]{1,0:T(8,128)(2,1)S(1)}, bf16[2048,256]{1,0:T(8,128)(2,1)}, u32[]{:S(2)}, u32[]{:S(2)}) collective-permute-start(bf16[2048,256]{1,0:T(8,128)(2,1)S(1)} %pad_maximum_fusion.refs_2_), channel_id=1, source_target_pairs={{0,56},{8,0},{16,8},{24,16},{32,24},{40,32},{48,40},{56,48},{1,57}... | collective-permute-start | bytes 3145736 | tf_op jit(solution)/shard_map/ppermute | solution.py:184
  28.2 68.6 %all-to-all-start = ((bf16[8,64,2176]{2,1,0:T(8,128)(2,1)}), bf16[8,64,2176]{2,1,0:T(8,128)(2,1)}, u32[]{:S(2)}, u32[]{:S(2)}) async-start(bf16[8,64,2176]{2,1,0:T(8,128)(2,1)} %bitcast.67), calls=%async_computation | async-start | bytes 4456448 | tf_op jit(solution)/shard_map/all_to_all | solution.py:283
  42.2 27.1 %collective-permute-start.2 = (bf16[2048,256]{1,0:T(8,128)(2,1)S(1)}, bf16[2048,256]{1,0:T(8,128)(2,1)}, u32[]{:S(2)}, u32[]{:S(2)}) collective-permute-start(bf16[2048,256]{1,0:T(8,128)(2,1)S(1)} %collective-permute-done.refs_4_), channel_id=1, source_target_pairs={{0,8},{8,16},{16,24},{24,32},{32,40},{40,48},{48,56},{56,0},{1,9},... | collective-permute-start | bytes 3145736 | tf_op jit(solution)/shard_map/ppermute | solution.py:184
  45.4 26.3 %collective-permute-start.5 = (bf16[2048,256]{1,0:T(8,128)(2,1)}, bf16[2048,256]{1,0:T(8,128)(2,1)}, u32[]{:S(2)}, u32[]{:S(2)}) collective-permute-start(bf16[2048,256]{1,0:T(8,128)(2,1)} %collective-permute-done.1.refs_6_), channel_id=1, source_target_pairs={{0,56},{8,0},{16,8},{24,16},{32,24},{40,32},{48,40},{56,48},{1,57}... | collective-permute-start | bytes 3145736 | tf_op jit(solution)/shard_map/ppermute | solution.py:184
  49.5 33.4 %collective-permute-start.10 = (bf16[128,2048]{1,0:T(8,128)(2,1)S(1)}, bf16[128,2048]{1,0:T(8,128)(2,1)}, u32[]{:S(2)}, u32[]{:S(2)}) collective-permute-start(bf16[128,2048]{1,0:T(8,128)(2,1)S(1)} %bitcast.62), channel_id=1, source_target_pairs={{0,56},{8,0},{16,8},{24,16},{32,24},{40,32},{48,40},{56,48},{1,57}... | collective-permute-start | bytes 1572872 | tf_op jit(solution)/shard_map/ppermute | solution.py:184
  52.8 34.1 %collective-permute-start.8 = (bf16[128,2048]{1,0:T(8,128)(2,1)S(1)}, bf16[128,2048]{1,0:T(8,128)(2,1)}, u32[]{:S(2)}, u32[]{:S(2)}) collective-permute-start(bf16[128,2048]{1,0:T(8,128)(2,1)S(1)} %bitcast.63), channel_id=1, source_target_pairs={{0,8},{8,16},{16,24},{24,32},{32,40},{40,48},{48,56},{56,0},{1,9},... | collective-permute-start | bytes 1572872 | tf_op jit(solution)/shard_map/ppermute | solution.py:184
  69.3 56.0 %collective-permute-start.3 = (bf16[2048,256]{1,0:T(8,128)(2,1)}, bf16[2048,256]{1,0:T(8,128)(2,1)S(1)}, u32[]{:S(2)}, u32[]{:S(2)}) collective-permute-start(bf16[2048,256]{1,0:T(8,128)(2,1)} %collective-permute-done.2.refs_2_), channel_id=1, source_target_pairs={{0,8},{8,16},{16,24},{24,32},{32,40},{40,48},{48,56},{56,0},{1,9},... | collective-permute-start | bytes 3145736 | tf_op jit(solution)/shard_map/ppermute | solution.py:184
  71.6 57.2 %collective-permute-start.6 = (bf16[2048,256]{1,0:T(8,128)(2,1)}, bf16[2048,256]{1,0:T(8,128)(2,1)}, u32[]{:S(2)}, u32[]{:S(2)}) collective-permute-start(bf16[2048,256]{1,0:T(8,128)(2,1)} %collective-permute-done.5.refs_4_), channel_id=1, source_target_pairs={{0,56},{8,0},{16,8},{24,16},{32,24},{40,32},{48,40},{56,48},{1,57}... | collective-permute-start | bytes 3145736 | tf_op jit(solution)/shard_map/ppermute | solution.py:184
  82.9 33.7 %collective-permute-start.11 = (bf16[128,2048]{1,0:T(8,128)(2,1)}, bf16[128,2048]{1,0:T(8,128)(2,1)}, u32[]{:S(2)}, u32[]{:S(2)}) collective-permute-start(bf16[128,2048]{1,0:T(8,128)(2,1)} %collective-permute-done.10.refs_7_), channel_id=1, source_target_pairs={{0,56},{8,0},{16,8},{24,16},{32,24},{40,32},{48,40},{56,48},{1,57}... | collective-permute-start | bytes 1572872 | tf_op jit(solution)/shard_map/ppermute | solution.py:184
  86.9 29.6 %collective-permute-start.9 = (bf16[128,2048]{1,0:T(8,128)(2,1)}, bf16[128,2048]{1,0:T(8,128)(2,1)}, u32[]{:S(2)}, u32[]{:S(2)}) collective-permute-start(bf16[128,2048]{1,0:T(8,128)(2,1)} %collective-permute-done.8.refs_5_), channel_id=1, source_target_pairs={{0,8},{8,16},{16,24},{24,32},{32,40},{40,48},{48,56},{56,0},{1,9},... | collective-permute-start | bytes 1572872 | tf_op jit(solution)/shard_map/ppermute | solution.py:184
  116.6 28.6 %collective-permute-start.12 = (bf16[128,2048]{1,0:T(8,128)(2,1)}, bf16[128,2048]{1,0:T(8,128)(2,1)}, u32[]{:S(2)}, u32[]{:S(2)}) collective-permute-start(bf16[128,2048]{1,0:T(8,128)(2,1)} %collective-permute-done.9.refs_3_), channel_id=1, source_target_pairs={{0,8},{8,16},{16,24},{24,32},{32,40},{40,48},{48,56},{56,0},{1,9},... | collective-permute-start | bytes 1572872 | tf_op jit(solution)/shard_map/ppermute | solution.py:184
  120.5 24.7 %collective-permute-start.13 = (bf16[128,2048]{1,0:T(8,128)(2,1)}, bf16[128,2048]{1,0:T(8,128)(2,1)}, u32[]{:S(2)}, u32[]{:S(2)}) collective-permute-start(bf16[128,2048]{1,0:T(8,128)(2,1)} %collective-permute-done.11.refs_5_), channel_id=1, source_target_pairs={{0,56},{8,0},{16,8},{24,16},{32,24},{40,32},{48,40},{56,48},{1,57}... | collective-permute-start | bytes 1572872 | tf_op jit(solution)/shard_map/ppermute | solution.py:184
  126.1 32.1 %collective-permute-start.4 = (bf16[1024,256]{1,0:T(8,128)(2,1)}, bf16[1024,256]{1,0:T(8,128)(2,1)}, u32[]{:S(2)}, u32[]{:S(2)}) collective-permute-start(bf16[1024,256]{1,0:T(8,128)(2,1)} %slice.42), channel_id=1, source_target_pairs={{0,8},{8,16},{16,24},{24,32},{32,40},{40,48},{48,56},{56,0},{1,9},... | collective-permute-start | bytes 1572872 | tf_op jit(solution)/shard_map/ppermute | solution.py:184
  130.7 27.5 %collective-permute-start.7 = (bf16[1024,256]{1,0:T(8,128)(2,1)}, bf16[1024,256]{1,0:T(8,128)(2,1)}, u32[]{:S(2)}, u32[]{:S(2)}) collective-permute-start(bf16[1024,256]{1,0:T(8,128)(2,1)} %slice.43), channel_id=1, source_target_pairs={{0,56},{8,0},{16,8},{24,16},{32,24},{40,32},{48,40},{56,48},{1,57}... | collective-permute-start | bytes 1572872 | tf_op jit(solution)/shard_map/ppermute | solution.py:184
  146.2 12.0 %collective-permute-start.14 = (bf16[64,2048]{1,0:T(8,128)(2,1)S(1)}, bf16[64,2048]{1,0:T(8,128)(2,1)S(1)}, u32[]{:S(2)}, u32[]{:S(2)}) collective-permute-start(bf16[64,2048]{1,0:T(8,128)(2,1)S(1)} %slice.34), channel_id=1, source_target_pairs={{0,8},{8,16},{16,24},{24,32},{32,40},{40,48},{48,56},{56,0},{1,9},... | collective-permute-start | bytes 786440 | tf_op jit(solution)/shard_map/ppermute | solution.py:184
  149.1 9.1 %collective-permute-start.15 = (bf16[64,2048]{1,0:T(8,128)(2,1)S(1)}, bf16[64,2048]{1,0:T(8,128)(2,1)S(1)}, u32[]{:S(2)}, u32[]{:S(2)}) collective-permute-start(bf16[64,2048]{1,0:T(8,128)(2,1)S(1)} %slice.35), channel_id=1, source_target_pairs={{0,56},{8,0},{16,8},{24,16},{32,24},{40,32},{48,40},{56,48},{1,57}... | collective-permute-start | bytes 786440 | tf_op jit(solution)/shard_map/ppermute | solution.py:184
  162.3 8.5 %collective-permute-start.18 = (bf16[20,2048]{1,0:T(8,128)(2,1)S(1)}, bf16[20,2048]{1,0:T(8,128)(2,1)S(1)}, u32[]{:S(2)}, u32[]{:S(2)}) collective-permute-start(bf16[20,2048]{1,0:T(8,128)(2,1)S(1)} %convert_element_type.140), channel_id=1, source_target_pairs={{0,8},{8,0},{16,24},{24,16},{32,40},{40,32},{48,56},{56,48},{1,9},... | collective-permute-start | bytes 245768 | tf_op jit(solution)/shard_map/ppermute | solution.py:197
  164.2 49.7 %copy-start.11 = (f32[128,2048]{1,0:T(8,128)S(1)}, f32[128,2048]{1,0:T(8,128)}, u32[]{:S(2)}) copy-start(f32[128,2048]{1,0:T(8,128)} %copy-done.10) | copy-start | bytes 3145732
  164.2 49.7 %copy-start.23 = (s32[128]{0:T(128)S(1)}, s32[128]{0:T(128)}, u32[]{:S(2)}) copy-start(s32[128]{0:T(128)} %get-tuple-element.69) | copy-start | bytes 1540
  164.2 49.7 %copy-start.29 = (f32[1,128,1]{1,2,0:T(1,128)S(1)}, f32[1,128,1]{1,2,0:T(1,128)}, u32[]{:S(2)}) copy-start(f32[1,128,1]{1,2,0:T(1,128)} %param.23) | copy-start | bytes 1540
  164.2 49.7 %all-to-all-start.1 = ((bf16[8,40,2048]{2,1,0:T(8,128)(2,1)}), bf16[8,40,2048]{2,1,0:T(8,128)(2,1)S(1)}, u32[]{:S(2)}, u32[]{:S(2)}) async-start(bf16[8,40,2048]{2,1,0:T(8,128)(2,1)} %bitcast.22), calls=%async_computation.1 | async-start | bytes 2621440 | tf_op jit(solution)/shard_map/all_to_all | solution.py:312
  170.7 8.5 %collective-permute-start.19 = (bf16[20,2048]{1,0:T(8,128)(2,1)S(1)}, bf16[20,2048]{1,0:T(8,128)(2,1)S(1)}, u32[]{:S(2)}, u32[]{:S(2)}) collective-permute-start(bf16[20,2048]{1,0:T(8,128)(2,1)S(1)} %add_convert_fusion.5), channel_id=1, source_target_pairs={{0,16},{8,24},{16,0},{24,8},{32,48},{40,56},{48,32},{56,40},{1,17}... | collective-permute-start | bytes 245768 | tf_op jit(solution)/shard_map/ppermute | solution.py:197
  179.2 35.3 %copy-start.15 = (bf16[1,128,2048]{2,1,0:T(8,128)(2,1)S(1)}, bf16[1,128,2048]{2,1,0:T(8,128)(2,1)}, u32[]{:S(2)}) copy-start(bf16[1,128,2048]{2,1,0:T(8,128)(2,1)} %param.26) | copy-start | bytes 1572868
  179.3 35.3 %copy-start.19 = (pred[128]{0:T(512)(128)(4,1)S(1)}, pred[128]{0:T(512)(128)(4,1)}, u32[]{:S(2)}) copy-start(pred[128]{0:T(512)(128)(4,1)} %copy-done.18) | copy-start | bytes 388
  179.3 35.3 %copy-start.21 = (f32[128]{0:T(128)S(1)}, f32[128]{0:T(128)}, u32[]{:S(2)}) copy-start(f32[128]{0:T(128)} %copy-done.20) | copy-start | bytes 1540
  179.3 10.0 %collective-permute-start.20 = (bf16[20,2048]{1,0:T(8,128)(2,1)S(1)}, bf16[20,2048]{1,0:T(8,128)(2,1)S(1)}, u32[]{:S(2)}, u32[]{:S(2)}) collective-permute-start(bf16[20,2048]{1,0:T(8,128)(2,1)S(1)} %add_convert_fusion.4), channel_id=1, source_target_pairs={{0,32},{8,40},{16,48},{24,56},{32,0},{40,8},{48,16},{56,24},{1,33}... | collective-permute-start | bytes 245768 | tf_op jit(solution)/shard_map/ppermute | solution.py:197
  189.3 9.2 %collective-permute-start.21 = (bf16[20,2048]{1,0:T(8,128)(2,1)S(1)}, bf16[20,2048]{1,0:T(8,128)(2,1)S(1)}, u32[]{:S(2)}, u32[]{:S(2)}) collective-permute-start(bf16[20,2048]{1,0:T(8,128)(2,1)S(1)} %add_convert_fusion.3), channel_id=1, source_target_pairs={{0,1},{1,0},{2,3},{3,2},{4,5},{5,4},{6,7},{7,6},{8,9},{9,8},{10,11... | collective-permute-start | bytes 245768 | tf_op jit(solution)/shard_map/ppermute | solution.py:197
  198.5 8.8 %collective-permute-start.22 = (bf16[20,2048]{1,0:T(8,128)(2,1)S(1)}, bf16[20,2048]{1,0:T(8,128)(2,1)S(1)}, u32[]{:S(2)}, u32[]{:S(2)}) collective-permute-start(bf16[20,2048]{1,0:T(8,128)(2,1)S(1)} %add_convert_fusion.2), channel_id=1, source_target_pairs={{0,2},{1,3},{2,0},{3,1},{4,6},{5,7},{6,4},{7,5},{8,10},{9,11},{10,... | collective-permute-start | bytes 245768 | tf_op jit(solution)/shard_map/ppermute | solution.py:197
  207.3 22.8 %collective-permute-start.23 = (bf16[20,2048]{1,0:T(8,128)(2,1)S(1)}, bf16[20,2048]{1,0:T(8,128)(2,1)S(1)}, u32[]{:S(2)}, u32[]{:S(2)}) collective-permute-start(bf16[20,2048]{1,0:T(8,128)(2,1)S(1)} %add_convert_fusion.1), channel_id=1, source_target_pairs={{0,4},{1,5},{2,6},{3,7},{4,0},{5,1},{6,2},{7,3},{8,12},{9,13},{10,... | collective-permute-start | bytes 245768 | tf_op jit(solution)/shard_map/ppermute | solution.py:197
  215.7 19.0 %collective-permute-start.17 = (bf16[128,2048]{1,0:T(8,128)(2,1)}, bf16[128,2048]{1,0:T(8,128)(2,1)S(1)}, u32[]{:S(2)}, u32[]{:S(2)}) collective-permute-start(bf16[128,2048]{1,0:T(8,128)(2,1)} %select_convert_fusion), channel_id=1, source_target_pairs={{64,0},{128,64},{192,128},{256,192},{320,256},{384,320},{448,384},... | collective-permute-start | bytes 1572872 | tf_op jit(solution)/shard_map/ppermute | solution.py:190
  227.1 9.1 %collective-permute-start.16 = (bf16[128,2048]{1,0:T(8,128)(2,1)S(1)}, bf16[128,2048]{1,0:T(8,128)(2,1)S(1)}, u32[]{:S(2)}, u32[]{:S(2)}) collective-permute-start(bf16[128,2048]{1,0:T(8,128)(2,1)S(1)} %fusion.5), channel_id=1, source_target_pairs={{0,64},{64,128},{128,192},{192,256},{256,320},{320,384},{384,448},... | collective-permute-start | bytes 1572872 | tf_op jit(solution)/shard_map/ppermute | solution.py:190
  (28 other events, 257.6 us)

commit v4 on v3

--- a/solution.py
+++ b/solution.py
@@ -18,6 +18,8 @@
 FWD_AT = 16
 EXTRA = 128
 NO_SLOT = 31
+LOW_AT = 32
+VMEM_MIB = 18
 
 EPS = 1e-06
 BF16 = jnp.bfloat16
@@ -68,12 +70,12 @@
     acc_ref = None
     if has_acc:
         acc_ref, _ = refs.pop(0), refs.pop(0)
-    slot_refs = [refs.pop(0) for _ in range(5)] if final else None
+    slot_refs = [refs.pop(0) for _ in range(4)] if final else None
     out_ref, note_ref = refs.pop(0), refs.pop(0)
     gu_ref, down_ref, sems = refs.pop(0), refs.pop(0), refs.pop(0)
 
     blocks = x_ref.shape[0] // ROWS
-    width = x_ref.shape[1]
+    width = c_ref.shape[1]
     step = 512
     contract = (((1,), (1,)), ((), ()))
     row = lax.broadcasted_iota(jnp.int32, (blocks, ROWS - FWD_AT, 1), 1) + FWD_AT
@@ -94,7 +96,7 @@
         for copy in group:
             copy.wait()
         down = down_ref[number]
-        gu_out = jnp.dot(x_ref[...], gu_ref[number], preferred_element_type=F32)
+        gu_out = jnp.dot(x_ref[:, :width], gu_ref[number], preferred_element_type=F32)
         half = gu_out.shape[1] // 2
         hidden_grad = lax.dot_general(c_ref[...], down, contract, preferred_element_type=F32)
         gate = gu_out[:, :half].reshape(blocks, ROWS, half)
@@ -128,10 +130,17 @@
             out_ref[:, cols] = value.astype(out_ref.dtype)
 
     if final:
-        weighing_ref, gain_ref, slot_in_ref, scale_ref, cot_ref = slot_refs
-        both = jnp.dot(weighing_ref[...], out_ref[...], preferred_element_type=F32)
-        count = weighing_ref.shape[0] // 2
-        slot_q = (both[:count] + both[count:]) * gain_ref[...]
+        gain_ref, slot_in_ref, scale_ref, cot_ref = slot_refs
+        count = slot_in_ref.shape[0]
+        notes = x_ref[:, width:].astype(F32)
+        lane = lax.broadcasted_iota(jnp.int32, notes.shape, 1).astype(F32)
+        high = jnp.where(lane == notes[:, 2:3], notes[:, 0:1], 0.0)
+        low = jnp.where(lane - LOW_AT == notes[:, 2:3], notes[:, 1:2], 0.0)
+        weighing = jnp.where(lane < LOW_AT, high, low).astype(BF16)
+        both = lax.dot_general(
+            weighing, out_ref[...], (((0,), (0,)), ((), ())), preferred_element_type=F32
+        )
+        slot_q = (both[:count] + both[LOW_AT : LOW_AT + count]) * gain_ref[...]
         slot_in = slot_in_ref[...]
         scale = scale_ref[...]
         inner = jnp.mean(slot_in * slot_q, axis=1, keepdims=True)
@@ -154,14 +163,14 @@
     if final:
         operands += list(slot_data)
         specs += [near] * len(slot_data)
-    shape = rows.shape
+    shape = (rows.shape[0], cots.shape[1])
     gu_shape = (sum(g.shape[0] for g in shards[0][0]), shards[0][0][0].shape[1])
     d_shape = (sum(d.shape[0] for d in shards[0][1]), shape[1])
     hidden = len(shards) * d_shape[0]
     cost = pl.CostEstimate(
         flops=2 * hidden * shape[1] * (2 * shape[0] + 4 * cots.shape[0]),
         transcendentals=hidden * 2 * cots.shape[0],
-        bytes_accessed=sum(o.size * o.dtype.itemsize for o in operands) + 4 * rows.size,
+        bytes_accessed=sum(o.size * o.dtype.itemsize for o in operands) + 4 * shape[0] * shape[1],
     )
     note = (SLOTS if final else 8, shape[1] if final else 128)
     return pl.pallas_call(
@@ -174,7 +183,7 @@
             pltpu.VMEM((len(shards), *d_shape), BF16),
             pltpu.SemaphoreType.DMA((len(shards), 2, max(parts))),
         ],
-        compiler_params=pltpu.CompilerParams(vmem_limit_bytes=32 * 1024 * 1024),
+        compiler_params=pltpu.CompilerParams(vmem_limit_bytes=VMEM_MIB * 1024 * 1024),
         cost_estimate=cost,
     )(*operands)
 
@@ -281,31 +290,20 @@
     packed = packed.reshape(EXPERTS, BLOCK, width + EXTRA)
     packed, _ = lax.optimization_barrier((packed, gu_ring[1]))
     arrived = lax.all_to_all(packed, "column", split_axis=0, concat_axis=0, tiled=True)
-    rows = arrived[:, :ROWS, :width].reshape(EXPERTS * ROWS, width)
+    rows = arrived[:, :ROWS].reshape(EXPERTS * ROWS, width + EXTRA)
     cots = arrived[:, ROWS:, :width].reshape(EXPERTS * COT_ROWS, width)
-    notes = arrived[:, :ROWS, width : width + 3].astype(F32).reshape(EXPERTS * ROWS, 3)
-
-    at_slot = notes[:, 2][None, :] == jnp.arange(SLOTS, dtype=F32)[:, None]
-    weighing = jnp.concatenate(
-        [jnp.where(at_slot, notes[:, 0][None, :], 0.0), jnp.where(at_slot, notes[:, 1][None, :], 0.0)], axis=0
-    ).astype(BF16)
+
     slot_in = flat_table.astype(F32)
     slot_scale = lax.rsqrt(jnp.mean(slot_in * slot_in, axis=1, keepdims=True) + EPS)
     slot_cot = jnp.dot(jnp.transpose(selector.astype(BF16)), cotangent, preferred_element_type=F32)
-    slot_data = (weighing, norm_gain, slot_in, slot_scale, slot_cot)
+    slot_data = (norm_gain, slot_in, slot_scale, slot_cot)
 
     acc, note = expert_step(rows, cots, [((own_gu,), (own_d,))] + shards(1))
     note = held_back(d_ring, note)
     onward(d_ring)
     acc, note = expert_step(rows, cots, shards(2), (acc, note))
     note = held_back(d_ring, note)
-    gu_up, gu_down = gu_ring[-1]
-    d_up, d_down = d_ring[-1]
-    half_k, half_h = width // 2, own_d.shape[0] // 2
-    last = (
-        (rotated(gu_up[:half_k], "split", 1), rotated(gu_down[half_k:], "split", -1)),
-        (rotated(d_up[:half_h], "split", 1), rotated(d_down[half_h:], "split", -1)),
-    )
+    last = ((rotated(gu_ring[-1][0], "split", 1),), (rotated(d_ring[-1][1], "split", -1),))
     before = expert_step(rows, cots, shards(3), (acc, note))
     partial, local_sums = expert_step(rows, cots, [last], before, slot_data)
 

time: 239 us -> 230 us (0.962)
  starting transfers between devices: 111 us -> 101 us
  local copies, waits for them, and re-layouts: 18.6 us -> 15.1 us
  waiting for transfers between devices: 75.4 us -> 78.4 us
    ppermute x16 -> x14, starting transfers between devices: 52.2 us -> 43.1 us  [rotated(): lax.ppermute(value, axis, [(i, (i + distance) % size) for i in range(size)])]
    ppermute x16 -> x14, waiting for transfers between devices: 42.4 us -> 50 us  [rotated(): lax.ppermute(value, axis, [(i, (i + distance) % size) for i in range(size)])]
    slice x7 -> x1, local copies, waits for them, and re-layouts: 7.76 us -> 1.44 us  [on_device(): rows = arrived[:, :ROWS].reshape(EXPERTS * ROWS, width + EXTRA)]
    unnamed x74 -> x73, local copies, waits for them, and re-layouts: 7.52 us -> 12.3 us
    ppermute x6, waiting for transfers between devices: 20 us -> 16.1 us  [summed(): lax.ppermute(value.astype(BF16), axis, [(i, i ^ distance) for i in range(...]
    ppermute x2, starting transfers between devices: 13.9 us -> 10.8 us  [shifted(): return lax.ppermute(block, axis, route)]
  transfers between devices with their start and end apart: 26 -> 24, of which waited for: 13 -> 16; matrix products, arithmetic and copies ran while one was open for 11% -> 7% of each run, Pallas kernels for 6% -> 6%
where the time goes in v4:
time: 230 us; the launch traced here: 228 us
  starting transfers between devices  101 us (44%)
  waiting for transfers between devices  78.4 us (34%)
  Pallas kernels  18.2 us (8%)
  local copies, waits for them, and re-layouts  15.1 us (7%)
  matrix products  8.15 us (4%)
  other arithmetic  5.91 us (3%)
    ppermute x14, waiting for transfers between devices, rotated(): lax.ppermute(value, axis, [(i, (i + distance) % size) for i in range(size)])  50 us
    ppermute x14, starting transfers between devices, rotated(): lax.ppermute(value, axis, [(i, (i + distance) % size) for i in range(size)])  43.1 us
    ppermute x6, starting transfers between devices, summed(): lax.ppermute(value.astype(BF16), axis, [(i, i ^ distance) for i in range(...  27.1 us
    pallas_call x4, Pallas kernels, expert_step(): pl.pallas_call(functools.partial(expert_kernel, parts, before is not None...  18.2 us
    ppermute x6, waiting for transfers between devices, summed(): lax.ppermute(value.astype(BF16), axis, [(i, i ^ distance) for i in range(...  16.1 us
    all_to_all x1, starting transfers between devices, on_device(): lax.all_to_all(packed, 'column', split_axis=0, concat_axis=0, tiled=True)  13.9 us
    unnamed x73, local copies, waits for them, and re-layouts  12.3 us
    ppermute x2, starting transfers between devices, shifted(): return lax.ppermute(block, axis, route)  10.8 us
  transfers between devices with their start and end apart: 24, of which 16 were waited for; matrix products, arithmetic and copies ran while one was open for 7% of the time, Pallas kernels for 6%

profile of v4, /device:TPU:1, one launch (start us, length us, event | category | flops | bytes accessed | tf_op | source)
XLA Modules:
  0.0 228.2 jit_solution(6083098082641052741)
XLA Ops:
  2.1 4.2 %collective-permute-start = (bf16[2048,256]{1,0:T(8,128)(2,1)S(1)}, bf16[2048,256]{1,0:T(8,128)(2,1)S(1)}, u32[]{:S(2)}, u32[]{:S(2)}) collective-permute-start(bf16[2048,256]{1,0:T(8,128)(2,1)S(1)} %pad_maximum_fusion.refs_2_), channel_id=1, source_target_pairs={{0,8},{8,16},{16,24},{24,32},{32,40},{40,48},{48,56},{56,0},{1,9},... | collective-permute-start | bytes 3145736 | tf_op jit(solution)/shard_map/ppermute | solution.py:193
  6.3 3.8 %collective-permute-start.1 = (bf16[2048,256]{1,0:T(8,128)(2,1)S(1)}, bf16[2048,256]{1,0:T(8,128)(2,1)S(1)}, u32[]{:S(2)}, u32[]{:S(2)}) collective-permute-start(bf16[2048,256]{1,0:T(8,128)(2,1)S(1)} %pad_maximum_fusion.refs_2_), channel_id=1, source_target_pairs={{0,56},{8,0},{16,8},{24,16},{32,24},{40,32},{48,40},{56,48},{1,57}... | collective-permute-start | bytes 3145736 | tf_op jit(solution)/shard_map/ppermute | solution.py:193
  15.6 2.7 %convolution_convert_fusion = bf16[512,2176]{1,0:T(8,128)(2,1)} fusion(bf16[128,2048]{1,0:T(8,128)(2,1)S(1)} %bitcast.66, bf16[128,2048]{1,0:T(8,128)(2,1)S(1)} %get-tuple-element.57, bf16[128,128]{1,0:T(8,128)(2,1)S(1)} %select_convert_fusion.1, bf16[128,2048]{1,0:T(8,128)(2,1)S(1)} %get-tuple-element.56, s32[384]{0:T(512)S(1)} %pad_add_fusion), kind=kOutput, calls=%fused_computation.2 | convolution fusion | flops 868646912 | bytes 3835392 | tf_op jit(solution)/shard_map/dot_general | solution.py:289
  18.3 7.5 %collective-permute-done.refs_4_ = bf16[2048,256]{1,0:T(8,128)(2,1)S(1)} collective-permute-done((bf16[2048,256]{1,0:T(8,128)(2,1)S(1)}, bf16[2048,256]{1,0:T(8,128)(2,1)S(1)}, u32[]{:S(2)}, u32[]{:S(2)}) %collective-permute-start) | collective-permute-done | bytes 1048608 | tf_op jit(solution)/shard_map/ppermute | solution.py:193
  28.1 13.9 %all-to-all-start = ((bf16[8,64,2176]{2,1,0:T(8,128)(2,1)}), bf16[8,64,2176]{2,1,0:T(8,128)(2,1)}, u32[]{:S(2)}, u32[]{:S(2)}) async-start(bf16[8,64,2176]{2,1,0:T(8,128)(2,1)} %bitcast.65), calls=%async_computation | async-start | bytes 4456448 | tf_op jit(solution)/shard_map/all_to_all | solution.py:292
  42.0 3.2 %collective-permute-start.2 = (bf16[2048,256]{1,0:T(8,128)(2,1)S(1)}, bf16[2048,256]{1,0:T(8,128)(2,1)}, u32[]{:S(2)}, u32[]{:S(2)}) collective-permute-start(bf16[2048,256]{1,0:T(8,128)(2,1)S(1)} %collective-permute-done.refs_4_), channel_id=1, source_target_pairs={{0,8},{8,16},{16,24},{24,32},{32,40},{40,48},{48,56},{56,0},{1,9},... | collective-permute-start | bytes 3145736 | tf_op jit(solution)/shard_map/ppermute | solution.py:193
  45.2 4.1 %collective-permute-start.11 = (bf16[2048,256]{1,0:T(8,128)(2,1)S(1)}, bf16[2048,256]{1,0:T(8,128)(2,1)S(1)}, u32[]{:S(2)}, u32[]{:S(2)}) collective-permute-start(bf16[2048,256]{1,0:T(8,128)(2,1)S(1)} %collective-permute-done.1.refs_6_), channel_id=1, source_target_pairs={{0,56},{8,0},{16,8},{24,16},{32,24},{40,32},{48,40},{56,48},{1,57}... | collective-permute-start | bytes 3145736 | tf_op jit(solution)/shard_map/ppermute | solution.py:193
  51.7 4.1 %collective-permute-start.7 = (bf16[128,2048]{1,0:T(8,128)(2,1)}, bf16[128,2048]{1,0:T(8,128)(2,1)}, u32[]{:S(2)}, u32[]{:S(2)}) collective-permute-start(bf16[128,2048]{1,0:T(8,128)(2,1)} %bitcast.61), channel_id=1, source_target_pairs={{0,56},{8,0},{16,8},{24,16},{32,24},{40,32},{48,40},{56,48},{1,57}... | collective-permute-start | bytes 1572872 | tf_op jit(solution)/shard_map/ppermute | solution.py:193
  55.7 13.3 %collective-permute-done.2.refs_2_ = bf16[2048,256]{1,0:T(8,128)(2,1)} collective-permute-done((bf16[2048,256]{1,0:T(8,128)(2,1)S(1)}, bf16[2048,256]{1,0:T(8,128)(2,1)}, u32[]{:S(2)}, u32[]{:S(2)}) %collective-permute-start.2) | collective-permute-done | bytes 1048608 | tf_op jit(solution)/shard_map/ppermute | solution.py:193
  70.9 9.3 %collective-permute-done.5.refs_5_ = bf16[128,2048]{1,0:T(8,128)(2,1)} collective-permute-done((bf16[128,2048]{1,0:T(8,128)(2,1)}, bf16[128,2048]{1,0:T(8,128)(2,1)}, u32[]{:S(2)}, u32[]{:S(2)}) %collective-permute-start.5) | collective-permute-done | bytes 524320 | tf_op jit(solution)/shard_map/ppermute | solution.py:193
  82.4 4.3 %collective-permute-start.8 = (bf16[128,2048]{1,0:T(8,128)(2,1)}, bf16[128,2048]{1,0:T(8,128)(2,1)}, u32[]{:S(2)}, u32[]{:S(2)}) collective-permute-start(bf16[128,2048]{1,0:T(8,128)(2,1)} %collective-permute-done.7.refs_7_), channel_id=1, source_target_pairs={{0,56},{8,0},{16,8},{24,16},{32,24},{40,32},{48,40},{56,48},{1,57}... | collective-permute-start | bytes 1572872 | tf_op jit(solution)/shard_map/ppermute | solution.py:193
  88.7 7.8 %all-to-all-done = bf16[8,64,2176]{2,1,0:T(8,128)(2,1)} async-done(((bf16[8,64,2176]{2,1,0:T(8,128)(2,1)}), bf16[8,64,2176]{2,1,0:T(8,128)(2,1)}, u32[]{:S(2)}, u32[]{:S(2)}) %all-to-all-start) | async-done | bytes 2228256 | tf_op jit(solution)/shard_map/all_to_all | solution.py:292
  103.9 4.9 %shard_map.175 = (f32[320,2048]{1,0:T(8,128)S(1)}, f32[8,128]{1,0:T(8,128)S(1)}) custom-call(bf16[320,2176]{1,0:T(8,128)(2,1)S(1)} %bitcast.50, bf16[192,2048]{1,0:T(8,128)(2,1)S(1)} %bitcast.54, bf16[2048,256]{1,0:T(8,128)(2,1)S(1)} %copy-done.3, bf16[128,2048]{1,0:T(8,128)(2,1)S(1)} %bitcast.62, bf16[2048,256]{1,0:T(8,128)(2,1)S(1)} %copy-done.8, ...), custom_call_target="tpu_custom_call" | custom-call | flops 2214592512 | bytes 9519104 | tf_op jit(solution)/shard_map/pallas_call | solution.py:176
  108.8 5.1 %collective-permute-done.6.refs_3_ = bf16[128,2048]{1,0:T(8,128)(2,1)} collective-permute-done((bf16[128,2048]{1,0:T(8,128)(2,1)}, bf16[128,2048]{1,0:T(8,128)(2,1)}, u32[]{:S(2)}, u32[]{:S(2)}) %collective-permute-start.6) | collective-permute-done | bytes 524320 | tf_op jit(solution)/shard_map/ppermute | solution.py:193
  114.0 3.1 %collective-permute-start.10 = (bf16[128,2048]{1,0:T(8,128)(2,1)}, bf16[128,2048]{1,0:T(8,128)(2,1)}, u32[]{:S(2)}, u32[]{:S(2)}) collective-permute-start(bf16[128,2048]{1,0:T(8,128)(2,1)} %collective-permute-done.8.refs_5_), channel_id=1, source_target_pairs={{0,56},{8,0},{16,8},{24,16},{32,24},{40,32},{48,40},{56,48},{1,57}... | collective-permute-start | bytes 1572872 | tf_op jit(solution)/shard_map/ppermute | solution.py:193
  121.6 4.5 %shard_map.176 = (f32[320,2048]{1,0:T(8,128)S(1)}, f32[8,128]{1,0:T(8,128)S(1)}) custom-call(bf16[320,2176]{1,0:T(8,128)(2,1)S(1)} %bitcast.51, bf16[192,2048]{1,0:T(8,128)(2,1)S(1)} %bitcast.55, bf16[2048,256]{1,0:T(8,128)(2,1)} %collective-permute-done.2.refs_2_, bf16[128,2048]{1,0:T(8,128)(2,1)} %collective-permute-done.6.refs_3_, ...), custom_call_target="tpu_custom_call" | custom-call | flops 1476395008 | bytes 10571776 | tf_op jit(solution)/shard_map/pallas_call | solution.py:176
  131.5 3.9 %collective-permute-start.12 = (bf16[128,2048]{1,0:T(8,128)(2,1)}, bf16[128,2048]{1,0:T(8,128)(2,1)}, u32[]{:S(2)}, u32[]{:S(2)}) collective-permute-start(bf16[128,2048]{1,0:T(8,128)(2,1)} %collective-permute-done.10.refs_5_), channel_id=1, source_target_pairs={{0,56},{8,0},{16,8},{24,16},{32,24},{40,32},{48,40},{56,48},{1,57}... | collective-permute-start | bytes 1572872 | tf_op jit(solution)/shard_map/ppermute | solution.py:193
  139.8 4.4 %shard_map.177 = (f32[320,2048]{1,0:T(8,128)S(1)}, f32[8,128]{1,0:T(8,128)S(1)}) custom-call(bf16[320,2176]{1,0:T(8,128)(2,1)S(1)} %bitcast.52, bf16[192,2048]{1,0:T(8,128)(2,1)S(1)} %bitcast.56, bf16[2048,256]{1,0:T(8,128)(2,1)} %collective-permute-done.3.refs_2_, bf16[128,2048]{1,0:T(8,128)(2,1)S(1)} %copy-done.5, ...), custom_call_target="tpu_custom_call" | custom-call | flops 1476395008 | bytes 10571776 | tf_op jit(solution)/shard_map/pallas_call | solution.py:176
  144.2 9.2 %collective-permute-done.4.refs_2_ = bf16[2048,256]{1,0:T(8,128)(2,1)} collective-permute-done((bf16[2048,256]{1,0:T(8,128)(2,1)}, bf16[2048,256]{1,0:T(8,128)(2,1)}, u32[]{:S(2)}, u32[]{:S(2)}) %collective-permute-start.4) | collective-permute-done | bytes 1048608 | tf_op jit(solution)/shard_map/ppermute | solution.py:193
  153.3 4.3 %shard_map.178 = (bf16[320,2048]{1,0:T(8,128)(2,1)}, f32[20,2048]{1,0:T(8,128)S(1)}) custom-call(bf16[320,2176]{1,0:T(8,128)(2,1)S(1)} %bitcast.53, bf16[192,2048]{1,0:T(8,128)(2,1)S(1)} %bitcast.57, bf16[2048,256]{1,0:T(8,128)(2,1)} %collective-permute-done.4.refs_2_, bf16[128,2048]{1,0:T(8,128)(2,1)} %collective-permute-done.12.refs_3_, ...), custom_call_target="tpu_custom_call" | custom-call | flops 738197504 | bytes 9334864 | tf_op jit(solution)/shard_map/pallas_call | solution.py:176
  159.7 6.2 %all-to-all-start.1 = ((bf16[8,40,2048]{2,1,0:T(8,128)(2,1)}), bf16[8,40,2048]{2,1,0:T(8,128)(2,1)S(1)}, u32[]{:S(2)}, u32[]{:S(2)}) async-start(bf16[8,40,2048]{2,1,0:T(8,128)(2,1)} %bitcast.22), calls=%async_computation.1 | async-start | bytes 2621440 | tf_op jit(solution)/shard_map/all_to_all | solution.py:310
  165.9 3.1 %collective-permute-start.17 = (bf16[20,2048]{1,0:T(8,128)(2,1)S(1)}, bf16[20,2048]{1,0:T(8,128)(2,1)S(1)}, u32[]{:S(2)}, u32[]{:S(2)}) collective-permute-start(bf16[20,2048]{1,0:T(8,128)(2,1)S(1)} %add_convert_fusion.5), channel_id=1, source_target_pairs={{0,16},{8,24},{16,0},{24,8},{32,48},{40,56},{48,32},{56,40},{1,17}... | collective-permute-start | bytes 245768 | tf_op jit(solution)/shard_map/ppermute | solution.py:206
  169.0 3.1 %collective-permute-done.17 = bf16[20,2048]{1,0:T(8,128)(2,1)S(1)} collective-permute-done((bf16[20,2048]{1,0:T(8,128)(2,1)S(1)}, bf16[20,2048]{1,0:T(8,128)(2,1)S(1)}, u32[]{:S(2)}, u32[]{:S(2)}) %collective-permute-start.17) | collective-permute-done | bytes 81952 | tf_op jit(solution)/shard_map/ppermute | solution.py:206
  172.2 6.1 %collective-permute-start.18 = (bf16[20,2048]{1,0:T(8,128)(2,1)S(1)}, bf16[20,2048]{1,0:T(8,128)(2,1)S(1)}, u32[]{:S(2)}, u32[]{:S(2)}) collective-permute-start(bf16[20,2048]{1,0:T(8,128)(2,1)S(1)} %add_convert_fusion.4), channel_id=1, source_target_pairs={{0,32},{8,40},{16,48},{24,56},{32,0},{40,8},{48,16},{56,24},{1,33}... | collective-permute-start | bytes 245768 | tf_op jit(solution)/shard_map/ppermute | solution.py:206
  178.3 3.4 %collective-permute-done.18 = bf16[20,2048]{1,0:T(8,128)(2,1)S(1)} collective-permute-done((bf16[20,2048]{1,0:T(8,128)(2,1)S(1)}, bf16[20,2048]{1,0:T(8,128)(2,1)S(1)}, u32[]{:S(2)}, u32[]{:S(2)}) %collective-permute-start.18) | collective-permute-done | bytes 81952 | tf_op jit(solution)/shard_map/ppermute | solution.py:206
  181.8 3.3 %collective-permute-start.19 = (bf16[20,2048]{1,0:T(8,128)(2,1)S(1)}, bf16[20,2048]{1,0:T(8,128)(2,1)S(1)}, u32[]{:S(2)}, u32[]{:S(2)}) collective-permute-start(bf16[20,2048]{1,0:T(8,128)(2,1)S(1)} %add_convert_fusion.3), channel_id=1, source_target_pairs={{0,1},{1,0},{2,3},{3,2},{4,5},{5,4},{6,7},{7,6},{8,9},{9,8},{10,11... | collective-permute-start | bytes 245768 | tf_op jit(solution)/shard_map/ppermute | solution.py:206
  185.0 7.1 %collective-permute-done.19 = bf16[20,2048]{1,0:T(8,128)(2,1)S(1)} collective-permute-done((bf16[20,2048]{1,0:T(8,128)(2,1)S(1)}, bf16[20,2048]{1,0:T(8,128)(2,1)S(1)}, u32[]{:S(2)}, u32[]{:S(2)}) %collective-permute-start.19) | collective-permute-done | bytes 81952 | tf_op jit(solution)/shard_map/ppermute | solution.py:206
  192.1 6.3 %collective-permute-start.20 = (bf16[20,2048]{1,0:T(8,128)(2,1)S(1)}, bf16[20,2048]{1,0:T(8,128)(2,1)S(1)}, u32[]{:S(2)}, u32[]{:S(2)}) collective-permute-start(bf16[20,2048]{1,0:T(8,128)(2,1)S(1)} %add_convert_fusion.2), channel_id=1, source_target_pairs={{0,2},{1,3},{2,0},{3,1},{4,6},{5,7},{6,4},{7,5},{8,10},{9,11},{10,... | collective-permute-start | bytes 245768 | tf_op jit(solution)/shard_map/ppermute | solution.py:206
  201.0 6.4 %collective-permute-start.21 = (bf16[20,2048]{1,0:T(8,128)(2,1)S(1)}, bf16[20,2048]{1,0:T(8,128)(2,1)}, u32[]{:S(2)}, u32[]{:S(2)}) collective-permute-start(bf16[20,2048]{1,0:T(8,128)(2,1)S(1)} %add_convert_fusion.1), channel_id=1, source_target_pairs={{0,4},{1,5},{2,6},{3,7},{4,0},{5,1},{6,2},{7,3},{8,12},{9,13},{10,... | collective-permute-start | bytes 245768 | tf_op jit(solution)/shard_map/ppermute | solution.py:206
  209.2 7.8 %collective-permute-start.15 = (bf16[128,2048]{1,0:T(8,128)(2,1)}, bf16[128,2048]{1,0:T(8,128)(2,1)S(1)}, u32[]{:S(2)}, u32[]{:S(2)}) collective-permute-start(bf16[128,2048]{1,0:T(8,128)(2,1)} %select_convert_fusion), channel_id=1, source_target_pairs={{64,0},{128,64},{192,128},{256,192},{320,256},{384,320},{448,384},... | collective-permute-start | bytes 1572872 | tf_op jit(solution)/shard_map/ppermute | solution.py:199
  217.5 3.0 %collective-permute-start.14 = (bf16[128,2048]{1,0:T(8,128)(2,1)S(1)}, bf16[128,2048]{1,0:T(8,128)(2,1)S(1)}, u32[]{:S(2)}, u32[]{:S(2)}) collective-permute-start(bf16[128,2048]{1,0:T(8,128)(2,1)S(1)} %fusion.5), channel_id=1, source_target_pairs={{0,64},{64,128},{128,192},{192,256},{256,320},{320,384},{384,448},... | collective-permute-start | bytes 1572872 | tf_op jit(solution)/shard_map/ppermute | solution.py:199
  222.2 2.9 %collective-permute-done.15 = bf16[128,2048]{1,0:T(8,128)(2,1)S(1)} collective-permute-done((bf16[128,2048]{1,0:T(8,128)(2,1)}, bf16[128,2048]{1,0:T(8,128)(2,1)S(1)}, u32[]{:S(2)}, u32[]{:S(2)}) %collective-permute-start.15) | collective-permute-done | bytes 524320 | tf_op jit(solution)/shard_map/ppermute | solution.py:199
  (136 shorter events, 50.5 us)
Async XLA Ops:
  2.1 23.7 %collective-permute-start = (bf16[2048,256]{1,0:T(8,128)(2,1)S(1)}, bf16[2048,256]{1,0:T(8,128)(2,1)S(1)}, u32[]{:S(2)}, u32[]{:S(2)}) collective-permute-start(bf16[2048,256]{1,0:T(8,128)(2,1)S(1)} %pad_maximum_fusion.refs_2_), channel_id=1, source_target_pairs={{0,8},{8,16},{16,24},{24,32},{32,40},{40,48},{48,56},{56,0},{1,9},... | collective-permute-start | bytes 3145736 | tf_op jit(solution)/shard_map/ppermute | solution.py:193
  6.3 21.8 %collective-permute-start.1 = (bf16[2048,256]{1,0:T(8,128)(2,1)S(1)}, bf16[2048,256]{1,0:T(8,128)(2,1)S(1)}, u32[]{:S(2)}, u32[]{:S(2)}) collective-permute-start(bf16[2048,256]{1,0:T(8,128)(2,1)S(1)} %pad_maximum_fusion.refs_2_), channel_id=1, source_target_pairs={{0,56},{8,0},{16,8},{24,16},{32,24},{40,32},{48,40},{56,48},{1,57}... | collective-permute-start | bytes 3145736 | tf_op jit(solution)/shard_map/ppermute | solution.py:193
  28.1 17.1 %copy-start.9 = (bf16[2048,256]{1,0:T(8,128)(2,1)}, bf16[2048,256]{1,0:T(8,128)(2,1)S(1)}, u32[]{:S(2)}) copy-start(bf16[2048,256]{1,0:T(8,128)(2,1)S(1)} %collective-permute-done.1.refs_6_) | copy-start | bytes 3145732
  28.1 68.5 %all-to-all-start = ((bf16[8,64,2176]{2,1,0:T(8,128)(2,1)}), bf16[8,64,2176]{2,1,0:T(8,128)(2,1)}, u32[]{:S(2)}, u32[]{:S(2)}) async-start(bf16[8,64,2176]{2,1,0:T(8,128)(2,1)} %bitcast.65), calls=%async_computation | async-start | bytes 4456448 | tf_op jit(solution)/shard_map/all_to_all | solution.py:292
  42.0 27.1 %collective-permute-start.2 = (bf16[2048,256]{1,0:T(8,128)(2,1)S(1)}, bf16[2048,256]{1,0:T(8,128)(2,1)}, u32[]{:S(2)}, u32[]{:S(2)}) collective-permute-start(bf16[2048,256]{1,0:T(8,128)(2,1)S(1)} %collective-permute-done.refs_4_), channel_id=1, source_target_pairs={{0,8},{8,16},{16,24},{24,32},{32,40},{40,48},{48,56},{56,0},{1,9},... | collective-permute-start | bytes 3145736 | tf_op jit(solution)/shard_map/ppermute | solution.py:193
  45.2 41.6 %collective-permute-start.11 = (bf16[2048,256]{1,0:T(8,128)(2,1)S(1)}, bf16[2048,256]{1,0:T(8,128)(2,1)S(1)}, u32[]{:S(2)}, u32[]{:S(2)}) collective-permute-start(bf16[2048,256]{1,0:T(8,128)(2,1)S(1)} %collective-permute-done.1.refs_6_), channel_id=1, source_target_pairs={{0,56},{8,0},{16,8},{24,16},{32,24},{40,32},{48,40},{56,48},{1,57}... | collective-permute-start | bytes 3145736 | tf_op jit(solution)/shard_map/ppermute | solution.py:193
  49.2 31.0 %collective-permute-start.5 = (bf16[128,2048]{1,0:T(8,128)(2,1)}, bf16[128,2048]{1,0:T(8,128)(2,1)}, u32[]{:S(2)}, u32[]{:S(2)}) collective-permute-start(bf16[128,2048]{1,0:T(8,128)(2,1)} %bitcast.60), channel_id=1, source_target_pairs={{0,8},{8,16},{16,24},{24,32},{32,40},{40,48},{48,56},{56,0},{1,9},... | collective-permute-start | bytes 1572872 | tf_op jit(solution)/shard_map/ppermute | solution.py:193
  51.7 30.8 %collective-permute-start.7 = (bf16[128,2048]{1,0:T(8,128)(2,1)}, bf16[128,2048]{1,0:T(8,128)(2,1)}, u32[]{:S(2)}, u32[]{:S(2)}) collective-permute-start(bf16[128,2048]{1,0:T(8,128)(2,1)} %bitcast.61), channel_id=1, source_target_pairs={{0,56},{8,0},{16,8},{24,16},{32,24},{40,32},{48,40},{56,48},{1,57}... | collective-permute-start | bytes 1572872 | tf_op jit(solution)/shard_map/ppermute | solution.py:193
  69.0 50.2 %collective-permute-start.3 = (bf16[2048,256]{1,0:T(8,128)(2,1)}, bf16[2048,256]{1,0:T(8,128)(2,1)}, u32[]{:S(2)}, u32[]{:S(2)}) collective-permute-start(bf16[2048,256]{1,0:T(8,128)(2,1)} %collective-permute-done.2.refs_2_), channel_id=1, source_target_pairs={{0,8},{8,16},{16,24},{24,32},{32,40},{40,48},{48,56},{56,0},{1,9},... | collective-permute-start | bytes 3145736 | tf_op jit(solution)/shard_map/ppermute | solution.py:193
  80.3 33.7 %collective-permute-start.6 = (bf16[128,2048]{1,0:T(8,128)(2,1)}, bf16[128,2048]{1,0:T(8,128)(2,1)}, u32[]{:S(2)}, u32[]{:S(2)}) collective-permute-start(bf16[128,2048]{1,0:T(8,128)(2,1)} %collective-permute-done.5.refs_5_), channel_id=1, source_target_pairs={{0,8},{8,16},{16,24},{24,32},{32,40},{40,48},{48,56},{56,0},{1,9},... | collective-permute-start | bytes 1572872 | tf_op jit(solution)/shard_map/ppermute | solution.py:193
  82.4 31.5 %collective-permute-start.8 = (bf16[128,2048]{1,0:T(8,128)(2,1)}, bf16[128,2048]{1,0:T(8,128)(2,1)}, u32[]{:S(2)}, u32[]{:S(2)}) collective-permute-start(bf16[128,2048]{1,0:T(8,128)(2,1)} %collective-permute-done.7.refs_7_), channel_id=1, source_target_pairs={{0,56},{8,0},{16,8},{24,16},{32,24},{40,32},{48,40},{56,48},{1,57}... | collective-permute-start | bytes 1572872 | tf_op jit(solution)/shard_map/ppermute | solution.py:193
  86.8 50.2 %collective-permute-start.13 = (bf16[2048,256]{1,0:T(8,128)(2,1)S(1)}, bf16[2048,256]{1,0:T(8,128)(2,1)}, u32[]{:S(2)}, u32[]{:S(2)}) collective-permute-start(bf16[2048,256]{1,0:T(8,128)(2,1)S(1)} %collective-permute-done.11.refs_4_), channel_id=1, source_target_pairs={{0,56},{8,0},{16,8},{24,16},{32,24},{40,32},{48,40},{56,48},{1,57}... | collective-permute-start | bytes 3145736 | tf_op jit(solution)/shard_map/ppermute | solution.py:193
  103.9 17.5 %copy-start.19 = (bf16[20,2048]{1,0:T(8,128)(2,1)S(1)}, bf16[20,2048]{1,0:T(8,128)(2,1)}, u32[]{:S(2)}) copy-start(bf16[20,2048]{1,0:T(8,128)(2,1)} %copy-done.18) | copy-start | bytes 245764
  103.9 17.6 %copy-start.21 = (bf16[1,2,10,2048]{3,1,2,0:T(2,128)(2,1)S(1)}, bf16[1,2,10,2048]{3,1,2,0:T(2,128)(2,1)}, u32[]{:S(2)}) copy-start(bf16[1,2,10,2048]{3,1,2,0:T(2,128)(2,1)} %param.27) | copy-start | bytes 245764
  114.0 16.2 %collective-permute-start.10 = (bf16[128,2048]{1,0:T(8,128)(2,1)}, bf16[128,2048]{1,0:T(8,128)(2,1)}, u32[]{:S(2)}, u32[]{:S(2)}) collective-permute-start(bf16[128,2048]{1,0:T(8,128)(2,1)} %collective-permute-done.8.refs_5_), channel_id=1, source_target_pairs={{0,56},{8,0},{16,8},{24,16},{32,24},{40,32},{48,40},{56,48},{1,57}... | collective-permute-start | bytes 1572872 | tf_op jit(solution)/shard_map/ppermute | solution.py:193
  117.0 13.7 %collective-permute-start.9 = (bf16[128,2048]{1,0:T(8,128)(2,1)}, bf16[128,2048]{1,0:T(8,128)(2,1)S(1)}, u32[]{:S(2)}, u32[]{:S(2)}) collective-permute-start(bf16[128,2048]{1,0:T(8,128)(2,1)} %collective-permute-done.6.refs_3_), channel_id=1, source_target_pairs={{0,8},{8,16},{16,24},{24,32},{32,40},{40,48},{48,56},{56,0},{1,9},... | collective-permute-start | bytes 1572872 | tf_op jit(solution)/shard_map/ppermute | solution.py:193
  119.3 34.1 %collective-permute-start.4 = (bf16[2048,256]{1,0:T(8,128)(2,1)}, bf16[2048,256]{1,0:T(8,128)(2,1)}, u32[]{:S(2)}, u32[]{:S(2)}) collective-permute-start(bf16[2048,256]{1,0:T(8,128)(2,1)} %collective-permute-done.3.refs_2_), channel_id=1, source_target_pairs={{0,8},{8,16},{16,24},{24,32},{32,40},{40,48},{48,56},{56,0},{1,9},... | collective-permute-start | bytes 3145736 | tf_op jit(solution)/shard_map/ppermute | solution.py:193
  131.5 21.8 %collective-permute-start.12 = (bf16[128,2048]{1,0:T(8,128)(2,1)}, bf16[128,2048]{1,0:T(8,128)(2,1)}, u32[]{:S(2)}, u32[]{:S(2)}) collective-permute-start(bf16[128,2048]{1,0:T(8,128)(2,1)} %collective-permute-done.10.refs_5_), channel_id=1, source_target_pairs={{0,56},{8,0},{16,8},{24,16},{32,24},{40,32},{48,40},{56,48},{1,57}... | collective-permute-start | bytes 1572872 | tf_op jit(solution)/shard_map/ppermute | solution.py:193
  157.7 8.2 %collective-permute-start.16 = (bf16[20,2048]{1,0:T(8,128)(2,1)S(1)}, bf16[20,2048]{1,0:T(8,128)(2,1)S(1)}, u32[]{:S(2)}, u32[]{:S(2)}) collective-permute-start(bf16[20,2048]{1,0:T(8,128)(2,1)S(1)} %convert_element_type.138), channel_id=1, source_target_pairs={{0,8},{8,0},{16,24},{24,16},{32,40},{40,32},{48,56},{56,48},{1,9},... | collective-permute-start | bytes 245768 | tf_op jit(solution)/shard_map/ppermute | solution.py:206
  159.6 47.7 %copy-start.13 = (f32[128,2048]{1,0:T(8,128)S(1)}, f32[128,2048]{1,0:T(8,128)}, u32[]{:S(2)}) copy-start(f32[128,2048]{1,0:T(8,128)} %copy-done.12) | copy-start | bytes 3145732
  159.6 47.7 %copy-start.23 = (s32[128]{0:T(128)S(1)}, s32[128]{0:T(128)}, u32[]{:S(2)}) copy-start(s32[128]{0:T(128)} %get-tuple-element.58) | copy-start | bytes 1540
  159.6 47.7 %copy-start.29 = (f32[1,128,1]{1,2,0:T(1,128)S(1)}, f32[1,128,1]{1,2,0:T(1,128)}, u32[]{:S(2)}) copy-start(f32[1,128,1]{1,2,0:T(1,128)} %param.23) | copy-start | bytes 1540
  159.7 47.7 %all-to-all-start.1 = ((bf16[8,40,2048]{2,1,0:T(8,128)(2,1)}), bf16[8,40,2048]{2,1,0:T(8,128)(2,1)S(1)}, u32[]{:S(2)}, u32[]{:S(2)}) async-start(bf16[8,40,2048]{2,1,0:T(8,128)(2,1)} %bitcast.22), calls=%async_computation.1 | async-start | bytes 2621440 | tf_op jit(solution)/shard_map/all_to_all | solution.py:310
  165.9 6.3 %collective-permute-start.17 = (bf16[20,2048]{1,0:T(8,128)(2,1)S(1)}, bf16[20,2048]{1,0:T(8,128)(2,1)S(1)}, u32[]{:S(2)}, u32[]{:S(2)}) collective-permute-start(bf16[20,2048]{1,0:T(8,128)(2,1)S(1)} %add_convert_fusion.5), channel_id=1, source_target_pairs={{0,16},{8,24},{16,0},{24,8},{32,48},{40,56},{48,32},{56,40},{1,17}... | collective-permute-start | bytes 245768 | tf_op jit(solution)/shard_map/ppermute | solution.py:206
  172.2 35.8 %copy-start.17 = (bf16[1,128,2048]{2,1,0:T(8,128)(2,1)S(1)}, bf16[1,128,2048]{2,1,0:T(8,128)(2,1)}, u32[]{:S(2)}) copy-start(bf16[1,128,2048]{2,1,0:T(8,128)(2,1)} %param.26) | copy-start | bytes 1572868
  172.2 35.8 %copy-start.31 = (f32[128]{0:T(128)S(1)}, f32[128]{0:T(128)}, u32[]{:S(2)}) copy-start(f32[128]{0:T(128)} %get-tuple-element.63) | copy-start | bytes 1540
  172.2 9.5 %collective-permute-start.18 = (bf16[20,2048]{1,0:T(8,128)(2,1)S(1)}, bf16[20,2048]{1,0:T(8,128)(2,1)S(1)}, u32[]{:S(2)}, u32[]{:S(2)}) collective-permute-start(bf16[20,2048]{1,0:T(8,128)(2,1)S(1)} %add_convert_fusion.4), channel_id=1, source_target_pairs={{0,32},{8,40},{16,48},{24,56},{32,0},{40,8},{48,16},{56,24},{1,33}... | collective-permute-start | bytes 245768 | tf_op jit(solution)/shard_map/ppermute | solution.py:206
  181.8 10.3 %collective-permute-start.19 = (bf16[20,2048]{1,0:T(8,128)(2,1)S(1)}, bf16[20,2048]{1,0:T(8,128)(2,1)S(1)}, u32[]{:S(2)}, u32[]{:S(2)}) collective-permute-start(bf16[20,2048]{1,0:T(8,128)(2,1)S(1)} %add_convert_fusion.3), channel_id=1, source_target_pairs={{0,1},{1,0},{2,3},{3,2},{4,5},{5,4},{6,7},{7,6},{8,9},{9,8},{10,11... | collective-permute-start | bytes 245768 | tf_op jit(solution)/shard_map/ppermute | solution.py:206
  192.1 8.8 %collective-permute-start.20 = (bf16[20,2048]{1,0:T(8,128)(2,1)S(1)}, bf16[20,2048]{1,0:T(8,128)(2,1)S(1)}, u32[]{:S(2)}, u32[]{:S(2)}) collective-permute-start(bf16[20,2048]{1,0:T(8,128)(2,1)S(1)} %add_convert_fusion.2), channel_id=1, source_target_pairs={{0,2},{1,3},{2,0},{3,1},{4,6},{5,7},{6,4},{7,5},{8,10},{9,11},{10,... | collective-permute-start | bytes 245768 | tf_op jit(solution)/shard_map/ppermute | solution.py:206
  201.0 19.6 %collective-permute-start.21 = (bf16[20,2048]{1,0:T(8,128)(2,1)S(1)}, bf16[20,2048]{1,0:T(8,128)(2,1)}, u32[]{:S(2)}, u32[]{:S(2)}) collective-permute-start(bf16[20,2048]{1,0:T(8,128)(2,1)S(1)} %add_convert_fusion.1), channel_id=1, source_target_pairs={{0,4},{1,5},{2,6},{3,7},{4,0},{5,1},{6,2},{7,3},{8,12},{9,13},{10,... | collective-permute-start | bytes 245768 | tf_op jit(solution)/shard_map/ppermute | solution.py:206
  209.2 16.0 %collective-permute-start.15 = (bf16[128,2048]{1,0:T(8,128)(2,1)}, bf16[128,2048]{1,0:T(8,128)(2,1)S(1)}, u32[]{:S(2)}, u32[]{:S(2)}) collective-permute-start(bf16[128,2048]{1,0:T(8,128)(2,1)} %select_convert_fusion), channel_id=1, source_target_pairs={{64,0},{128,64},{192,128},{256,192},{320,256},{384,320},{448,384},... | collective-permute-start | bytes 1572872 | tf_op jit(solution)/shard_map/ppermute | solution.py:199
  217.5 9.1 %collective-permute-start.14 = (bf16[128,2048]{1,0:T(8,128)(2,1)S(1)}, bf16[128,2048]{1,0:T(8,128)(2,1)S(1)}, u32[]{:S(2)}, u32[]{:S(2)}) collective-permute-start(bf16[128,2048]{1,0:T(8,128)(2,1)S(1)} %fusion.5), channel_id=1, source_target_pairs={{0,64},{64,128},{128,192},{192,256},{256,320},{320,384},{384,448},... | collective-permute-start | bytes 1572872 | tf_op jit(solution)/shard_map/ppermute | solution.py:199
  (26 other events, 177.3 us)

commit v5 on v4

--- a/solution.py
+++ b/solution.py
@@ -20,6 +20,7 @@
 NO_SLOT = 31
 LOW_AT = 32
 VMEM_MIB = 18
+SHARD_SPACE = pltpu.HBM
 
 EPS = 1e-06
 BF16 = jnp.bfloat16
@@ -60,13 +61,36 @@
     return jnp.sum(same.astype(jnp.int32), axis=1)
 
 
-def expert_kernel(parts, has_acc, final, *refs):
+def shard_kernel(gate_ref, up_ref, down_ref, front_ref, rest_ref):
+    width, half = gate_ref.shape
+    cut = front_ref.shape[0]
+    front_ref[:, :half] = gate_ref[:cut, :]
+    front_ref[:, half:] = up_ref[:cut, :]
+    rest_ref[: width - cut, :half] = gate_ref[cut:, :]
+    rest_ref[: width - cut, half:] = up_ref[cut:, :]
+    for k in range(width // (2 * half)):
+        rows = slice(width - cut + k * half, width - cut + (k + 1) * half)
+        rest_ref[rows, :] = down_ref[:, 2 * half * k : 2 * half * (k + 1)]
+
+
+def shard_arrays(gate, upper, down):
+    width, half = gate.shape
+    cut = 3 * width // 4
+    near = pl.BlockSpec(memory_space=pltpu.VMEM)
+    shape = jax.ShapeDtypeStruct((cut, 2 * half), BF16)
+    return pl.pallas_call(
+        shard_kernel,
+        out_shape=(shape, shape),
+        in_specs=[near] * 3,
+        out_specs=(near, near),
+        compiler_params=pltpu.CompilerParams(vmem_limit_bytes=VMEM_MIB * 1024 * 1024),
+    )(gate, upper, down)
+
+
+def expert_kernel(count, has_acc, final, *refs):
     refs = list(refs)
     x_ref, c_ref = refs.pop(0), refs.pop(0)
-    sources = []
-    for count in parts:
-        sources.append((refs[:count], refs[count : 2 * count]))
-        refs = refs[2 * count :]
+    sources = [(refs.pop(0), refs.pop(0)) for _ in range(count)]
     acc_ref = None
     if has_acc:
         acc_ref, _ = refs.pop(0), refs.pop(0)
@@ -82,20 +106,31 @@
     is_fwd = (row >= CAP) & (row < 2 * CAP)
 
     fetches = []
-    for number, pair in enumerate(sources):
-        group = []
-        for side, (pieces, held) in enumerate(zip(pair, (gu_ref, down_ref))):
-            for k, ref in enumerate(pieces):
-                into = held.at[number, pl.ds(k * ref.shape[0], ref.shape[0]), :]
-                group.append(pltpu.make_async_copy(ref, into, sems.at[number, side, k]))
+    for number, (front, rest) in enumerate(sources):
+        cut = front.shape[0]
+        group = [
+            pltpu.make_async_copy(front, gu_ref.at[number, pl.ds(0, cut), :], sems.at[number, 0]),
+            pltpu.make_async_copy(
+                rest.at[pl.ds(0, width - cut), :],
+                gu_ref.at[number, pl.ds(cut, width - cut), :],
+                sems.at[number, 1],
+            ),
+            pltpu.make_async_copy(
+                rest.at[pl.ds(width - cut, down_ref.shape[1]), :], down_ref.at[number], sems.at[number, 2]
+            ),
+        ]
         fetches.append(group)
         for copy in group:
             copy.start()
 
+    folds = width // gu_ref.shape[2]
+    deep = down_ref.shape[1] // folds
     for number, group in enumerate(fetches):
         for copy in group:
             copy.wait()
-        down = down_ref[number]
+        down = jnp.concatenate(
+            [down_ref[number, k * deep : (k + 1) * deep, :] for k in range(folds)], axis=1
+        )
         gu_out = jnp.dot(x_ref[:, :width], gu_ref[number], preferred_element_type=F32)
         half = gu_out.shape[1] // 2
         hidden_grad = lax.dot_general(c_ref[...], down, contract, preferred_element_type=F32)
@@ -115,7 +150,7 @@
         for n in range(width // step):
             cols = slice(n * step, (n + 1) * step)
             back = lax.dot_general(grads, gu_ref[number, cols, :], contract, preferred_element_type=F32)
-            fwd = jnp.dot(hidden, down_ref[number, :, cols], preferred_element_type=F32)
+            fwd = jnp.dot(hidden, down[:, cols], preferred_element_type=F32)
             back = back.reshape(blocks, COT_ROWS, step)
             fwd = fwd.reshape(blocks, ROWS - FWD_AT, step)
             pieces = [
@@ -131,7 +166,7 @@
 
     if final:
         gain_ref, slot_in_ref, scale_ref, cot_ref = slot_refs
-        count = slot_in_ref.shape[0]
+        slots = slot_in_ref.shape[0]
         notes = x_ref[:, width:].astype(F32)
         lane = lax.broadcasted_iota(jnp.int32, notes.shape, 1).astype(F32)
         high = jnp.where(lane == notes[:, 2:3], notes[:, 0:1], 0.0)
@@ -140,7 +175,7 @@
         both = lax.dot_general(
             weighing, out_ref[...], (((0,), (0,)), ((), ())), preferred_element_type=F32
         )
-        slot_q = (both[:count] + both[LOW_AT : LOW_AT + count]) * gain_ref[...]
+        slot_q = (both[:slots] + both[LOW_AT : LOW_AT + slots]) * gain_ref[...]
         slot_in = slot_in_ref[...]
         scale = scale_ref[...]
         inner = jnp.mean(slot_in * slot_q, axis=1, keepdims=True)
@@ -151,12 +186,11 @@
 
 def expert_step(rows, cots, shards, before=None, slot_data=None):
     final = slot_data is not None
-    parts = tuple(len(gu) for gu, _ in shards)
     operands = [rows, cots]
-    for gu, d in shards:
-        operands += list(gu) + list(d)
+    for pair in shards:
+        operands += [pltpu.with_memory_space_constraint(part, pltpu.HBM) for part in pair]
     near = pl.BlockSpec(memory_space=pltpu.VMEM)
-    specs = [near, near] + [pl.BlockSpec(memory_space=pl.ANY)] * (len(operands) - 2)
+    specs = [near, near] + [pl.BlockSpec(memory_space=SHARD_SPACE)] * (len(operands) - 2)
     if before is not None:
         operands += list(before)
         specs += [near, near]
@@ -164,9 +198,9 @@
         operands += list(slot_data)
         specs += [near] * len(slot_data)
     shape = (rows.shape[0], cots.shape[1])
-    gu_shape = (sum(g.shape[0] for g in shards[0][0]), shards[0][0][0].shape[1])
-    d_shape = (sum(d.shape[0] for d in shards[0][1]), shape[1])
-    hidden = len(shards) * d_shape[0]
+    lanes = shards[0][0].shape[1]
+    deep = shards[0][0].shape[0] + shards[0][1].shape[0] - shape[1]
+    hidden = len(shards) * lanes // 2
     cost = pl.CostEstimate(
         flops=2 * hidden * shape[1] * (2 * shape[0] + 4 * cots.shape[0]),
         transcendentals=hidden * 2 * cots.shape[0],
@@ -174,14 +208,14 @@
     )
     note = (SLOTS if final else 8, shape[1] if final else 128)
     return pl.pallas_call(
-        functools.partial(expert_kernel, parts, before is not None, final),
+        functools.partial(expert_kernel, len(shards), before is not None, final),
         out_shape=(jax.ShapeDtypeStruct(shape, BF16 if final else F32), jax.ShapeDtypeStruct(note, F32)),
         in_specs=specs,
         out_specs=(near, near),
         scratch_shapes=[
-            pltpu.VMEM((len(shards), *gu_shape), BF16),
-            pltpu.VMEM((len(shards), *d_shape), BF16),
-            pltpu.SemaphoreType.DMA((len(shards), 2, max(parts))),
+            pltpu.VMEM((len(shards), shape[1], lanes), BF16),
+            pltpu.VMEM((len(shards), deep, lanes), BF16),
+            pltpu.SemaphoreType.DMA((len(shards), 3)),
         ],
         compiler_params=pltpu.CompilerParams(vmem_limit_bytes=VMEM_MIB * 1024 * 1024),
         cost_estimate=cost,
@@ -231,9 +265,8 @@
     gain_row = norm_gain[0]
     flat_table = prompts[0].reshape(SLOTS, width)
 
-    own_gu = jnp.concatenate([w_gate[0, 0], w_up[0, 0]], axis=1)
-    own_d = w_down[0, 0]
-    gu_ring, d_ring = [(own_gu, own_gu)], [(own_d, own_d)]
+    own_front, own_rest = shard_arrays(w_gate[0, 0], w_up[0, 0], w_down[0, 0])
+    front_ring, rest_ring = [(own_front, own_front)], [(own_rest, own_rest)]
 
     def onward(ring):
         up, down = ring[-1]
@@ -245,12 +278,12 @@
         return note
 
     def shards(step):
-        return [((gu_ring[step][k],), (d_ring[step][k],)) for k in range(2)]
+        return [(front_ring[step][k], rest_ring[step][k]) for k in range(2)]
 
     for _ in range(2):
-        onward(gu_ring)
-        onward(d_ring)
-    onward(gu_ring)
+        onward(front_ring)
+        onward(rest_ring)
+    onward(front_ring)
 
     first_row = (lax.axis_index("split") * lax.axis_size("column") + lax.axis_index("column")) * tok_count
     fwd_in, _, fwd_normed, _, _, _ = prepare(
@@ -288,7 +321,7 @@
     picker = target[None, :] == jnp.arange(EXPERTS * BLOCK, dtype=jnp.int32)[:, None]
     packed = jnp.dot(picker.astype(BF16), sources, preferred_element_type=F32).astype(BF16)
     packed = packed.reshape(EXPERTS, BLOCK, width + EXTRA)
-    packed, _ = lax.optimization_barrier((packed, gu_ring[1]))
+    packed, _ = lax.optimization_barrier((packed, front_ring[1]))
     arrived = lax.all_to_all(packed, "column", split_axis=0, concat_axis=0, tiled=True)
     rows = arrived[:, :ROWS].reshape(EXPERTS * ROWS, width + EXTRA)
     cots = arrived[:, ROWS:, :width].reshape(EXPERTS * COT_ROWS, width)
@@ -298,12 +331,12 @@
     slot_cot = jnp.dot(jnp.transpose(selector.astype(BF16)), cotangent, preferred_element_type=F32)
     slot_data = (norm_gain, slot_in, slot_scale, slot_cot)
 
-    acc, note = expert_step(rows, cots, [((own_gu,), (own_d,))] + shards(1))
-    note = held_back(d_ring, note)
-    onward(d_ring)
+    acc, note = expert_step(rows, cots, [(own_front, own_rest)] + shards(1))
+    note = held_back(rest_ring, note)
+    onward(rest_ring)
     acc, note = expert_step(rows, cots, shards(2), (acc, note))
-    note = held_back(d_ring, note)
-    last = ((rotated(gu_ring[-1][0], "split", 1),), (rotated(d_ring[-1][1], "split", -1),))
+    note = held_back(rest_ring, note)
+    last = (rotated(front_ring[-1][0], "split", 1), rotated(rest_ring[-1][1], "split", -1))
     before = expert_step(rows, cots, shards(3), (acc, note))
     partial, local_sums = expert_step(rows, cots, [last], before, slot_data)
 

time: 230 us -> 237 us (1.030)
  waiting for transfers between devices: 78.4 us -> 89.2 us
  matrix products: 8.15 us -> 5.75 us
    all_to_all x1, waiting for transfers between devices: 7.82 us -> 14.3 us  [on_device(): lax.all_to_all(packed, 'column', split_axis=0, concat_axis=0, tiled=True)]
    ppermute x6, waiting for transfers between devices: 16.1 us -> 20.1 us  [summed(): lax.ppermute(value.astype(BF16), axis, [(i, i ^ distance) for i in range(...]
    all_to_all x1, starting transfers between devices: 6.22 us -> 3.58 us  [on_device(): lax.all_to_all(partial.reshape(EXPERTS, ROWS, width), 'column', split_axi...]
    unnamed x73 -> x47, local copies, waits for them, and re-layouts: 12.3 us -> 10 us
    pallas_call x4 -> x5, Pallas kernels: 18.2 us -> 19.7 us  [the longest x4 19.5 us: expert_step(): pl.pallas_call(functools.partial(expert_kernel, len(shards), before is no...]
where the time goes in v5:
time: 237 us; the launch traced here: 234 us
  starting transfers between devices  98.8 us (42%)
  waiting for transfers between devices  89.2 us (38%)
  Pallas kernels  19.7 us (8%)
  local copies, waits for them, and re-layouts  12.8 us (5%)
  other arithmetic  5.97 us (3%)
  matrix products  5.75 us (2%)
    ppermute x14, waiting for transfers between devices, rotated(): lax.ppermute(value, axis, [(i, (i + distance) % size) for i in range(size)])  50 us
    ppermute x14, starting transfers between devices, rotated(): lax.ppermute(value, axis, [(i, (i + distance) % size) for i in range(size)])  43.9 us
    ppermute x6, starting transfers between devices, summed(): lax.ppermute(value.astype(BF16), axis, [(i, i ^ distance) for i in range(...  27.6 us
    ppermute x6, waiting for transfers between devices, summed(): lax.ppermute(value.astype(BF16), axis, [(i, i ^ distance) for i in range(...  20.1 us
    pallas_call x4, Pallas kernels, expert_step(): pl.pallas_call(functools.partial(expert_kernel, len(shards), before is no...  19.5 us
    all_to_all x1, waiting for transfers between devices, on_device(): lax.all_to_all(packed, 'column', split_axis=0, concat_axis=0, tiled=True)  14.3 us
    all_to_all x1, starting transfers between devices, on_device(): lax.all_to_all(packed, 'column', split_axis=0, concat_axis=0, tiled=True)  13.9 us
    unnamed x47, local copies, waits for them, and re-layouts  10 us
  transfers between devices with their start and end apart: 24, of which 16 were waited for; matrix products, arithmetic and copies ran while one was open for 7% of the time, Pallas kernels for 6%

profile of v5, /device:TPU:1, one launch (start us, length us, event | category | flops | bytes accessed | tf_op | source)
XLA Modules:
  0.0 233.6 jit_solution(10100118124881064208)
XLA Ops:
  4.1 4.2 %collective-permute-start = (bf16[1536,256]{1,0:T(8,128)(2,1)S(1)}, bf16[1536,256]{1,0:T(8,128)(2,1)}, u32[]{:S(2)}, u32[]{:S(2)}) collective-permute-start(bf16[1536,256]{1,0:T(8,128)(2,1)S(1)} %get-tuple-element.20.refs_2_), channel_id=1, source_target_pairs={{0,8},{8,16},{16,24},{24,32},{32,40},{40,48},{48,56},{56,0},{1,9},... | collective-permute-start | bytes 2359304 | tf_op jit(solution)/shard_map/ppermute | solution.py:227
  8.2 3.8 %collective-permute-start.1 = (bf16[1536,256]{1,0:T(8,128)(2,1)S(1)}, bf16[1536,256]{1,0:T(8,128)(2,1)}, u32[]{:S(2)}, u32[]{:S(2)}) collective-permute-start(bf16[1536,256]{1,0:T(8,128)(2,1)S(1)} %get-tuple-element.20.refs_2_), channel_id=1, source_target_pairs={{0,56},{8,0},{16,8},{24,16},{32,24},{40,32},{48,40},{56,48},{1,57}... | collective-permute-start | bytes 2359304 | tf_op jit(solution)/shard_map/ppermute | solution.py:227
  18.7 2.7 %convolution_convert_fusion = bf16[512,2176]{1,0:T(8,128)(2,1)} fusion(bf16[128,2048]{1,0:T(8,128)(2,1)S(1)} %bitcast.66, bf16[128,2048]{1,0:T(8,128)(2,1)S(1)} %get-tuple-element.61, bf16[128,128]{1,0:T(8,128)(2,1)S(1)} %select_convert_fusion.1, bf16[128,2048]{1,0:T(8,128)(2,1)S(1)} %get-tuple-element.60, s32[384]{0:T(512)S(1)} %pad_add_fusion), kind=kOutput, calls=%fused_computation.2 | convolution fusion | flops 868646912 | bytes 3835392 | tf_op jit(solution)/shard_map/dot_general | solution.py:322
  24.5 13.9 %all-to-all-start = ((bf16[8,64,2176]{2,1,0:T(8,128)(2,1)}), bf16[8,64,2176]{2,1,0:T(8,128)(2,1)}, u32[]{:S(2)}, u32[]{:S(2)}) async-start(bf16[8,64,2176]{2,1,0:T(8,128)(2,1)} %bitcast.65), calls=%async_computation | async-start | bytes 4456448 | tf_op jit(solution)/shard_map/all_to_all | solution.py:325
  38.4 3.2 %collective-permute-start.5 = (bf16[1536,256]{1,0:T(8,128)(2,1)S(1)}, bf16[1536,256]{1,0:T(8,128)(2,1)}, u32[]{:S(2)}, u32[]{:S(2)}) collective-permute-start(bf16[1536,256]{1,0:T(8,128)(2,1)S(1)} %get-tuple-element.22.refs_3_), channel_id=1, source_target_pairs={{0,8},{8,16},{16,24},{24,32},{32,40},{40,48},{48,56},{56,0},{1,9},... | collective-permute-start | bytes 2359304 | tf_op jit(solution)/shard_map/ppermute | solution.py:227
  41.6 4.1 %collective-permute-start.7 = (bf16[1536,256]{1,0:T(8,128)(2,1)S(1)}, bf16[1536,256]{1,0:T(8,128)(2,1)}, u32[]{:S(2)}, u32[]{:S(2)}) collective-permute-start(bf16[1536,256]{1,0:T(8,128)(2,1)S(1)} %get-tuple-element.22.refs_3_), channel_id=1, source_target_pairs={{0,56},{8,0},{16,8},{24,16},{32,24},{40,32},{48,40},{56,48},{1,57}... | collective-permute-start | bytes 2359304 | tf_op jit(solution)/shard_map/ppermute | solution.py:227
  45.6 2.4 %collective-permute-start.2 = (bf16[1536,256]{1,0:T(8,128)(2,1)}, bf16[1536,256]{1,0:T(8,128)(2,1)}, u32[]{:S(2)}, u32[]{:S(2)}) collective-permute-start(bf16[1536,256]{1,0:T(8,128)(2,1)} %collective-permute-done.refs_4_), channel_id=1, source_target_pairs={{0,8},{8,16},{16,24},{24,32},{32,40},{40,48},{48,56},{56,0},{1,9},... | collective-permute-start | bytes 2359304 | tf_op jit(solution)/shard_map/ppermute | solution.py:227
  48.1 11.7 %collective-permute-done.5.refs_5_ = bf16[1536,256]{1,0:T(8,128)(2,1)} collective-permute-done((bf16[1536,256]{1,0:T(8,128)(2,1)S(1)}, bf16[1536,256]{1,0:T(8,128)(2,1)}, u32[]{:S(2)}, u32[]{:S(2)}) %collective-permute-start.5) | collective-permute-done | bytes 786464 | tf_op jit(solution)/shard_map/ppermute | solution.py:227
  62.0 4.3 %collective-permute-start.8 = (bf16[1536,256]{1,0:T(8,128)(2,1)}, bf16[1536,256]{1,0:T(8,128)(2,1)}, u32[]{:S(2)}, u32[]{:S(2)}) collective-permute-start(bf16[1536,256]{1,0:T(8,128)(2,1)} %collective-permute-done.7.refs_7_), channel_id=1, source_target_pairs={{0,56},{8,0},{16,8},{24,16},{32,24},{40,32},{48,40},{56,48},{1,57}... | collective-permute-start | bytes 2359304 | tf_op jit(solution)/shard_map/ppermute | solution.py:227
  68.2 8.4 %collective-permute-done.2.refs_2_ = bf16[1536,256]{1,0:T(8,128)(2,1)} collective-permute-done((bf16[1536,256]{1,0:T(8,128)(2,1)}, bf16[1536,256]{1,0:T(8,128)(2,1)}, u32[]{:S(2)}, u32[]{:S(2)}) %collective-permute-start.2) | collective-permute-done | bytes 786464 | tf_op jit(solution)/shard_map/ppermute | solution.py:227
  78.6 14.3 %all-to-all-done = bf16[8,64,2176]{2,1,0:T(8,128)(2,1)} async-done(((bf16[8,64,2176]{2,1,0:T(8,128)(2,1)}), bf16[8,64,2176]{2,1,0:T(8,128)(2,1)}, u32[]{:S(2)}, u32[]{:S(2)}) %all-to-all-start) | async-done | bytes 2228256 | tf_op jit(solution)/shard_map/all_to_all | solution.py:325
  95.6 6.1 %shard_map.176 = (f32[320,2048]{1,0:T(8,128)S(1)}, f32[8,128]{1,0:T(8,128)S(1)}) custom-call(bf16[320,2176]{1,0:T(8,128)(2,1)S(1)} %bitcast.50, bf16[192,2048]{1,0:T(8,128)(2,1)S(1)} %bitcast.54, bf16[1536,256]{1,0:T(8,128)(2,1)} %copy-done.6, bf16[1536,256]{1,0:T(8,128)(2,1)} %copy-done.7, bf16[1536,256]{1,0:T(8,128)(2,1)} %collective-permute-done.refs_4_, ...), custom_call_target="tpu_custom_call" | custom-call | flops 2214592512 | bytes 9519104 | tf_op jit(solution)/shard_map/pallas_call | solution.py:210
  101.7 5.3 %collective-permute-start.10 = (bf16[1536,256]{1,0:T(8,128)(2,1)}, bf16[1536,256]{1,0:T(8,128)(2,1)}, u32[]{:S(2)}, u32[]{:S(2)}) collective-permute-start(bf16[1536,256]{1,0:T(8,128)(2,1)} %collective-permute-done.8.refs_5_), channel_id=1, source_target_pairs={{0,56},{8,0},{16,8},{24,16},{32,24},{40,32},{48,40},{56,48},{1,57}... | collective-permute-start | bytes 2359304 | tf_op jit(solution)/shard_map/ppermute | solution.py:227
  109.0 4.6 %collective-permute-start.13 = (bf16[1536,256]{1,0:T(8,128)(2,1)}, bf16[1536,256]{1,0:T(8,128)(2,1)}, u32[]{:S(2)}, u32[]{:S(2)}) collective-permute-start(bf16[1536,256]{1,0:T(8,128)(2,1)} %collective-permute-done.11.refs_4_), channel_id=1, source_target_pairs={{0,56},{8,0},{16,8},{24,16},{32,24},{40,32},{48,40},{56,48},{1,57}... | collective-permute-start | bytes 2359304 | tf_op jit(solution)/shard_map/ppermute | solution.py:227
  115.5 4.6 %shard_map.177 = (f32[320,2048]{1,0:T(8,128)S(1)}, f32[8,128]{1,0:T(8,128)S(1)}) custom-call(bf16[320,2176]{1,0:T(8,128)(2,1)S(1)} %bitcast.51, bf16[192,2048]{1,0:T(8,128)(2,1)S(1)} %bitcast.55, bf16[1536,256]{1,0:T(8,128)(2,1)} %collective-permute-done.2.refs_2_, bf16[1536,256]{1,0:T(8,128)(2,1)} %collective-permute-done.6.refs_3_, ...), custom_call_target="tpu_custom_call" | custom-call | flops 1476395008 | bytes 10571776 | tf_op jit(solution)/shard_map/pallas_call | solution.py:210
  123.7 4.9 %collective-permute-done.9.refs_3_ = bf16[1536,256]{1,0:T(8,128)(2,1)S(1)} collective-permute-done((bf16[1536,256]{1,0:T(8,128)(2,1)}, bf16[1536,256]{1,0:T(8,128)(2,1)S(1)}, u32[]{:S(2)}, u32[]{:S(2)}) %collective-permute-start.9) | collective-permute-done | bytes 786464 | tf_op jit(solution)/shard_map/ppermute | solution.py:227
  131.7 8.9 %collective-permute-done.13.refs_4_ = bf16[1536,256]{1,0:T(8,128)(2,1)} collective-permute-done((bf16[1536,256]{1,0:T(8,128)(2,1)}, bf16[1536,256]{1,0:T(8,128)(2,1)}, u32[]{:S(2)}, u32[]{:S(2)}) %collective-permute-start.13) | collective-permute-done | bytes 786464 | tf_op jit(solution)/shard_map/ppermute | solution.py:227
  142.3 4.5 %shard_map.178 = (f32[320,2048]{1,0:T(8,128)S(1)}, f32[8,128]{1,0:T(8,128)S(1)}) custom-call(bf16[320,2176]{1,0:T(8,128)(2,1)S(1)} %bitcast.52, bf16[192,2048]{1,0:T(8,128)(2,1)S(1)} %bitcast.56, bf16[1536,256]{1,0:T(8,128)(2,1)} %collective-permute-done.3.refs_2_, bf16[1536,256]{1,0:T(8,128)(2,1)} %copy-done.13, ...), custom_call_target="tpu_custom_call" | custom-call | flops 1476395008 | bytes 10571776 | tf_op jit(solution)/shard_map/pallas_call | solution.py:210
  146.9 10.6 %collective-permute-done.12.refs_3_ = bf16[1536,256]{1,0:T(8,128)(2,1)} collective-permute-done((bf16[1536,256]{1,0:T(8,128)(2,1)}, bf16[1536,256]{1,0:T(8,128)(2,1)}, u32[]{:S(2)}, u32[]{:S(2)}) %collective-permute-start.12) | collective-permute-done | bytes 786464 | tf_op jit(solution)/shard_map/ppermute | solution.py:227
  157.4 4.3 %shard_map.179 = (bf16[320,2048]{1,0:T(8,128)(2,1)}, f32[20,2048]{1,0:T(8,128)S(1)}) custom-call(bf16[320,2176]{1,0:T(8,128)(2,1)S(1)} %bitcast.53, bf16[192,2048]{1,0:T(8,128)(2,1)S(1)} %bitcast.57, bf16[1536,256]{1,0:T(8,128)(2,1)} %collective-permute-done.4.refs_2_, bf16[1536,256]{1,0:T(8,128)(2,1)} %collective-permute-done.12.refs_3_, ...), custom_call_target="tpu_custom_call" | custom-call | flops 738197504 | bytes 9334864 | tf_op jit(solution)/shard_map/pallas_call | solution.py:210
  161.8 3.6 %collective-permute-start.16 = (bf16[20,2048]{1,0:T(8,128)(2,1)S(1)}, bf16[20,2048]{1,0:T(8,128)(2,1)S(1)}, u32[]{:S(2)}, u32[]{:S(2)}) collective-permute-start(bf16[20,2048]{1,0:T(8,128)(2,1)S(1)} %convert_element_type.138), channel_id=1, source_target_pairs={{0,8},{8,0},{16,24},{24,16},{32,40},{40,32},{48,56},{56,48},{1,9},... | collective-permute-start | bytes 245768 | tf_op jit(solution)/shard_map/ppermute | solution.py:240
  165.4 3.6 %all-to-all-start.1 = ((bf16[8,40,2048]{2,1,0:T(8,128)(2,1)}), bf16[8,40,2048]{2,1,0:T(8,128)(2,1)S(1)}, u32[]{:S(2)}, u32[]{:S(2)}) async-start(bf16[8,40,2048]{2,1,0:T(8,128)(2,1)} %bitcast.22), calls=%async_computation.1 | async-start | bytes 2621440 | tf_op jit(solution)/shard_map/all_to_all | solution.py:343
  169.1 6.3 %collective-permute-start.17 = (bf16[20,2048]{1,0:T(8,128)(2,1)S(1)}, bf16[20,2048]{1,0:T(8,128)(2,1)S(1)}, u32[]{:S(2)}, u32[]{:S(2)}) collective-permute-start(bf16[20,2048]{1,0:T(8,128)(2,1)S(1)} %add_convert_fusion.5), channel_id=1, source_target_pairs={{0,16},{8,24},{16,0},{24,8},{32,48},{40,56},{48,32},{56,40},{1,17}... | collective-permute-start | bytes 245768 | tf_op jit(solution)/shard_map/ppermute | solution.py:240
  175.4 3.1 %collective-permute-done.17 = bf16[20,2048]{1,0:T(8,128)(2,1)S(1)} collective-permute-done((bf16[20,2048]{1,0:T(8,128)(2,1)S(1)}, bf16[20,2048]{1,0:T(8,128)(2,1)S(1)}, u32[]{:S(2)}, u32[]{:S(2)}) %collective-permute-start.17) | collective-permute-done | bytes 81952 | tf_op jit(solution)/shard_map/ppermute | solution.py:240
  180.4 8.2 %collective-permute-done.18 = bf16[20,2048]{1,0:T(8,128)(2,1)S(1)} collective-permute-done((bf16[20,2048]{1,0:T(8,128)(2,1)S(1)}, bf16[20,2048]{1,0:T(8,128)(2,1)S(1)}, u32[]{:S(2)}, u32[]{:S(2)}) %collective-permute-start.18) | collective-permute-done | bytes 81952 | tf_op jit(solution)/shard_map/ppermute | solution.py:240
  188.6 3.5 %collective-permute-start.19 = (bf16[20,2048]{1,0:T(8,128)(2,1)S(1)}, bf16[20,2048]{1,0:T(8,128)(2,1)S(1)}, u32[]{:S(2)}, u32[]{:S(2)}) collective-permute-start(bf16[20,2048]{1,0:T(8,128)(2,1)S(1)} %add_convert_fusion.3), channel_id=1, source_target_pairs={{0,1},{1,0},{2,3},{3,2},{4,5},{5,4},{6,7},{7,6},{8,9},{9,8},{10,11... | collective-permute-start | bytes 245768 | tf_op jit(solution)/shard_map/ppermute | solution.py:240
  192.1 6.9 %collective-permute-done.19 = bf16[20,2048]{1,0:T(8,128)(2,1)S(1)} collective-permute-done((bf16[20,2048]{1,0:T(8,128)(2,1)S(1)}, bf16[20,2048]{1,0:T(8,128)(2,1)S(1)}, u32[]{:S(2)}, u32[]{:S(2)}) %collective-permute-start.19) | collective-permute-done | bytes 81952 | tf_op jit(solution)/shard_map/ppermute | solution.py:240
  199.1 4.8 %collective-permute-start.20 = (bf16[20,2048]{1,0:T(8,128)(2,1)S(1)}, bf16[20,2048]{1,0:T(8,128)(2,1)S(1)}, u32[]{:S(2)}, u32[]{:S(2)}) collective-permute-start(bf16[20,2048]{1,0:T(8,128)(2,1)S(1)} %add_convert_fusion.2), channel_id=1, source_target_pairs={{0,2},{1,3},{2,0},{3,1},{4,6},{5,7},{6,4},{7,5},{8,10},{9,11},{10,... | collective-permute-start | bytes 245768 | tf_op jit(solution)/shard_map/ppermute | solution.py:240
  205.8 7.5 %collective-permute-start.21 = (bf16[20,2048]{1,0:T(8,128)(2,1)S(1)}, bf16[20,2048]{1,0:T(8,128)(2,1)}, u32[]{:S(2)}, u32[]{:S(2)}) collective-permute-start(bf16[20,2048]{1,0:T(8,128)(2,1)S(1)} %add_convert_fusion.1), channel_id=1, source_target_pairs={{0,4},{1,5},{2,6},{3,7},{4,0},{5,1},{6,2},{7,3},{8,12},{9,13},{10,... | collective-permute-start | bytes 245768 | tf_op jit(solution)/shard_map/ppermute | solution.py:240
  214.4 6.9 %collective-permute-start.15 = (bf16[128,2048]{1,0:T(8,128)(2,1)S(1)}, bf16[128,2048]{1,0:T(8,128)(2,1)S(1)}, u32[]{:S(2)}, u32[]{:S(2)}) collective-permute-start(bf16[128,2048]{1,0:T(8,128)(2,1)S(1)} %select_convert_fusion), channel_id=1, source_target_pairs={{64,0},{128,64},{192,128},{256,192},{320,256},{384,320},{448,384},... | collective-permute-start | bytes 1572872 | tf_op jit(solution)/shard_map/ppermute | solution.py:233
  222.6 3.0 %collective-permute-start.14 = (bf16[128,2048]{1,0:T(8,128)(2,1)}, bf16[128,2048]{1,0:T(8,128)(2,1)S(1)}, u32[]{:S(2)}, u32[]{:S(2)}) collective-permute-start(bf16[128,2048]{1,0:T(8,128)(2,1)} %fusion.5), channel_id=1, source_target_pairs={{0,64},{64,128},{128,192},{192,256},{256,320},{320,384},{384,448},... | collective-permute-start | bytes 1572872 | tf_op jit(solution)/shard_map/ppermute | solution.py:233
  229.2 2.8 %collective-permute-done.14 = bf16[128,2048]{1,0:T(8,128)(2,1)S(1)} collective-permute-done((bf16[128,2048]{1,0:T(8,128)(2,1)}, bf16[128,2048]{1,0:T(8,128)(2,1)S(1)}, u32[]{:S(2)}, u32[]{:S(2)}) %collective-permute-start.14) | collective-permute-done | bytes 524320 | tf_op jit(solution)/shard_map/ppermute | solution.py:233
  (110 shorter events, 45.3 us)
Async XLA Ops:
  4.0 14.3 %copy-start.6 = (bf16[1536,256]{1,0:T(8,128)(2,1)}, bf16[1536,256]{1,0:T(8,128)(2,1)S(1)}, u32[]{:S(2)}) copy-start(bf16[1536,256]{1,0:T(8,128)(2,1)S(1)} %get-tuple-element.20.refs_2_) | copy-start | bytes 2359300
  4.0 37.6 %copy-start.7 = (bf16[1536,256]{1,0:T(8,128)(2,1)}, bf16[1536,256]{1,0:T(8,128)(2,1)S(1)}, u32[]{:S(2)}) copy-start(bf16[1536,256]{1,0:T(8,128)(2,1)S(1)} %get-tuple-element.22.refs_3_) | copy-start | bytes 2359300
  4.0 13.6 %copy-start.19 = (f32[1,128,1]{1,2,0:T(1,128)S(1)}, f32[1,128,1]{1,2,0:T(1,128)}, u32[]{:S(2)}) copy-start(f32[1,128,1]{1,2,0:T(1,128)} %param.23) | copy-start | bytes 1540
  4.0 13.6 %copy-start.17 = (s32[1,128,1]{1,2,0:T(1,128)S(1)}, s32[1,128,1]{1,2,0:T(1,128)}, u32[]{:S(2)}) copy-start(s32[1,128,1]{1,2,0:T(1,128)} %param.22) | copy-start | bytes 1540
  4.0 13.7 %copy-start.18 = (s32[1,128,1]{1,2,0:T(1,128)S(1)}, s32[1,128,1]{1,2,0:T(1,128)}, u32[]{:S(2)}) copy-start(s32[1,128,1]{1,2,0:T(1,128)} %param.17) | copy-start | bytes 1540
  4.0 14.0 %copy-start.5 = (f32[1,2048]{1,0:T(1,128)S(1)}, f32[1,2048]{1,0:T(1,128)}, u32[]{:S(2)}) copy-start(f32[1,2048]{1,0:T(1,128)} %refs_6_.1) | copy-start | bytes 24580
  4.1 18.2 %collective-permute-start = (bf16[1536,256]{1,0:T(8,128)(2,1)S(1)}, bf16[1536,256]{1,0:T(8,128)(2,1)}, u32[]{:S(2)}, u32[]{:S(2)}) collective-permute-start(bf16[1536,256]{1,0:T(8,128)(2,1)S(1)} %get-tuple-element.20.refs_2_), channel_id=1, source_target_pairs={{0,8},{8,16},{16,24},{24,32},{32,40},{40,48},{48,56},{56,0},{1,9},... | collective-permute-start | bytes 2359304 | tf_op jit(solution)/shard_map/ppermute | solution.py:227
  8.2 16.3 %collective-permute-start.1 = (bf16[1536,256]{1,0:T(8,128)(2,1)S(1)}, bf16[1536,256]{1,0:T(8,128)(2,1)}, u32[]{:S(2)}, u32[]{:S(2)}) collective-permute-start(bf16[1536,256]{1,0:T(8,128)(2,1)S(1)} %get-tuple-element.20.refs_2_), channel_id=1, source_target_pairs={{0,56},{8,0},{16,8},{24,16},{32,24},{40,32},{48,40},{56,48},{1,57}... | collective-permute-start | bytes 2359304 | tf_op jit(solution)/shard_map/ppermute | solution.py:227
  24.5 68.4 %all-to-all-start = ((bf16[8,64,2176]{2,1,0:T(8,128)(2,1)}), bf16[8,64,2176]{2,1,0:T(8,128)(2,1)}, u32[]{:S(2)}, u32[]{:S(2)}) async-start(bf16[8,64,2176]{2,1,0:T(8,128)(2,1)} %bitcast.65), calls=%async_computation | async-start | bytes 4456448 | tf_op jit(solution)/shard_map/all_to_all | solution.py:325
  38.4 21.5 %collective-permute-start.5 = (bf16[1536,256]{1,0:T(8,128)(2,1)S(1)}, bf16[1536,256]{1,0:T(8,128)(2,1)}, u32[]{:S(2)}, u32[]{:S(2)}) collective-permute-start(bf16[1536,256]{1,0:T(8,128)(2,1)S(1)} %get-tuple-element.22.refs_3_), channel_id=1, source_target_pairs={{0,8},{8,16},{16,24},{24,32},{32,40},{40,48},{48,56},{56,0},{1,9},... | collective-permute-start | bytes 2359304 | tf_op jit(solution)/shard_map/ppermute | solution.py:227
  41.6 20.4 %collective-permute-start.7 = (bf16[1536,256]{1,0:T(8,128)(2,1)S(1)}, bf16[1536,256]{1,0:T(8,128)(2,1)}, u32[]{:S(2)}, u32[]{:S(2)}) collective-permute-start(bf16[1536,256]{1,0:T(8,128)(2,1)S(1)} %get-tuple-element.22.refs_3_), channel_id=1, source_target_pairs={{0,56},{8,0},{16,8},{24,16},{32,24},{40,32},{48,40},{56,48},{1,57}... | collective-permute-start | bytes 2359304 | tf_op jit(solution)/shard_map/ppermute | solution.py:227
  45.6 31.0 %collective-permute-start.2 = (bf16[1536,256]{1,0:T(8,128)(2,1)}, bf16[1536,256]{1,0:T(8,128)(2,1)}, u32[]{:S(2)}, u32[]{:S(2)}) collective-permute-start(bf16[1536,256]{1,0:T(8,128)(2,1)} %collective-permute-done.refs_4_), channel_id=1, source_target_pairs={{0,8},{8,16},{16,24},{24,32},{32,40},{40,48},{48,56},{56,0},{1,9},... | collective-permute-start | bytes 2359304 | tf_op jit(solution)/shard_map/ppermute | solution.py:227
  59.8 41.9 %collective-permute-start.6 = (bf16[1536,256]{1,0:T(8,128)(2,1)}, bf16[1536,256]{1,0:T(8,128)(2,1)}, u32[]{:S(2)}, u32[]{:S(2)}) collective-permute-start(bf16[1536,256]{1,0:T(8,128)(2,1)} %collective-permute-done.5.refs_5_), channel_id=1, source_target_pairs={{0,8},{8,16},{16,24},{24,32},{32,40},{40,48},{48,56},{56,0},{1,9},... | collective-permute-start | bytes 2359304 | tf_op jit(solution)/shard_map/ppermute | solution.py:227
  62.0 39.7 %collective-permute-start.8 = (bf16[1536,256]{1,0:T(8,128)(2,1)}, bf16[1536,256]{1,0:T(8,128)(2,1)}, u32[]{:S(2)}, u32[]{:S(2)}) collective-permute-start(bf16[1536,256]{1,0:T(8,128)(2,1)} %collective-permute-done.7.refs_7_), channel_id=1, source_target_pairs={{0,56},{8,0},{16,8},{24,16},{32,24},{40,32},{48,40},{56,48},{1,57}... | collective-permute-start | bytes 2359304 | tf_op jit(solution)/shard_map/ppermute | solution.py:227
  66.3 42.7 %collective-permute-start.11 = (bf16[1536,256]{1,0:T(8,128)(2,1)}, bf16[1536,256]{1,0:T(8,128)(2,1)}, u32[]{:S(2)}, u32[]{:S(2)}) collective-permute-start(bf16[1536,256]{1,0:T(8,128)(2,1)} %collective-permute-done.1.refs_6_), channel_id=1, source_target_pairs={{0,56},{8,0},{16,8},{24,16},{32,24},{40,32},{48,40},{56,48},{1,57}... | collective-permute-start | bytes 2359304 | tf_op jit(solution)/shard_map/ppermute | solution.py:227
  76.7 36.9 %collective-permute-start.3 = (bf16[1536,256]{1,0:T(8,128)(2,1)}, bf16[1536,256]{1,0:T(8,128)(2,1)}, u32[]{:S(2)}, u32[]{:S(2)}) collective-permute-start(bf16[1536,256]{1,0:T(8,128)(2,1)} %collective-permute-done.2.refs_2_), channel_id=1, source_target_pairs={{0,8},{8,16},{16,24},{24,32},{32,40},{40,48},{48,56},{56,0},{1,9},... | collective-permute-start | bytes 2359304 | tf_op jit(solution)/shard_map/ppermute | solution.py:227
  101.7 22.0 %collective-permute-start.10 = (bf16[1536,256]{1,0:T(8,128)(2,1)}, bf16[1536,256]{1,0:T(8,128)(2,1)}, u32[]{:S(2)}, u32[]{:S(2)}) collective-permute-start(bf16[1536,256]{1,0:T(8,128)(2,1)} %collective-permute-done.8.refs_5_), channel_id=1, source_target_pairs={{0,56},{8,0},{16,8},{24,16},{32,24},{40,32},{48,40},{56,48},{1,57}... | collective-permute-start | bytes 2359304 | tf_op jit(solution)/shard_map/ppermute | solution.py:227
  107.1 21.6 %collective-permute-start.9 = (bf16[1536,256]{1,0:T(8,128)(2,1)}, bf16[1536,256]{1,0:T(8,128)(2,1)S(1)}, u32[]{:S(2)}, u32[]{:S(2)}) collective-permute-start(bf16[1536,256]{1,0:T(8,128)(2,1)} %collective-permute-done.6.refs_3_), channel_id=1, source_target_pairs={{0,8},{8,16},{16,24},{24,32},{32,40},{40,48},{48,56},{56,0},{1,9},... | collective-permute-start | bytes 2359304 | tf_op jit(solution)/shard_map/ppermute | solution.py:227
  109.0 31.6 %collective-permute-start.13 = (bf16[1536,256]{1,0:T(8,128)(2,1)}, bf16[1536,256]{1,0:T(8,128)(2,1)}, u32[]{:S(2)}, u32[]{:S(2)}) collective-permute-start(bf16[1536,256]{1,0:T(8,128)(2,1)} %collective-permute-done.11.refs_4_), channel_id=1, source_target_pairs={{0,56},{8,0},{16,8},{24,16},{32,24},{40,32},{48,40},{56,48},{1,57}... | collective-permute-start | bytes 2359304 | tf_op jit(solution)/shard_map/ppermute | solution.py:227
  113.6 33.3 %collective-permute-start.4 = (bf16[1536,256]{1,0:T(8,128)(2,1)}, bf16[1536,256]{1,0:T(8,128)(2,1)}, u32[]{:S(2)}, u32[]{:S(2)}) collective-permute-start(bf16[1536,256]{1,0:T(8,128)(2,1)} %collective-permute-done.3.refs_2_), channel_id=1, source_target_pairs={{0,8},{8,16},{16,24},{24,32},{32,40},{40,48},{48,56},{56,0},{1,9},... | collective-permute-start | bytes 2359304 | tf_op jit(solution)/shard_map/ppermute | solution.py:227
  115.5 15.5 %copy-start.16 = (bf16[1,2,10,2048]{3,1,2,0:T(2,128)(2,1)S(1)}, bf16[1,2,10,2048]{3,1,2,0:T(2,128)(2,1)}, u32[]{:S(2)}) copy-start(bf16[1,2,10,2048]{3,1,2,0:T(2,128)(2,1)} %param.27) | copy-start | bytes 245764
  128.6 28.8 %collective-permute-start.12 = (bf16[1536,256]{1,0:T(8,128)(2,1)}, bf16[1536,256]{1,0:T(8,128)(2,1)}, u32[]{:S(2)}, u32[]{:S(2)}) collective-permute-start(bf16[1536,256]{1,0:T(8,128)(2,1)} %collective-permute-done.10.refs_5_), channel_id=1, source_target_pairs={{0,56},{8,0},{16,8},{24,16},{32,24},{40,32},{48,40},{56,48},{1,57}... | collective-permute-start | bytes 2359304 | tf_op jit(solution)/shard_map/ppermute | solution.py:227
  161.8 51.6 %copy-start.9 = (f32[128,2048]{1,0:T(8,128)S(1)}, f32[128,2048]{1,0:T(8,128)}, u32[]{:S(2)}) copy-start(f32[128,2048]{1,0:T(8,128)} %copy-done.8) | copy-start | bytes 3145732
  161.8 7.2 %collective-permute-start.16 = (bf16[20,2048]{1,0:T(8,128)(2,1)S(1)}, bf16[20,2048]{1,0:T(8,128)(2,1)S(1)}, u32[]{:S(2)}, u32[]{:S(2)}) collective-permute-start(bf16[20,2048]{1,0:T(8,128)(2,1)S(1)} %convert_element_type.138), channel_id=1, source_target_pairs={{0,8},{8,0},{16,24},{24,16},{32,40},{40,32},{48,56},{56,48},{1,9},... | collective-permute-start | bytes 245768 | tf_op jit(solution)/shard_map/ppermute | solution.py:240
  165.4 47.9 %all-to-all-start.1 = ((bf16[8,40,2048]{2,1,0:T(8,128)(2,1)}), bf16[8,40,2048]{2,1,0:T(8,128)(2,1)S(1)}, u32[]{:S(2)}, u32[]{:S(2)}) async-start(bf16[8,40,2048]{2,1,0:T(8,128)(2,1)} %bitcast.22), calls=%async_computation.1 | async-start | bytes 2621440 | tf_op jit(solution)/shard_map/all_to_all | solution.py:343
  169.1 9.4 %collective-permute-start.17 = (bf16[20,2048]{1,0:T(8,128)(2,1)S(1)}, bf16[20,2048]{1,0:T(8,128)(2,1)S(1)}, u32[]{:S(2)}, u32[]{:S(2)}) collective-permute-start(bf16[20,2048]{1,0:T(8,128)(2,1)S(1)} %add_convert_fusion.5), channel_id=1, source_target_pairs={{0,16},{8,24},{16,0},{24,8},{32,48},{40,56},{48,32},{56,40},{1,17}... | collective-permute-start | bytes 245768 | tf_op jit(solution)/shard_map/ppermute | solution.py:240
  178.5 10.1 %collective-permute-start.18 = (bf16[20,2048]{1,0:T(8,128)(2,1)S(1)}, bf16[20,2048]{1,0:T(8,128)(2,1)S(1)}, u32[]{:S(2)}, u32[]{:S(2)}) collective-permute-start(bf16[20,2048]{1,0:T(8,128)(2,1)S(1)} %add_convert_fusion.4), channel_id=1, source_target_pairs={{0,32},{8,40},{16,48},{24,56},{32,0},{40,8},{48,16},{56,24},{1,33}... | collective-permute-start | bytes 245768 | tf_op jit(solution)/shard_map/ppermute | solution.py:240
  188.6 10.4 %collective-permute-start.19 = (bf16[20,2048]{1,0:T(8,128)(2,1)S(1)}, bf16[20,2048]{1,0:T(8,128)(2,1)S(1)}, u32[]{:S(2)}, u32[]{:S(2)}) collective-permute-start(bf16[20,2048]{1,0:T(8,128)(2,1)S(1)} %add_convert_fusion.3), channel_id=1, source_target_pairs={{0,1},{1,0},{2,3},{3,2},{4,5},{5,4},{6,7},{7,6},{8,9},{9,8},{10,11... | collective-permute-start | bytes 245768 | tf_op jit(solution)/shard_map/ppermute | solution.py:240
  199.1 6.8 %collective-permute-start.20 = (bf16[20,2048]{1,0:T(8,128)(2,1)S(1)}, bf16[20,2048]{1,0:T(8,128)(2,1)S(1)}, u32[]{:S(2)}, u32[]{:S(2)}) collective-permute-start(bf16[20,2048]{1,0:T(8,128)(2,1)S(1)} %add_convert_fusion.2), channel_id=1, source_target_pairs={{0,2},{1,3},{2,0},{3,1},{4,6},{5,7},{6,4},{7,5},{8,10},{9,11},{10,... | collective-permute-start | bytes 245768 | tf_op jit(solution)/shard_map/ppermute | solution.py:240
  205.8 19.8 %collective-permute-start.21 = (bf16[20,2048]{1,0:T(8,128)(2,1)S(1)}, bf16[20,2048]{1,0:T(8,128)(2,1)}, u32[]{:S(2)}, u32[]{:S(2)}) collective-permute-start(bf16[20,2048]{1,0:T(8,128)(2,1)S(1)} %add_convert_fusion.1), channel_id=1, source_target_pairs={{0,4},{1,5},{2,6},{3,7},{4,0},{5,1},{6,2},{7,3},{8,12},{9,13},{10,... | collective-permute-start | bytes 245768 | tf_op jit(solution)/shard_map/ppermute | solution.py:240
  214.4 14.9 %collective-permute-start.15 = (bf16[128,2048]{1,0:T(8,128)(2,1)S(1)}, bf16[128,2048]{1,0:T(8,128)(2,1)S(1)}, u32[]{:S(2)}, u32[]{:S(2)}) collective-permute-start(bf16[128,2048]{1,0:T(8,128)(2,1)S(1)} %select_convert_fusion), channel_id=1, source_target_pairs={{64,0},{128,64},{192,128},{256,192},{320,256},{384,320},{448,384},... | collective-permute-start | bytes 1572872 | tf_op jit(solution)/shard_map/ppermute | solution.py:233
  222.6 9.4 %collective-permute-start.14 = (bf16[128,2048]{1,0:T(8,128)(2,1)}, bf16[128,2048]{1,0:T(8,128)(2,1)S(1)}, u32[]{:S(2)}, u32[]{:S(2)}) collective-permute-start(bf16[128,2048]{1,0:T(8,128)(2,1)} %fusion.5), channel_id=1, source_target_pairs={{0,64},{64,128},{128,192},{192,256},{256,320},{320,384},{384,448},... | collective-permute-start | bytes 1572872 | tf_op jit(solution)/shard_map/ppermute | solution.py:233
  (13 other events, 53.4 us)

commit v6 on v5

--- a/solution.py
+++ b/solution.py
@@ -19,7 +19,7 @@
 EXTRA = 128
 NO_SLOT = 31
 LOW_AT = 32
-VMEM_MIB = 18
+VMEM_MIB = 24
 SHARD_SPACE = pltpu.HBM
 
 EPS = 1e-06
@@ -27,64 +27,148 @@
 F32 = jnp.float32
 
 
-def token_layout(lengths, tenants, first_row, tok_count):
-    count = lengths.shape[0]
-    token_index = first_row + jnp.arange(tok_count, dtype=jnp.int32)
-    order = jnp.arange(count, dtype=jnp.int32)
-    earlier = order[:, None] < order[None, :]
-    seg_starts = jnp.sum(jnp.where(earlier, lengths[:, None], 0), axis=0)
-    seg_ends = seg_starts + lengths
-    chosen = (seg_starts[None, :] <= token_index[:, None]) & (token_index[:, None] < seg_ends[None, :])
-    position = token_index - jnp.sum(jnp.where(chosen, seg_starts[None, :], 0), axis=1)
-    tenant = jnp.sum(jnp.where(chosen, tenants[None, :], 0), axis=1)
-    return position, tenant
-
-
-def prepare(acts, lengths, tenants, flat_table, gain_row, first_row):
-    tok_count = acts.shape[0]
-    position, tenant = token_layout(lengths, tenants, first_row, tok_count)
-    prompt_slot = position < PLEN
-    slot = jnp.where(prompt_slot, tenant * PLEN + position, NO_SLOT)
-    selector = slot[:, None] == jnp.arange(SLOTS, dtype=jnp.int32)[None, :]
-    prompt_rows = jnp.dot(selector.astype(BF16), flat_table, preferred_element_type=F32).astype(BF16)
-    inputs = jnp.where(prompt_slot[:, None], prompt_rows, acts)
-    widened = inputs.astype(F32)
-    inv_scale = lax.rsqrt(jnp.mean(widened * widened, axis=1, keepdims=True) + EPS)
-    normed = (widened * inv_scale * gain_row[None, :]).astype(BF16)
-    return inputs, inv_scale, normed, prompt_slot, slot, selector
-
-
-def ranks(routes):
-    tok_count = routes.shape[0]
-    at = jnp.arange(tok_count, dtype=jnp.int32)
-    same = (routes[None, :] == routes[:, None]) & (at[None, :] < at[:, None])
-    return jnp.sum(same.astype(jnp.int32), axis=1)
-
-
-def shard_kernel(gate_ref, up_ref, down_ref, front_ref, rest_ref):
-    width, half = gate_ref.shape
+def column(row):
+    size = row.shape[1]
+    down = lax.broadcasted_iota(jnp.int32, (size, size), 0)
+    across = lax.broadcasted_iota(jnp.int32, (size, size), 1)
+    return jnp.sum(jnp.where(down == across, row, 0.0), axis=1, keepdims=True)
+
+
+def row_of(col):
+    size = col.shape[0]
+    down = lax.broadcasted_iota(jnp.int32, (size, size), 0)
+    across = lax.broadcasted_iota(jnp.int32, (size, size), 1)
+    return jnp.sum(jnp.where(down == across, col, 0.0), axis=0, keepdims=True)
+
+
+def slots_of(lengths, tenants, token):
+    count = lengths.shape[1]
+    down = lax.broadcasted_iota(jnp.int32, (count, count), 0)
+    across = lax.broadcasted_iota(jnp.int32, (count, count), 1)
+    starts = jnp.sum(jnp.where(down < across, column(lengths), 0.0), axis=0, keepdims=True)
+    chosen = (starts <= token) & (token < starts + lengths)
+    position = token - jnp.sum(jnp.where(chosen, starts, 0.0), axis=1, keepdims=True)
+    tenant = jnp.sum(jnp.where(chosen, tenants, 0.0), axis=1, keepdims=True)
+    return jnp.where(position < PLEN, tenant * PLEN + position, float(NO_SLOT))
+
+
+def inputs_of(acts, slot, table):
+    lane = lax.broadcasted_iota(jnp.int32, (acts.shape[0], table.shape[0]), 1).astype(F32)
+    rows = jnp.dot((lane == slot).astype(BF16), table, preferred_element_type=F32)
+    wide = jnp.where(slot < SLOTS, rows, acts.astype(F32))
+    scale = lax.rsqrt(jnp.mean(wide * wide, axis=1, keepdims=True) + EPS)
+    return wide, scale
+
+
+def experts_of(routes_row):
+    size = routes_row.shape[1]
+    down = lax.broadcasted_iota(jnp.int32, (size, size), 0)
+    across = lax.broadcasted_iota(jnp.int32, (size, size), 1)
+    expert = column(routes_row)
+    earlier = (routes_row == expert) & (across < down)
+    rank = jnp.sum(jnp.where(earlier, 1.0, 0.0), axis=1, keepdims=True)
+    return expert, rank
+
+
+def prepare_kernel(first_ref, *refs):
+    far, refs = refs[:15], refs[15:]
+    packed_ref, fin_ref, bin_ref, marks_ref, front_ref, rest_ref, source_ref = refs[:7]
+    held, sems, ring_sems = refs[7:-2], refs[-2], refs[-1]
+    gate, upper, down = far[12:]
+    width, half = gate.shape
     cut = front_ref.shape[0]
-    front_ref[:, :half] = gate_ref[:cut, :]
-    front_ref[:, half:] = up_ref[:cut, :]
-    rest_ref[: width - cut, :half] = gate_ref[cut:, :]
-    rest_ref[: width - cut, half:] = up_ref[cut:, :]
+    pairs = [
+        (gate.at[pl.ds(0, cut), :], front_ref.at[:, pl.ds(0, half)]),
+        (upper.at[pl.ds(0, cut), :], front_ref.at[:, pl.ds(half, half)]),
+        (gate.at[pl.ds(cut, width - cut), :], rest_ref.at[pl.ds(0, width - cut), pl.ds(0, half)]),
+        (upper.at[pl.ds(cut, width - cut), :], rest_ref.at[pl.ds(0, width - cut), pl.ds(half, half)]),
+    ]
     for k in range(width // (2 * half)):
-        rows = slice(width - cut + k * half, width - cut + (k + 1) * half)
-        rest_ref[rows, :] = down_ref[:, 2 * half * k : 2 * half * (k + 1)]
-
-
-def shard_arrays(gate, upper, down):
-    width, half = gate.shape
+        into = rest_ref.at[pl.ds(width - cut + k * half, half), :]
+        pairs.append((down.at[:, pl.ds(2 * half * k, 2 * half)], into))
+    fetches = [pltpu.make_async_copy(a, b, sems.at[k]) for k, (a, b) in enumerate(zip(far[:12], held))]
+    ring_copies = [pltpu.make_async_copy(a, b, ring_sems.at[k]) for k, (a, b) in enumerate(pairs)]
+    for copy in fetches + ring_copies:
+        copy.start()
+    for copy in fetches:
+        copy.wait()
+    flen_ref, ften_ref, blen_ref, bten_ref, froute_ref, broute_ref, weight_ref, table_ref, gain_ref = held[:9]
+    facts_ref, bacts_ref, cot_ref = held[9:]
+    tok = facts_ref.shape[0]
+    token = lax.broadcasted_iota(jnp.int32, (tok, 1), 0).astype(F32) + first_ref[0, 0].astype(F32)
+    table = table_ref[...]
+    gain = gain_ref[...]
+    f_slot = slots_of(flen_ref[...].astype(F32), ften_ref[...].astype(F32), token)
+    b_slot = slots_of(blen_ref[...].astype(F32), bten_ref[...].astype(F32), token)
+    f_wide, f_scale = inputs_of(facts_ref[...], f_slot, table)
+    b_wide, b_scale = inputs_of(bacts_ref[...], b_slot, table)
+    fin_ref[...] = f_wide.astype(BF16)
+    bin_ref[...] = b_wide.astype(BF16)
+    f_expert, f_rank = experts_of(froute_ref[...].astype(F32))
+    b_expert, b_rank = experts_of(broute_ref[...].astype(F32))
+    weight = column(weight_ref[...])
+    high = weight.astype(BF16).astype(F32)
+    lane = lax.broadcasted_iota(jnp.int32, (tok, EXTRA), 1)
+    extra = jnp.where(lane == 0, high, jnp.where(lane == 1, weight - high, jnp.where(lane == 2, b_slot, 0.0)))
+    blank = jnp.zeros((tok, EXTRA), BF16)
+    source_ref[0:tok, 0:width] = (b_wide * b_scale * gain).astype(BF16)
+    source_ref[tok : 2 * tok, 0:width] = (f_wide * f_scale * gain).astype(BF16)
+    source_ref[2 * tok : 3 * tok, 0:width] = cot_ref[...]
+    source_ref[0:tok, width:] = extra.astype(BF16)
+    source_ref[tok : 2 * tok, width:] = blank
+    source_ref[2 * tok : 3 * tok, width:] = blank
+    target = jnp.concatenate(
+        [
+            row_of(b_expert * BLOCK + b_rank),
+            row_of(f_expert * BLOCK + (CAP + f_rank)),
+            row_of(b_expert * BLOCK + (ROWS + b_rank)),
+        ],
+        axis=1,
+    )
+    total = packed_ref.shape[0]
+    place = lax.broadcasted_iota(jnp.int32, (total, 3 * tok), 0).astype(F32)
+    picker = (place == target).astype(BF16)
+    step = 512
+    for at in range(0, width + EXTRA, step):
+        cols = slice(at, min(at + step, width + EXTRA))
+        packed_ref[:, cols] = jnp.dot(picker, source_ref[:, cols], preferred_element_type=F32).astype(BF16)
+    marks_ref[...] = jnp.where(
+        lane == 0,
+        b_slot,
+        jnp.where(
+            lane == 1,
+            b_scale,
+            jnp.where(lane == 2, f_expert * ROWS + (CAP + f_rank), b_expert * ROWS + b_rank),
+        ),
+    )
+    for copy in ring_copies:
+        copy.wait()
+
+
+def prepared(*operands):
+    tok, width = operands[10].shape
+    half = operands[13].shape[1]
     cut = 3 * width // 4
-    near = pl.BlockSpec(memory_space=pltpu.VMEM)
-    shape = jax.ShapeDtypeStruct((cut, 2 * half), BF16)
+    near, away = pl.BlockSpec(memory_space=pltpu.VMEM), pl.BlockSpec(memory_space=pl.ANY)
+    ring = jax.ShapeDtypeStruct((cut, 2 * half), BF16)
+    held = jax.ShapeDtypeStruct((tok, width), BF16)
     return pl.pallas_call(
-        shard_kernel,
-        out_shape=(shape, shape),
-        in_specs=[near] * 3,
-        out_specs=(near, near),
+        prepare_kernel,
+        out_shape=(
+            jax.ShapeDtypeStruct((EXPERTS * BLOCK, width + EXTRA), BF16),
+            held,
+            held,
+            jax.ShapeDtypeStruct((tok, EXTRA), F32),
+            ring,
+            ring,
+        ),
+        in_specs=[pl.BlockSpec(memory_space=pltpu.SMEM)] + [away] * 15,
+        out_specs=(near,) * 4 + (away, away),
+        scratch_shapes=[pltpu.VMEM((3 * tok, width + EXTRA), BF16)]
+        + [pltpu.VMEM(o.shape, o.dtype) for o in operands[1:13]]
+        + [pltpu.SemaphoreType.DMA((12,)), pltpu.SemaphoreType.DMA((4 + width // (2 * half),))],
         compiler_params=pltpu.CompilerParams(vmem_limit_bytes=VMEM_MIB * 1024 * 1024),
-    )(gate, upper, down)
+    )(operands[0], *[pltpu.with_memory_space_constraint(o, pltpu.HBM) for o in operands[1:]])
 
 
 def expert_kernel(count, has_acc, final, *refs):
@@ -265,7 +349,28 @@
     gain_row = norm_gain[0]
     flat_table = prompts[0].reshape(SLOTS, width)
 
-    own_front, own_rest = shard_arrays(w_gate[0, 0], w_up[0, 0], w_down[0, 0])
+    first_row = (lax.axis_index("split") * lax.axis_size("column") + lax.axis_index("column")) * tok_count
+    cotangent = bwd_cotangent[0]
+    packed, fwd_in, bwd_in, marks, own_front, own_rest = prepared(
+        first_row.astype(jnp.int32).reshape(1, 1),
+        fwd_lengths,
+        fwd_tenants,
+        bwd_lengths,
+        bwd_tenants,
+        fwd_routes.reshape(1, tok_count),
+        bwd_routes.reshape(1, tok_count),
+        bwd_weights.reshape(1, tok_count),
+        jnp.pad(flat_table, ((0, LOW_AT - SLOTS), (0, 0))),
+        norm_gain,
+        fwd_acts[0],
+        bwd_acts[0],
+        cotangent,
+        w_gate[0, 0],
+        w_up[0, 0],
+        w_down[0, 0],
+    )
+    slot, bwd_scale = marks[:, 0:1], marks[:, 1:2]
+
     front_ring, rest_ring = [(own_front, own_front)], [(own_rest, own_rest)]
 
     def onward(ring):
@@ -280,61 +385,23 @@
     def shards(step):
         return [(front_ring[step][k], rest_ring[step][k]) for k in range(2)]
 
-    for _ in range(2):
+    for _ in range(3):
         onward(front_ring)
         onward(rest_ring)
-    onward(front_ring)
-
-    first_row = (lax.axis_index("split") * lax.axis_size("column") + lax.axis_index("column")) * tok_count
-    fwd_in, _, fwd_normed, _, _, _ = prepare(
-        fwd_acts[0], fwd_lengths[0], fwd_tenants[0], flat_table, gain_row, first_row
-    )
-    bwd_in, bwd_scale, bwd_normed, bwd_slot, slot, selector = prepare(
-        bwd_acts[0], bwd_lengths[0], bwd_tenants[0], flat_table, gain_row, first_row
-    )
-    cotangent = bwd_cotangent[0]
-    f_route, b_route = fwd_routes[0, :, 0], bwd_routes[0, :, 0]
-    f_rank, b_rank = ranks(f_route), ranks(b_route)
-    weight_b = bwd_weights[0, :, 0]
-    high = lax.reduce_precision(weight_b, 8, 7)
-    low = weight_b - high
-    lane = jnp.arange(EXTRA, dtype=jnp.int32)[None, :]
-    extra = jnp.where(lane == 0, high[:, None], 0.0)
-    extra = jnp.where(lane == 1, low[:, None], extra)
-    extra = jnp.where(lane == 2, slot.astype(F32)[:, None], extra).astype(BF16)
-    blank = jnp.zeros((tok_count, EXTRA), BF16)
-    sources = jnp.concatenate(
-        [
-            jnp.concatenate([bwd_normed, extra], axis=1),
-            jnp.concatenate([fwd_normed, blank], axis=1),
-            jnp.concatenate([cotangent, blank], axis=1),
-        ],
-        axis=0,
-    )
-    target = jnp.concatenate(
-        [
-            b_route * BLOCK + b_rank,
-            f_route * BLOCK + CAP + f_rank,
-            b_route * BLOCK + ROWS + b_rank,
-        ]
-    )
-    picker = target[None, :] == jnp.arange(EXPERTS * BLOCK, dtype=jnp.int32)[:, None]
-    packed = jnp.dot(picker.astype(BF16), sources, preferred_element_type=F32).astype(BF16)
+
     packed = packed.reshape(EXPERTS, BLOCK, width + EXTRA)
-    packed, _ = lax.optimization_barrier((packed, front_ring[1]))
     arrived = lax.all_to_all(packed, "column", split_axis=0, concat_axis=0, tiled=True)
     rows = arrived[:, :ROWS].reshape(EXPERTS * ROWS, width + EXTRA)
     cots = arrived[:, ROWS:, :width].reshape(EXPERTS * COT_ROWS, width)
 
     slot_in = flat_table.astype(F32)
     slot_scale = lax.rsqrt(jnp.mean(slot_in * slot_in, axis=1, keepdims=True) + EPS)
-    slot_cot = jnp.dot(jnp.transpose(selector.astype(BF16)), cotangent, preferred_element_type=F32)
+    selector = (slot == jnp.arange(SLOTS, dtype=F32)[None, :]).astype(BF16)
+    slot_cot = jnp.dot(jnp.transpose(selector), cotangent, preferred_element_type=F32)
     slot_data = (norm_gain, slot_in, slot_scale, slot_cot)
 
-    acc, note = expert_step(rows, cots, [(own_front, own_rest)] + shards(1))
-    note = held_back(rest_ring, note)
-    onward(rest_ring)
-    acc, note = expert_step(rows, cots, shards(2), (acc, note))
+    early = [(own_front, own_rest)] + shards(1) + shards(2)
+    acc, note = expert_step(rows, cots, early)
     note = held_back(rest_ring, note)
     last = (rotated(front_ring[-1][0], "split", 1), rotated(rest_ring[-1][1], "split", -1))
     before = expert_step(rows, cots, shards(3), (acc, note))
@@ -346,9 +413,9 @@
     totals = summed(summed(local_sums, "split"), "column")
     prompt_grads = totals.astype(BF16).reshape(1, TENANTS, PLEN, width)
 
-    home = jnp.arange(EXPERTS * ROWS, dtype=jnp.int32)[None, :]
-    f_take = ((f_route * ROWS + CAP + f_rank)[:, None] == home).astype(BF16)
-    b_take = ((b_route * ROWS + b_rank)[:, None] == home).astype(BF16)
+    home = jnp.arange(EXPERTS * ROWS, dtype=jnp.int32).astype(F32)[None, :]
+    f_take = (marks[:, 2:3] == home).astype(BF16)
+    b_take = (marks[:, 3:4] == home).astype(BF16)
     f_out = jnp.dot(f_take, returned, preferred_element_type=F32)
     leaving = (fwd_in.astype(F32) + fwd_weights[0] * f_out).astype(BF16)
     next_acts = shifted(leaving, "phase", 1)
@@ -357,7 +424,7 @@
     wide = bwd_in.astype(F32)
     inner = jnp.mean(wide * scaled, axis=1, keepdims=True)
     input_grad = cotangent.astype(F32) + bwd_scale * scaled - wide * bwd_scale**3 * inner
-    to_prev = jnp.where(bwd_slot[:, None], 0.0, input_grad).astype(BF16)
+    to_prev = jnp.where(slot < SLOTS, 0.0, input_grad).astype(BF16)
     prev_grads = shifted(to_prev, "phase", -1)
     return next_acts[None], prev_grads[None], prompt_grads
 

time: 237 us -> 226 us (0.954)
  starting transfers between devices: 98.8 us -> 91.8 us
  other arithmetic: 5.97 us -> 1.12 us
  matrix products: 5.75 us -> 1.4 us
  waiting for transfers between devices: 89.2 us -> 93.1 us
  Pallas kernels: 19.7 us -> 23 us
    ppermute x14, waiting for transfers between devices: 50 us -> 68.6 us  [rotated(): lax.ppermute(value, axis, [(i, (i + distance) % size) for i in range(size)])]
    all_to_all x1, waiting for transfers between devices: 14.3 us -> 0.01 us  [on_device(): lax.all_to_all(packed, 'column', split_axis=0, concat_axis=0, tiled=True)]
    pallas_call x1, Pallas kernels: 0.21 us -> 5.83 us  [prepared(): pl.pallas_call(prepare_kernel, out_shape=(jax.ShapeDtypeStruct((EXPERTS *...]
    ppermute x14, starting transfers between devices: 43.9 us -> 38.7 us  [rotated(): lax.ppermute(value, axis, [(i, (i + distance) % size) for i in range(size)])]
    dot_general x4 -> x1, matrix products: 3.86 us -> 0.3 us  [on_device(): jnp.dot(jnp.transpose(selector), cotangent, preferred_element_type=F32)]
    all_to_all x1, starting transfers between devices: 13.9 us -> 10.9 us  [on_device(): lax.all_to_all(packed, 'column', split_axis=0, concat_axis=0, tiled=True)]
    all_to_all x1, starting transfers between devices: 3.58 us -> 6.34 us  [on_device(): lax.all_to_all(partial.reshape(EXPERTS, ROWS, width), 'column', split_axi...]
    reduce_sum x5 -> x0, other arithmetic: 2.59 us -> none  [the longest x2 1.48 us: token_layout(): seg_starts = jnp.sum(jnp.where(earlier, lengths[:, None], 0), axis=0)]
  transfers between devices with their start and end apart: 24 -> 24, of which waited for: 16 -> 14; matrix products, arithmetic and copies ran while one was open for 7% -> 3% of each run, Pallas kernels for 6% -> 6%
where the time goes in v6:
time: 226 us; the launch traced here: 224 us
  waiting for transfers between devices  93.1 us (41%)
  starting transfers between devices  91.8 us (41%)
  Pallas kernels  23 us (10%)
  local copies, waits for them, and re-layouts  12.4 us (5%)
    ppermute x14, waiting for transfers between devices, rotated(): lax.ppermute(value, axis, [(i, (i + distance) % size) for i in range(size)])  68.6 us
    ppermute x14, starting transfers between devices, rotated(): lax.ppermute(value, axis, [(i, (i + distance) % size) for i in range(size)])  38.7 us
    ppermute x6, starting transfers between devices, summed(): lax.ppermute(value.astype(BF16), axis, [(i, i ^ distance) for i in range(...  26.9 us
    ppermute x6, waiting for transfers between devices, summed(): lax.ppermute(value.astype(BF16), axis, [(i, i ^ distance) for i in range(...  19.1 us
    pallas_call x3, Pallas kernels, expert_step(): pl.pallas_call(functools.partial(expert_kernel, len(shards), before is no...  17.1 us
    all_to_all x1, starting transfers between devices, on_device(): lax.all_to_all(packed, 'column', split_axis=0, concat_axis=0, tiled=True)  10.9 us
    ppermute x2, starting transfers between devices, shifted(): return lax.ppermute(block, axis, route)  9.04 us
    unnamed x45, local copies, waits for them, and re-layouts  8.91 us
  transfers between devices with their start and end apart: 24, of which 14 were waited for; matrix products, arithmetic and copies ran while one was open for 3% of the time, Pallas kernels for 6%

profile of v6, /device:TPU:1, one launch (start us, length us, event | category | flops | bytes accessed | tf_op | source)
XLA Modules:
  0.0 223.9 jit_solution(1126984022878609652)
XLA Ops:
  2.3 5.8 %shard_map.175 = (bf16[512,2176]{1,0:T(8,128)(2,1)}, bf16[128,2048]{1,0:T(8,128)(2,1)S(1)}, bf16[128,2048]{1,0:T(8,128)(2,1)S(1)}, f32[128,128]{1,0:T(8,128)S(1)...) custom-call(s32[1,1]{1,0:T(1,128)} %bitcast.first_ref, s32[1,16]{1,0:T(1,128)} %refs_0_.1, ...), custom_call_target="tpu_custom_call" | custom-call | tf_op jit(solution)/shard_map/pallas_call | solution.py:155
  8.9 10.9 %all-to-all-start = ((bf16[8,64,2176]{2,1,0:T(8,128)(2,1)}), bf16[8,64,2176]{2,1,0:T(8,128)(2,1)}, u32[]{:S(2)}, u32[]{:S(2)}) async-start(bf16[8,64,2176]{2,1,0:T(8,128)(2,1)} %bitcast.11), calls=%async_computation | async-start | bytes 4456448 | tf_op jit(solution)/shard_map/all_to_all | solution.py:393
  19.8 3.2 %collective-permute-start = (bf16[1536,256]{1,0:T(8,128)(2,1)S(1)}, bf16[1536,256]{1,0:T(8,128)(2,1)S(1)}, u32[]{:S(2)}, u32[]{:S(2)}) collective-permute-start(bf16[1536,256]{1,0:T(8,128)(2,1)S(1)} %get-tuple-element.21.refs_2_), channel_id=1, source_target_pairs={{0,8},{8,16},{16,24},{24,32},{32,40},{40,48},{48,56},{56,0},{1,9},... | collective-permute-start | bytes 2359304 | tf_op jit(solution)/shard_map/ppermute | solution.py:311
  23.0 3.2 %collective-permute-start.4 = (bf16[1536,256]{1,0:T(8,128)(2,1)S(1)}, bf16[1536,256]{1,0:T(8,128)(2,1)S(1)}, u32[]{:S(2)}, u32[]{:S(2)}) collective-permute-start(bf16[1536,256]{1,0:T(8,128)(2,1)S(1)} %get-tuple-element.22.refs_3_), channel_id=1, source_target_pairs={{0,8},{8,16},{16,24},{24,32},{32,40},{40,48},{48,56},{56,0},{1,9},... | collective-permute-start | bytes 2359304 | tf_op jit(solution)/shard_map/ppermute | solution.py:311
  26.2 3.3 %collective-permute-start.7 = (bf16[1536,256]{1,0:T(8,128)(2,1)S(1)}, bf16[1536,256]{1,0:T(8,128)(2,1)S(1)}, u32[]{:S(2)}, u32[]{:S(2)}) collective-permute-start(bf16[1536,256]{1,0:T(8,128)(2,1)S(1)} %get-tuple-element.22.refs_3_), channel_id=1, source_target_pairs={{0,56},{8,0},{16,8},{24,16},{32,24},{40,32},{48,40},{56,48},{1,57}... | collective-permute-start | bytes 2359304 | tf_op jit(solution)/shard_map/ppermute | solution.py:311
  29.5 2.6 %collective-permute-start.10 = (bf16[1536,256]{1,0:T(8,128)(2,1)S(1)}, bf16[1536,256]{1,0:T(8,128)(2,1)S(1)}, u32[]{:S(2)}, u32[]{:S(2)}) collective-permute-start(bf16[1536,256]{1,0:T(8,128)(2,1)S(1)} %get-tuple-element.21.refs_2_), channel_id=1, source_target_pairs={{0,56},{8,0},{16,8},{24,16},{32,24},{40,32},{48,40},{56,48},{1,57}... | collective-permute-start | bytes 2359304 | tf_op jit(solution)/shard_map/ppermute | solution.py:311
  32.1 9.8 %collective-permute-done.refs_4_ = bf16[1536,256]{1,0:T(8,128)(2,1)S(1)} collective-permute-done((bf16[1536,256]{1,0:T(8,128)(2,1)S(1)}, bf16[1536,256]{1,0:T(8,128)(2,1)S(1)}, u32[]{:S(2)}, u32[]{:S(2)}) %collective-permute-start) | collective-permute-done | bytes 786464 | tf_op jit(solution)/shard_map/ppermute | solution.py:311
  43.8 14.9 %collective-permute-done.4.refs_5_ = bf16[1536,256]{1,0:T(8,128)(2,1)S(1)} collective-permute-done((bf16[1536,256]{1,0:T(8,128)(2,1)S(1)}, bf16[1536,256]{1,0:T(8,128)(2,1)S(1)}, u32[]{:S(2)}, u32[]{:S(2)}) %collective-permute-start.4) | collective-permute-done | bytes 786464 | tf_op jit(solution)/shard_map/ppermute | solution.py:311
  60.7 4.6 %collective-permute-start.8 = (bf16[1536,256]{1,0:T(8,128)(2,1)S(1)}, bf16[1536,256]{1,0:T(8,128)(2,1)}, u32[]{:S(2)}, u32[]{:S(2)}) collective-permute-start(bf16[1536,256]{1,0:T(8,128)(2,1)S(1)} %collective-permute-done.7.refs_7_), channel_id=1, source_target_pairs={{0,56},{8,0},{16,8},{24,16},{32,24},{40,32},{48,40},{56,48},{1,57}... | collective-permute-start | bytes 2359304 | tf_op jit(solution)/shard_map/ppermute | solution.py:311
  67.2 8.3 %collective-permute-done.1.refs_8_ = bf16[1536,256]{1,0:T(8,128)(2,1)S(1)} collective-permute-done((bf16[1536,256]{1,0:T(8,128)(2,1)S(1)}, bf16[1536,256]{1,0:T(8,128)(2,1)S(1)}, u32[]{:S(2)}, u32[]{:S(2)}) %collective-permute-start.1) | collective-permute-done | bytes 786464 | tf_op jit(solution)/shard_map/ppermute | solution.py:311
  77.4 15.0 %collective-permute-done.5.refs_9_ = bf16[1536,256]{1,0:T(8,128)(2,1)} collective-permute-done((bf16[1536,256]{1,0:T(8,128)(2,1)S(1)}, bf16[1536,256]{1,0:T(8,128)(2,1)}, u32[]{:S(2)}, u32[]{:S(2)}) %collective-permute-start.5) | collective-permute-done | bytes 786464 | tf_op jit(solution)/shard_map/ppermute | solution.py:311
  94.4 4.6 %collective-permute-start.9 = (bf16[1536,256]{1,0:T(8,128)(2,1)}, bf16[1536,256]{1,0:T(8,128)(2,1)}, u32[]{:S(2)}, u32[]{:S(2)}) collective-permute-start(bf16[1536,256]{1,0:T(8,128)(2,1)} %collective-permute-done.8.refs_11_), channel_id=1, source_target_pairs={{0,56},{8,0},{16,8},{24,16},{32,24},{40,32},{48,40},{56,48},{1,57}... | collective-permute-start | bytes 2359304 | tf_op jit(solution)/shard_map/ppermute | solution.py:311
  101.5 7.8 %collective-permute-done.2.refs_2_ = bf16[1536,256]{1,0:T(8,128)(2,1)} collective-permute-done((bf16[1536,256]{1,0:T(8,128)(2,1)S(1)}, bf16[1536,256]{1,0:T(8,128)(2,1)}, u32[]{:S(2)}, u32[]{:S(2)}) %collective-permute-start.2) | collective-permute-done | bytes 786464 | tf_op jit(solution)/shard_map/ppermute | solution.py:311
  113.9 9.2 %shard_map.176 = (f32[320,2048]{1,0:T(8,128)S(1)}, f32[8,128]{1,0:T(8,128)S(1)}) custom-call(bf16[320,2176]{1,0:T(8,128)(2,1)S(1)} %bitcast.25, bf16[192,2048]{1,0:T(8,128)(2,1)S(1)} %bitcast.28, bf16[1536,256]{1,0:T(8,128)(2,1)} %copy-done.6, bf16[1536,256]{1,0:T(8,128)(2,1)} %copy-done.7, bf16[1536,256]{1,0:T(8,128)(2,1)} %copy-done.15, ...), custom_call_target="tpu_custom_call" | custom-call | flops 3690987520 | bytes 12664832 | tf_op jit(solution)/shard_map/pallas_call | solution.py:294
  126.2 3.3 %collective-permute-start.12 = (bf16[1536,256]{1,0:T(8,128)(2,1)}, bf16[1536,256]{1,0:T(8,128)(2,1)}, u32[]{:S(2)}, u32[]{:S(2)}) collective-permute-start(bf16[1536,256]{1,0:T(8,128)(2,1)} %collective-permute-done.9.refs_5_), channel_id=1, source_target_pairs={{0,56},{8,0},{16,8},{24,16},{32,24},{40,32},{48,40},{56,48},{1,57}... | collective-permute-start | bytes 2359304 | tf_op jit(solution)/shard_map/ppermute | solution.py:311
  132.2 4.5 %shard_map.177 = (f32[320,2048]{1,0:T(8,128)S(1)}, f32[8,128]{1,0:T(8,128)S(1)}) custom-call(bf16[320,2176]{1,0:T(8,128)(2,1)S(1)} %bitcast.26, bf16[192,2048]{1,0:T(8,128)(2,1)S(1)} %bitcast.29, bf16[1536,256]{1,0:T(8,128)(2,1)} %collective-permute-done.2.refs_2_, bf16[1536,256]{1,0:T(8,128)(2,1)} %collective-permute-done.6.refs_3_, ...), custom_call_target="tpu_custom_call" | custom-call | flops 1476395008 | bytes 10571776 | tf_op jit(solution)/shard_map/pallas_call | solution.py:294
  136.7 6.3 %collective-permute-done.3.refs_2_ = bf16[1536,256]{1,0:T(8,128)(2,1)} collective-permute-done((bf16[1536,256]{1,0:T(8,128)(2,1)}, bf16[1536,256]{1,0:T(8,128)(2,1)}, u32[]{:S(2)}, u32[]{:S(2)}) %collective-permute-start.3) | collective-permute-done | bytes 786464 | tf_op jit(solution)/shard_map/ppermute | solution.py:311
  143.0 5.0 %collective-permute-done.12.refs_3_ = bf16[1536,256]{1,0:T(8,128)(2,1)} collective-permute-done((bf16[1536,256]{1,0:T(8,128)(2,1)}, bf16[1536,256]{1,0:T(8,128)(2,1)}, u32[]{:S(2)}, u32[]{:S(2)}) %collective-permute-start.12) | collective-permute-done | bytes 786464 | tf_op jit(solution)/shard_map/ppermute | solution.py:311
  148.0 3.4 %shard_map.178 = (bf16[320,2048]{1,0:T(8,128)(2,1)S(1)}, f32[20,2048]{1,0:T(8,128)S(1)}) custom-call(bf16[320,2176]{1,0:T(8,128)(2,1)S(1)} %bitcast.27, bf16[192,2048]{1,0:T(8,128)(2,1)S(1)} %bitcast.30, bf16[1536,256]{1,0:T(8,128)(2,1)} %collective-permute-done.3.refs_2_, bf16[1536,256]{1,0:T(8,128)(2,1)} %collective-permute-done.12.refs_3_, ...), custom_call_target="tpu_custom_call" | custom-call | flops 738197504 | bytes 9334864 | tf_op jit(solution)/shard_map/pallas_call | solution.py:294
  154.4 6.3 %all-to-all-start.1 = ((bf16[8,40,2048]{2,1,0:T(8,128)(2,1)}), bf16[8,40,2048]{2,1,0:T(8,128)(2,1)S(1)}, u32[]{:S(2)}, u32[]{:S(2)}) async-start(bf16[8,40,2048]{2,1,0:T(8,128)(2,1)} %bitcast.31), calls=%async_computation.1 | async-start | bytes 2621440 | tf_op jit(solution)/shard_map/all_to_all | solution.py:410
  160.8 6.9 %collective-permute-start.17 = (bf16[20,2048]{1,0:T(8,128)(2,1)S(1)}, bf16[20,2048]{1,0:T(8,128)(2,1)S(1)}, u32[]{:S(2)}, u32[]{:S(2)}) collective-permute-start(bf16[20,2048]{1,0:T(8,128)(2,1)S(1)} %add_convert_fusion.5), channel_id=1, source_target_pairs={{0,16},{8,24},{16,0},{24,8},{32,48},{40,56},{48,32},{56,40},{1,17}... | collective-permute-start | bytes 245768 | tf_op jit(solution)/shard_map/ppermute | solution.py:324
  167.7 2.8 %collective-permute-done.17 = bf16[20,2048]{1,0:T(8,128)(2,1)S(1)} collective-permute-done((bf16[20,2048]{1,0:T(8,128)(2,1)S(1)}, bf16[20,2048]{1,0:T(8,128)(2,1)S(1)}, u32[]{:S(2)}, u32[]{:S(2)}) %collective-permute-start.17) | collective-permute-done | bytes 81952 | tf_op jit(solution)/shard_map/ppermute | solution.py:324
  170.5 2.6 %collective-permute-start.18 = (bf16[20,2048]{1,0:T(8,128)(2,1)S(1)}, bf16[20,2048]{1,0:T(8,128)(2,1)S(1)}, u32[]{:S(2)}, u32[]{:S(2)}) collective-permute-start(bf16[20,2048]{1,0:T(8,128)(2,1)S(1)} %add_convert_fusion.4), channel_id=1, source_target_pairs={{0,32},{8,40},{16,48},{24,56},{32,0},{40,8},{48,16},{56,24},{1,33}... | collective-permute-start | bytes 245768 | tf_op jit(solution)/shard_map/ppermute | solution.py:324
  173.1 7.5 %collective-permute-done.18 = bf16[20,2048]{1,0:T(8,128)(2,1)S(1)} collective-permute-done((bf16[20,2048]{1,0:T(8,128)(2,1)S(1)}, bf16[20,2048]{1,0:T(8,128)(2,1)S(1)}, u32[]{:S(2)}, u32[]{:S(2)}) %collective-permute-start.18) | collective-permute-done | bytes 81952 | tf_op jit(solution)/shard_map/ppermute | solution.py:324
  180.7 3.4 %collective-permute-start.19 = (bf16[20,2048]{1,0:T(8,128)(2,1)S(1)}, bf16[20,2048]{1,0:T(8,128)(2,1)S(1)}, u32[]{:S(2)}, u32[]{:S(2)}) collective-permute-start(bf16[20,2048]{1,0:T(8,128)(2,1)S(1)} %add_convert_fusion.3), channel_id=1, source_target_pairs={{0,1},{1,0},{2,3},{3,2},{4,5},{5,4},{6,7},{7,6},{8,9},{9,8},{10,11... | collective-permute-start | bytes 245768 | tf_op jit(solution)/shard_map/ppermute | solution.py:324
  184.2 5.0 %collective-permute-done.19 = bf16[20,2048]{1,0:T(8,128)(2,1)S(1)} collective-permute-done((bf16[20,2048]{1,0:T(8,128)(2,1)S(1)}, bf16[20,2048]{1,0:T(8,128)(2,1)S(1)}, u32[]{:S(2)}, u32[]{:S(2)}) %collective-permute-start.19) | collective-permute-done | bytes 81952 | tf_op jit(solution)/shard_map/ppermute | solution.py:324
  189.2 4.8 %collective-permute-start.20 = (bf16[20,2048]{1,0:T(8,128)(2,1)S(1)}, bf16[20,2048]{1,0:T(8,128)(2,1)S(1)}, u32[]{:S(2)}, u32[]{:S(2)}) collective-permute-start(bf16[20,2048]{1,0:T(8,128)(2,1)S(1)} %add_convert_fusion.2), channel_id=1, source_target_pairs={{0,2},{1,3},{2,0},{3,1},{4,6},{5,7},{6,4},{7,5},{8,10},{9,11},{10,... | collective-permute-start | bytes 245768 | tf_op jit(solution)/shard_map/ppermute | solution.py:324
  194.1 3.8 %collective-permute-done.20 = bf16[20,2048]{1,0:T(8,128)(2,1)S(1)} collective-permute-done((bf16[20,2048]{1,0:T(8,128)(2,1)S(1)}, bf16[20,2048]{1,0:T(8,128)(2,1)S(1)}, u32[]{:S(2)}, u32[]{:S(2)}) %collective-permute-start.20) | collective-permute-done | bytes 81952 | tf_op jit(solution)/shard_map/ppermute | solution.py:324
  197.9 7.2 %collective-permute-start.21 = (bf16[20,2048]{1,0:T(8,128)(2,1)S(1)}, bf16[20,2048]{1,0:T(8,128)(2,1)S(1)}, u32[]{:S(2)}, u32[]{:S(2)}) collective-permute-start(bf16[20,2048]{1,0:T(8,128)(2,1)S(1)} %add_convert_fusion.1), channel_id=1, source_target_pairs={{0,4},{1,5},{2,6},{3,7},{4,0},{5,1},{6,2},{7,3},{8,12},{9,13},{10,... | collective-permute-start | bytes 245768 | tf_op jit(solution)/shard_map/ppermute | solution.py:324
  206.6 6.0 %collective-permute-start.15 = (bf16[128,2048]{1,0:T(8,128)(2,1)S(1)}, bf16[128,2048]{1,0:T(8,128)(2,1)S(1)}, u32[]{:S(2)}, u32[]{:S(2)}) collective-permute-start(bf16[128,2048]{1,0:T(8,128)(2,1)S(1)} %fusion.6), channel_id=1, source_target_pairs={{64,0},{128,64},{192,128},{256,192},{320,256},{384,320},{448,384},... | collective-permute-start | bytes 1572872 | tf_op jit(solution)/shard_map/ppermute | solution.py:317
  213.2 3.0 %collective-permute-start.14 = (bf16[128,2048]{1,0:T(8,128)(2,1)S(1)}, bf16[128,2048]{1,0:T(8,128)(2,1)S(1)}, u32[]{:S(2)}, u32[]{:S(2)}) collective-permute-start(bf16[128,2048]{1,0:T(8,128)(2,1)S(1)} %fusion.2), channel_id=1, source_target_pairs={{0,64},{64,128},{128,192},{192,256},{256,320},{320,384},{384,448},... | collective-permute-start | bytes 1572872 | tf_op jit(solution)/shard_map/ppermute | solution.py:317
  217.0 3.6 %collective-permute-done.15 = bf16[128,2048]{1,0:T(8,128)(2,1)S(1)} collective-permute-done((bf16[128,2048]{1,0:T(8,128)(2,1)S(1)}, bf16[128,2048]{1,0:T(8,128)(2,1)S(1)}, u32[]{:S(2)}, u32[]{:S(2)}) %collective-permute-start.15) | collective-permute-done | bytes 524320 | tf_op jit(solution)/shard_map/ppermute | solution.py:317
  (89 shorter events, 34.0 us)
Async XLA Ops:
  8.9 17.3 %copy-start.7 = (bf16[1536,256]{1,0:T(8,128)(2,1)}, bf16[1536,256]{1,0:T(8,128)(2,1)S(1)}, u32[]{:S(2)}) copy-start(bf16[1536,256]{1,0:T(8,128)(2,1)S(1)} %get-tuple-element.22.refs_3_) | copy-start | bytes 2359300
  8.9 20.6 %copy-start.6 = (bf16[1536,256]{1,0:T(8,128)(2,1)}, bf16[1536,256]{1,0:T(8,128)(2,1)S(1)}, u32[]{:S(2)}) copy-start(bf16[1536,256]{1,0:T(8,128)(2,1)S(1)} %get-tuple-element.21.refs_2_) | copy-start | bytes 2359300
  8.9 102.3 %all-to-all-start = ((bf16[8,64,2176]{2,1,0:T(8,128)(2,1)}), bf16[8,64,2176]{2,1,0:T(8,128)(2,1)}, u32[]{:S(2)}, u32[]{:S(2)}) async-start(bf16[8,64,2176]{2,1,0:T(8,128)(2,1)} %bitcast.11), calls=%async_computation | async-start | bytes 4456448 | tf_op jit(solution)/shard_map/all_to_all | solution.py:393
  19.8 22.1 %collective-permute-start = (bf16[1536,256]{1,0:T(8,128)(2,1)S(1)}, bf16[1536,256]{1,0:T(8,128)(2,1)S(1)}, u32[]{:S(2)}, u32[]{:S(2)}) collective-permute-start(bf16[1536,256]{1,0:T(8,128)(2,1)S(1)} %get-tuple-element.21.refs_2_), channel_id=1, source_target_pairs={{0,8},{8,16},{16,24},{24,32},{32,40},{40,48},{48,56},{56,0},{1,9},... | collective-permute-start | bytes 2359304 | tf_op jit(solution)/shard_map/ppermute | solution.py:311
  23.0 35.8 %collective-permute-start.4 = (bf16[1536,256]{1,0:T(8,128)(2,1)S(1)}, bf16[1536,256]{1,0:T(8,128)(2,1)S(1)}, u32[]{:S(2)}, u32[]{:S(2)}) collective-permute-start(bf16[1536,256]{1,0:T(8,128)(2,1)S(1)} %get-tuple-element.22.refs_3_), channel_id=1, source_target_pairs={{0,8},{8,16},{16,24},{24,32},{32,40},{40,48},{48,56},{56,0},{1,9},... | collective-permute-start | bytes 2359304 | tf_op jit(solution)/shard_map/ppermute | solution.py:311
  26.2 34.5 %collective-permute-start.7 = (bf16[1536,256]{1,0:T(8,128)(2,1)S(1)}, bf16[1536,256]{1,0:T(8,128)(2,1)S(1)}, u32[]{:S(2)}, u32[]{:S(2)}) collective-permute-start(bf16[1536,256]{1,0:T(8,128)(2,1)S(1)} %get-tuple-element.22.refs_3_), channel_id=1, source_target_pairs={{0,56},{8,0},{16,8},{24,16},{32,24},{40,32},{48,40},{56,48},{1,57}... | collective-permute-start | bytes 2359304 | tf_op jit(solution)/shard_map/ppermute | solution.py:311
  29.5 35.8 %collective-permute-start.10 = (bf16[1536,256]{1,0:T(8,128)(2,1)S(1)}, bf16[1536,256]{1,0:T(8,128)(2,1)S(1)}, u32[]{:S(2)}, u32[]{:S(2)}) collective-permute-start(bf16[1536,256]{1,0:T(8,128)(2,1)S(1)} %get-tuple-element.21.refs_2_), channel_id=1, source_target_pairs={{0,56},{8,0},{16,8},{24,16},{32,24},{40,32},{48,40},{56,48},{1,57}... | collective-permute-start | bytes 2359304 | tf_op jit(solution)/shard_map/ppermute | solution.py:311
  41.9 23.4 %copy-start.15 = (bf16[1536,256]{1,0:T(8,128)(2,1)}, bf16[1536,256]{1,0:T(8,128)(2,1)S(1)}, u32[]{:S(2)}) copy-start(bf16[1536,256]{1,0:T(8,128)(2,1)S(1)} %collective-permute-done.refs_4_) | copy-start | bytes 2359300
  41.9 33.6 %collective-permute-start.1 = (bf16[1536,256]{1,0:T(8,128)(2,1)S(1)}, bf16[1536,256]{1,0:T(8,128)(2,1)S(1)}, u32[]{:S(2)}, u32[]{:S(2)}) collective-permute-start(bf16[1536,256]{1,0:T(8,128)(2,1)S(1)} %collective-permute-done.refs_4_), channel_id=1, source_target_pairs={{0,8},{8,16},{16,24},{24,32},{32,40},{40,48},{48,56},{56,0},{1,9},... | collective-permute-start | bytes 2359304 | tf_op jit(solution)/shard_map/ppermute | solution.py:311
  58.8 16.8 %copy-start.16 = (bf16[1536,256]{1,0:T(8,128)(2,1)}, bf16[1536,256]{1,0:T(8,128)(2,1)S(1)}, u32[]{:S(2)}) copy-start(bf16[1536,256]{1,0:T(8,128)(2,1)S(1)} %collective-permute-done.4.refs_5_) | copy-start | bytes 2359300
  58.8 33.7 %collective-permute-start.5 = (bf16[1536,256]{1,0:T(8,128)(2,1)S(1)}, bf16[1536,256]{1,0:T(8,128)(2,1)}, u32[]{:S(2)}, u32[]{:S(2)}) collective-permute-start(bf16[1536,256]{1,0:T(8,128)(2,1)S(1)} %collective-permute-done.4.refs_5_), channel_id=1, source_target_pairs={{0,8},{8,16},{16,24},{24,32},{32,40},{40,48},{48,56},{56,0},{1,9},... | collective-permute-start | bytes 2359304 | tf_op jit(solution)/shard_map/ppermute | solution.py:311
  60.7 31.8 %copy-start.17 = (bf16[1536,256]{1,0:T(8,128)(2,1)}, bf16[1536,256]{1,0:T(8,128)(2,1)S(1)}, u32[]{:S(2)}) copy-start(bf16[1536,256]{1,0:T(8,128)(2,1)S(1)} %collective-permute-done.7.refs_7_) | copy-start | bytes 2359300
  60.7 33.7 %collective-permute-start.8 = (bf16[1536,256]{1,0:T(8,128)(2,1)S(1)}, bf16[1536,256]{1,0:T(8,128)(2,1)}, u32[]{:S(2)}, u32[]{:S(2)}) collective-permute-start(bf16[1536,256]{1,0:T(8,128)(2,1)S(1)} %collective-permute-done.7.refs_7_), channel_id=1, source_target_pairs={{0,56},{8,0},{16,8},{24,16},{32,24},{40,32},{48,40},{56,48},{1,57}... | collective-permute-start | bytes 2359304 | tf_op jit(solution)/shard_map/ppermute | solution.py:311
  65.3 29.1 %copy-start.18 = (bf16[1536,256]{1,0:T(8,128)(2,1)}, bf16[1536,256]{1,0:T(8,128)(2,1)S(1)}, u32[]{:S(2)}) copy-start(bf16[1536,256]{1,0:T(8,128)(2,1)S(1)} %collective-permute-done.10.refs_6_) | copy-start | bytes 2359300
  65.3 33.7 %collective-permute-start.11 = (bf16[1536,256]{1,0:T(8,128)(2,1)S(1)}, bf16[1536,256]{1,0:T(8,128)(2,1)}, u32[]{:S(2)}, u32[]{:S(2)}) collective-permute-start(bf16[1536,256]{1,0:T(8,128)(2,1)S(1)} %collective-permute-done.10.refs_6_), channel_id=1, source_target_pairs={{0,56},{8,0},{16,8},{24,16},{32,24},{40,32},{48,40},{56,48},{1,57}... | collective-permute-start | bytes 2359304 | tf_op jit(solution)/shard_map/ppermute | solution.py:311
  75.5 23.5 %copy-start.19 = (bf16[1536,256]{1,0:T(8,128)(2,1)}, bf16[1536,256]{1,0:T(8,128)(2,1)S(1)}, u32[]{:S(2)}) copy-start(bf16[1536,256]{1,0:T(8,128)(2,1)S(1)} %collective-permute-done.1.refs_8_) | copy-start | bytes 2359300
  75.5 33.8 %collective-permute-start.2 = (bf16[1536,256]{1,0:T(8,128)(2,1)S(1)}, bf16[1536,256]{1,0:T(8,128)(2,1)}, u32[]{:S(2)}, u32[]{:S(2)}) collective-permute-start(bf16[1536,256]{1,0:T(8,128)(2,1)S(1)} %collective-permute-done.1.refs_8_), channel_id=1, source_target_pairs={{0,8},{8,16},{16,24},{24,32},{32,40},{40,48},{48,56},{56,0},{1,9},... | collective-permute-start | bytes 2359304 | tf_op jit(solution)/shard_map/ppermute | solution.py:311
  92.5 33.7 %collective-permute-start.6 = (bf16[1536,256]{1,0:T(8,128)(2,1)}, bf16[1536,256]{1,0:T(8,128)(2,1)}, u32[]{:S(2)}, u32[]{:S(2)}) collective-permute-start(bf16[1536,256]{1,0:T(8,128)(2,1)} %collective-permute-done.5.refs_9_), channel_id=1, source_target_pairs={{0,8},{8,16},{16,24},{24,32},{32,40},{40,48},{48,56},{56,0},{1,9},... | collective-permute-start | bytes 2359304 | tf_op jit(solution)/shard_map/ppermute | solution.py:311
  94.4 31.8 %collective-permute-start.9 = (bf16[1536,256]{1,0:T(8,128)(2,1)}, bf16[1536,256]{1,0:T(8,128)(2,1)}, u32[]{:S(2)}, u32[]{:S(2)}) collective-permute-start(bf16[1536,256]{1,0:T(8,128)(2,1)} %collective-permute-done.8.refs_11_), channel_id=1, source_target_pairs={{0,56},{8,0},{16,8},{24,16},{32,24},{40,32},{48,40},{56,48},{1,57}... | collective-permute-start | bytes 2359304 | tf_op jit(solution)/shard_map/ppermute | solution.py:311
  99.0 31.4 %collective-permute-start.13 = (bf16[1536,256]{1,0:T(8,128)(2,1)}, bf16[1536,256]{1,0:T(8,128)(2,1)}, u32[]{:S(2)}, u32[]{:S(2)}) collective-permute-start(bf16[1536,256]{1,0:T(8,128)(2,1)} %collective-permute-done.11.refs_10_), channel_id=1, source_target_pairs={{0,56},{8,0},{16,8},{24,16},{32,24},{40,32},{48,40},{56,48},{1,57}... | collective-permute-start | bytes 2359304 | tf_op jit(solution)/shard_map/ppermute | solution.py:311
  109.3 33.7 %collective-permute-start.3 = (bf16[1536,256]{1,0:T(8,128)(2,1)}, bf16[1536,256]{1,0:T(8,128)(2,1)}, u32[]{:S(2)}, u32[]{:S(2)}) collective-permute-start(bf16[1536,256]{1,0:T(8,128)(2,1)} %collective-permute-done.2.refs_2_), channel_id=1, source_target_pairs={{0,8},{8,16},{16,24},{24,32},{32,40},{40,48},{48,56},{56,0},{1,9},... | collective-permute-start | bytes 2359304 | tf_op jit(solution)/shard_map/ppermute | solution.py:311
  126.2 21.8 %collective-permute-start.12 = (bf16[1536,256]{1,0:T(8,128)(2,1)}, bf16[1536,256]{1,0:T(8,128)(2,1)}, u32[]{:S(2)}, u32[]{:S(2)}) collective-permute-start(bf16[1536,256]{1,0:T(8,128)(2,1)} %collective-permute-done.9.refs_5_), channel_id=1, source_target_pairs={{0,56},{8,0},{16,8},{24,16},{32,24},{40,32},{48,40},{56,48},{1,57}... | collective-permute-start | bytes 2359304 | tf_op jit(solution)/shard_map/ppermute | solution.py:311
  152.5 8.3 %collective-permute-start.16 = (bf16[20,2048]{1,0:T(8,128)(2,1)S(1)}, bf16[20,2048]{1,0:T(8,128)(2,1)S(1)}, u32[]{:S(2)}, u32[]{:S(2)}) collective-permute-start(bf16[20,2048]{1,0:T(8,128)(2,1)S(1)} %convert_element_type.105), channel_id=1, source_target_pairs={{0,8},{8,0},{16,24},{24,16},{32,40},{40,32},{48,56},{56,48},{1,9},... | collective-permute-start | bytes 245768 | tf_op jit(solution)/shard_map/ppermute | solution.py:324
  154.4 50.7 %all-to-all-start.1 = ((bf16[8,40,2048]{2,1,0:T(8,128)(2,1)}), bf16[8,40,2048]{2,1,0:T(8,128)(2,1)S(1)}, u32[]{:S(2)}, u32[]{:S(2)}) async-start(bf16[8,40,2048]{2,1,0:T(8,128)(2,1)} %bitcast.31), calls=%async_computation.1 | async-start | bytes 2621440 | tf_op jit(solution)/shard_map/all_to_all | solution.py:410
  160.8 44.4 %copy-start.13 = (f32[1,128,1]{1,2,0:T(1,128)S(1)}, f32[1,128,1]{1,2,0:T(1,128)}, u32[]{:S(2)}) copy-start(f32[1,128,1]{1,2,0:T(1,128)} %param.23) | copy-start | bytes 1540
  160.8 9.7 %collective-permute-start.17 = (bf16[20,2048]{1,0:T(8,128)(2,1)S(1)}, bf16[20,2048]{1,0:T(8,128)(2,1)S(1)}, u32[]{:S(2)}, u32[]{:S(2)}) collective-permute-start(bf16[20,2048]{1,0:T(8,128)(2,1)S(1)} %add_convert_fusion.5), channel_id=1, source_target_pairs={{0,16},{8,24},{16,0},{24,8},{32,48},{40,56},{48,32},{56,40},{1,17}... | collective-permute-start | bytes 245768 | tf_op jit(solution)/shard_map/ppermute | solution.py:324
  170.5 10.1 %collective-permute-start.18 = (bf16[20,2048]{1,0:T(8,128)(2,1)S(1)}, bf16[20,2048]{1,0:T(8,128)(2,1)S(1)}, u32[]{:S(2)}, u32[]{:S(2)}) collective-permute-start(bf16[20,2048]{1,0:T(8,128)(2,1)S(1)} %add_convert_fusion.4), channel_id=1, source_target_pairs={{0,32},{8,40},{16,48},{24,56},{32,0},{40,8},{48,16},{56,24},{1,33}... | collective-permute-start | bytes 245768 | tf_op jit(solution)/shard_map/ppermute | solution.py:324
  180.7 8.6 %collective-permute-start.19 = (bf16[20,2048]{1,0:T(8,128)(2,1)S(1)}, bf16[20,2048]{1,0:T(8,128)(2,1)S(1)}, u32[]{:S(2)}, u32[]{:S(2)}) collective-permute-start(bf16[20,2048]{1,0:T(8,128)(2,1)S(1)} %add_convert_fusion.3), channel_id=1, source_target_pairs={{0,1},{1,0},{2,3},{3,2},{4,5},{5,4},{6,7},{7,6},{8,9},{9,8},{10,11... | collective-permute-start | bytes 245768 | tf_op jit(solution)/shard_map/ppermute | solution.py:324
  189.2 8.7 %collective-permute-start.20 = (bf16[20,2048]{1,0:T(8,128)(2,1)S(1)}, bf16[20,2048]{1,0:T(8,128)(2,1)S(1)}, u32[]{:S(2)}, u32[]{:S(2)}) collective-permute-start(bf16[20,2048]{1,0:T(8,128)(2,1)S(1)} %add_convert_fusion.2), channel_id=1, source_target_pairs={{0,2},{1,3},{2,0},{3,1},{4,6},{5,7},{6,4},{7,5},{8,10},{9,11},{10,... | collective-permute-start | bytes 245768 | tf_op jit(solution)/shard_map/ppermute | solution.py:324
  197.9 18.3 %collective-permute-start.21 = (bf16[20,2048]{1,0:T(8,128)(2,1)S(1)}, bf16[20,2048]{1,0:T(8,128)(2,1)S(1)}, u32[]{:S(2)}, u32[]{:S(2)}) collective-permute-start(bf16[20,2048]{1,0:T(8,128)(2,1)S(1)} %add_convert_fusion.1), channel_id=1, source_target_pairs={{0,4},{1,5},{2,6},{3,7},{4,0},{5,1},{6,2},{7,3},{8,12},{9,13},{10,... | collective-permute-start | bytes 245768 | tf_op jit(solution)/shard_map/ppermute | solution.py:324
  206.6 14.0 %collective-permute-start.15 = (bf16[128,2048]{1,0:T(8,128)(2,1)S(1)}, bf16[128,2048]{1,0:T(8,128)(2,1)S(1)}, u32[]{:S(2)}, u32[]{:S(2)}) collective-permute-start(bf16[128,2048]{1,0:T(8,128)(2,1)S(1)} %fusion.6), channel_id=1, source_target_pairs={{64,0},{128,64},{192,128},{256,192},{320,256},{384,320},{448,384},... | collective-permute-start | bytes 1572872 | tf_op jit(solution)/shard_map/ppermute | solution.py:317
  213.2 9.1 %collective-permute-start.14 = (bf16[128,2048]{1,0:T(8,128)(2,1)S(1)}, bf16[128,2048]{1,0:T(8,128)(2,1)S(1)}, u32[]{:S(2)}, u32[]{:S(2)}) collective-permute-start(bf16[128,2048]{1,0:T(8,128)(2,1)S(1)} %fusion.2), channel_id=1, source_target_pairs={{0,64},{64,128},{128,192},{192,256},{256,320},{320,384},{384,448},... | collective-permute-start | bytes 1572872 | tf_op jit(solution)/shard_map/ppermute | solution.py:317
  (12 other events, 83.0 us)

commit v7 on v6

--- a/solution.py
+++ b/solution.py
@@ -171,14 +171,27 @@
     )(operands[0], *[pltpu.with_memory_space_constraint(o, pltpu.HBM) for o in operands[1:]])
 
 
-def expert_kernel(count, has_acc, final, *refs):
+def slot_weights(notes):
+    notes = notes.astype(F32)
+    lane = lax.broadcasted_iota(jnp.int32, notes.shape, 1).astype(F32)
+    high = jnp.where(lane == notes[:, 2:3], notes[:, 0:1], 0.0)
+    low = jnp.where(lane - LOW_AT == notes[:, 2:3], notes[:, 1:2], 0.0)
+    return jnp.where(lane < LOW_AT, high, low)
+
+
+def slot_sums(weighing, values):
+    both = lax.dot_general(weighing, values, (((0,), (0,)), ((), ())), preferred_element_type=F32)
+    return both[:LOW_AT] + both[LOW_AT : 2 * LOW_AT]
+
+
+def expert_kernel(count, has_acc, slots, final, *refs):
     refs = list(refs)
     x_ref, c_ref = refs.pop(0), refs.pop(0)
     sources = [(refs.pop(0), refs.pop(0)) for _ in range(count)]
     acc_ref = None
     if has_acc:
         acc_ref, _ = refs.pop(0), refs.pop(0)
-    slot_refs = [refs.pop(0) for _ in range(4)] if final else None
+    slot_refs = [refs.pop(0) for _ in range(6)] if slots else None
     out_ref, note_ref = refs.pop(0), refs.pop(0)
     gu_ref, down_ref, sems = refs.pop(0), refs.pop(0), refs.pop(0)
 
@@ -212,6 +225,8 @@
     for number, group in enumerate(fetches):
         for copy in group:
             copy.wait()
+        if slots and number == count - 1:
+            break
         down = jnp.concatenate(
             [down_ref[number, k * deep : (k + 1) * deep, :] for k in range(folds)], axis=1
         )
@@ -248,28 +263,37 @@
                 value = value + source[:, cols]
             out_ref[:, cols] = value.astype(out_ref.dtype)
 
-    if final:
-        gain_ref, slot_in_ref, scale_ref, cot_ref = slot_refs
-        slots = slot_in_ref.shape[0]
-        notes = x_ref[:, width:].astype(F32)
-        lane = lax.broadcasted_iota(jnp.int32, notes.shape, 1).astype(F32)
-        high = jnp.where(lane == notes[:, 2:3], notes[:, 0:1], 0.0)
-        low = jnp.where(lane - LOW_AT == notes[:, 2:3], notes[:, 1:2], 0.0)
-        weighing = jnp.where(lane < LOW_AT, high, low).astype(BF16)
-        both = lax.dot_general(
-            weighing, out_ref[...], (((0,), (0,)), ((), ())), preferred_element_type=F32
+    if slots:
+        gain_ref, slot_in_ref, scale_ref, slot_cot_ref, normed_ref, far_ref = slot_refs
+        number = count - 1
+        down = jnp.concatenate(
+            [down_ref[number, k * deep : (k + 1) * deep, :] for k in range(folds)], axis=1
         )
-        slot_q = (both[:slots] + both[LOW_AT : LOW_AT + slots]) * gain_ref[...]
+        gu_out = jnp.dot(normed_ref[...], gu_ref[number], preferred_element_type=F32)
+        half = gu_out.shape[1] // 2
+        gate, upper = gu_out[:, :half], gu_out[:, half:]
+        hidden_grad = lax.dot_general(far_ref[...], down, contract, preferred_element_type=F32)
+        sig = 1.0 / (1.0 + jnp.exp(-gate))
+        gate_grad = hidden_grad * upper * sig * (1.0 + gate * (1.0 - sig))
+        up_grad = hidden_grad * (gate * sig)
+        grads = jnp.concatenate([gate_grad.astype(BF16), up_grad.astype(BF16)], axis=1)
+        far = lax.dot_general(grads, gu_ref[number], contract, preferred_element_type=F32)
+        weighing = slot_weights(x_ref[:, width:]).astype(BF16)
+        slot_q = (slot_sums(weighing, out_ref[...].astype(BF16)) + far)[:SLOTS] * gain_ref[...]
         slot_in = slot_in_ref[...]
         scale = scale_ref[...]
         inner = jnp.mean(slot_in * slot_q, axis=1, keepdims=True)
-        note_ref[...] = cot_ref[...] + scale * slot_q - slot_in * (scale * scale * scale * inner)
-    else:
+        note_ref[...] = slot_cot_ref[...] + scale * slot_q - slot_in * (scale * scale * scale * inner)
+    elif final:
         note_ref[...] = jnp.zeros_like(note_ref)
-
-
-def expert_step(rows, cots, shards, before=None, slot_data=None):
-    final = slot_data is not None
+    elif not has_acc:
+        weighing = slot_weights(x_ref[:, width:]).reshape(blocks, ROWS, EXTRA)[:, :COT_ROWS]
+        weighing = weighing.reshape(blocks * COT_ROWS, EXTRA).astype(BF16)
+        note_ref[...] = slot_sums(weighing, c_ref[...]).astype(note_ref.dtype)
+
+
+def expert_step(rows, cots, shards, before=None, slot_data=(), final=False):
+    slots = bool(slot_data)
     operands = [rows, cots]
     for pair in shards:
         operands += [pltpu.with_memory_space_constraint(part, pltpu.HBM) for part in pair]
@@ -278,9 +302,8 @@
     if before is not None:
         operands += list(before)
         specs += [near, near]
-    if final:
-        operands += list(slot_data)
-        specs += [near] * len(slot_data)
+    operands += list(slot_data)
+    specs += [near] * len(slot_data)
     shape = (rows.shape[0], cots.shape[1])
     lanes = shards[0][0].shape[1]
     deep = shards[0][0].shape[0] + shards[0][1].shape[0] - shape[1]
@@ -290,10 +313,15 @@
         transcendentals=hidden * 2 * cots.shape[0],
         bytes_accessed=sum(o.size * o.dtype.itemsize for o in operands) + 4 * shape[0] * shape[1],
     )
-    note = (SLOTS if final else 8, shape[1] if final else 128)
+    if slots:
+        note = jax.ShapeDtypeStruct((SLOTS, shape[1]), F32)
+    elif final:
+        note = jax.ShapeDtypeStruct((8, 128), F32)
+    else:
+        note = jax.ShapeDtypeStruct((LOW_AT, shape[1]), BF16)
     return pl.pallas_call(
-        functools.partial(expert_kernel, len(shards), before is not None, final),
-        out_shape=(jax.ShapeDtypeStruct(shape, BF16 if final else F32), jax.ShapeDtypeStruct(note, F32)),
+        functools.partial(expert_kernel, len(shards), before is not None, slots, final),
+        out_shape=(jax.ShapeDtypeStruct(shape, BF16 if final else F32), note),
         in_specs=specs,
         out_specs=(near, near),
         scratch_shapes=[
@@ -398,14 +426,16 @@
     slot_scale = lax.rsqrt(jnp.mean(slot_in * slot_in, axis=1, keepdims=True) + EPS)
     selector = (slot == jnp.arange(SLOTS, dtype=F32)[None, :]).astype(BF16)
     slot_cot = jnp.dot(jnp.transpose(selector), cotangent, preferred_element_type=F32)
-    slot_data = (norm_gain, slot_in, slot_scale, slot_cot)
+    slot_normed = jnp.pad((slot_in * slot_scale * norm_gain).astype(BF16), ((0, LOW_AT - SLOTS), (0, 0)))
 
     early = [(own_front, own_rest)] + shards(1) + shards(2)
     acc, note = expert_step(rows, cots, early)
+    far_sums = rotated(note, "split", lax.axis_size("split") // 2)
     note = held_back(rest_ring, note)
     last = (rotated(front_ring[-1][0], "split", 1), rotated(rest_ring[-1][1], "split", -1))
-    before = expert_step(rows, cots, shards(3), (acc, note))
-    partial, local_sums = expert_step(rows, cots, [last], before, slot_data)
+    slot_data = (norm_gain, slot_in, slot_scale, slot_cot, slot_normed, far_sums)
+    acc, local_sums = expert_step(rows, cots, shards(3) + [(own_front, own_rest)], (acc, note), slot_data)
+    partial, _ = expert_step(rows, cots, [last], (acc, local_sums), final=True)
 
     returned = lax.all_to_all(
         partial.reshape(EXPERTS, ROWS, width), "column", split_axis=0, concat_axis=0, tiled=True

time: 226 us -> 240 us (1.062)
  starting transfers between devices: 91.8 us -> 103 us
    ppermute x14 -> x15, starting transfers between devices: 38.7 us -> 44.9 us  [rotated(): lax.ppermute(value, axis, [(i, (i + distance) % size) for i in range(size)])]
    ppermute x6, starting transfers between devices: 26.9 us -> 31.2 us  [summed(): lax.ppermute(value.astype(BF16), axis, [(i, i ^ distance) for i in range(...]
    ppermute x14 -> x15, waiting for transfers between devices: 68.6 us -> 68 us  [rotated(): lax.ppermute(value, axis, [(i, (i + distance) % size) for i in range(size)])]
    unnamed x45 -> x35, local copies, waits for them, and re-layouts: 8.91 us -> 8.84 us
  transfers between devices with their start and end apart: 24 -> 25, of which waited for: 14 -> 13; matrix products, arithmetic and copies ran while one was open for 3% -> 3% of each run, Pallas kernels for 6% -> 8%
where the time goes in v7:
time: 240 us; the launch traced here: 239 us
  starting transfers between devices  103 us (43%)
  waiting for transfers between devices  94.1 us (39%)
  Pallas kernels  24.6 us (10%)
  local copies, waits for them, and re-layouts  12.4 us (5%)
  matrix products  2.44 us (1%)
    ppermute x15, waiting for transfers between devices, rotated(): lax.ppermute(value, axis, [(i, (i + distance) % size) for i in range(size)])  68 us
    ppermute x15, starting transfers between devices, rotated(): lax.ppermute(value, axis, [(i, (i + distance) % size) for i in range(size)])  44.9 us
    ppermute x6, starting transfers between devices, summed(): lax.ppermute(value.astype(BF16), axis, [(i, i ^ distance) for i in range(...  31.2 us
    ppermute x6, waiting for transfers between devices, summed(): lax.ppermute(value.astype(BF16), axis, [(i, i ^ distance) for i in range(...  20.8 us
    pallas_call x3, Pallas kernels, expert_step(): pl.pallas_call(functools.partial(expert_kernel, len(shards), before is no...  18.8 us
    all_to_all x1, starting transfers between devices, on_device(): lax.all_to_all(packed, 'column', split_axis=0, concat_axis=0, tiled=True)  10.9 us
    ppermute x2, starting transfers between devices, shifted(): return lax.ppermute(block, axis, route)  9.83 us
    unnamed x35, local copies, waits for them, and re-layouts  8.84 us
  transfers between devices with their start and end apart: 25, of which 13 were waited for; matrix products, arithmetic and copies ran while one was open for 3% of the time, Pallas kernels for 8%

profile of v7, /device:TPU:1, one launch (start us, length us, event | category | flops | bytes accessed | tf_op | source)
XLA Modules:
  0.0 238.6 jit_solution(17509768655725738287)
XLA Ops:
  2.3 5.8 %shard_map.175 = (bf16[512,2176]{1,0:T(8,128)(2,1)}, bf16[128,2048]{1,0:T(8,128)(2,1)S(1)}, bf16[128,2048]{1,0:T(8,128)(2,1)S(1)}, f32[128,128]{1,0:T(8,128)S(1)...) custom-call(s32[1,1]{1,0:T(1,128)} %bitcast.first_ref, s32[1,16]{1,0:T(1,128)} %refs_0_.1, ...), custom_call_target="tpu_custom_call" | custom-call | tf_op jit(solution)/shard_map/pallas_call | solution.py:155
  8.9 10.9 %all-to-all-start = ((bf16[8,64,2176]{2,1,0:T(8,128)(2,1)}), bf16[8,64,2176]{2,1,0:T(8,128)(2,1)}, u32[]{:S(2)}, u32[]{:S(2)}) async-start(bf16[8,64,2176]{2,1,0:T(8,128)(2,1)} %bitcast.11), calls=%async_computation | async-start | bytes 4456448 | tf_op jit(solution)/shard_map/all_to_all | solution.py:421
  19.8 3.2 %collective-permute-start = (bf16[1536,256]{1,0:T(8,128)(2,1)S(1)}, bf16[1536,256]{1,0:T(8,128)(2,1)S(1)}, u32[]{:S(2)}, u32[]{:S(2)}) collective-permute-start(bf16[1536,256]{1,0:T(8,128)(2,1)S(1)} %get-tuple-element.20.refs_2_.refs_6_), channel_id=1, source_target_pairs={{0,8},{8,16},{16,24},{24,32},{32,40},{40,48},{48,56},{56,0},{1,9},... | collective-permute-start | bytes 2359304 | tf_op jit(solution)/shard_map/ppermute | solution.py:339
  23.0 3.2 %collective-permute-start.4 = (bf16[1536,256]{1,0:T(8,128)(2,1)S(1)}, bf16[1536,256]{1,0:T(8,128)(2,1)S(1)}, u32[]{:S(2)}, u32[]{:S(2)}) collective-permute-start(bf16[1536,256]{1,0:T(8,128)(2,1)S(1)} %get-tuple-element.21.refs_3_.refs_7_), channel_id=1, source_target_pairs={{0,8},{8,16},{16,24},{24,32},{32,40},{40,48},{48,56},{56,0},{1,9},... | collective-permute-start | bytes 2359304 | tf_op jit(solution)/shard_map/ppermute | solution.py:339
  26.2 3.3 %collective-permute-start.7 = (bf16[1536,256]{1,0:T(8,128)(2,1)S(1)}, bf16[1536,256]{1,0:T(8,128)(2,1)S(1)}, u32[]{:S(2)}, u32[]{:S(2)}) collective-permute-start(bf16[1536,256]{1,0:T(8,128)(2,1)S(1)} %get-tuple-element.21.refs_3_.refs_7_), channel_id=1, source_target_pairs={{0,56},{8,0},{16,8},{24,16},{32,24},{40,32},{48,40},{56,48},{1,57}... | collective-permute-start | bytes 2359304 | tf_op jit(solution)/shard_map/ppermute | solution.py:339
  29.5 2.6 %collective-permute-start.10 = (bf16[1536,256]{1,0:T(8,128)(2,1)S(1)}, bf16[1536,256]{1,0:T(8,128)(2,1)}, u32[]{:S(2)}, u32[]{:S(2)}) collective-permute-start(bf16[1536,256]{1,0:T(8,128)(2,1)S(1)} %get-tuple-element.20.refs_2_.refs_6_), channel_id=1, source_target_pairs={{0,56},{8,0},{16,8},{24,16},{32,24},{40,32},{48,40},{56,48},{1,57}... | collective-permute-start | bytes 2359304 | tf_op jit(solution)/shard_map/ppermute | solution.py:339
  32.1 9.8 %collective-permute-done.refs_4_ = bf16[1536,256]{1,0:T(8,128)(2,1)S(1)} collective-permute-done((bf16[1536,256]{1,0:T(8,128)(2,1)S(1)}, bf16[1536,256]{1,0:T(8,128)(2,1)S(1)}, u32[]{:S(2)}, u32[]{:S(2)}) %collective-permute-start) | collective-permute-done | bytes 786464 | tf_op jit(solution)/shard_map/ppermute | solution.py:339
  43.8 14.9 %collective-permute-done.4.refs_5_ = bf16[1536,256]{1,0:T(8,128)(2,1)S(1)} collective-permute-done((bf16[1536,256]{1,0:T(8,128)(2,1)S(1)}, bf16[1536,256]{1,0:T(8,128)(2,1)S(1)}, u32[]{:S(2)}, u32[]{:S(2)}) %collective-permute-start.4) | collective-permute-done | bytes 786464 | tf_op jit(solution)/shard_map/ppermute | solution.py:339
  60.7 4.6 %collective-permute-start.8 = (bf16[1536,256]{1,0:T(8,128)(2,1)S(1)}, bf16[1536,256]{1,0:T(8,128)(2,1)}, u32[]{:S(2)}, u32[]{:S(2)}) collective-permute-start(bf16[1536,256]{1,0:T(8,128)(2,1)S(1)} %collective-permute-done.7.refs_7_), channel_id=1, source_target_pairs={{0,56},{8,0},{16,8},{24,16},{32,24},{40,32},{48,40},{56,48},{1,57}... | collective-permute-start | bytes 2359304 | tf_op jit(solution)/shard_map/ppermute | solution.py:339
  67.2 8.4 %collective-permute-done.1.refs_8_ = bf16[1536,256]{1,0:T(8,128)(2,1)} collective-permute-done((bf16[1536,256]{1,0:T(8,128)(2,1)S(1)}, bf16[1536,256]{1,0:T(8,128)(2,1)}, u32[]{:S(2)}, u32[]{:S(2)}) %collective-permute-start.1) | collective-permute-done | bytes 786464 | tf_op jit(solution)/shard_map/ppermute | solution.py:339
  77.5 14.9 %collective-permute-done.5.refs_9_ = bf16[1536,256]{1,0:T(8,128)(2,1)} collective-permute-done((bf16[1536,256]{1,0:T(8,128)(2,1)S(1)}, bf16[1536,256]{1,0:T(8,128)(2,1)}, u32[]{:S(2)}, u32[]{:S(2)}) %collective-permute-start.5) | collective-permute-done | bytes 786464 | tf_op jit(solution)/shard_map/ppermute | solution.py:339
  94.4 4.6 %collective-permute-start.9 = (bf16[1536,256]{1,0:T(8,128)(2,1)}, bf16[1536,256]{1,0:T(8,128)(2,1)}, u32[]{:S(2)}, u32[]{:S(2)}) collective-permute-start(bf16[1536,256]{1,0:T(8,128)(2,1)} %collective-permute-done.8.refs_11_), channel_id=1, source_target_pairs={{0,56},{8,0},{16,8},{24,16},{32,24},{40,32},{48,40},{56,48},{1,57}... | collective-permute-start | bytes 2359304 | tf_op jit(solution)/shard_map/ppermute | solution.py:339
  101.5 7.8 %collective-permute-done.2.refs_2_ = bf16[1536,256]{1,0:T(8,128)(2,1)} collective-permute-done((bf16[1536,256]{1,0:T(8,128)(2,1)}, bf16[1536,256]{1,0:T(8,128)(2,1)}, u32[]{:S(2)}, u32[]{:S(2)}) %collective-permute-start.2) | collective-permute-done | bytes 786464 | tf_op jit(solution)/shard_map/ppermute | solution.py:339
  113.9 9.3 %shard_map.176 = (f32[320,2048]{1,0:T(8,128)S(1)}, bf16[32,2048]{1,0:T(8,128)(2,1)S(1)}) custom-call(bf16[320,2176]{1,0:T(8,128)(2,1)S(1)} %bitcast.25, bf16[192,2048]{1,0:T(8,128)(2,1)S(1)} %bitcast.28, bf16[1536,256]{1,0:T(8,128)(2,1)} %copy-done.3, bf16[1536,256]{1,0:T(8,128)(2,1)} %copy-done.4, bf16[1536,256]{1,0:T(8,128)(2,1)} %copy-done.12, ...), custom_call_target="tpu_custom_call" | custom-call | flops 3690987520 | bytes 12664832 | tf_op jit(solution)/shard_map/pallas_call | solution.py:322
  126.2 3.1 %collective-permute-start.12 = (bf16[1536,256]{1,0:T(8,128)(2,1)}, bf16[1536,256]{1,0:T(8,128)(2,1)}, u32[]{:S(2)}, u32[]{:S(2)}) collective-permute-start(bf16[1536,256]{1,0:T(8,128)(2,1)} %collective-permute-done.9.refs_5_), channel_id=1, source_target_pairs={{0,56},{8,0},{16,8},{24,16},{32,24},{40,32},{48,40},{56,48},{1,57}... | collective-permute-start | bytes 2359304 | tf_op jit(solution)/shard_map/ppermute | solution.py:339
  129.8 6.8 %collective-permute-start.14 = (bf16[32,2048]{1,0:T(8,128)(2,1)S(1)}, bf16[32,2048]{1,0:T(8,128)(2,1)S(1)}, u32[]{:S(2)}, u32[]{:S(2)}) collective-permute-start(bf16[32,2048]{1,0:T(8,128)(2,1)S(1)} %get-tuple-element.26.refs_9_), channel_id=1, source_target_pairs={{0,32},{8,40},{16,48},{24,56},{32,0},{40,8},{48,16},{56,24},{1,33}... | collective-permute-start | bytes 393224 | tf_op jit(solution)/shard_map/ppermute | solution.py:339
  137.9 10.6 %collective-permute-done.14.refs_15_ = bf16[32,2048]{1,0:T(8,128)(2,1)S(1)} collective-permute-done((bf16[32,2048]{1,0:T(8,128)(2,1)S(1)}, bf16[32,2048]{1,0:T(8,128)(2,1)S(1)}, u32[]{:S(2)}, u32[]{:S(2)}) %collective-permute-start.14) | collective-permute-done | bytes 131104 | tf_op jit(solution)/shard_map/ppermute | solution.py:339
  150.3 6.1 %shard_map.177 = (f32[320,2048]{1,0:T(8,128)S(1)}, f32[20,2048]{1,0:T(8,128)S(1)}) custom-call(bf16[320,2176]{1,0:T(8,128)(2,1)S(1)} %bitcast.26, bf16[192,2048]{1,0:T(8,128)(2,1)S(1)} %bitcast.29, bf16[1536,256]{1,0:T(8,128)(2,1)} %collective-permute-done.2.refs_2_, bf16[1536,256]{1,0:T(8,128)(2,1)} %collective-permute-done.6.refs_3_, ...), custom_call_target="tpu_custom_call" | custom-call | flops 2214592512 | bytes 12869712 | tf_op jit(solution)/shard_map/pallas_call | solution.py:322
  156.4 9.9 %collective-permute-start.17 = (bf16[20,2048]{1,0:T(8,128)(2,1)S(1)}, bf16[20,2048]{1,0:T(8,128)(2,1)S(1)}, u32[]{:S(2)}, u32[]{:S(2)}) collective-permute-start(bf16[20,2048]{1,0:T(8,128)(2,1)S(1)} %convert_element_type.110), channel_id=1, source_target_pairs={{0,8},{8,0},{16,24},{24,16},{32,40},{40,32},{48,56},{56,48},{1,9},... | collective-permute-start | bytes 245768 | tf_op jit(solution)/shard_map/ppermute | solution.py:352
  166.3 3.4 %shard_map.178 = (bf16[320,2048]{1,0:T(8,128)(2,1)S(1)}, f32[8,128]{1,0:T(8,128)}) custom-call(bf16[320,2176]{1,0:T(8,128)(2,1)S(1)} %bitcast.27, bf16[192,2048]{1,0:T(8,128)(2,1)S(1)} %bitcast.30, bf16[1536,256]{1,0:T(8,128)(2,1)} %collective-permute-done.3.refs_2_, bf16[1536,256]{1,0:T(8,128)(2,1)} %collective-permute-done.12.refs_3_, ...), custom_call_target="tpu_custom_call" | custom-call | flops 738197504 | bytes 9158656 | tf_op jit(solution)/shard_map/pallas_call | solution.py:322
  170.8 5.8 %all-to-all-start.1 = ((bf16[8,40,2048]{2,1,0:T(8,128)(2,1)}), bf16[8,40,2048]{2,1,0:T(8,128)(2,1)S(1)}, u32[]{:S(2)}, u32[]{:S(2)}) async-start(bf16[8,40,2048]{2,1,0:T(8,128)(2,1)} %bitcast.31), calls=%async_computation.1 | async-start | bytes 2621440 | tf_op jit(solution)/shard_map/all_to_all | solution.py:440
  178.6 5.1 %collective-permute-done.18 = bf16[20,2048]{1,0:T(8,128)(2,1)S(1)} collective-permute-done((bf16[20,2048]{1,0:T(8,128)(2,1)S(1)}, bf16[20,2048]{1,0:T(8,128)(2,1)S(1)}, u32[]{:S(2)}, u32[]{:S(2)}) %collective-permute-start.18) | collective-permute-done | bytes 81952 | tf_op jit(solution)/shard_map/ppermute | solution.py:352
  183.7 2.4 %collective-permute-start.19 = (bf16[20,2048]{1,0:T(8,128)(2,1)S(1)}, bf16[20,2048]{1,0:T(8,128)(2,1)S(1)}, u32[]{:S(2)}, u32[]{:S(2)}) collective-permute-start(bf16[20,2048]{1,0:T(8,128)(2,1)S(1)} %add_convert_fusion.4), channel_id=1, source_target_pairs={{0,32},{8,40},{16,48},{24,56},{32,0},{40,8},{48,16},{56,24},{1,33}... | collective-permute-start | bytes 245768 | tf_op jit(solution)/shard_map/ppermute | solution.py:352
  186.2 7.2 %collective-permute-done.19 = bf16[20,2048]{1,0:T(8,128)(2,1)S(1)} collective-permute-done((bf16[20,2048]{1,0:T(8,128)(2,1)S(1)}, bf16[20,2048]{1,0:T(8,128)(2,1)S(1)}, u32[]{:S(2)}, u32[]{:S(2)}) %collective-permute-start.19) | collective-permute-done | bytes 81952 | tf_op jit(solution)/shard_map/ppermute | solution.py:352
  193.4 3.4 %collective-permute-start.20 = (bf16[20,2048]{1,0:T(8,128)(2,1)S(1)}, bf16[20,2048]{1,0:T(8,128)(2,1)S(1)}, u32[]{:S(2)}, u32[]{:S(2)}) collective-permute-start(bf16[20,2048]{1,0:T(8,128)(2,1)S(1)} %add_convert_fusion.3), channel_id=1, source_target_pairs={{0,1},{1,0},{2,3},{3,2},{4,5},{5,4},{6,7},{7,6},{8,9},{9,8},{10,11... | collective-permute-start | bytes 245768 | tf_op jit(solution)/shard_map/ppermute | solution.py:352
  196.8 5.4 %collective-permute-done.20 = bf16[20,2048]{1,0:T(8,128)(2,1)S(1)} collective-permute-done((bf16[20,2048]{1,0:T(8,128)(2,1)S(1)}, bf16[20,2048]{1,0:T(8,128)(2,1)S(1)}, u32[]{:S(2)}, u32[]{:S(2)}) %collective-permute-start.20) | collective-permute-done | bytes 81952 | tf_op jit(solution)/shard_map/ppermute | solution.py:352
  202.2 4.7 %collective-permute-start.21 = (bf16[20,2048]{1,0:T(8,128)(2,1)S(1)}, bf16[20,2048]{1,0:T(8,128)(2,1)S(1)}, u32[]{:S(2)}, u32[]{:S(2)}) collective-permute-start(bf16[20,2048]{1,0:T(8,128)(2,1)S(1)} %add_convert_fusion.2), channel_id=1, source_target_pairs={{0,2},{1,3},{2,0},{3,1},{4,6},{5,7},{6,4},{7,5},{8,10},{9,11},{10,... | collective-permute-start | bytes 245768 | tf_op jit(solution)/shard_map/ppermute | solution.py:352
  207.0 3.1 %collective-permute-done.21 = bf16[20,2048]{1,0:T(8,128)(2,1)S(1)} collective-permute-done((bf16[20,2048]{1,0:T(8,128)(2,1)S(1)}, bf16[20,2048]{1,0:T(8,128)(2,1)S(1)}, u32[]{:S(2)}, u32[]{:S(2)}) %collective-permute-start.21) | collective-permute-done | bytes 81952 | tf_op jit(solution)/shard_map/ppermute | solution.py:352
  210.2 8.9 %collective-permute-start.22 = (bf16[20,2048]{1,0:T(8,128)(2,1)S(1)}, bf16[20,2048]{1,0:T(8,128)(2,1)S(1)}, u32[]{:S(2)}, u32[]{:S(2)}) collective-permute-start(bf16[20,2048]{1,0:T(8,128)(2,1)S(1)} %add_convert_fusion.1), channel_id=1, source_target_pairs={{0,4},{1,5},{2,6},{3,7},{4,0},{5,1},{6,2},{7,3},{8,12},{9,13},{10,... | collective-permute-start | bytes 245768 | tf_op jit(solution)/shard_map/ppermute | solution.py:352
  220.5 6.8 %collective-permute-start.16 = (bf16[128,2048]{1,0:T(8,128)(2,1)S(1)}, bf16[128,2048]{1,0:T(8,128)(2,1)S(1)}, u32[]{:S(2)}, u32[]{:S(2)}) collective-permute-start(bf16[128,2048]{1,0:T(8,128)(2,1)S(1)} %fusion.6), channel_id=1, source_target_pairs={{64,0},{128,64},{192,128},{256,192},{320,256},{384,320},{448,384},... | collective-permute-start | bytes 1572872 | tf_op jit(solution)/shard_map/ppermute | solution.py:345
  227.9 3.0 %collective-permute-start.15 = (bf16[128,2048]{1,0:T(8,128)(2,1)S(1)}, bf16[128,2048]{1,0:T(8,128)(2,1)S(1)}, u32[]{:S(2)}, u32[]{:S(2)}) collective-permute-start(bf16[128,2048]{1,0:T(8,128)(2,1)S(1)} %fusion.2), channel_id=1, source_target_pairs={{0,64},{64,128},{128,192},{192,256},{256,320},{320,384},{384,448},... | collective-permute-start | bytes 1572872 | tf_op jit(solution)/shard_map/ppermute | solution.py:345
  231.7 3.6 %collective-permute-done.16 = bf16[128,2048]{1,0:T(8,128)(2,1)S(1)} collective-permute-done((bf16[128,2048]{1,0:T(8,128)(2,1)S(1)}, bf16[128,2048]{1,0:T(8,128)(2,1)S(1)}, u32[]{:S(2)}, u32[]{:S(2)}) %collective-permute-start.16) | collective-permute-done | bytes 524320 | tf_op jit(solution)/shard_map/ppermute | solution.py:345
  (84 shorter events, 34.7 us)
Async XLA Ops:
  8.1 18.1 %copy-start.4 = (bf16[1536,256]{1,0:T(8,128)(2,1)}, bf16[1536,256]{1,0:T(8,128)(2,1)S(1)}, u32[]{:S(2)}) copy-start(bf16[1536,256]{1,0:T(8,128)(2,1)S(1)} %get-tuple-element.21.refs_3_.refs_7_) | copy-start | bytes 2359300
  8.1 21.4 %copy-start.3 = (bf16[1536,256]{1,0:T(8,128)(2,1)}, bf16[1536,256]{1,0:T(8,128)(2,1)S(1)}, u32[]{:S(2)}) copy-start(bf16[1536,256]{1,0:T(8,128)(2,1)S(1)} %get-tuple-element.20.refs_2_.refs_6_) | copy-start | bytes 2359300
  8.1 90.9 %copy-start.9 = (bf16[1,2,10,2048]{3,1,2,0:T(2,128)(2,1)S(1)}, bf16[1,2,10,2048]{3,1,2,0:T(2,128)(2,1)}, u32[]{:S(2)}) copy-start(bf16[1,2,10,2048]{3,1,2,0:T(2,128)(2,1)} %param.27) | copy-start | bytes 245764
  8.9 102.3 %all-to-all-start = ((bf16[8,64,2176]{2,1,0:T(8,128)(2,1)}), bf16[8,64,2176]{2,1,0:T(8,128)(2,1)}, u32[]{:S(2)}, u32[]{:S(2)}) async-start(bf16[8,64,2176]{2,1,0:T(8,128)(2,1)} %bitcast.11), calls=%async_computation | async-start | bytes 4456448 | tf_op jit(solution)/shard_map/all_to_all | solution.py:421
  19.8 22.1 %collective-permute-start = (bf16[1536,256]{1,0:T(8,128)(2,1)S(1)}, bf16[1536,256]{1,0:T(8,128)(2,1)S(1)}, u32[]{:S(2)}, u32[]{:S(2)}) collective-permute-start(bf16[1536,256]{1,0:T(8,128)(2,1)S(1)} %get-tuple-element.20.refs_2_.refs_6_), channel_id=1, source_target_pairs={{0,8},{8,16},{16,24},{24,32},{32,40},{40,48},{48,56},{56,0},{1,9},... | collective-permute-start | bytes 2359304 | tf_op jit(solution)/shard_map/ppermute | solution.py:339
  23.0 35.8 %collective-permute-start.4 = (bf16[1536,256]{1,0:T(8,128)(2,1)S(1)}, bf16[1536,256]{1,0:T(8,128)(2,1)S(1)}, u32[]{:S(2)}, u32[]{:S(2)}) collective-permute-start(bf16[1536,256]{1,0:T(8,128)(2,1)S(1)} %get-tuple-element.21.refs_3_.refs_7_), channel_id=1, source_target_pairs={{0,8},{8,16},{16,24},{24,32},{32,40},{40,48},{48,56},{56,0},{1,9},... | collective-permute-start | bytes 2359304 | tf_op jit(solution)/shard_map/ppermute | solution.py:339
  26.2 34.5 %collective-permute-start.7 = (bf16[1536,256]{1,0:T(8,128)(2,1)S(1)}, bf16[1536,256]{1,0:T(8,128)(2,1)S(1)}, u32[]{:S(2)}, u32[]{:S(2)}) collective-permute-start(bf16[1536,256]{1,0:T(8,128)(2,1)S(1)} %get-tuple-element.21.refs_3_.refs_7_), channel_id=1, source_target_pairs={{0,56},{8,0},{16,8},{24,16},{32,24},{40,32},{48,40},{56,48},{1,57}... | collective-permute-start | bytes 2359304 | tf_op jit(solution)/shard_map/ppermute | solution.py:339
  29.5 35.8 %collective-permute-start.10 = (bf16[1536,256]{1,0:T(8,128)(2,1)S(1)}, bf16[1536,256]{1,0:T(8,128)(2,1)}, u32[]{:S(2)}, u32[]{:S(2)}) collective-permute-start(bf16[1536,256]{1,0:T(8,128)(2,1)S(1)} %get-tuple-element.20.refs_2_.refs_6_), channel_id=1, source_target_pairs={{0,56},{8,0},{16,8},{24,16},{32,24},{40,32},{48,40},{56,48},{1,57}... | collective-permute-start | bytes 2359304 | tf_op jit(solution)/shard_map/ppermute | solution.py:339
  41.9 52.5 %copy-start.12 = (bf16[1536,256]{1,0:T(8,128)(2,1)}, bf16[1536,256]{1,0:T(8,128)(2,1)S(1)}, u32[]{:S(2)}) copy-start(bf16[1536,256]{1,0:T(8,128)(2,1)S(1)} %collective-permute-done.refs_4_) | copy-start | bytes 2359300
  41.9 33.7 %collective-permute-start.1 = (bf16[1536,256]{1,0:T(8,128)(2,1)S(1)}, bf16[1536,256]{1,0:T(8,128)(2,1)}, u32[]{:S(2)}, u32[]{:S(2)}) collective-permute-start(bf16[1536,256]{1,0:T(8,128)(2,1)S(1)} %collective-permute-done.refs_4_), channel_id=1, source_target_pairs={{0,8},{8,16},{16,24},{24,32},{32,40},{40,48},{48,56},{56,0},{1,9},... | collective-permute-start | bytes 2359304 | tf_op jit(solution)/shard_map/ppermute | solution.py:339
  58.8 35.6 %copy-start.13 = (bf16[1536,256]{1,0:T(8,128)(2,1)}, bf16[1536,256]{1,0:T(8,128)(2,1)S(1)}, u32[]{:S(2)}) copy-start(bf16[1536,256]{1,0:T(8,128)(2,1)S(1)} %collective-permute-done.4.refs_5_) | copy-start | bytes 2359300
  58.8 33.7 %collective-permute-start.5 = (bf16[1536,256]{1,0:T(8,128)(2,1)S(1)}, bf16[1536,256]{1,0:T(8,128)(2,1)}, u32[]{:S(2)}, u32[]{:S(2)}) collective-permute-start(bf16[1536,256]{1,0:T(8,128)(2,1)S(1)} %collective-permute-done.4.refs_5_), channel_id=1, source_target_pairs={{0,8},{8,16},{16,24},{24,32},{32,40},{40,48},{48,56},{56,0},{1,9},... | collective-permute-start | bytes 2359304 | tf_op jit(solution)/shard_map/ppermute | solution.py:339
  60.7 33.7 %copy-start.14 = (bf16[1536,256]{1,0:T(8,128)(2,1)}, bf16[1536,256]{1,0:T(8,128)(2,1)S(1)}, u32[]{:S(2)}) copy-start(bf16[1536,256]{1,0:T(8,128)(2,1)S(1)} %collective-permute-done.7.refs_7_) | copy-start | bytes 2359300
  60.7 33.7 %collective-permute-start.8 = (bf16[1536,256]{1,0:T(8,128)(2,1)S(1)}, bf16[1536,256]{1,0:T(8,128)(2,1)}, u32[]{:S(2)}, u32[]{:S(2)}) collective-permute-start(bf16[1536,256]{1,0:T(8,128)(2,1)S(1)} %collective-permute-done.7.refs_7_), channel_id=1, source_target_pairs={{0,56},{8,0},{16,8},{24,16},{32,24},{40,32},{48,40},{56,48},{1,57}... | collective-permute-start | bytes 2359304 | tf_op jit(solution)/shard_map/ppermute | solution.py:339
  65.3 34.1 %collective-permute-start.11 = (bf16[1536,256]{1,0:T(8,128)(2,1)}, bf16[1536,256]{1,0:T(8,128)(2,1)}, u32[]{:S(2)}, u32[]{:S(2)}) collective-permute-start(bf16[1536,256]{1,0:T(8,128)(2,1)} %collective-permute-done.10.refs_6_), channel_id=1, source_target_pairs={{0,56},{8,0},{16,8},{24,16},{32,24},{40,32},{48,40},{56,48},{1,57}... | collective-permute-start | bytes 2359304 | tf_op jit(solution)/shard_map/ppermute | solution.py:339
  75.6 33.7 %collective-permute-start.2 = (bf16[1536,256]{1,0:T(8,128)(2,1)}, bf16[1536,256]{1,0:T(8,128)(2,1)}, u32[]{:S(2)}, u32[]{:S(2)}) collective-permute-start(bf16[1536,256]{1,0:T(8,128)(2,1)} %collective-permute-done.1.refs_8_), channel_id=1, source_target_pairs={{0,8},{8,16},{16,24},{24,32},{32,40},{40,48},{48,56},{56,0},{1,9},... | collective-permute-start | bytes 2359304 | tf_op jit(solution)/shard_map/ppermute | solution.py:339
  92.5 33.7 %collective-permute-start.6 = (bf16[1536,256]{1,0:T(8,128)(2,1)}, bf16[1536,256]{1,0:T(8,128)(2,1)}, u32[]{:S(2)}, u32[]{:S(2)}) collective-permute-start(bf16[1536,256]{1,0:T(8,128)(2,1)} %collective-permute-done.5.refs_9_), channel_id=1, source_target_pairs={{0,8},{8,16},{16,24},{24,32},{32,40},{40,48},{48,56},{56,0},{1,9},... | collective-permute-start | bytes 2359304 | tf_op jit(solution)/shard_map/ppermute | solution.py:339
  94.4 31.8 %collective-permute-start.9 = (bf16[1536,256]{1,0:T(8,128)(2,1)}, bf16[1536,256]{1,0:T(8,128)(2,1)}, u32[]{:S(2)}, u32[]{:S(2)}) collective-permute-start(bf16[1536,256]{1,0:T(8,128)(2,1)} %collective-permute-done.8.refs_11_), channel_id=1, source_target_pairs={{0,56},{8,0},{16,8},{24,16},{32,24},{40,32},{48,40},{56,48},{1,57}... | collective-permute-start | bytes 2359304 | tf_op jit(solution)/shard_map/ppermute | solution.py:339
  99.4 38.5 %collective-permute-start.13 = (bf16[1536,256]{1,0:T(8,128)(2,1)}, bf16[1536,256]{1,0:T(8,128)(2,1)}, u32[]{:S(2)}, u32[]{:S(2)}) collective-permute-start(bf16[1536,256]{1,0:T(8,128)(2,1)} %collective-permute-done.11.refs_10_), channel_id=1, source_target_pairs={{0,56},{8,0},{16,8},{24,16},{32,24},{40,32},{48,40},{56,48},{1,57}... | collective-permute-start | bytes 2359304 | tf_op jit(solution)/shard_map/ppermute | solution.py:339
  109.3 57.0 %collective-permute-start.3 = (bf16[1536,256]{1,0:T(8,128)(2,1)}, bf16[1536,256]{1,0:T(8,128)(2,1)}, u32[]{:S(2)}, u32[]{:S(2)}) collective-permute-start(bf16[1536,256]{1,0:T(8,128)(2,1)} %collective-permute-done.2.refs_2_), channel_id=1, source_target_pairs={{0,8},{8,16},{16,24},{24,32},{32,40},{40,48},{48,56},{56,0},{1,9},... | collective-permute-start | bytes 2359304 | tf_op jit(solution)/shard_map/ppermute | solution.py:339
  126.2 40.1 %collective-permute-start.12 = (bf16[1536,256]{1,0:T(8,128)(2,1)}, bf16[1536,256]{1,0:T(8,128)(2,1)}, u32[]{:S(2)}, u32[]{:S(2)}) collective-permute-start(bf16[1536,256]{1,0:T(8,128)(2,1)} %collective-permute-done.9.refs_5_), channel_id=1, source_target_pairs={{0,56},{8,0},{16,8},{24,16},{32,24},{40,32},{48,40},{56,48},{1,57}... | collective-permute-start | bytes 2359304 | tf_op jit(solution)/shard_map/ppermute | solution.py:339
  129.8 18.8 %collective-permute-start.14 = (bf16[32,2048]{1,0:T(8,128)(2,1)S(1)}, bf16[32,2048]{1,0:T(8,128)(2,1)S(1)}, u32[]{:S(2)}, u32[]{:S(2)}) collective-permute-start(bf16[32,2048]{1,0:T(8,128)(2,1)S(1)} %get-tuple-element.26.refs_9_), channel_id=1, source_target_pairs={{0,32},{8,40},{16,48},{24,56},{32,0},{40,8},{48,16},{56,24},{1,33}... | collective-permute-start | bytes 393224 | tf_op jit(solution)/shard_map/ppermute | solution.py:339
  156.4 20.2 %collective-permute-start.17 = (bf16[20,2048]{1,0:T(8,128)(2,1)S(1)}, bf16[20,2048]{1,0:T(8,128)(2,1)S(1)}, u32[]{:S(2)}, u32[]{:S(2)}) collective-permute-start(bf16[20,2048]{1,0:T(8,128)(2,1)S(1)} %convert_element_type.110), channel_id=1, source_target_pairs={{0,8},{8,0},{16,24},{24,16},{32,40},{40,32},{48,56},{56,48},{1,9},... | collective-permute-start | bytes 245768 | tf_op jit(solution)/shard_map/ppermute | solution.py:352
  170.8 48.2 %all-to-all-start.1 = ((bf16[8,40,2048]{2,1,0:T(8,128)(2,1)}), bf16[8,40,2048]{2,1,0:T(8,128)(2,1)S(1)}, u32[]{:S(2)}, u32[]{:S(2)}) async-start(bf16[8,40,2048]{2,1,0:T(8,128)(2,1)} %bitcast.31), calls=%async_computation.1 | async-start | bytes 2621440 | tf_op jit(solution)/shard_map/all_to_all | solution.py:440
  176.6 42.4 %copy-start.10 = (f32[1,128,1]{1,2,0:T(1,128)S(1)}, f32[1,128,1]{1,2,0:T(1,128)}, u32[]{:S(2)}) copy-start(f32[1,128,1]{1,2,0:T(1,128)} %param.23) | copy-start | bytes 1540
  176.7 7.0 %collective-permute-start.18 = (bf16[20,2048]{1,0:T(8,128)(2,1)S(1)}, bf16[20,2048]{1,0:T(8,128)(2,1)S(1)}, u32[]{:S(2)}, u32[]{:S(2)}) collective-permute-start(bf16[20,2048]{1,0:T(8,128)(2,1)S(1)} %add_convert_fusion.5), channel_id=1, source_target_pairs={{0,16},{8,24},{16,0},{24,8},{32,48},{40,56},{48,32},{56,40},{1,17}... | collective-permute-start | bytes 245768 | tf_op jit(solution)/shard_map/ppermute | solution.py:352
  183.7 9.6 %collective-permute-start.19 = (bf16[20,2048]{1,0:T(8,128)(2,1)S(1)}, bf16[20,2048]{1,0:T(8,128)(2,1)S(1)}, u32[]{:S(2)}, u32[]{:S(2)}) collective-permute-start(bf16[20,2048]{1,0:T(8,128)(2,1)S(1)} %add_convert_fusion.4), channel_id=1, source_target_pairs={{0,32},{8,40},{16,48},{24,56},{32,0},{40,8},{48,16},{56,24},{1,33}... | collective-permute-start | bytes 245768 | tf_op jit(solution)/shard_map/ppermute | solution.py:352
  193.4 8.9 %collective-permute-start.20 = (bf16[20,2048]{1,0:T(8,128)(2,1)S(1)}, bf16[20,2048]{1,0:T(8,128)(2,1)S(1)}, u32[]{:S(2)}, u32[]{:S(2)}) collective-permute-start(bf16[20,2048]{1,0:T(8,128)(2,1)S(1)} %add_convert_fusion.3), channel_id=1, source_target_pairs={{0,1},{1,0},{2,3},{3,2},{4,5},{5,4},{6,7},{7,6},{8,9},{9,8},{10,11... | collective-permute-start | bytes 245768 | tf_op jit(solution)/shard_map/ppermute | solution.py:352
  202.2 7.9 %collective-permute-start.21 = (bf16[20,2048]{1,0:T(8,128)(2,1)S(1)}, bf16[20,2048]{1,0:T(8,128)(2,1)S(1)}, u32[]{:S(2)}, u32[]{:S(2)}) collective-permute-start(bf16[20,2048]{1,0:T(8,128)(2,1)S(1)} %add_convert_fusion.2), channel_id=1, source_target_pairs={{0,2},{1,3},{2,0},{3,1},{4,6},{5,7},{6,4},{7,5},{8,10},{9,11},{10,... | collective-permute-start | bytes 245768 | tf_op jit(solution)/shard_map/ppermute | solution.py:352
  210.2 20.7 %collective-permute-start.22 = (bf16[20,2048]{1,0:T(8,128)(2,1)S(1)}, bf16[20,2048]{1,0:T(8,128)(2,1)S(1)}, u32[]{:S(2)}, u32[]{:S(2)}) collective-permute-start(bf16[20,2048]{1,0:T(8,128)(2,1)S(1)} %add_convert_fusion.1), channel_id=1, source_target_pairs={{0,4},{1,5},{2,6},{3,7},{4,0},{5,1},{6,2},{7,3},{8,12},{9,13},{10,... | collective-permute-start | bytes 245768 | tf_op jit(solution)/shard_map/ppermute | solution.py:352
  220.5 14.8 %collective-permute-start.16 = (bf16[128,2048]{1,0:T(8,128)(2,1)S(1)}, bf16[128,2048]{1,0:T(8,128)(2,1)S(1)}, u32[]{:S(2)}, u32[]{:S(2)}) collective-permute-start(bf16[128,2048]{1,0:T(8,128)(2,1)S(1)} %fusion.6), channel_id=1, source_target_pairs={{64,0},{128,64},{192,128},{256,192},{320,256},{384,320},{448,384},... | collective-permute-start | bytes 1572872 | tf_op jit(solution)/shard_map/ppermute | solution.py:345
  227.9 9.1 %collective-permute-start.15 = (bf16[128,2048]{1,0:T(8,128)(2,1)S(1)}, bf16[128,2048]{1,0:T(8,128)(2,1)S(1)}, u32[]{:S(2)}, u32[]{:S(2)}) collective-permute-start(bf16[128,2048]{1,0:T(8,128)(2,1)S(1)} %fusion.2), channel_id=1, source_target_pairs={{0,64},{64,128},{128,192},{192,256},{256,320},{320,384},{384,448},... | collective-permute-start | bytes 1572872 | tf_op jit(solution)/shard_map/ppermute | solution.py:345
  (8 other events, 36.0 us)

commit v8 on v6

--- a/solution.py
+++ b/solution.py
@@ -377,11 +377,6 @@
         up, down = ring[-1]
         ring.append((rotated(up, "split", 1), rotated(down, "split", -1)))
 
-    def held_back(ring, note):
-        up, down, note = lax.optimization_barrier((*ring[-1], note))
-        ring[-1] = (up, down)
-        return note
-
     def shards(step):
         return [(front_ring[step][k], rest_ring[step][k]) for k in range(2)]
 
@@ -402,7 +397,6 @@
 
     early = [(own_front, own_rest)] + shards(1) + shards(2)
     acc, note = expert_step(rows, cots, early)
-    note = held_back(rest_ring, note)
     last = (rotated(front_ring[-1][0], "split", 1), rotated(rest_ring[-1][1], "split", -1))
     before = expert_step(rows, cots, shards(3), (acc, note))
     partial, local_sums = expert_step(rows, cots, [last], before, slot_data)

time: 226 us -> 225 us (level)
  starting transfers between devices: 91.8 us -> 101 us
  waiting for transfers between devices: 93.1 us -> 84.7 us
  local copies, waits for them, and re-layouts: 12.4 us -> 6.82 us
    ppermute x14, waiting for transfers between devices: 68.6 us -> 60.5 us  [rotated(): lax.ppermute(value, axis, [(i, (i + distance) % size) for i in range(size)])]
    ppermute x14, starting transfers between devices: 38.7 us -> 46.1 us  [rotated(): lax.ppermute(value, axis, [(i, (i + distance) % size) for i in range(size)])]
    unnamed x45 -> x29, local copies, waits for them, and re-layouts: 8.91 us -> 3.37 us
  transfers between devices with their start and end apart: 24 -> 24, of which waited for: 14 -> 13; matrix products, arithmetic and copies ran while one was open for 3% -> 3% of each run, Pallas kernels for 6% -> 6%
where the time goes in v8:
time: 225 us; the launch traced here: 221 us
  starting transfers between devices  101 us (45%)
  waiting for transfers between devices  84.7 us (38%)
  Pallas kernels  23.7 us (11%)
  local copies, waits for them, and re-layouts  6.82 us (3%)
    ppermute x14, waiting for transfers between devices, rotated(): lax.ppermute(value, axis, [(i, (i + distance) % size) for i in range(size)])  60.5 us
    ppermute x14, starting transfers between devices, rotated(): lax.ppermute(value, axis, [(i, (i + distance) % size) for i in range(size)])  46.1 us
    ppermute x6, starting transfers between devices, summed(): lax.ppermute(value.astype(BF16), axis, [(i, i ^ distance) for i in range(...  27.9 us
    ppermute x6, waiting for transfers between devices, summed(): lax.ppermute(value.astype(BF16), axis, [(i, i ^ distance) for i in range(...  18.9 us
    pallas_call x3, Pallas kernels, expert_step(): pl.pallas_call(functools.partial(expert_kernel, len(shards), before is no...  17.8 us
    all_to_all x1, starting transfers between devices, on_device(): lax.all_to_all(packed, 'column', split_axis=0, concat_axis=0, tiled=True)  11 us
    ppermute x2, starting transfers between devices, shifted(): return lax.ppermute(block, axis, route)  10 us
    all_to_all x1, starting transfers between devices, on_device(): lax.all_to_all(partial.reshape(EXPERTS, ROWS, width), 'column', split_axi...  6.38 us
  transfers between devices with their start and end apart: 24, of which 13 were waited for; matrix products, arithmetic and copies ran while one was open for 3% of the time, Pallas kernels for 6%

profile of v8, /device:TPU:1, one launch (start us, length us, event | category | flops | bytes accessed | tf_op | source)
XLA Modules:
  0.0 221.1 jit_solution(15809139589362854567)
XLA Ops:
  2.3 5.8 %shard_map.175 = (bf16[512,2176]{1,0:T(8,128)(2,1)}, bf16[128,2048]{1,0:T(8,128)(2,1)S(1)}, bf16[128,2048]{1,0:T(8,128)(2,1)S(1)}, f32[128,128]{1,0:T(8,128)S(1)...) custom-call(s32[1,1]{1,0:T(1,128)} %bitcast.first_ref, s32[1,16]{1,0:T(1,128)} %refs_0_.1, ...), custom_call_target="tpu_custom_call" | custom-call | tf_op jit(solution)/shard_map/pallas_call | solution.py:155
  8.1 11.0 %all-to-all-start = ((bf16[8,64,2176]{2,1,0:T(8,128)(2,1)}), bf16[8,64,2176]{2,1,0:T(8,128)(2,1)}, u32[]{:S(2)}, u32[]{:S(2)}) async-start(bf16[8,64,2176]{2,1,0:T(8,128)(2,1)} %bitcast.11), calls=%async_computation | async-start | bytes 4456448 | tf_op jit(solution)/shard_map/all_to_all | solution.py:388
  19.2 3.2 %collective-permute-start = (bf16[1536,256]{1,0:T(8,128)(2,1)S(1)}, bf16[1536,256]{1,0:T(8,128)(2,1)S(1)}, u32[]{:S(2)}, u32[]{:S(2)}) collective-permute-start(bf16[1536,256]{1,0:T(8,128)(2,1)S(1)} %get-tuple-element.18.refs_2_), channel_id=1, source_target_pairs={{0,8},{8,16},{16,24},{24,32},{32,40},{40,48},{48,56},{56,0},{1,9},... | collective-permute-start | bytes 2359304 | tf_op jit(solution)/shard_map/ppermute | solution.py:311
  22.4 3.8 %collective-permute-start.4 = (bf16[1536,256]{1,0:T(8,128)(2,1)S(1)}, bf16[1536,256]{1,0:T(8,128)(2,1)S(1)}, u32[]{:S(2)}, u32[]{:S(2)}) collective-permute-start(bf16[1536,256]{1,0:T(8,128)(2,1)S(1)} %get-tuple-element.19.refs_3_), channel_id=1, source_target_pairs={{0,56},{8,0},{16,8},{24,16},{32,24},{40,32},{48,40},{56,48},{1,57}... | collective-permute-start | bytes 2359304 | tf_op jit(solution)/shard_map/ppermute | solution.py:311
  28.1 4.6 %collective-permute-start.11 = (bf16[1536,256]{1,0:T(8,128)(2,1)S(1)}, bf16[1536,256]{1,0:T(8,128)(2,1)S(1)}, u32[]{:S(2)}, u32[]{:S(2)}) collective-permute-start(bf16[1536,256]{1,0:T(8,128)(2,1)S(1)} %get-tuple-element.18.refs_2_), channel_id=1, source_target_pairs={{0,56},{8,0},{16,8},{24,16},{32,24},{40,32},{48,40},{56,48},{1,57}... | collective-permute-start | bytes 2359304 | tf_op jit(solution)/shard_map/ppermute | solution.py:311
  32.7 8.6 %collective-permute-done.refs_4_ = bf16[1536,256]{1,0:T(8,128)(2,1)S(1)} collective-permute-done((bf16[1536,256]{1,0:T(8,128)(2,1)S(1)}, bf16[1536,256]{1,0:T(8,128)(2,1)S(1)}, u32[]{:S(2)}, u32[]{:S(2)}) %collective-permute-start) | collective-permute-done | bytes 786464 | tf_op jit(solution)/shard_map/ppermute | solution.py:311
  43.2 4.6 %collective-permute-start.5 = (bf16[1536,256]{1,0:T(8,128)(2,1)S(1)}, bf16[1536,256]{1,0:T(8,128)(2,1)}, u32[]{:S(2)}, u32[]{:S(2)}) collective-permute-start(bf16[1536,256]{1,0:T(8,128)(2,1)S(1)} %collective-permute-done.4.refs_7_), channel_id=1, source_target_pairs={{0,56},{8,0},{16,8},{24,16},{32,24},{40,32},{48,40},{56,48},{1,57}... | collective-permute-start | bytes 2359304 | tf_op jit(solution)/shard_map/ppermute | solution.py:311
  47.8 10.3 %collective-permute-done.8.refs_5_ = bf16[1536,256]{1,0:T(8,128)(2,1)S(1)} collective-permute-done((bf16[1536,256]{1,0:T(8,128)(2,1)S(1)}, bf16[1536,256]{1,0:T(8,128)(2,1)S(1)}, u32[]{:S(2)}, u32[]{:S(2)}) %collective-permute-start.8) | collective-permute-done | bytes 786464 | tf_op jit(solution)/shard_map/ppermute | solution.py:311
  60.1 4.6 %collective-permute-start.12 = (bf16[1536,256]{1,0:T(8,128)(2,1)S(1)}, bf16[1536,256]{1,0:T(8,128)(2,1)}, u32[]{:S(2)}, u32[]{:S(2)}) collective-permute-start(bf16[1536,256]{1,0:T(8,128)(2,1)S(1)} %collective-permute-done.11.refs_6_), channel_id=1, source_target_pairs={{0,56},{8,0},{16,8},{24,16},{32,24},{40,32},{48,40},{56,48},{1,57}... | collective-permute-start | bytes 2359304 | tf_op jit(solution)/shard_map/ppermute | solution.py:311
  64.7 10.3 %collective-permute-done.1.refs_8_ = bf16[1536,256]{1,0:T(8,128)(2,1)} collective-permute-done((bf16[1536,256]{1,0:T(8,128)(2,1)S(1)}, bf16[1536,256]{1,0:T(8,128)(2,1)}, u32[]{:S(2)}, u32[]{:S(2)}) %collective-permute-start.1) | collective-permute-done | bytes 786464 | tf_op jit(solution)/shard_map/ppermute | solution.py:311
  76.9 4.6 %collective-permute-start.6 = (bf16[1536,256]{1,0:T(8,128)(2,1)}, bf16[1536,256]{1,0:T(8,128)(2,1)}, u32[]{:S(2)}, u32[]{:S(2)}) collective-permute-start(bf16[1536,256]{1,0:T(8,128)(2,1)} %collective-permute-done.5.refs_11_), channel_id=1, source_target_pairs={{0,56},{8,0},{16,8},{24,16},{32,24},{40,32},{48,40},{56,48},{1,57}... | collective-permute-start | bytes 2359304 | tf_op jit(solution)/shard_map/ppermute | solution.py:311
  81.7 10.1 %collective-permute-done.9.refs_9_ = bf16[1536,256]{1,0:T(8,128)(2,1)} collective-permute-done((bf16[1536,256]{1,0:T(8,128)(2,1)S(1)}, bf16[1536,256]{1,0:T(8,128)(2,1)}, u32[]{:S(2)}, u32[]{:S(2)}) %collective-permute-start.9) | collective-permute-done | bytes 786464 | tf_op jit(solution)/shard_map/ppermute | solution.py:311
  93.8 4.6 %collective-permute-start.13 = (bf16[1536,256]{1,0:T(8,128)(2,1)}, bf16[1536,256]{1,0:T(8,128)(2,1)}, u32[]{:S(2)}, u32[]{:S(2)}) collective-permute-start(bf16[1536,256]{1,0:T(8,128)(2,1)} %collective-permute-done.12.refs_10_), channel_id=1, source_target_pairs={{0,56},{8,0},{16,8},{24,16},{32,24},{40,32},{48,40},{56,48},{1,57}... | collective-permute-start | bytes 2359304 | tf_op jit(solution)/shard_map/ppermute | solution.py:311
  98.6 10.0 %collective-permute-done.2.refs_2_ = bf16[1536,256]{1,0:T(8,128)(2,1)S(1)} collective-permute-done((bf16[1536,256]{1,0:T(8,128)(2,1)}, bf16[1536,256]{1,0:T(8,128)(2,1)S(1)}, u32[]{:S(2)}, u32[]{:S(2)}) %collective-permute-start.2) | collective-permute-done | bytes 786464 | tf_op jit(solution)/shard_map/ppermute | solution.py:311
  110.5 4.8 %collective-permute-start.7 = (bf16[1536,256]{1,0:T(8,128)(2,1)}, bf16[1536,256]{1,0:T(8,128)(2,1)}, u32[]{:S(2)}, u32[]{:S(2)}) collective-permute-start(bf16[1536,256]{1,0:T(8,128)(2,1)} %collective-permute-done.6.refs_5_), channel_id=1, source_target_pairs={{0,56},{8,0},{16,8},{24,16},{32,24},{40,32},{48,40},{56,48},{1,57}... | collective-permute-start | bytes 2359304 | tf_op jit(solution)/shard_map/ppermute | solution.py:311
  118.5 9.1 %shard_map.176 = (f32[320,2048]{1,0:T(8,128)S(1)}, f32[8,128]{1,0:T(8,128)S(1)}) custom-call(bf16[320,2176]{1,0:T(8,128)(2,1)S(1)} %bitcast.25, bf16[192,2048]{1,0:T(8,128)(2,1)S(1)} %bitcast.28, bf16[1536,256]{1,0:T(8,128)(2,1)} %copy-done.1, bf16[1536,256]{1,0:T(8,128)(2,1)} %copy-done.2, bf16[1536,256]{1,0:T(8,128)(2,1)} %copy-done.8, ...), custom_call_target="tpu_custom_call" | custom-call | flops 3690987520 | bytes 12664832 | tf_op jit(solution)/shard_map/pallas_call | solution.py:294
  127.7 4.5 %shard_map.177 = (f32[320,2048]{1,0:T(8,128)S(1)}, f32[8,128]{1,0:T(8,128)S(1)}) custom-call(bf16[320,2176]{1,0:T(8,128)(2,1)S(1)} %bitcast.26, bf16[192,2048]{1,0:T(8,128)(2,1)S(1)} %bitcast.29, bf16[1536,256]{1,0:T(8,128)(2,1)} %copy-done.4, bf16[1536,256]{1,0:T(8,128)(2,1)} %collective-permute-done.10.refs_3_, ...), custom_call_target="tpu_custom_call" | custom-call | flops 1476395008 | bytes 10571776 | tf_op jit(solution)/shard_map/pallas_call | solution.py:294
  132.1 10.3 %collective-permute-done.3.refs_2_ = bf16[1536,256]{1,0:T(8,128)(2,1)} collective-permute-done((bf16[1536,256]{1,0:T(8,128)(2,1)S(1)}, bf16[1536,256]{1,0:T(8,128)(2,1)}, u32[]{:S(2)}, u32[]{:S(2)}) %collective-permute-start.3) | collective-permute-done | bytes 786464 | tf_op jit(solution)/shard_map/ppermute | solution.py:311
  143.3 4.3 %shard_map.178 = (bf16[320,2048]{1,0:T(8,128)(2,1)}, f32[20,2048]{1,0:T(8,128)S(1)}) custom-call(bf16[320,2176]{1,0:T(8,128)(2,1)S(1)} %bitcast.27, bf16[192,2048]{1,0:T(8,128)(2,1)S(1)} %bitcast.30, bf16[1536,256]{1,0:T(8,128)(2,1)} %collective-permute-done.3.refs_2_, bf16[1536,256]{1,0:T(8,128)(2,1)} %collective-permute-done.7.refs_3_, ...), custom_call_target="tpu_custom_call" | custom-call | flops 738197504 | bytes 9334864 | tf_op jit(solution)/shard_map/pallas_call | solution.py:294
  147.6 3.2 %collective-permute-start.16 = (bf16[20,2048]{1,0:T(8,128)(2,1)S(1)}, bf16[20,2048]{1,0:T(8,128)(2,1)S(1)}, u32[]{:S(2)}, u32[]{:S(2)}) collective-permute-start(bf16[20,2048]{1,0:T(8,128)(2,1)S(1)} %convert_element_type.105), channel_id=1, source_target_pairs={{0,8},{8,0},{16,24},{24,16},{32,40},{40,32},{48,56},{56,48},{1,9},... | collective-permute-start | bytes 245768 | tf_op jit(solution)/shard_map/ppermute | solution.py:324
  150.8 6.4 %all-to-all-start.1 = ((bf16[8,40,2048]{2,1,0:T(8,128)(2,1)}), bf16[8,40,2048]{2,1,0:T(8,128)(2,1)S(1)}, u32[]{:S(2)}, u32[]{:S(2)}) async-start(bf16[8,40,2048]{2,1,0:T(8,128)(2,1)} %bitcast.14), calls=%async_computation.1 | async-start | bytes 2621440 | tf_op jit(solution)/shard_map/all_to_all | solution.py:404
  157.2 6.6 %collective-permute-start.17 = (bf16[20,2048]{1,0:T(8,128)(2,1)S(1)}, bf16[20,2048]{1,0:T(8,128)(2,1)S(1)}, u32[]{:S(2)}, u32[]{:S(2)}) collective-permute-start(bf16[20,2048]{1,0:T(8,128)(2,1)S(1)} %add_convert_fusion.5), channel_id=1, source_target_pairs={{0,16},{8,24},{16,0},{24,8},{32,48},{40,56},{48,32},{56,40},{1,17}... | collective-permute-start | bytes 245768 | tf_op jit(solution)/shard_map/ppermute | solution.py:324
  163.9 3.1 %collective-permute-done.17 = bf16[20,2048]{1,0:T(8,128)(2,1)S(1)} collective-permute-done((bf16[20,2048]{1,0:T(8,128)(2,1)S(1)}, bf16[20,2048]{1,0:T(8,128)(2,1)S(1)}, u32[]{:S(2)}, u32[]{:S(2)}) %collective-permute-start.17) | collective-permute-done | bytes 81952 | tf_op jit(solution)/shard_map/ppermute | solution.py:324
  166.9 3.3 %collective-permute-start.18 = (bf16[20,2048]{1,0:T(8,128)(2,1)S(1)}, bf16[20,2048]{1,0:T(8,128)(2,1)S(1)}, u32[]{:S(2)}, u32[]{:S(2)}) collective-permute-start(bf16[20,2048]{1,0:T(8,128)(2,1)S(1)} %add_convert_fusion.4), channel_id=1, source_target_pairs={{0,32},{8,40},{16,48},{24,56},{32,0},{40,8},{48,16},{56,24},{1,33}... | collective-permute-start | bytes 245768 | tf_op jit(solution)/shard_map/ppermute | solution.py:324
  170.2 6.6 %collective-permute-done.18 = bf16[20,2048]{1,0:T(8,128)(2,1)S(1)} collective-permute-done((bf16[20,2048]{1,0:T(8,128)(2,1)S(1)}, bf16[20,2048]{1,0:T(8,128)(2,1)S(1)}, u32[]{:S(2)}, u32[]{:S(2)}) %collective-permute-start.18) | collective-permute-done | bytes 81952 | tf_op jit(solution)/shard_map/ppermute | solution.py:324
  176.9 3.4 %collective-permute-start.19 = (bf16[20,2048]{1,0:T(8,128)(2,1)S(1)}, bf16[20,2048]{1,0:T(8,128)(2,1)S(1)}, u32[]{:S(2)}, u32[]{:S(2)}) collective-permute-start(bf16[20,2048]{1,0:T(8,128)(2,1)S(1)} %add_convert_fusion.3), channel_id=1, source_target_pairs={{0,1},{1,0},{2,3},{3,2},{4,5},{5,4},{6,7},{7,6},{8,9},{9,8},{10,11... | collective-permute-start | bytes 245768 | tf_op jit(solution)/shard_map/ppermute | solution.py:324
  180.3 5.3 %collective-permute-done.19 = bf16[20,2048]{1,0:T(8,128)(2,1)S(1)} collective-permute-done((bf16[20,2048]{1,0:T(8,128)(2,1)S(1)}, bf16[20,2048]{1,0:T(8,128)(2,1)S(1)}, u32[]{:S(2)}, u32[]{:S(2)}) %collective-permute-start.19) | collective-permute-done | bytes 81952 | tf_op jit(solution)/shard_map/ppermute | solution.py:324
  185.7 4.8 %collective-permute-start.20 = (bf16[20,2048]{1,0:T(8,128)(2,1)S(1)}, bf16[20,2048]{1,0:T(8,128)(2,1)S(1)}, u32[]{:S(2)}, u32[]{:S(2)}) collective-permute-start(bf16[20,2048]{1,0:T(8,128)(2,1)S(1)} %add_convert_fusion.2), channel_id=1, source_target_pairs={{0,2},{1,3},{2,0},{3,1},{4,6},{5,7},{6,4},{7,5},{8,10},{9,11},{10,... | collective-permute-start | bytes 245768 | tf_op jit(solution)/shard_map/ppermute | solution.py:324
  190.5 3.8 %collective-permute-done.20 = bf16[20,2048]{1,0:T(8,128)(2,1)S(1)} collective-permute-done((bf16[20,2048]{1,0:T(8,128)(2,1)S(1)}, bf16[20,2048]{1,0:T(8,128)(2,1)S(1)}, u32[]{:S(2)}, u32[]{:S(2)}) %collective-permute-start.20) | collective-permute-done | bytes 81952 | tf_op jit(solution)/shard_map/ppermute | solution.py:324
  194.3 6.7 %collective-permute-start.21 = (bf16[20,2048]{1,0:T(8,128)(2,1)S(1)}, bf16[20,2048]{1,0:T(8,128)(2,1)S(1)}, u32[]{:S(2)}, u32[]{:S(2)}) collective-permute-start(bf16[20,2048]{1,0:T(8,128)(2,1)S(1)} %add_convert_fusion.1), channel_id=1, source_target_pairs={{0,4},{1,5},{2,6},{3,7},{4,0},{5,1},{6,2},{7,3},{8,12},{9,13},{10,... | collective-permute-start | bytes 245768 | tf_op jit(solution)/shard_map/ppermute | solution.py:324
  202.9 7.0 %collective-permute-start.15 = (bf16[128,2048]{1,0:T(8,128)(2,1)}, bf16[128,2048]{1,0:T(8,128)(2,1)S(1)}, u32[]{:S(2)}, u32[]{:S(2)}) collective-permute-start(bf16[128,2048]{1,0:T(8,128)(2,1)} %fusion.6), channel_id=1, source_target_pairs={{64,0},{128,64},{192,128},{256,192},{320,256},{384,320},{448,384},... | collective-permute-start | bytes 1572872 | tf_op jit(solution)/shard_map/ppermute | solution.py:317
  214.3 3.8 %collective-permute-done.15 = bf16[128,2048]{1,0:T(8,128)(2,1)S(1)} collective-permute-done((bf16[128,2048]{1,0:T(8,128)(2,1)}, bf16[128,2048]{1,0:T(8,128)(2,1)S(1)}, u32[]{:S(2)}, u32[]{:S(2)}) %collective-permute-start.15) | collective-permute-done | bytes 524320 | tf_op jit(solution)/shard_map/ppermute | solution.py:317
  (73 shorter events, 27.0 us)
Async XLA Ops:
  8.1 20.0 %copy-start.1 = (bf16[1536,256]{1,0:T(8,128)(2,1)}, bf16[1536,256]{1,0:T(8,128)(2,1)S(1)}, u32[]{:S(2)}) copy-start(bf16[1536,256]{1,0:T(8,128)(2,1)S(1)} %get-tuple-element.18.refs_2_) | copy-start | bytes 2359300
  8.1 73.4 %copy-start.5 = (bf16[1,2,10,2048]{3,1,2,0:T(2,128)(2,1)S(1)}, bf16[1,2,10,2048]{3,1,2,0:T(2,128)(2,1)}, u32[]{:S(2)}) copy-start(bf16[1,2,10,2048]{3,1,2,0:T(2,128)(2,1)} %param.27) | copy-start | bytes 245764
  8.1 107.4 %copy-start.3 = (bf16[1,128,2048]{2,1,0:T(8,128)(2,1)S(1)}, bf16[1,128,2048]{2,1,0:T(8,128)(2,1)}, u32[]{:S(2)}) copy-start(bf16[1,128,2048]{2,1,0:T(8,128)(2,1)} %param.26) | copy-start | bytes 1572868
  8.1 107.7 %all-to-all-start = ((bf16[8,64,2176]{2,1,0:T(8,128)(2,1)}), bf16[8,64,2176]{2,1,0:T(8,128)(2,1)}, u32[]{:S(2)}, u32[]{:S(2)}) async-start(bf16[8,64,2176]{2,1,0:T(8,128)(2,1)} %bitcast.11), calls=%async_computation | async-start | bytes 4456448 | tf_op jit(solution)/shard_map/all_to_all | solution.py:388
  19.2 22.1 %collective-permute-start = (bf16[1536,256]{1,0:T(8,128)(2,1)S(1)}, bf16[1536,256]{1,0:T(8,128)(2,1)S(1)}, u32[]{:S(2)}, u32[]{:S(2)}) collective-permute-start(bf16[1536,256]{1,0:T(8,128)(2,1)S(1)} %get-tuple-element.18.refs_2_), channel_id=1, source_target_pairs={{0,8},{8,16},{16,24},{24,32},{32,40},{40,48},{48,56},{56,0},{1,9},... | collective-permute-start | bytes 2359304 | tf_op jit(solution)/shard_map/ppermute | solution.py:311
  22.4 20.9 %collective-permute-start.4 = (bf16[1536,256]{1,0:T(8,128)(2,1)S(1)}, bf16[1536,256]{1,0:T(8,128)(2,1)S(1)}, u32[]{:S(2)}, u32[]{:S(2)}) collective-permute-start(bf16[1536,256]{1,0:T(8,128)(2,1)S(1)} %get-tuple-element.19.refs_3_), channel_id=1, source_target_pairs={{0,56},{8,0},{16,8},{24,16},{32,24},{40,32},{48,40},{56,48},{1,57}... | collective-permute-start | bytes 2359304 | tf_op jit(solution)/shard_map/ppermute | solution.py:311
  26.2 32.0 %collective-permute-start.8 = (bf16[1536,256]{1,0:T(8,128)(2,1)S(1)}, bf16[1536,256]{1,0:T(8,128)(2,1)S(1)}, u32[]{:S(2)}, u32[]{:S(2)}) collective-permute-start(bf16[1536,256]{1,0:T(8,128)(2,1)S(1)} %get-tuple-element.19.refs_3_), channel_id=1, source_target_pairs={{0,8},{8,16},{16,24},{24,32},{32,40},{40,48},{48,56},{56,0},{1,9},... | collective-permute-start | bytes 2359304 | tf_op jit(solution)/shard_map/ppermute | solution.py:311
  28.1 31.9 %collective-permute-start.11 = (bf16[1536,256]{1,0:T(8,128)(2,1)S(1)}, bf16[1536,256]{1,0:T(8,128)(2,1)S(1)}, u32[]{:S(2)}, u32[]{:S(2)}) collective-permute-start(bf16[1536,256]{1,0:T(8,128)(2,1)S(1)} %get-tuple-element.18.refs_2_), channel_id=1, source_target_pairs={{0,56},{8,0},{16,8},{24,16},{32,24},{40,32},{48,40},{56,48},{1,57}... | collective-permute-start | bytes 2359304 | tf_op jit(solution)/shard_map/ppermute | solution.py:311
  41.3 35.6 %copy-start.8 = (bf16[1536,256]{1,0:T(8,128)(2,1)}, bf16[1536,256]{1,0:T(8,128)(2,1)S(1)}, u32[]{:S(2)}) copy-start(bf16[1536,256]{1,0:T(8,128)(2,1)S(1)} %collective-permute-done.refs_4_) | copy-start | bytes 2359300
  41.3 33.7 %collective-permute-start.1 = (bf16[1536,256]{1,0:T(8,128)(2,1)S(1)}, bf16[1536,256]{1,0:T(8,128)(2,1)}, u32[]{:S(2)}, u32[]{:S(2)}) collective-permute-start(bf16[1536,256]{1,0:T(8,128)(2,1)S(1)} %collective-permute-done.refs_4_), channel_id=1, source_target_pairs={{0,8},{8,16},{16,24},{24,32},{32,40},{40,48},{48,56},{56,0},{1,9},... | collective-permute-start | bytes 2359304 | tf_op jit(solution)/shard_map/ppermute | solution.py:311
  43.2 33.7 %copy-start.9 = (bf16[1536,256]{1,0:T(8,128)(2,1)}, bf16[1536,256]{1,0:T(8,128)(2,1)S(1)}, u32[]{:S(2)}) copy-start(bf16[1536,256]{1,0:T(8,128)(2,1)S(1)} %collective-permute-done.4.refs_7_) | copy-start | bytes 2359300
  43.2 33.7 %collective-permute-start.5 = (bf16[1536,256]{1,0:T(8,128)(2,1)S(1)}, bf16[1536,256]{1,0:T(8,128)(2,1)}, u32[]{:S(2)}, u32[]{:S(2)}) collective-permute-start(bf16[1536,256]{1,0:T(8,128)(2,1)S(1)} %collective-permute-done.4.refs_7_), channel_id=1, source_target_pairs={{0,56},{8,0},{16,8},{24,16},{32,24},{40,32},{48,40},{56,48},{1,57}... | collective-permute-start | bytes 2359304 | tf_op jit(solution)/shard_map/ppermute | solution.py:311
  58.1 40.2 %copy-start.10 = (bf16[1536,256]{1,0:T(8,128)(2,1)}, bf16[1536,256]{1,0:T(8,128)(2,1)S(1)}, u32[]{:S(2)}) copy-start(bf16[1536,256]{1,0:T(8,128)(2,1)S(1)} %collective-permute-done.8.refs_5_) | copy-start | bytes 2359300
  58.1 33.7 %collective-permute-start.9 = (bf16[1536,256]{1,0:T(8,128)(2,1)S(1)}, bf16[1536,256]{1,0:T(8,128)(2,1)}, u32[]{:S(2)}, u32[]{:S(2)}) collective-permute-start(bf16[1536,256]{1,0:T(8,128)(2,1)S(1)} %collective-permute-done.8.refs_5_), channel_id=1, source_target_pairs={{0,8},{8,16},{16,24},{24,32},{32,40},{40,48},{48,56},{56,0},{1,9},... | collective-permute-start | bytes 2359304 | tf_op jit(solution)/shard_map/ppermute | solution.py:311
  60.1 38.3 %copy-start.11 = (bf16[1536,256]{1,0:T(8,128)(2,1)}, bf16[1536,256]{1,0:T(8,128)(2,1)S(1)}, u32[]{:S(2)}) copy-start(bf16[1536,256]{1,0:T(8,128)(2,1)S(1)} %collective-permute-done.11.refs_6_) | copy-start | bytes 2359300
  60.1 33.7 %collective-permute-start.12 = (bf16[1536,256]{1,0:T(8,128)(2,1)S(1)}, bf16[1536,256]{1,0:T(8,128)(2,1)}, u32[]{:S(2)}, u32[]{:S(2)}) collective-permute-start(bf16[1536,256]{1,0:T(8,128)(2,1)S(1)} %collective-permute-done.11.refs_6_), channel_id=1, source_target_pairs={{0,56},{8,0},{16,8},{24,16},{32,24},{40,32},{48,40},{56,48},{1,57}... | collective-permute-start | bytes 2359304 | tf_op jit(solution)/shard_map/ppermute | solution.py:311
  75.0 33.6 %collective-permute-start.2 = (bf16[1536,256]{1,0:T(8,128)(2,1)}, bf16[1536,256]{1,0:T(8,128)(2,1)S(1)}, u32[]{:S(2)}, u32[]{:S(2)}) collective-permute-start(bf16[1536,256]{1,0:T(8,128)(2,1)} %collective-permute-done.1.refs_8_), channel_id=1, source_target_pairs={{0,8},{8,16},{16,24},{24,32},{32,40},{40,48},{48,56},{56,0},{1,9},... | collective-permute-start | bytes 2359304 | tf_op jit(solution)/shard_map/ppermute | solution.py:311
  76.9 33.6 %collective-permute-start.6 = (bf16[1536,256]{1,0:T(8,128)(2,1)}, bf16[1536,256]{1,0:T(8,128)(2,1)}, u32[]{:S(2)}, u32[]{:S(2)}) collective-permute-start(bf16[1536,256]{1,0:T(8,128)(2,1)} %collective-permute-done.5.refs_11_), channel_id=1, source_target_pairs={{0,56},{8,0},{16,8},{24,16},{32,24},{40,32},{48,40},{56,48},{1,57}... | collective-permute-start | bytes 2359304 | tf_op jit(solution)/shard_map/ppermute | solution.py:311
  91.8 35.8 %collective-permute-start.10 = (bf16[1536,256]{1,0:T(8,128)(2,1)}, bf16[1536,256]{1,0:T(8,128)(2,1)}, u32[]{:S(2)}, u32[]{:S(2)}) collective-permute-start(bf16[1536,256]{1,0:T(8,128)(2,1)} %collective-permute-done.9.refs_9_), channel_id=1, source_target_pairs={{0,8},{8,16},{16,24},{24,32},{32,40},{40,48},{48,56},{56,0},{1,9},... | collective-permute-start | bytes 2359304 | tf_op jit(solution)/shard_map/ppermute | solution.py:311
  93.8 33.9 %collective-permute-start.13 = (bf16[1536,256]{1,0:T(8,128)(2,1)}, bf16[1536,256]{1,0:T(8,128)(2,1)}, u32[]{:S(2)}, u32[]{:S(2)}) collective-permute-start(bf16[1536,256]{1,0:T(8,128)(2,1)} %collective-permute-done.12.refs_10_), channel_id=1, source_target_pairs={{0,56},{8,0},{16,8},{24,16},{32,24},{40,32},{48,40},{56,48},{1,57}... | collective-permute-start | bytes 2359304 | tf_op jit(solution)/shard_map/ppermute | solution.py:311
  108.6 33.8 %collective-permute-start.3 = (bf16[1536,256]{1,0:T(8,128)(2,1)S(1)}, bf16[1536,256]{1,0:T(8,128)(2,1)}, u32[]{:S(2)}, u32[]{:S(2)}) collective-permute-start(bf16[1536,256]{1,0:T(8,128)(2,1)S(1)} %collective-permute-done.2.refs_2_), channel_id=1, source_target_pairs={{0,8},{8,16},{16,24},{24,32},{32,40},{40,48},{48,56},{56,0},{1,9},... | collective-permute-start | bytes 2359304 | tf_op jit(solution)/shard_map/ppermute | solution.py:311
  110.5 32.7 %collective-permute-start.7 = (bf16[1536,256]{1,0:T(8,128)(2,1)}, bf16[1536,256]{1,0:T(8,128)(2,1)}, u32[]{:S(2)}, u32[]{:S(2)}) collective-permute-start(bf16[1536,256]{1,0:T(8,128)(2,1)} %collective-permute-done.6.refs_5_), channel_id=1, source_target_pairs={{0,56},{8,0},{16,8},{24,16},{32,24},{40,32},{48,40},{56,48},{1,57}... | collective-permute-start | bytes 2359304 | tf_op jit(solution)/shard_map/ppermute | solution.py:311
  147.6 9.6 %collective-permute-start.16 = (bf16[20,2048]{1,0:T(8,128)(2,1)S(1)}, bf16[20,2048]{1,0:T(8,128)(2,1)S(1)}, u32[]{:S(2)}, u32[]{:S(2)}) collective-permute-start(bf16[20,2048]{1,0:T(8,128)(2,1)S(1)} %convert_element_type.105), channel_id=1, source_target_pairs={{0,8},{8,0},{16,24},{24,16},{32,40},{40,32},{48,56},{56,48},{1,9},... | collective-permute-start | bytes 245768 | tf_op jit(solution)/shard_map/ppermute | solution.py:324
  150.8 50.3 %all-to-all-start.1 = ((bf16[8,40,2048]{2,1,0:T(8,128)(2,1)}), bf16[8,40,2048]{2,1,0:T(8,128)(2,1)S(1)}, u32[]{:S(2)}, u32[]{:S(2)}) async-start(bf16[8,40,2048]{2,1,0:T(8,128)(2,1)} %bitcast.14), calls=%async_computation.1 | async-start | bytes 2621440 | tf_op jit(solution)/shard_map/all_to_all | solution.py:404
  157.2 43.9 %copy-start.6 = (f32[1,128,1]{1,2,0:T(1,128)S(1)}, f32[1,128,1]{1,2,0:T(1,128)}, u32[]{:S(2)}) copy-start(f32[1,128,1]{1,2,0:T(1,128)} %param.23) | copy-start | bytes 1540
  157.2 9.7 %collective-permute-start.17 = (bf16[20,2048]{1,0:T(8,128)(2,1)S(1)}, bf16[20,2048]{1,0:T(8,128)(2,1)S(1)}, u32[]{:S(2)}, u32[]{:S(2)}) collective-permute-start(bf16[20,2048]{1,0:T(8,128)(2,1)S(1)} %add_convert_fusion.5), channel_id=1, source_target_pairs={{0,16},{8,24},{16,0},{24,8},{32,48},{40,56},{48,32},{56,40},{1,17}... | collective-permute-start | bytes 245768 | tf_op jit(solution)/shard_map/ppermute | solution.py:324
  166.9 9.9 %collective-permute-start.18 = (bf16[20,2048]{1,0:T(8,128)(2,1)S(1)}, bf16[20,2048]{1,0:T(8,128)(2,1)S(1)}, u32[]{:S(2)}, u32[]{:S(2)}) collective-permute-start(bf16[20,2048]{1,0:T(8,128)(2,1)S(1)} %add_convert_fusion.4), channel_id=1, source_target_pairs={{0,32},{8,40},{16,48},{24,56},{32,0},{40,8},{48,16},{56,24},{1,33}... | collective-permute-start | bytes 245768 | tf_op jit(solution)/shard_map/ppermute | solution.py:324
  176.9 8.8 %collective-permute-start.19 = (bf16[20,2048]{1,0:T(8,128)(2,1)S(1)}, bf16[20,2048]{1,0:T(8,128)(2,1)S(1)}, u32[]{:S(2)}, u32[]{:S(2)}) collective-permute-start(bf16[20,2048]{1,0:T(8,128)(2,1)S(1)} %add_convert_fusion.3), channel_id=1, source_target_pairs={{0,1},{1,0},{2,3},{3,2},{4,5},{5,4},{6,7},{7,6},{8,9},{9,8},{10,11... | collective-permute-start | bytes 245768 | tf_op jit(solution)/shard_map/ppermute | solution.py:324
  185.7 8.6 %collective-permute-start.20 = (bf16[20,2048]{1,0:T(8,128)(2,1)S(1)}, bf16[20,2048]{1,0:T(8,128)(2,1)S(1)}, u32[]{:S(2)}, u32[]{:S(2)}) collective-permute-start(bf16[20,2048]{1,0:T(8,128)(2,1)S(1)} %add_convert_fusion.2), channel_id=1, source_target_pairs={{0,2},{1,3},{2,0},{3,1},{4,6},{5,7},{6,4},{7,5},{8,10},{9,11},{10,... | collective-permute-start | bytes 245768 | tf_op jit(solution)/shard_map/ppermute | solution.py:324
  194.3 19.1 %collective-permute-start.21 = (bf16[20,2048]{1,0:T(8,128)(2,1)S(1)}, bf16[20,2048]{1,0:T(8,128)(2,1)S(1)}, u32[]{:S(2)}, u32[]{:S(2)}) collective-permute-start(bf16[20,2048]{1,0:T(8,128)(2,1)S(1)} %add_convert_fusion.1), channel_id=1, source_target_pairs={{0,4},{1,5},{2,6},{3,7},{4,0},{5,1},{6,2},{7,3},{8,12},{9,13},{10,... | collective-permute-start | bytes 245768 | tf_op jit(solution)/shard_map/ppermute | solution.py:324
  202.9 15.2 %collective-permute-start.15 = (bf16[128,2048]{1,0:T(8,128)(2,1)}, bf16[128,2048]{1,0:T(8,128)(2,1)S(1)}, u32[]{:S(2)}, u32[]{:S(2)}) collective-permute-start(bf16[128,2048]{1,0:T(8,128)(2,1)} %fusion.6), channel_id=1, source_target_pairs={{64,0},{128,64},{192,128},{256,192},{320,256},{384,320},{448,384},... | collective-permute-start | bytes 1572872 | tf_op jit(solution)/shard_map/ppermute | solution.py:317
  210.5 9.1 %collective-permute-start.14 = (bf16[128,2048]{1,0:T(8,128)(2,1)S(1)}, bf16[128,2048]{1,0:T(8,128)(2,1)S(1)}, u32[]{:S(2)}, u32[]{:S(2)}) collective-permute-start(bf16[128,2048]{1,0:T(8,128)(2,1)S(1)} %fusion.2), channel_id=1, source_target_pairs={{0,64},{64,128},{128,192},{192,256},{256,320},{320,384},{384,448},... | collective-permute-start | bytes 1572872 | tf_op jit(solution)/shard_map/ppermute | solution.py:317
  (4 other events, 50.7 us)

commit v9 on v8

--- a/solution.py
+++ b/solution.py
@@ -319,11 +319,11 @@
 
 def summed(value, axis):
     size = lax.axis_size(axis)
-    distance = 1
-    while distance < size:
+    distance = size // 2
+    while distance:
         other = lax.ppermute(value.astype(BF16), axis, [(i, i ^ distance) for i in range(size)])
         value = value.astype(BF16).astype(F32) + other.astype(F32)
-        distance *= 2
+        distance //= 2
     return value
 
 

time: 225 us -> 227 us (level); the launches traced: 221 us -> 225 us
  waiting for transfers between devices: 84.7 us -> 95 us
  starting transfers between devices: 101 us -> 95.5 us
    ppermute x6, waiting for transfers between devices: 18.9 us -> 29.1 us  [summed(): lax.ppermute(value.astype(BF16), axis, [(i, i ^ distance) for i in range(...]
    ppermute x6, starting transfers between devices: 27.9 us -> 22.3 us  [summed(): lax.ppermute(value.astype(BF16), axis, [(i, i ^ distance) for i in range(...]
where the time goes in v9:
time: 227 us; the launch traced here: 225 us
  starting transfers between devices  95.5 us (42%)
  waiting for transfers between devices  95 us (42%)
  Pallas kernels  23.7 us (10%)
  local copies, waits for them, and re-layouts  6.82 us (3%)
    ppermute x14, waiting for transfers between devices, rotated(): lax.ppermute(value, axis, [(i, (i + distance) % size) for i in range(size)])  60.5 us
    ppermute x14, starting transfers between devices, rotated(): lax.ppermute(value, axis, [(i, (i + distance) % size) for i in range(size)])  46.1 us
    ppermute x6, waiting for transfers between devices, summed(): lax.ppermute(value.astype(BF16), axis, [(i, i ^ distance) for i in range(...  29.1 us
    ppermute x6, starting transfers between devices, summed(): lax.ppermute(value.astype(BF16), axis, [(i, i ^ distance) for i in range(...  22.3 us
    pallas_call x3, Pallas kernels, expert_step(): pl.pallas_call(functools.partial(expert_kernel, len(shards), before is no...  17.8 us
    all_to_all x1, starting transfers between devices, on_device(): lax.all_to_all(packed, 'column', split_axis=0, concat_axis=0, tiled=True)  11 us
    ppermute x2, starting transfers between devices, shifted(): return lax.ppermute(block, axis, route)  9.74 us
    all_to_all x1, starting transfers between devices, on_device(): lax.all_to_all(partial.reshape(EXPERTS, ROWS, width), 'column', split_axi...  6.38 us
  transfers between devices with their start and end apart: 24, of which 13 were waited for; matrix products, arithmetic and copies ran while one was open for 3% of the time, Pallas kernels for 6%

profile of v9, /device:TPU:1, one launch (start us, length us, event | category | flops | bytes accessed | tf_op | source)
XLA Modules:
  0.0 225.5 jit_solution(14793816822618926587)
XLA Ops:
  2.3 5.8 %shard_map.175 = (bf16[512,2176]{1,0:T(8,128)(2,1)}, bf16[128,2048]{1,0:T(8,128)(2,1)S(1)}, bf16[128,2048]{1,0:T(8,128)(2,1)S(1)}, f32[128,128]{1,0:T(8,128)S(1)...) custom-call(s32[1,1]{1,0:T(1,128)} %bitcast.first_ref, s32[1,16]{1,0:T(1,128)} %refs_0_.1, ...), custom_call_target="tpu_custom_call" | custom-call | tf_op jit(solution)/shard_map/pallas_call | solution.py:155
  8.1 11.0 %all-to-all-start = ((bf16[8,64,2176]{2,1,0:T(8,128)(2,1)}), bf16[8,64,2176]{2,1,0:T(8,128)(2,1)}, u32[]{:S(2)}, u32[]{:S(2)}) async-start(bf16[8,64,2176]{2,1,0:T(8,128)(2,1)} %bitcast.11), calls=%async_computation | async-start | bytes 4456448 | tf_op jit(solution)/shard_map/all_to_all | solution.py:388
  19.2 3.2 %collective-permute-start = (bf16[1536,256]{1,0:T(8,128)(2,1)S(1)}, bf16[1536,256]{1,0:T(8,128)(2,1)S(1)}, u32[]{:S(2)}, u32[]{:S(2)}) collective-permute-start(bf16[1536,256]{1,0:T(8,128)(2,1)S(1)} %get-tuple-element.18.refs_2_), channel_id=1, source_target_pairs={{0,8},{8,16},{16,24},{24,32},{32,40},{40,48},{48,56},{56,0},{1,9},... | collective-permute-start | bytes 2359304 | tf_op jit(solution)/shard_map/ppermute | solution.py:311
  22.4 3.8 %collective-permute-start.4 = (bf16[1536,256]{1,0:T(8,128)(2,1)S(1)}, bf16[1536,256]{1,0:T(8,128)(2,1)S(1)}, u32[]{:S(2)}, u32[]{:S(2)}) collective-permute-start(bf16[1536,256]{1,0:T(8,128)(2,1)S(1)} %get-tuple-element.19.refs_3_), channel_id=1, source_target_pairs={{0,56},{8,0},{16,8},{24,16},{32,24},{40,32},{48,40},{56,48},{1,57}... | collective-permute-start | bytes 2359304 | tf_op jit(solution)/shard_map/ppermute | solution.py:311
  26.2 1.9 collective-permute-start.8
  28.1 4.6 %collective-permute-start.11 = (bf16[1536,256]{1,0:T(8,128)(2,1)S(1)}, bf16[1536,256]{1,0:T(8,128)(2,1)S(1)}, u32[]{:S(2)}, u32[]{:S(2)}) collective-permute-start(bf16[1536,256]{1,0:T(8,128)(2,1)S(1)} %get-tuple-element.18.refs_2_), channel_id=1, source_target_pairs={{0,56},{8,0},{16,8},{24,16},{32,24},{40,32},{48,40},{56,48},{1,57}... | collective-permute-start | bytes 2359304 | tf_op jit(solution)/shard_map/ppermute | solution.py:311
  32.7 8.6 %collective-permute-done.refs_4_ = bf16[1536,256]{1,0:T(8,128)(2,1)S(1)} collective-permute-done((bf16[1536,256]{1,0:T(8,128)(2,1)S(1)}, bf16[1536,256]{1,0:T(8,128)(2,1)S(1)}, u32[]{:S(2)}, u32[]{:S(2)}) %collective-permute-start) | collective-permute-done | bytes 786464 | tf_op jit(solution)/shard_map/ppermute | solution.py:311
  43.2 4.6 %collective-permute-start.5 = (bf16[1536,256]{1,0:T(8,128)(2,1)S(1)}, bf16[1536,256]{1,0:T(8,128)(2,1)}, u32[]{:S(2)}, u32[]{:S(2)}) collective-permute-start(bf16[1536,256]{1,0:T(8,128)(2,1)S(1)} %collective-permute-done.4.refs_7_), channel_id=1, source_target_pairs={{0,56},{8,0},{16,8},{24,16},{32,24},{40,32},{48,40},{56,48},{1,57}... | collective-permute-start | bytes 2359304 | tf_op jit(solution)/shard_map/ppermute | solution.py:311
  47.8 10.3 %collective-permute-done.8.refs_5_ = bf16[1536,256]{1,0:T(8,128)(2,1)S(1)} collective-permute-done((bf16[1536,256]{1,0:T(8,128)(2,1)S(1)}, bf16[1536,256]{1,0:T(8,128)(2,1)S(1)}, u32[]{:S(2)}, u32[]{:S(2)}) %collective-permute-start.8) | collective-permute-done | bytes 786464 | tf_op jit(solution)/shard_map/ppermute | solution.py:311
  60.1 4.6 %collective-permute-start.12 = (bf16[1536,256]{1,0:T(8,128)(2,1)S(1)}, bf16[1536,256]{1,0:T(8,128)(2,1)}, u32[]{:S(2)}, u32[]{:S(2)}) collective-permute-start(bf16[1536,256]{1,0:T(8,128)(2,1)S(1)} %collective-permute-done.11.refs_6_), channel_id=1, source_target_pairs={{0,56},{8,0},{16,8},{24,16},{32,24},{40,32},{48,40},{56,48},{1,57}... | collective-permute-start | bytes 2359304 | tf_op jit(solution)/shard_map/ppermute | solution.py:311
  64.7 10.3 %collective-permute-done.1.refs_8_ = bf16[1536,256]{1,0:T(8,128)(2,1)} collective-permute-done((bf16[1536,256]{1,0:T(8,128)(2,1)S(1)}, bf16[1536,256]{1,0:T(8,128)(2,1)}, u32[]{:S(2)}, u32[]{:S(2)}) %collective-permute-start.1) | collective-permute-done | bytes 786464 | tf_op jit(solution)/shard_map/ppermute | solution.py:311
  76.9 4.6 %collective-permute-start.6 = (bf16[1536,256]{1,0:T(8,128)(2,1)}, bf16[1536,256]{1,0:T(8,128)(2,1)}, u32[]{:S(2)}, u32[]{:S(2)}) collective-permute-start(bf16[1536,256]{1,0:T(8,128)(2,1)} %collective-permute-done.5.refs_11_), channel_id=1, source_target_pairs={{0,56},{8,0},{16,8},{24,16},{32,24},{40,32},{48,40},{56,48},{1,57}... | collective-permute-start | bytes 2359304 | tf_op jit(solution)/shard_map/ppermute | solution.py:311
  81.7 10.1 %collective-permute-done.9.refs_9_ = bf16[1536,256]{1,0:T(8,128)(2,1)} collective-permute-done((bf16[1536,256]{1,0:T(8,128)(2,1)S(1)}, bf16[1536,256]{1,0:T(8,128)(2,1)}, u32[]{:S(2)}, u32[]{:S(2)}) %collective-permute-start.9) | collective-permute-done | bytes 786464 | tf_op jit(solution)/shard_map/ppermute | solution.py:311
  93.8 4.6 %collective-permute-start.13 = (bf16[1536,256]{1,0:T(8,128)(2,1)}, bf16[1536,256]{1,0:T(8,128)(2,1)}, u32[]{:S(2)}, u32[]{:S(2)}) collective-permute-start(bf16[1536,256]{1,0:T(8,128)(2,1)} %collective-permute-done.12.refs_10_), channel_id=1, source_target_pairs={{0,56},{8,0},{16,8},{24,16},{32,24},{40,32},{48,40},{56,48},{1,57}... | collective-permute-start | bytes 2359304 | tf_op jit(solution)/shard_map/ppermute | solution.py:311
  98.6 10.0 %collective-permute-done.2.refs_2_ = bf16[1536,256]{1,0:T(8,128)(2,1)S(1)} collective-permute-done((bf16[1536,256]{1,0:T(8,128)(2,1)}, bf16[1536,256]{1,0:T(8,128)(2,1)S(1)}, u32[]{:S(2)}, u32[]{:S(2)}) %collective-permute-start.2) | collective-permute-done | bytes 786464 | tf_op jit(solution)/shard_map/ppermute | solution.py:311
  110.5 4.8 %collective-permute-start.7 = (bf16[1536,256]{1,0:T(8,128)(2,1)}, bf16[1536,256]{1,0:T(8,128)(2,1)}, u32[]{:S(2)}, u32[]{:S(2)}) collective-permute-start(bf16[1536,256]{1,0:T(8,128)(2,1)} %collective-permute-done.6.refs_5_), channel_id=1, source_target_pairs={{0,56},{8,0},{16,8},{24,16},{32,24},{40,32},{48,40},{56,48},{1,57}... | collective-permute-start | bytes 2359304 | tf_op jit(solution)/shard_map/ppermute | solution.py:311
  118.5 9.1 %shard_map.176 = (f32[320,2048]{1,0:T(8,128)S(1)}, f32[8,128]{1,0:T(8,128)S(1)}) custom-call(bf16[320,2176]{1,0:T(8,128)(2,1)S(1)} %bitcast.25, bf16[192,2048]{1,0:T(8,128)(2,1)S(1)} %bitcast.28, bf16[1536,256]{1,0:T(8,128)(2,1)} %copy-done.1, bf16[1536,256]{1,0:T(8,128)(2,1)} %copy-done.2, bf16[1536,256]{1,0:T(8,128)(2,1)} %copy-done.8, ...), custom_call_target="tpu_custom_call" | custom-call | flops 3690987520 | bytes 12664832 | tf_op jit(solution)/shard_map/pallas_call | solution.py:294
  127.7 4.5 %shard_map.177 = (f32[320,2048]{1,0:T(8,128)S(1)}, f32[8,128]{1,0:T(8,128)S(1)}) custom-call(bf16[320,2176]{1,0:T(8,128)(2,1)S(1)} %bitcast.26, bf16[192,2048]{1,0:T(8,128)(2,1)S(1)} %bitcast.29, bf16[1536,256]{1,0:T(8,128)(2,1)} %copy-done.4, bf16[1536,256]{1,0:T(8,128)(2,1)} %collective-permute-done.10.refs_3_, ...), custom_call_target="tpu_custom_call" | custom-call | flops 1476395008 | bytes 10571776 | tf_op jit(solution)/shard_map/pallas_call | solution.py:294
  132.1 10.3 %collective-permute-done.3.refs_2_ = bf16[1536,256]{1,0:T(8,128)(2,1)} collective-permute-done((bf16[1536,256]{1,0:T(8,128)(2,1)S(1)}, bf16[1536,256]{1,0:T(8,128)(2,1)}, u32[]{:S(2)}, u32[]{:S(2)}) %collective-permute-start.3) | collective-permute-done | bytes 786464 | tf_op jit(solution)/shard_map/ppermute | solution.py:311
  143.3 4.3 %shard_map.178 = (bf16[320,2048]{1,0:T(8,128)(2,1)}, f32[20,2048]{1,0:T(8,128)S(1)}) custom-call(bf16[320,2176]{1,0:T(8,128)(2,1)S(1)} %bitcast.27, bf16[192,2048]{1,0:T(8,128)(2,1)S(1)} %bitcast.30, bf16[1536,256]{1,0:T(8,128)(2,1)} %collective-permute-done.3.refs_2_, bf16[1536,256]{1,0:T(8,128)(2,1)} %collective-permute-done.7.refs_3_, ...), custom_call_target="tpu_custom_call" | custom-call | flops 738197504 | bytes 9334864 | tf_op jit(solution)/shard_map/pallas_call | solution.py:294
  147.6 6.6 %collective-permute-start.16 = (bf16[20,2048]{1,0:T(8,128)(2,1)S(1)}, bf16[20,2048]{1,0:T(8,128)(2,1)S(1)}, u32[]{:S(2)}, u32[]{:S(2)}) collective-permute-start(bf16[20,2048]{1,0:T(8,128)(2,1)S(1)} %convert_element_type.105), channel_id=1, source_target_pairs={{0,32},{8,40},{16,48},{24,56},{32,0},{40,8},{48,16},{56,24},{1,33}... | collective-permute-start | bytes 245768 | tf_op jit(solution)/shard_map/ppermute | solution.py:324
  154.2 6.4 %all-to-all-start.1 = ((bf16[8,40,2048]{2,1,0:T(8,128)(2,1)}), bf16[8,40,2048]{2,1,0:T(8,128)(2,1)S(1)}, u32[]{:S(2)}, u32[]{:S(2)}) async-start(bf16[8,40,2048]{2,1,0:T(8,128)(2,1)} %bitcast.14), calls=%async_computation.1 | async-start | bytes 2621440 | tf_op jit(solution)/shard_map/all_to_all | solution.py:404
  160.6 2.3 %collective-permute-start.17 = (bf16[20,2048]{1,0:T(8,128)(2,1)S(1)}, bf16[20,2048]{1,0:T(8,128)(2,1)S(1)}, u32[]{:S(2)}, u32[]{:S(2)}) collective-permute-start(bf16[20,2048]{1,0:T(8,128)(2,1)S(1)} %add_convert_fusion.5), channel_id=1, source_target_pairs={{0,16},{8,24},{16,0},{24,8},{32,48},{40,56},{48,32},{56,40},{1,17}... | collective-permute-start | bytes 245768 | tf_op jit(solution)/shard_map/ppermute | solution.py:324
  163.0 5.0 %collective-permute-done.17 = bf16[20,2048]{1,0:T(8,128)(2,1)S(1)} collective-permute-done((bf16[20,2048]{1,0:T(8,128)(2,1)S(1)}, bf16[20,2048]{1,0:T(8,128)(2,1)S(1)}, u32[]{:S(2)}, u32[]{:S(2)}) %collective-permute-start.17) | collective-permute-done | bytes 81952 | tf_op jit(solution)/shard_map/ppermute | solution.py:324
  168.0 1.9 collective-permute-start.18
  169.9 3.7 %collective-permute-done.18 = bf16[20,2048]{1,0:T(8,128)(2,1)S(1)} collective-permute-done((bf16[20,2048]{1,0:T(8,128)(2,1)S(1)}, bf16[20,2048]{1,0:T(8,128)(2,1)S(1)}, u32[]{:S(2)}, u32[]{:S(2)}) %collective-permute-start.18) | collective-permute-done | bytes 81952 | tf_op jit(solution)/shard_map/ppermute | solution.py:324
  173.7 7.6 %collective-permute-start.19 = (bf16[20,2048]{1,0:T(8,128)(2,1)S(1)}, bf16[20,2048]{1,0:T(8,128)(2,1)S(1)}, u32[]{:S(2)}, u32[]{:S(2)}) collective-permute-start(bf16[20,2048]{1,0:T(8,128)(2,1)S(1)} %add_convert_fusion.3), channel_id=1, source_target_pairs={{0,4},{1,5},{2,6},{3,7},{4,0},{5,1},{6,2},{7,3},{8,12},{9,13},{10,... | collective-permute-start | bytes 245768 | tf_op jit(solution)/shard_map/ppermute | solution.py:324
  181.3 16.1 %collective-permute-done.19 = bf16[20,2048]{1,0:T(8,128)(2,1)S(1)} collective-permute-done((bf16[20,2048]{1,0:T(8,128)(2,1)S(1)}, bf16[20,2048]{1,0:T(8,128)(2,1)S(1)}, u32[]{:S(2)}, u32[]{:S(2)}) %collective-permute-start.19) | collective-permute-done | bytes 81952 | tf_op jit(solution)/shard_map/ppermute | solution.py:324
  199.4 4.3 %collective-permute-done.20 = bf16[20,2048]{1,0:T(8,128)(2,1)S(1)} collective-permute-done((bf16[20,2048]{1,0:T(8,128)(2,1)S(1)}, bf16[20,2048]{1,0:T(8,128)(2,1)S(1)}, u32[]{:S(2)}, u32[]{:S(2)}) %collective-permute-start.20) | collective-permute-done | bytes 81952 | tf_op jit(solution)/shard_map/ppermute | solution.py:324
  207.5 6.7 %collective-permute-start.15 = (bf16[128,2048]{1,0:T(8,128)(2,1)}, bf16[128,2048]{1,0:T(8,128)(2,1)S(1)}, u32[]{:S(2)}, u32[]{:S(2)}) collective-permute-start(bf16[128,2048]{1,0:T(8,128)(2,1)} %fusion.6), channel_id=1, source_target_pairs={{64,0},{128,64},{192,128},{256,192},{320,256},{384,320},{448,384},... | collective-permute-start | bytes 1572872 | tf_op jit(solution)/shard_map/ppermute | solution.py:317
  214.8 3.0 %collective-permute-start.14 = (bf16[128,2048]{1,0:T(8,128)(2,1)S(1)}, bf16[128,2048]{1,0:T(8,128)(2,1)S(1)}, u32[]{:S(2)}, u32[]{:S(2)}) collective-permute-start(bf16[128,2048]{1,0:T(8,128)(2,1)S(1)} %fusion.2), channel_id=1, source_target_pairs={{0,64},{64,128},{128,192},{192,256},{256,320},{320,384},{384,448},... | collective-permute-start | bytes 1572872 | tf_op jit(solution)/shard_map/ppermute | solution.py:317
  218.6 3.8 %collective-permute-done.15 = bf16[128,2048]{1,0:T(8,128)(2,1)S(1)} collective-permute-done((bf16[128,2048]{1,0:T(8,128)(2,1)}, bf16[128,2048]{1,0:T(8,128)(2,1)S(1)}, u32[]{:S(2)}, u32[]{:S(2)}) %collective-permute-start.15) | collective-permute-done | bytes 524320 | tf_op jit(solution)/shard_map/ppermute | solution.py:317
  (73 shorter events, 25.9 us)
Async XLA Ops:
  8.1 20.0 %copy-start.1 = (bf16[1536,256]{1,0:T(8,128)(2,1)}, bf16[1536,256]{1,0:T(8,128)(2,1)S(1)}, u32[]{:S(2)}) copy-start(bf16[1536,256]{1,0:T(8,128)(2,1)S(1)} %get-tuple-element.18.refs_2_) | copy-start | bytes 2359300
  8.1 73.4 %copy-start.5 = (bf16[1,2,10,2048]{3,1,2,0:T(2,128)(2,1)S(1)}, bf16[1,2,10,2048]{3,1,2,0:T(2,128)(2,1)}, u32[]{:S(2)}) copy-start(bf16[1,2,10,2048]{3,1,2,0:T(2,128)(2,1)} %param.27) | copy-start | bytes 245764
  8.1 107.4 %copy-start.3 = (bf16[1,128,2048]{2,1,0:T(8,128)(2,1)S(1)}, bf16[1,128,2048]{2,1,0:T(8,128)(2,1)}, u32[]{:S(2)}) copy-start(bf16[1,128,2048]{2,1,0:T(8,128)(2,1)} %param.26) | copy-start | bytes 1572868
  8.1 107.7 %all-to-all-start = ((bf16[8,64,2176]{2,1,0:T(8,128)(2,1)}), bf16[8,64,2176]{2,1,0:T(8,128)(2,1)}, u32[]{:S(2)}, u32[]{:S(2)}) async-start(bf16[8,64,2176]{2,1,0:T(8,128)(2,1)} %bitcast.11), calls=%async_computation | async-start | bytes 4456448 | tf_op jit(solution)/shard_map/all_to_all | solution.py:388
  19.2 22.1 %collective-permute-start = (bf16[1536,256]{1,0:T(8,128)(2,1)S(1)}, bf16[1536,256]{1,0:T(8,128)(2,1)S(1)}, u32[]{:S(2)}, u32[]{:S(2)}) collective-permute-start(bf16[1536,256]{1,0:T(8,128)(2,1)S(1)} %get-tuple-element.18.refs_2_), channel_id=1, source_target_pairs={{0,8},{8,16},{16,24},{24,32},{32,40},{40,48},{48,56},{56,0},{1,9},... | collective-permute-start | bytes 2359304 | tf_op jit(solution)/shard_map/ppermute | solution.py:311
  22.4 20.9 %collective-permute-start.4 = (bf16[1536,256]{1,0:T(8,128)(2,1)S(1)}, bf16[1536,256]{1,0:T(8,128)(2,1)S(1)}, u32[]{:S(2)}, u32[]{:S(2)}) collective-permute-start(bf16[1536,256]{1,0:T(8,128)(2,1)S(1)} %get-tuple-element.19.refs_3_), channel_id=1, source_target_pairs={{0,56},{8,0},{16,8},{24,16},{32,24},{40,32},{48,40},{56,48},{1,57}... | collective-permute-start | bytes 2359304 | tf_op jit(solution)/shard_map/ppermute | solution.py:311
  26.2 32.0 %collective-permute-start.8 = (bf16[1536,256]{1,0:T(8,128)(2,1)S(1)}, bf16[1536,256]{1,0:T(8,128)(2,1)S(1)}, u32[]{:S(2)}, u32[]{:S(2)}) collective-permute-start(bf16[1536,256]{1,0:T(8,128)(2,1)S(1)} %get-tuple-element.19.refs_3_), channel_id=1, source_target_pairs={{0,8},{8,16},{16,24},{24,32},{32,40},{40,48},{48,56},{56,0},{1,9},... | collective-permute-start | bytes 2359304 | tf_op jit(solution)/shard_map/ppermute | solution.py:311
  28.1 31.9 %collective-permute-start.11 = (bf16[1536,256]{1,0:T(8,128)(2,1)S(1)}, bf16[1536,256]{1,0:T(8,128)(2,1)S(1)}, u32[]{:S(2)}, u32[]{:S(2)}) collective-permute-start(bf16[1536,256]{1,0:T(8,128)(2,1)S(1)} %get-tuple-element.18.refs_2_), channel_id=1, source_target_pairs={{0,56},{8,0},{16,8},{24,16},{32,24},{40,32},{48,40},{56,48},{1,57}... | collective-permute-start | bytes 2359304 | tf_op jit(solution)/shard_map/ppermute | solution.py:311
  41.3 35.6 %copy-start.8 = (bf16[1536,256]{1,0:T(8,128)(2,1)}, bf16[1536,256]{1,0:T(8,128)(2,1)S(1)}, u32[]{:S(2)}) copy-start(bf16[1536,256]{1,0:T(8,128)(2,1)S(1)} %collective-permute-done.refs_4_) | copy-start | bytes 2359300
  41.3 33.7 %collective-permute-start.1 = (bf16[1536,256]{1,0:T(8,128)(2,1)S(1)}, bf16[1536,256]{1,0:T(8,128)(2,1)}, u32[]{:S(2)}, u32[]{:S(2)}) collective-permute-start(bf16[1536,256]{1,0:T(8,128)(2,1)S(1)} %collective-permute-done.refs_4_), channel_id=1, source_target_pairs={{0,8},{8,16},{16,24},{24,32},{32,40},{40,48},{48,56},{56,0},{1,9},... | collective-permute-start | bytes 2359304 | tf_op jit(solution)/shard_map/ppermute | solution.py:311
  43.2 33.7 %copy-start.9 = (bf16[1536,256]{1,0:T(8,128)(2,1)}, bf16[1536,256]{1,0:T(8,128)(2,1)S(1)}, u32[]{:S(2)}) copy-start(bf16[1536,256]{1,0:T(8,128)(2,1)S(1)} %collective-permute-done.4.refs_7_) | copy-start | bytes 2359300
  43.2 33.7 %collective-permute-start.5 = (bf16[1536,256]{1,0:T(8,128)(2,1)S(1)}, bf16[1536,256]{1,0:T(8,128)(2,1)}, u32[]{:S(2)}, u32[]{:S(2)}) collective-permute-start(bf16[1536,256]{1,0:T(8,128)(2,1)S(1)} %collective-permute-done.4.refs_7_), channel_id=1, source_target_pairs={{0,56},{8,0},{16,8},{24,16},{32,24},{40,32},{48,40},{56,48},{1,57}... | collective-permute-start | bytes 2359304 | tf_op jit(solution)/shard_map/ppermute | solution.py:311
  58.1 40.2 %copy-start.10 = (bf16[1536,256]{1,0:T(8,128)(2,1)}, bf16[1536,256]{1,0:T(8,128)(2,1)S(1)}, u32[]{:S(2)}) copy-start(bf16[1536,256]{1,0:T(8,128)(2,1)S(1)} %collective-permute-done.8.refs_5_) | copy-start | bytes 2359300
  58.1 33.7 %collective-permute-start.9 = (bf16[1536,256]{1,0:T(8,128)(2,1)S(1)}, bf16[1536,256]{1,0:T(8,128)(2,1)}, u32[]{:S(2)}, u32[]{:S(2)}) collective-permute-start(bf16[1536,256]{1,0:T(8,128)(2,1)S(1)} %collective-permute-done.8.refs_5_), channel_id=1, source_target_pairs={{0,8},{8,16},{16,24},{24,32},{32,40},{40,48},{48,56},{56,0},{1,9},... | collective-permute-start | bytes 2359304 | tf_op jit(solution)/shard_map/ppermute | solution.py:311
  60.1 38.3 %copy-start.11 = (bf16[1536,256]{1,0:T(8,128)(2,1)}, bf16[1536,256]{1,0:T(8,128)(2,1)S(1)}, u32[]{:S(2)}) copy-start(bf16[1536,256]{1,0:T(8,128)(2,1)S(1)} %collective-permute-done.11.refs_6_) | copy-start | bytes 2359300
  60.1 33.7 %collective-permute-start.12 = (bf16[1536,256]{1,0:T(8,128)(2,1)S(1)}, bf16[1536,256]{1,0:T(8,128)(2,1)}, u32[]{:S(2)}, u32[]{:S(2)}) collective-permute-start(bf16[1536,256]{1,0:T(8,128)(2,1)S(1)} %collective-permute-done.11.refs_6_), channel_id=1, source_target_pairs={{0,56},{8,0},{16,8},{24,16},{32,24},{40,32},{48,40},{56,48},{1,57}... | collective-permute-start | bytes 2359304 | tf_op jit(solution)/shard_map/ppermute | solution.py:311
  75.0 33.6 %collective-permute-start.2 = (bf16[1536,256]{1,0:T(8,128)(2,1)}, bf16[1536,256]{1,0:T(8,128)(2,1)S(1)}, u32[]{:S(2)}, u32[]{:S(2)}) collective-permute-start(bf16[1536,256]{1,0:T(8,128)(2,1)} %collective-permute-done.1.refs_8_), channel_id=1, source_target_pairs={{0,8},{8,16},{16,24},{24,32},{32,40},{40,48},{48,56},{56,0},{1,9},... | collective-permute-start | bytes 2359304 | tf_op jit(solution)/shard_map/ppermute | solution.py:311
  76.9 33.6 %collective-permute-start.6 = (bf16[1536,256]{1,0:T(8,128)(2,1)}, bf16[1536,256]{1,0:T(8,128)(2,1)}, u32[]{:S(2)}, u32[]{:S(2)}) collective-permute-start(bf16[1536,256]{1,0:T(8,128)(2,1)} %collective-permute-done.5.refs_11_), channel_id=1, source_target_pairs={{0,56},{8,0},{16,8},{24,16},{32,24},{40,32},{48,40},{56,48},{1,57}... | collective-permute-start | bytes 2359304 | tf_op jit(solution)/shard_map/ppermute | solution.py:311
  91.8 35.8 %collective-permute-start.10 = (bf16[1536,256]{1,0:T(8,128)(2,1)}, bf16[1536,256]{1,0:T(8,128)(2,1)}, u32[]{:S(2)}, u32[]{:S(2)}) collective-permute-start(bf16[1536,256]{1,0:T(8,128)(2,1)} %collective-permute-done.9.refs_9_), channel_id=1, source_target_pairs={{0,8},{8,16},{16,24},{24,32},{32,40},{40,48},{48,56},{56,0},{1,9},... | collective-permute-start | bytes 2359304 | tf_op jit(solution)/shard_map/ppermute | solution.py:311
  93.8 33.9 %collective-permute-start.13 = (bf16[1536,256]{1,0:T(8,128)(2,1)}, bf16[1536,256]{1,0:T(8,128)(2,1)}, u32[]{:S(2)}, u32[]{:S(2)}) collective-permute-start(bf16[1536,256]{1,0:T(8,128)(2,1)} %collective-permute-done.12.refs_10_), channel_id=1, source_target_pairs={{0,56},{8,0},{16,8},{24,16},{32,24},{40,32},{48,40},{56,48},{1,57}... | collective-permute-start | bytes 2359304 | tf_op jit(solution)/shard_map/ppermute | solution.py:311
  108.6 33.8 %collective-permute-start.3 = (bf16[1536,256]{1,0:T(8,128)(2,1)S(1)}, bf16[1536,256]{1,0:T(8,128)(2,1)}, u32[]{:S(2)}, u32[]{:S(2)}) collective-permute-start(bf16[1536,256]{1,0:T(8,128)(2,1)S(1)} %collective-permute-done.2.refs_2_), channel_id=1, source_target_pairs={{0,8},{8,16},{16,24},{24,32},{32,40},{40,48},{48,56},{56,0},{1,9},... | collective-permute-start | bytes 2359304 | tf_op jit(solution)/shard_map/ppermute | solution.py:311
  110.5 32.7 %collective-permute-start.7 = (bf16[1536,256]{1,0:T(8,128)(2,1)}, bf16[1536,256]{1,0:T(8,128)(2,1)}, u32[]{:S(2)}, u32[]{:S(2)}) collective-permute-start(bf16[1536,256]{1,0:T(8,128)(2,1)} %collective-permute-done.6.refs_5_), channel_id=1, source_target_pairs={{0,56},{8,0},{16,8},{24,16},{32,24},{40,32},{48,40},{56,48},{1,57}... | collective-permute-start | bytes 2359304 | tf_op jit(solution)/shard_map/ppermute | solution.py:311
  147.6 13.0 %collective-permute-start.16 = (bf16[20,2048]{1,0:T(8,128)(2,1)S(1)}, bf16[20,2048]{1,0:T(8,128)(2,1)S(1)}, u32[]{:S(2)}, u32[]{:S(2)}) collective-permute-start(bf16[20,2048]{1,0:T(8,128)(2,1)S(1)} %convert_element_type.105), channel_id=1, source_target_pairs={{0,32},{8,40},{16,48},{24,56},{32,0},{40,8},{48,16},{56,24},{1,33}... | collective-permute-start | bytes 245768 | tf_op jit(solution)/shard_map/ppermute | solution.py:324
  154.2 51.5 %all-to-all-start.1 = ((bf16[8,40,2048]{2,1,0:T(8,128)(2,1)}), bf16[8,40,2048]{2,1,0:T(8,128)(2,1)S(1)}, u32[]{:S(2)}, u32[]{:S(2)}) async-start(bf16[8,40,2048]{2,1,0:T(8,128)(2,1)} %bitcast.14), calls=%async_computation.1 | async-start | bytes 2621440 | tf_op jit(solution)/shard_map/all_to_all | solution.py:404
  160.6 45.1 %copy-start.6 = (f32[1,128,1]{1,2,0:T(1,128)S(1)}, f32[1,128,1]{1,2,0:T(1,128)}, u32[]{:S(2)}) copy-start(f32[1,128,1]{1,2,0:T(1,128)} %param.23) | copy-start | bytes 1540
  160.6 7.3 %collective-permute-start.17 = (bf16[20,2048]{1,0:T(8,128)(2,1)S(1)}, bf16[20,2048]{1,0:T(8,128)(2,1)S(1)}, u32[]{:S(2)}, u32[]{:S(2)}) collective-permute-start(bf16[20,2048]{1,0:T(8,128)(2,1)S(1)} %add_convert_fusion.5), channel_id=1, source_target_pairs={{0,16},{8,24},{16,0},{24,8},{32,48},{40,56},{48,32},{56,40},{1,17}... | collective-permute-start | bytes 245768 | tf_op jit(solution)/shard_map/ppermute | solution.py:324
  168.0 5.7 %collective-permute-start.18 = (bf16[20,2048]{1,0:T(8,128)(2,1)S(1)}, bf16[20,2048]{1,0:T(8,128)(2,1)S(1)}, u32[]{:S(2)}, u32[]{:S(2)}) collective-permute-start(bf16[20,2048]{1,0:T(8,128)(2,1)S(1)} %add_convert_fusion.4), channel_id=1, source_target_pairs={{0,8},{8,0},{16,24},{24,16},{32,40},{40,32},{48,56},{56,48},{1,9},... | collective-permute-start | bytes 245768 | tf_op jit(solution)/shard_map/ppermute | solution.py:324
  173.7 23.8 %collective-permute-start.19 = (bf16[20,2048]{1,0:T(8,128)(2,1)S(1)}, bf16[20,2048]{1,0:T(8,128)(2,1)S(1)}, u32[]{:S(2)}, u32[]{:S(2)}) collective-permute-start(bf16[20,2048]{1,0:T(8,128)(2,1)S(1)} %add_convert_fusion.3), channel_id=1, source_target_pairs={{0,4},{1,5},{2,6},{3,7},{4,0},{5,1},{6,2},{7,3},{8,12},{9,13},{10,... | collective-permute-start | bytes 245768 | tf_op jit(solution)/shard_map/ppermute | solution.py:324
  197.5 6.3 %collective-permute-start.20 = (bf16[20,2048]{1,0:T(8,128)(2,1)S(1)}, bf16[20,2048]{1,0:T(8,128)(2,1)S(1)}, u32[]{:S(2)}, u32[]{:S(2)}) collective-permute-start(bf16[20,2048]{1,0:T(8,128)(2,1)S(1)} %add_convert_fusion.2), channel_id=1, source_target_pairs={{0,2},{1,3},{2,0},{3,1},{4,6},{5,7},{6,4},{7,5},{8,10},{9,11},{10,... | collective-permute-start | bytes 245768 | tf_op jit(solution)/shard_map/ppermute | solution.py:324
  203.8 14.0 %collective-permute-start.21 = (bf16[20,2048]{1,0:T(8,128)(2,1)S(1)}, bf16[20,2048]{1,0:T(8,128)(2,1)S(1)}, u32[]{:S(2)}, u32[]{:S(2)}) collective-permute-start(bf16[20,2048]{1,0:T(8,128)(2,1)S(1)} %add_convert_fusion.1), channel_id=1, source_target_pairs={{0,1},{1,0},{2,3},{3,2},{4,5},{5,4},{6,7},{7,6},{8,9},{9,8},{10,11... | collective-permute-start | bytes 245768 | tf_op jit(solution)/shard_map/ppermute | solution.py:324
  207.5 14.9 %collective-permute-start.15 = (bf16[128,2048]{1,0:T(8,128)(2,1)}, bf16[128,2048]{1,0:T(8,128)(2,1)S(1)}, u32[]{:S(2)}, u32[]{:S(2)}) collective-permute-start(bf16[128,2048]{1,0:T(8,128)(2,1)} %fusion.6), channel_id=1, source_target_pairs={{64,0},{128,64},{192,128},{256,192},{320,256},{384,320},{448,384},... | collective-permute-start | bytes 1572872 | tf_op jit(solution)/shard_map/ppermute | solution.py:317
  214.8 9.1 %collective-permute-start.14 = (bf16[128,2048]{1,0:T(8,128)(2,1)S(1)}, bf16[128,2048]{1,0:T(8,128)(2,1)S(1)}, u32[]{:S(2)}, u32[]{:S(2)}) collective-permute-start(bf16[128,2048]{1,0:T(8,128)(2,1)S(1)} %fusion.2), channel_id=1, source_target_pairs={{0,64},{64,128},{128,192},{192,256},{256,320},{320,384},{384,448},... | collective-permute-start | bytes 1572872 | tf_op jit(solution)/shard_map/ppermute | solution.py:317
  (4 other events, 50.4 us)
